TPU v7x, 256 devices: a whole 4x4x8 slice. The times are simulated.
256 devices in a mesh: depth: 8 (over y, x_lo), tile: 32 (over z, x_hi, core).
Axes of the slice: x: 4 (x_hi: 2, x_lo: 2; x = x_hi * 2 + x_lo), y: 4, z: 8, core: 2. Of those that a mesh axis runs over, the one named last changes fastest.
Arguments:
- warm_field: float32 [16, 2, 16, 256, 256], P(None, None, 'depth', 'tile'), may hold values from -6 to 6
- slowness_sq: float32 [16, 256, 256], P('depth', 'tile'), may hold values from 1.2 to 2.6
- adjoint_field: float32 [16, 2, 16, 256, 256], P(None, None, 'depth', 'tile'), may hold values from -6 to 6
- observed: float32 [16, 2, 256], replicated, may hold values from -6 to 6
- source_cell: int32 [16], replicated, may hold values from 0 to 1048575
- receiver_cell: int32 [16, 256], replicated, may hold values from 0 to 1048575
- pml_width: int32 [4], replicated, may hold values from 2 to 4
Outputs:
- new_field: float32 [16, 2, 16, 256, 256], P(None, None, 'depth', 'tile')
- misfit: float32 [16], replicated
- gradient: float32 [16, 256, 256], P('depth', 'tile')
All inputs are finite; a program needn't handle non-finite values.
Results may differ from a plain program's by a relative error of at most 0.00002.
Values sent between devices are 32-bit elements; how exact they have to be, the bound alone decides.
A program may use at most 64 MiB of HBM per device.

v0:
```python
import jax
import jax.numpy as jnp
from jax import lax
from jax.sharding import PartitionSpec as P

WAVE_SCALE = 1.9
PML_DAMP = 2.0
SOURCE_AMPLITUDE = 25.0
SHIFT_IMAG = 0.5
CENTER_WEIGHT = 128.0 / 30.0
LUMPED_DIAG = 2.0
LAP_WEIGHTS = (0.0, 14.0 / 30.0, 3.0 / 30.0, 1.0 / 30.0)
MASS_WEIGHTS = (1.0 / 6.0, 2.0 / 3.0, 1.0 / 6.0)


def extended(shard, sides, width):
    for axis, dim in sides:
        size, length = (lax.axis_size(axis), shard.shape[dim])
        up = [(i, (i + 1) % size) for i in range(size - 1)]
        down = [(j, i) for i, j in up]
        last = lax.slice_in_dim(shard, length - width, length, axis=dim)
        leading = lax.slice_in_dim(shard, 0, width, axis=dim)
        before = lax.ppermute(last, axis, up)
        after = lax.ppermute(leading, axis, down)
        shard = jnp.concatenate([before, shard, after], axis=dim)
    return shard


def shifted(value, axis, steps):
    count = lax.axis_size(axis)
    leading, last = (max(0, -steps), min(count, count - steps))
    return lax.ppermute(value, axis, [(source, source + steps) for source in range(leading, last)])


def damping_ramp(distance, extent):
    fraction = jnp.maximum((extent - distance) / extent, 0.0)
    return fraction * fraction


def damping_field(pml_width, depth_pos, width_pos, full_depth, full_width):
    widths = pml_width.astype(jnp.float32)
    depth_part = damping_ramp(depth_pos, widths[0]) + damping_ramp(
        full_depth - 1.0 - depth_pos, widths[1]
    )
    width_part = damping_ramp(width_pos, widths[2]) + damping_ramp(
        full_width - 1.0 - width_pos, widths[3]
    )
    return PML_DAMP * (depth_part[:, None] + width_part[None, :])


def pad_long(values):
    return jnp.pad(values, [(0, 0)] * (values.ndim - 1) + [(1, 1)])


def laplacian_from_padded(padded, depth_len, width_len, long_len):
    summed = CENTER_WEIGHT * padded[..., 1 : 1 + depth_len, 1 : 1 + width_len, 1 : 1 + long_len]
    for off_depth in (-1, 0, 1):
        for off_width in (-1, 0, 1):
            for off_long in (-1, 0, 1):
                order_no = abs(off_depth) + abs(off_width) + abs(off_long)
                if order_no > 0:
                    summed = (
                        summed
                        - LAP_WEIGHTS[order_no]
                        * padded[
                            ...,
                            1 + off_depth : 1 + off_depth + depth_len,
                            1 + off_width : 1 + off_width + width_len,
                            1 + off_long : 1 + off_long + long_len,
                        ]
                    )
    return summed


def lateral_smooth(padded, width_len, long_len):
    summed = None
    for off_width in range(3):
        for off_long in range(3):
            weighted = (
                MASS_WEIGHTS[off_width]
                * MASS_WEIGHTS[off_long]
                * padded[..., off_width : off_width + width_len, off_long : off_long + long_len]
            )
            summed = weighted if summed is None else summed + weighted
    return summed


def plane_coupling(padded, width_len, long_len):
    summed = None
    for off_width in range(3):
        for off_long in range(3):
            order_no = 1 + (off_width != 1) + (off_long != 1)
            weighted = (
                LAP_WEIGHTS[order_no]
                * padded[..., off_width : off_width + width_len, off_long : off_long + long_len]
            )
            summed = weighted if summed is None else summed + weighted
    return summed


def combine_operator(negative, mass, damping):
    real_out = negative[:, 0] - WAVE_SCALE * (mass[:, 0] - damping * mass[:, 1])
    imag_out = negative[:, 1] - WAVE_SCALE * (mass[:, 1] + damping * mass[:, 0])
    return jnp.stack([real_out, imag_out], axis=1)


def inverse_diagonal(slowness, damping):
    scaled = WAVE_SCALE * MASS_WEIGHTS[1] * MASS_WEIGHTS[1] * slowness
    diag_re = LUMPED_DIAG - scaled * (1.0 + SHIFT_IMAG * damping)
    diag_im = -scaled * (damping + SHIFT_IMAG)
    norm_sq = diag_re * diag_re + diag_im * diag_im
    return (diag_re / norm_sq, -diag_im / norm_sq)


def complex_scale(inv_re, inv_im, values):
    real_part = values[:, 0]
    imag_part = values[:, 1]
    return jnp.stack(
        [inv_re * real_part - inv_im * imag_part, inv_re * imag_part + inv_im * real_part], axis=1
    )


def per_device(
    warm_field, slowness_sq, adjoint_field, observed, source_cell, receiver_cell, pml_width
):
    shot_count, _, layer_len, width_len, long_len = warm_field.shape
    depth_index = lax.axis_index("depth")
    tile_index = lax.axis_index("tile")
    depth_count = lax.axis_size("depth")
    tile_count = lax.axis_size("tile")
    full_depth = layer_len * depth_count
    full_width = width_len * tile_count
    depth_cells = depth_index * layer_len + jnp.arange(layer_len, dtype=jnp.int32)
    width_cells = tile_index * width_len + jnp.arange(width_len, dtype=jnp.int32)
    width_wide = (tile_index * width_len - 1 + jnp.arange(width_len + 2, dtype=jnp.int32)).astype(
        jnp.float32
    )
    damping_wide = damping_field(
        pml_width, depth_cells.astype(jnp.float32), width_wide, full_depth * 1.0, full_width * 1.0
    )[:, :, None]
    damping = damping_wide[:, 1:-1]
    slowness_wide = extended(slowness_sq, (("tile", 1),), 1)

    def apply_operator(values):
        padded = extended(values, (("depth", 2), ("tile", 3)), 1)
        negative = laplacian_from_padded(pad_long(padded), layer_len, width_len, long_len)
        mass = lateral_smooth(pad_long(padded[:, :, 1:-1] * slowness_wide), width_len, long_len)
        return combine_operator(negative, mass, damping)

    cell_index = (
        depth_cells[:, None, None] * full_width + width_cells[None, :, None]
    ) * long_len + jnp.arange(long_len, dtype=jnp.int32)[None, None, :]
    hits = cell_index[None] == source_cell[:, None, None, None]
    source_re = jnp.where(hits, SOURCE_AMPLITUDE, 0.0).astype(jnp.float32)
    forcing = jnp.stack([source_re, jnp.zeros_like(source_re)], axis=1)
    residual = forcing - apply_operator(warm_field)
    inv_re, inv_im = inverse_diagonal(slowness_sq, damping)

    def couple(plane_in):
        with_rims = extended(plane_in, (("tile", 2),), 1)
        return plane_coupling(pad_long(with_rims), width_len, long_len)

    def down_section(source_part, incoming):
        previous = incoming
        layers_out = []
        for layer_no in range(layer_len):
            source_term = source_part[:, :, layer_no] + couple(previous)
            previous = complex_scale(inv_re[layer_no], inv_im[layer_no], source_term)
            layers_out.append(previous)
        return jnp.stack(layers_out, axis=2)

    def up_section(downward_part, incoming):
        previous = incoming
        layers_out = [None] * layer_len
        for layer_no in range(layer_len - 1, -1, -1):
            previous = downward_part[:, :, layer_no] + complex_scale(
                inv_re[layer_no], inv_im[layer_no], couple(previous)
            )
            layers_out[layer_no] = previous
        return jnp.stack(layers_out, axis=2)

    groups = 1
    per_group = shot_count // groups

    def run_chain(inputs, downward):
        position = depth_index if downward else depth_count - 1 - depth_index

        def segment_body(segment_no, state_pair):
            result, outgoing = state_pair
            if downward:
                incoming = shifted(outgoing, "depth", 1)
            else:
                incoming = shifted(outgoing, "depth", -1)
            group_no = segment_no - position
            is_valid = jnp.logical_and(group_no >= 0, group_no < groups)
            group_start = jnp.clip(group_no, 0, groups - 1) * per_group
            if downward:
                updated = down_section(inputs, incoming)
                edge_plane = updated[:, :, layer_len - 1]
            else:
                updated = up_section(inputs, incoming)
                edge_plane = updated[:, :, 0]
            current = result
            result = lax.dynamic_update_slice_in_dim(
                result, jnp.where(is_valid, updated, current), group_start, 0
            )
            outgoing = jnp.where(is_valid, edge_plane, outgoing)
            return (result, outgoing)

        initial = (
            jnp.zeros_like(inputs),
            jnp.zeros((per_group, 2, width_len, long_len), jnp.float32),
        )
        final_pair = lax.fori_loop(0, depth_count + groups - 1, segment_body, initial)
        return final_pair[0]

    downward = run_chain(residual, True)
    search = run_chain(downward, False)
    image_field = apply_operator(search)
    local_real = jnp.sum(
        image_field[:, 0] * residual[:, 0] + image_field[:, 1] * residual[:, 1], axis=(1, 2, 3)
    )
    local_imag = jnp.sum(
        image_field[:, 0] * residual[:, 1] - image_field[:, 1] * residual[:, 0], axis=(1, 2, 3)
    )
    local_norm = jnp.sum(
        image_field[:, 0] * image_field[:, 0] + image_field[:, 1] * image_field[:, 1],
        axis=(1, 2, 3),
    )
    dot_real, dot_imag, image_norm = lax.psum(
        (local_real, local_imag, local_norm), ("depth", "tile")
    )
    step_re = (dot_real / image_norm)[:, None, None, None]
    step_im = (dot_imag / image_norm)[:, None, None, None]
    new_re = warm_field[:, 0] + step_re * search[:, 0] - step_im * search[:, 1]
    new_im = warm_field[:, 1] + step_re * search[:, 1] + step_im * search[:, 0]
    new_field = jnp.stack([new_re, new_im], axis=1)
    plane_cells = full_width * long_len
    rec_depth = receiver_cell // plane_cells
    rec_width = receiver_cell // long_len % full_width
    rec_long = receiver_cell % long_len
    local_depth = rec_depth - depth_index * layer_len
    local_width = rec_width - tile_index * width_len
    is_owned = (
        (local_depth >= 0)
        & (local_depth < layer_len)
        & (local_width >= 0)
        & (local_width < width_len)
    )
    local_index = jnp.where(
        is_owned, (local_depth * width_len + local_width) * long_len + rec_long, 0
    )
    flattened = new_field.reshape(shot_count, 2, layer_len * width_len * long_len)
    sampled = jnp.take_along_axis(
        flattened,
        jnp.broadcast_to(local_index[:, None, :], (shot_count, 2, local_index.shape[1])),
        axis=2,
    )
    data_miss = sampled - observed
    squared = jnp.sum(data_miss * data_miss, axis=1)
    partial_misfit = 0.5 * jnp.sum(jnp.where(is_owned, squared, 0.0), axis=1)
    misfit = lax.psum(partial_misfit, ("depth", "tile"))
    adjoint_wide = extended(adjoint_field, (("tile", 3),), 1)
    adjoint_re = adjoint_wide[:, 0]
    adjoint_im = adjoint_wide[:, 1]
    weight_re = adjoint_re + damping_wide * adjoint_im
    weight_im = damping_wide * adjoint_re - adjoint_im
    smooth_re = lateral_smooth(pad_long(weight_re), width_len, long_len)
    smooth_im = lateral_smooth(pad_long(weight_im), width_len, long_len)
    gradient = -WAVE_SCALE / shot_count * jnp.sum(new_re * smooth_re - new_im * smooth_im, axis=0)
    return (new_field, misfit, gradient)


def solution(mesh):
    return jax.shard_map(
        per_device,
        mesh=mesh,
        in_specs=(
            P(None, None, "depth", "tile", None),
            P("depth", "tile", None),
            P(None, None, "depth", "tile", None),
            P(),
            P(),
            P(),
            P(),
        ),
        out_specs=(P(None, None, "depth", "tile", None), P(), P("depth", "tile", None)),
        check_vma=False,
    )
```

profile of v0, /device:TPU:1, one launch (start us, length us, event | category | flops | bytes accessed | tf_op | source)
XLA Modules:
  0.0 865.1 jit_solution(15573699056863108744)
XLA Ops:
  1.8 3.9 collective-permute-start.10
  8.4 5.2 collective-permute-start.14
  26.2 5.1 collective-permute-start.12
  34.8 5.1 collective-permute-start.20
  45.3 3.6 fusion.116
  49.3 257.9 %while.36 = (s32[]{:T(128)}, f32[16,2,2,8,256]{4,3,2,1,0:T(8,128)S(1)}, f32[16,2,8,256]{3,2,1,0:T(8,128)S(1)}, s32[]{:T(128)}, f32[2,8,256]{2,1,0:T(8,128)S(1)},...) while((s32[]{:T(128)}, ...), condition=%wide.region_1.2_spmd.clone, body=%wide.region_0.1_spmd.clone.sunk | while | flops 5369095 | bytes 13800788 | solution.py:214
  49.3 3.7 collective-permute-start
  53.0 3.8 collective-permute-done
  58.8 8.4 collective-permute-start.2
  71.8 5.8 collective-permute-start.4
  80.2 3.9 collective-permute-start
  84.1 3.3 collective-permute-done
  89.4 10.0 %collective-permute-start.2 = (f32[16,2,1,256]{3,2,1,0:T(1,128)S(1)}, f32[16,2,1,256]{3,2,1,0:T(1,128)S(1)}, u32[]{:S(2)}, u32[]{:S(2)}) collective-permute-start(f32[16,2,1,256]{3,2,1,0:T(1,128)S(1)} %get-tuple-element.677), channel_id=1, source_target_pairs={{0,1},{1,2},{2,3},{3,4},{4,5},{5,6},{6,7},{7,8},{8,9},{9,10},{10,1... | collective-permute-start | bytes 98312 | tf_op jit(solution)/shard_map/while/body/eval_jaxpr/ppermute | solution.py:23
  103.9 5.7 collective-permute-start.4
  112.2 4.1 collective-permute-start
  121.6 10.2 %collective-permute-start.2 = (f32[16,2,1,256]{3,2,1,0:T(1,128)S(1)}, f32[16,2,1,256]{3,2,1,0:T(1,128)S(1)}, u32[]{:S(2)}, u32[]{:S(2)}) collective-permute-start(f32[16,2,1,256]{3,2,1,0:T(1,128)S(1)} %get-tuple-element.677), channel_id=1, source_target_pairs={{0,1},{1,2},{2,3},{3,4},{4,5},{5,6},{6,7},{7,8},{8,9},{9,10},{10,1... | collective-permute-start | bytes 98312 | tf_op jit(solution)/shard_map/while/body/eval_jaxpr/ppermute | solution.py:23
  136.3 5.7 collective-permute-start.4
  144.7 4.4 collective-permute-start
  154.3 9.3 %collective-permute-start.2 = (f32[16,2,1,256]{3,2,1,0:T(1,128)S(1)}, f32[16,2,1,256]{3,2,1,0:T(1,128)S(1)}, u32[]{:S(2)}, u32[]{:S(2)}) collective-permute-start(f32[16,2,1,256]{3,2,1,0:T(1,128)S(1)} %get-tuple-element.677), channel_id=1, source_target_pairs={{0,1},{1,2},{2,3},{3,4},{4,5},{5,6},{6,7},{7,8},{8,9},{9,10},{10,1... | collective-permute-start | bytes 98312 | tf_op jit(solution)/shard_map/while/body/eval_jaxpr/ppermute | solution.py:23
  168.2 5.9 collective-permute-start.4
  176.7 5.0 collective-permute-start
  187.0 9.2 %collective-permute-start.2 = (f32[16,2,1,256]{3,2,1,0:T(1,128)S(1)}, f32[16,2,1,256]{3,2,1,0:T(1,128)S(1)}, u32[]{:S(2)}, u32[]{:S(2)}) collective-permute-start(f32[16,2,1,256]{3,2,1,0:T(1,128)S(1)} %get-tuple-element.677), channel_id=1, source_target_pairs={{0,1},{1,2},{2,3},{3,4},{4,5},{5,6},{6,7},{7,8},{8,9},{9,10},{10,1... | collective-permute-start | bytes 98312 | tf_op jit(solution)/shard_map/while/body/eval_jaxpr/ppermute | solution.py:23
  200.8 5.9 collective-permute-start.4
  209.3 5.0 collective-permute-start
  219.6 9.2 %collective-permute-start.2 = (f32[16,2,1,256]{3,2,1,0:T(1,128)S(1)}, f32[16,2,1,256]{3,2,1,0:T(1,128)S(1)}, u32[]{:S(2)}, u32[]{:S(2)}) collective-permute-start(f32[16,2,1,256]{3,2,1,0:T(1,128)S(1)} %get-tuple-element.677), channel_id=1, source_target_pairs={{0,1},{1,2},{2,3},{3,4},{4,5},{5,6},{6,7},{7,8},{8,9},{9,10},{10,1... | collective-permute-start | bytes 98312 | tf_op jit(solution)/shard_map/while/body/eval_jaxpr/ppermute | solution.py:23
  233.5 5.9 collective-permute-start.4
  242.0 5.0 collective-permute-start
  252.3 9.2 %collective-permute-start.2 = (f32[16,2,1,256]{3,2,1,0:T(1,128)S(1)}, f32[16,2,1,256]{3,2,1,0:T(1,128)S(1)}, u32[]{:S(2)}, u32[]{:S(2)}) collective-permute-start(f32[16,2,1,256]{3,2,1,0:T(1,128)S(1)} %get-tuple-element.677), channel_id=1, source_target_pairs={{0,1},{1,2},{2,3},{3,4},{4,5},{5,6},{6,7},{7,8},{8,9},{9,10},{10,1... | collective-permute-start | bytes 98312 | tf_op jit(solution)/shard_map/while/body/eval_jaxpr/ppermute | solution.py:23
  266.2 5.9 collective-permute-start.4
  274.6 5.0 collective-permute-start
  284.9 9.2 %collective-permute-start.2 = (f32[16,2,1,256]{3,2,1,0:T(1,128)S(1)}, f32[16,2,1,256]{3,2,1,0:T(1,128)S(1)}, u32[]{:S(2)}, u32[]{:S(2)}) collective-permute-start(f32[16,2,1,256]{3,2,1,0:T(1,128)S(1)} %get-tuple-element.677), channel_id=1, source_target_pairs={{0,1},{1,2},{2,3},{3,4},{4,5},{5,6},{6,7},{7,8},{8,9},{9,10},{10,1... | collective-permute-start | bytes 98312 | tf_op jit(solution)/shard_map/while/body/eval_jaxpr/ppermute | solution.py:23
  298.8 5.9 collective-permute-start.4
  307.3 248.7 %while.37 = (s32[]{:T(128)}, f32[16,2,2,8,256]{4,3,2,1,0:T(8,128)S(1)}, f32[16,2,8,256]{3,2,0,1:T(8,128)S(1)}, s32[]{:T(128)}, f32[16,2,2,8,256]{4,3,0,1,2:T(8,1...) while((s32[]{:T(128)}, ...), condition=%wide.region_3.4_spmd.clone, body=%wide.region_2.3_spmd.clone.sunk | while | flops 5318663 | bytes 15177044 | solution.py:214
  308.6 7.5 collective-permute-done.5
  318.1 9.0 %collective-permute-start.7 = (f32[16,2,1,256]{3,2,0,1:T(1,128)S(1)}, f32[16,2,1,256]{3,2,0,1:T(1,128)S(1)}, u32[]{:S(2)}, u32[]{:S(2)}) collective-permute-start(f32[16,2,1,256]{3,2,0,1:T(1,128)S(1)} %get-tuple-element.700), channel_id=1, source_target_pairs={{0,1},{1,2},{2,3},{3,4},{4,5},{5,6},{6,7},{7,8},{8,9},{9,10},{10,1... | collective-permute-start | bytes 98312 | tf_op jit(solution)/shard_map/while/body/eval_jaxpr/ppermute | solution.py:23
  331.1 5.9 collective-permute-start.9
  340.6 7.5 collective-permute-done.5
  350.1 9.3 %collective-permute-start.7 = (f32[16,2,1,256]{3,2,0,1:T(1,128)S(1)}, f32[16,2,1,256]{3,2,0,1:T(1,128)S(1)}, u32[]{:S(2)}, u32[]{:S(2)}) collective-permute-start(f32[16,2,1,256]{3,2,0,1:T(1,128)S(1)} %get-tuple-element.700), channel_id=1, source_target_pairs={{0,1},{1,2},{2,3},{3,4},{4,5},{5,6},{6,7},{7,8},{8,9},{9,10},{10,1... | collective-permute-start | bytes 98312 | tf_op jit(solution)/shard_map/while/body/eval_jaxpr/ppermute | solution.py:23
  363.3 5.8 collective-permute-start.9
  372.7 6.6 collective-permute-done.5
  381.3 9.2 %collective-permute-start.7 = (f32[16,2,1,256]{3,2,0,1:T(1,128)S(1)}, f32[16,2,1,256]{3,2,0,1:T(1,128)S(1)}, u32[]{:S(2)}, u32[]{:S(2)}) collective-permute-start(f32[16,2,1,256]{3,2,0,1:T(1,128)S(1)} %get-tuple-element.700), channel_id=1, source_target_pairs={{0,1},{1,2},{2,3},{3,4},{4,5},{5,6},{6,7},{7,8},{8,9},{9,10},{10,1... | collective-permute-start | bytes 98312 | tf_op jit(solution)/shard_map/while/body/eval_jaxpr/ppermute | solution.py:23
  394.5 5.9 collective-permute-start.9
  404.0 6.5 collective-permute-done.5
  412.5 9.1 %collective-permute-start.7 = (f32[16,2,1,256]{3,2,0,1:T(1,128)S(1)}, f32[16,2,1,256]{3,2,0,1:T(1,128)S(1)}, u32[]{:S(2)}, u32[]{:S(2)}) collective-permute-start(f32[16,2,1,256]{3,2,0,1:T(1,128)S(1)} %get-tuple-element.700), channel_id=1, source_target_pairs={{0,1},{1,2},{2,3},{3,4},{4,5},{5,6},{6,7},{7,8},{8,9},{9,10},{10,1... | collective-permute-start | bytes 98312 | tf_op jit(solution)/shard_map/while/body/eval_jaxpr/ppermute | solution.py:23
  425.6 5.9 collective-permute-start.9
  435.1 6.5 collective-permute-done.5
  443.6 9.1 %collective-permute-start.7 = (f32[16,2,1,256]{3,2,0,1:T(1,128)S(1)}, f32[16,2,1,256]{3,2,0,1:T(1,128)S(1)}, u32[]{:S(2)}, u32[]{:S(2)}) collective-permute-start(f32[16,2,1,256]{3,2,0,1:T(1,128)S(1)} %get-tuple-element.700), channel_id=1, source_target_pairs={{0,1},{1,2},{2,3},{3,4},{4,5},{5,6},{6,7},{7,8},{8,9},{9,10},{10,1... | collective-permute-start | bytes 98312 | tf_op jit(solution)/shard_map/while/body/eval_jaxpr/ppermute | solution.py:23
  456.7 5.9 collective-permute-start.9
  466.2 6.4 collective-permute-done.5
  474.6 9.0 %collective-permute-start.7 = (f32[16,2,1,256]{3,2,0,1:T(1,128)S(1)}, f32[16,2,1,256]{3,2,0,1:T(1,128)S(1)}, u32[]{:S(2)}, u32[]{:S(2)}) collective-permute-start(f32[16,2,1,256]{3,2,0,1:T(1,128)S(1)} %get-tuple-element.700), channel_id=1, source_target_pairs={{0,1},{1,2},{2,3},{3,4},{4,5},{5,6},{6,7},{7,8},{8,9},{9,10},{10,1... | collective-permute-start | bytes 98312 | tf_op jit(solution)/shard_map/while/body/eval_jaxpr/ppermute | solution.py:23
  487.6 6.1 collective-permute-start.9
  497.2 6.7 collective-permute-done.5
  505.9 8.7 %collective-permute-start.7 = (f32[16,2,1,256]{3,2,0,1:T(1,128)S(1)}, f32[16,2,1,256]{3,2,0,1:T(1,128)S(1)}, u32[]{:S(2)}, u32[]{:S(2)}) collective-permute-start(f32[16,2,1,256]{3,2,0,1:T(1,128)S(1)} %get-tuple-element.700), channel_id=1, source_target_pairs={{0,1},{1,2},{2,3},{3,4},{4,5},{5,6},{6,7},{7,8},{8,9},{9,10},{10,1... | collective-permute-start | bytes 98312 | tf_op jit(solution)/shard_map/while/body/eval_jaxpr/ppermute | solution.py:23
  518.6 5.7 collective-permute-start.9
  527.9 6.7 collective-permute-done.5
  536.6 7.4 collective-permute-start.7
  548.0 5.7 collective-permute-start.9
  556.0 4.2 collective-permute-start.16
  563.8 10.0 %collective-permute-done.17 = f32[16,2,1,8,256]{4,3,2,0,1:T(8,128)S(1)} collective-permute-done((f32[16,2,1,8,256]{4,3,2,0,1:T(8,128)S(1)}, f32[16,2,1,8,256]{4,3,2,0,1:T(8,128)S(1)}, u32[]{:S(2)}, u32[]{:S(2)}) %collective-permute-start.17) | collective-permute-done | bytes 262176 | tf_op jit(solution)/shard_map/ppermute | solution.py:24
  573.9 8.4 collective-permute-start.18
  584.8 5.4 collective-permute-done.19
  595.4 112.7 %all-reduce.11 = (f32[16]{0:T(128)S(1)}, f32[16]{0:T(128)S(1)}, f32[16]{0:T(128)S(1)}) all-reduce(f32[16]{0:T(128)S(1)} %get-tuple-element.462, f32[16]{0:T(128)S(1)} %get-tuple-element.463, f32[16]{0:T(128)S(1)} %get-tuple-element.461), channel_id=1, replica_groups=mesh['depth'=8,'tile'=32] {'depth','tile'}, use_global_device_ids=true, to_apply=%region_9.10 | all-reduce | flops 48 | bytes 384 | tf_op jit(solution)/shard_map/psum | solution.py:230
  710.2 78.9 %gather_fusion = f32[8192]{0:T(1024)S(1)} fusion(f32[16,2,4096]{2,0,1:T(8,128)S(1)} %pad_maximum_fusion.24, s32[8192]{0:T(1024)S(1)} %bitcast.171), kind=kCustom, calls=%fused_computation | custom fusion | bytes 163840 | tf_op jit(solution)/shard_map/jit(take_along_axis)/gather | solution.py:254
  790.9 73.3 %psum.31 = f32[16]{0:T(128)} all-reduce(f32[16]{0:T(128)S(1)} %broadcast_multiply_fusion.1), channel_id=1, replica_groups=mesh['depth'=8,'tile'=32] {'depth','tile'}, use_global_device_ids=true, to_apply=%region_12.13 | all-reduce | flops 16 | bytes 128 | tf_op jit(solution)/shard_map/psum | solution.py:262
  (454 shorter events, 208.2 us)
Async XLA Ops:
  1.8 23.4 %collective-permute-start.10 = (f32[16,2,1,8,256]{4,3,2,0,1:T(8,128)S(1)}, f32[16,2,1,8,256]{4,3,2,0,1:T(8,128)S(1)}, u32[]{:S(2)}, u32[]{:S(2)}) collective-permute-start(f32[16,2,1,8,256]{4,3,2,0,1:T(8,128)S(1)} %get-tuple-element.552), channel_id=1, source_target_pairs={{0,32},{32,64},{64,96},{96,128},{128,160},{160,192},{192,224},{1,3... | collective-permute-start | bytes 786440 | tf_op jit(solution)/shard_map/ppermute | solution.py:23
  5.7 19.5 %collective-permute-start.11 = (f32[16,2,1,8,256]{4,3,2,0,1:T(8,128)S(1)}, f32[16,2,1,8,256]{4,3,2,0,1:T(8,128)S(1)}, u32[]{:S(2)}, u32[]{:S(2)}) collective-permute-start(f32[16,2,1,8,256]{4,3,2,0,1:T(8,128)S(1)} %get-tuple-element.551), channel_id=1, source_target_pairs={{32,0},{64,32},{96,64},{128,96},{160,128},{192,160},{224,192},{33,... | collective-permute-start | bytes 786440 | tf_op jit(solution)/shard_map/ppermute | solution.py:24
  8.4 31.5 %collective-permute-start.14 = (f32[2,1,256]{2,1,0:T(1,128)}, f32[2,1,256]{2,1,0:T(1,128)}, u32[]{:S(2)}, u32[]{:S(2)}) collective-permute-start(f32[2,1,256]{2,1,0:T(1,128)} %get-tuple-element.555), channel_id=1, source_target_pairs={{0,1},{1,2},{2,3},{3,4},{4,5},{5,6},{6,7},{7,8},{8,9},{9,10},{10,1... | collective-permute-start | bytes 6152 | tf_op jit(solution)/shard_map/ppermute | solution.py:23
  13.6 28.3 %collective-permute-start.15 = (f32[2,1,256]{2,1,0:T(1,128)}, f32[2,1,256]{2,1,0:T(1,128)}, u32[]{:S(2)}, u32[]{:S(2)}) collective-permute-start(f32[2,1,256]{2,1,0:T(1,128)} %get-tuple-element.556), channel_id=1, source_target_pairs={{1,0},{2,1},{3,2},{4,3},{5,4},{6,5},{7,6},{8,7},{9,8},{10,9},{11,1... | collective-permute-start | bytes 6152 | tf_op jit(solution)/shard_map/ppermute | solution.py:24
  26.2 16.4 %collective-permute-start.12 = (f32[16,2,4,1,256]{4,3,2,0,1:T(1,128)}, f32[16,2,4,1,256]{4,3,2,0,1:T(1,128)}, u32[]{:S(2)}, u32[]{:S(2)}) collective-permute-start(f32[16,2,4,1,256]{4,3,2,0,1:T(1,128)} %get-tuple-element.545), channel_id=1, source_target_pairs={{0,1},{1,2},{2,3},{3,4},{4,5},{5,6},{6,7},{7,8},{8,9},{9,10},{10,1... | collective-permute-start | bytes 393224 | tf_op jit(solution)/shard_map/ppermute | solution.py:23
  31.4 11.3 %collective-permute-start.13 = (f32[16,2,4,1,256]{4,3,2,0,1:T(1,128)}, f32[16,2,4,1,256]{4,3,2,0,1:T(1,128)}, u32[]{:S(2)}, u32[]{:S(2)}) collective-permute-start(f32[16,2,4,1,256]{4,3,2,0,1:T(1,128)} %get-tuple-element.546), channel_id=1, source_target_pairs={{1,0},{2,1},{3,2},{4,3},{5,4},{6,5},{7,6},{8,7},{9,8},{10,9},{11,1... | collective-permute-start | bytes 393224 | tf_op jit(solution)/shard_map/ppermute | solution.py:24
  34.8 525.4 %collective-permute-start.20 = (f32[16,2,2,1,256]{4,3,2,0,1:T(1,128)}, f32[16,2,2,1,256]{4,3,2,0,1:T(1,128)}, u32[]{:S(2)}, u32[]{:S(2)}) collective-permute-start(f32[16,2,2,1,256]{4,3,2,0,1:T(1,128)} %get-tuple-element.547), channel_id=1, source_target_pairs={{0,1},{1,2},{2,3},{3,4},{4,5},{5,6},{6,7},{7,8},{8,9},{9,10},{10,1... | collective-permute-start | bytes 196616 | tf_op jit(solution)/shard_map/ppermute | solution.py:23
  40.0 520.3 %collective-permute-start.21 = (f32[16,2,2,1,256]{4,3,2,0,1:T(1,128)}, f32[16,2,2,1,256]{4,3,2,0,1:T(1,128)}, u32[]{:S(2)}, u32[]{:S(2)}) collective-permute-start(f32[16,2,2,1,256]{4,3,2,0,1:T(1,128)} %get-tuple-element.548), channel_id=1, source_target_pairs={{1,0},{2,1},{3,2},{4,3},{5,4},{6,5},{7,6},{8,7},{9,8},{10,9},{11,1... | collective-permute-start | bytes 196616 | tf_op jit(solution)/shard_map/ppermute | solution.py:24
  56.9 10.4 %collective-permute-start.1 = (f32[16,2,1,256]{3,2,1,0:T(1,128)S(1)}, f32[16,2,1,256]{3,2,1,0:T(1,128)S(1)}, u32[]{:S(2)}, u32[]{:S(2)}) collective-permute-start(f32[16,2,1,256]{3,2,1,0:T(1,128)S(1)} %get-tuple-element.676), channel_id=1, source_target_pairs={{1,0},{2,1},{3,2},{4,3},{5,4},{6,5},{7,6},{8,7},{9,8},{10,9},{11,1... | collective-permute-start | bytes 98312 | tf_op jit(solution)/shard_map/while/body/eval_jaxpr/ppermute | solution.py:24
  58.8 9.4 %collective-permute-start.2 = (f32[16,2,1,256]{3,2,1,0:T(1,128)S(1)}, f32[16,2,1,256]{3,2,1,0:T(1,128)S(1)}, u32[]{:S(2)}, u32[]{:S(2)}) collective-permute-start(f32[16,2,1,256]{3,2,1,0:T(1,128)S(1)} %get-tuple-element.677), channel_id=1, source_target_pairs={{0,1},{1,2},{2,3},{3,4},{4,5},{5,6},{6,7},{7,8},{8,9},{9,10},{10,1... | collective-permute-start | bytes 98312 | tf_op jit(solution)/shard_map/while/body/eval_jaxpr/ppermute | solution.py:23
  87.4 12.0 %collective-permute-start.1 = (f32[16,2,1,256]{3,2,1,0:T(1,128)S(1)}, f32[16,2,1,256]{3,2,1,0:T(1,128)S(1)}, u32[]{:S(2)}, u32[]{:S(2)}) collective-permute-start(f32[16,2,1,256]{3,2,1,0:T(1,128)S(1)} %get-tuple-element.676), channel_id=1, source_target_pairs={{1,0},{2,1},{3,2},{4,3},{5,4},{6,5},{7,6},{8,7},{9,8},{10,9},{11,1... | collective-permute-start | bytes 98312 | tf_op jit(solution)/shard_map/while/body/eval_jaxpr/ppermute | solution.py:24
  89.4 11.0 %collective-permute-start.2 = (f32[16,2,1,256]{3,2,1,0:T(1,128)S(1)}, f32[16,2,1,256]{3,2,1,0:T(1,128)S(1)}, u32[]{:S(2)}, u32[]{:S(2)}) collective-permute-start(f32[16,2,1,256]{3,2,1,0:T(1,128)S(1)} %get-tuple-element.677), channel_id=1, source_target_pairs={{0,1},{1,2},{2,3},{3,4},{4,5},{5,6},{6,7},{7,8},{8,9},{9,10},{10,1... | collective-permute-start | bytes 98312 | tf_op jit(solution)/shard_map/while/body/eval_jaxpr/ppermute | solution.py:23
  119.7 12.1 %collective-permute-start.1 = (f32[16,2,1,256]{3,2,1,0:T(1,128)S(1)}, f32[16,2,1,256]{3,2,1,0:T(1,128)S(1)}, u32[]{:S(2)}, u32[]{:S(2)}) collective-permute-start(f32[16,2,1,256]{3,2,1,0:T(1,128)S(1)} %get-tuple-element.676), channel_id=1, source_target_pairs={{1,0},{2,1},{3,2},{4,3},{5,4},{6,5},{7,6},{8,7},{9,8},{10,9},{11,1... | collective-permute-start | bytes 98312 | tf_op jit(solution)/shard_map/while/body/eval_jaxpr/ppermute | solution.py:24
  121.6 11.2 %collective-permute-start.2 = (f32[16,2,1,256]{3,2,1,0:T(1,128)S(1)}, f32[16,2,1,256]{3,2,1,0:T(1,128)S(1)}, u32[]{:S(2)}, u32[]{:S(2)}) collective-permute-start(f32[16,2,1,256]{3,2,1,0:T(1,128)S(1)} %get-tuple-element.677), channel_id=1, source_target_pairs={{0,1},{1,2},{2,3},{3,4},{4,5},{5,6},{6,7},{7,8},{8,9},{9,10},{10,1... | collective-permute-start | bytes 98312 | tf_op jit(solution)/shard_map/while/body/eval_jaxpr/ppermute | solution.py:23
  152.4 11.3 %collective-permute-start.1 = (f32[16,2,1,256]{3,2,1,0:T(1,128)S(1)}, f32[16,2,1,256]{3,2,1,0:T(1,128)S(1)}, u32[]{:S(2)}, u32[]{:S(2)}) collective-permute-start(f32[16,2,1,256]{3,2,1,0:T(1,128)S(1)} %get-tuple-element.676), channel_id=1, source_target_pairs={{1,0},{2,1},{3,2},{4,3},{5,4},{6,5},{7,6},{8,7},{9,8},{10,9},{11,1... | collective-permute-start | bytes 98312 | tf_op jit(solution)/shard_map/while/body/eval_jaxpr/ppermute | solution.py:24
  154.3 10.4 %collective-permute-start.2 = (f32[16,2,1,256]{3,2,1,0:T(1,128)S(1)}, f32[16,2,1,256]{3,2,1,0:T(1,128)S(1)}, u32[]{:S(2)}, u32[]{:S(2)}) collective-permute-start(f32[16,2,1,256]{3,2,1,0:T(1,128)S(1)} %get-tuple-element.677), channel_id=1, source_target_pairs={{0,1},{1,2},{2,3},{3,4},{4,5},{5,6},{6,7},{7,8},{8,9},{9,10},{10,1... | collective-permute-start | bytes 98312 | tf_op jit(solution)/shard_map/while/body/eval_jaxpr/ppermute | solution.py:23
  166.3 7.8 collective-permute-start.3
  176.7 8.3 collective-permute-start
  185.0 11.2 %collective-permute-start.1 = (f32[16,2,1,256]{3,2,1,0:T(1,128)S(1)}, f32[16,2,1,256]{3,2,1,0:T(1,128)S(1)}, u32[]{:S(2)}, u32[]{:S(2)}) collective-permute-start(f32[16,2,1,256]{3,2,1,0:T(1,128)S(1)} %get-tuple-element.676), channel_id=1, source_target_pairs={{1,0},{2,1},{3,2},{4,3},{5,4},{6,5},{7,6},{8,7},{9,8},{10,9},{11,1... | collective-permute-start | bytes 98312 | tf_op jit(solution)/shard_map/while/body/eval_jaxpr/ppermute | solution.py:24
  187.0 10.4 %collective-permute-start.2 = (f32[16,2,1,256]{3,2,1,0:T(1,128)S(1)}, f32[16,2,1,256]{3,2,1,0:T(1,128)S(1)}, u32[]{:S(2)}, u32[]{:S(2)}) collective-permute-start(f32[16,2,1,256]{3,2,1,0:T(1,128)S(1)} %get-tuple-element.677), channel_id=1, source_target_pairs={{0,1},{1,2},{2,3},{3,4},{4,5},{5,6},{6,7},{7,8},{8,9},{9,10},{10,1... | collective-permute-start | bytes 98312 | tf_op jit(solution)/shard_map/while/body/eval_jaxpr/ppermute | solution.py:23
  198.9 7.8 collective-permute-start.3
  209.3 8.3 collective-permute-start
  217.7 11.2 %collective-permute-start.1 = (f32[16,2,1,256]{3,2,1,0:T(1,128)S(1)}, f32[16,2,1,256]{3,2,1,0:T(1,128)S(1)}, u32[]{:S(2)}, u32[]{:S(2)}) collective-permute-start(f32[16,2,1,256]{3,2,1,0:T(1,128)S(1)} %get-tuple-element.676), channel_id=1, source_target_pairs={{1,0},{2,1},{3,2},{4,3},{5,4},{6,5},{7,6},{8,7},{9,8},{10,9},{11,1... | collective-permute-start | bytes 98312 | tf_op jit(solution)/shard_map/while/body/eval_jaxpr/ppermute | solution.py:24
  219.6 10.4 %collective-permute-start.2 = (f32[16,2,1,256]{3,2,1,0:T(1,128)S(1)}, f32[16,2,1,256]{3,2,1,0:T(1,128)S(1)}, u32[]{:S(2)}, u32[]{:S(2)}) collective-permute-start(f32[16,2,1,256]{3,2,1,0:T(1,128)S(1)} %get-tuple-element.677), channel_id=1, source_target_pairs={{0,1},{1,2},{2,3},{3,4},{4,5},{5,6},{6,7},{7,8},{8,9},{9,10},{10,1... | collective-permute-start | bytes 98312 | tf_op jit(solution)/shard_map/while/body/eval_jaxpr/ppermute | solution.py:23
  231.6 7.8 collective-permute-start.3
  242.0 8.3 collective-permute-start
  250.3 11.2 %collective-permute-start.1 = (f32[16,2,1,256]{3,2,1,0:T(1,128)S(1)}, f32[16,2,1,256]{3,2,1,0:T(1,128)S(1)}, u32[]{:S(2)}, u32[]{:S(2)}) collective-permute-start(f32[16,2,1,256]{3,2,1,0:T(1,128)S(1)} %get-tuple-element.676), channel_id=1, source_target_pairs={{1,0},{2,1},{3,2},{4,3},{5,4},{6,5},{7,6},{8,7},{9,8},{10,9},{11,1... | collective-permute-start | bytes 98312 | tf_op jit(solution)/shard_map/while/body/eval_jaxpr/ppermute | solution.py:24
  252.3 10.4 %collective-permute-start.2 = (f32[16,2,1,256]{3,2,1,0:T(1,128)S(1)}, f32[16,2,1,256]{3,2,1,0:T(1,128)S(1)}, u32[]{:S(2)}, u32[]{:S(2)}) collective-permute-start(f32[16,2,1,256]{3,2,1,0:T(1,128)S(1)} %get-tuple-element.677), channel_id=1, source_target_pairs={{0,1},{1,2},{2,3},{3,4},{4,5},{5,6},{6,7},{7,8},{8,9},{9,10},{10,1... | collective-permute-start | bytes 98312 | tf_op jit(solution)/shard_map/while/body/eval_jaxpr/ppermute | solution.py:23
  264.2 7.8 collective-permute-start.3
  274.6 8.3 collective-permute-start
  283.0 11.2 %collective-permute-start.1 = (f32[16,2,1,256]{3,2,1,0:T(1,128)S(1)}, f32[16,2,1,256]{3,2,1,0:T(1,128)S(1)}, u32[]{:S(2)}, u32[]{:S(2)}) collective-permute-start(f32[16,2,1,256]{3,2,1,0:T(1,128)S(1)} %get-tuple-element.676), channel_id=1, source_target_pairs={{1,0},{2,1},{3,2},{4,3},{5,4},{6,5},{7,6},{8,7},{9,8},{10,9},{11,1... | collective-permute-start | bytes 98312 | tf_op jit(solution)/shard_map/while/body/eval_jaxpr/ppermute | solution.py:24
  284.9 10.4 %collective-permute-start.2 = (f32[16,2,1,256]{3,2,1,0:T(1,128)S(1)}, f32[16,2,1,256]{3,2,1,0:T(1,128)S(1)}, u32[]{:S(2)}, u32[]{:S(2)}) collective-permute-start(f32[16,2,1,256]{3,2,1,0:T(1,128)S(1)} %get-tuple-element.677), channel_id=1, source_target_pairs={{0,1},{1,2},{2,3},{3,4},{4,5},{5,6},{6,7},{7,8},{8,9},{9,10},{10,1... | collective-permute-start | bytes 98312 | tf_op jit(solution)/shard_map/while/body/eval_jaxpr/ppermute | solution.py:23
  296.9 7.8 collective-permute-start.3
  307.3 8.8 %collective-permute-start.5 = (f32[16,2,8,256]{3,2,0,1:T(8,128)S(1)}, f32[16,2,8,256]{3,2,0,1:T(8,128)S(1)}, u32[]{:S(2)}, u32[]{:S(2)}) collective-permute-start(f32[16,2,8,256]{3,2,0,1:T(8,128)S(1)} %broadcast_select_fusion.5), channel_id=1, source_target_pairs={{32,0},{64,32},{96,64},{128,96},{160,128},{192,160},{224,192},{33,... | collective-permute-start | bytes 786440 | tf_op jit(solution)/shard_map/while/body/eval_jaxpr/ppermute | solution.py:32
  316.2 10.9 %collective-permute-start.6 = (f32[16,2,1,256]{3,2,0,1:T(1,128)S(1)}, f32[16,2,1,256]{3,2,0,1:T(1,128)S(1)}, u32[]{:S(2)}, u32[]{:S(2)}) collective-permute-start(f32[16,2,1,256]{3,2,0,1:T(1,128)S(1)} %get-tuple-element.699), channel_id=1, source_target_pairs={{1,0},{2,1},{3,2},{4,3},{5,4},{6,5},{7,6},{8,7},{9,8},{10,9},{11,1... | collective-permute-start | bytes 98312 | tf_op jit(solution)/shard_map/while/body/eval_jaxpr/ppermute | solution.py:24
  318.1 10.1 %collective-permute-start.7 = (f32[16,2,1,256]{3,2,0,1:T(1,128)S(1)}, f32[16,2,1,256]{3,2,0,1:T(1,128)S(1)}, u32[]{:S(2)}, u32[]{:S(2)}) collective-permute-start(f32[16,2,1,256]{3,2,0,1:T(1,128)S(1)} %get-tuple-element.700), channel_id=1, source_target_pairs={{0,1},{1,2},{2,3},{3,4},{4,5},{5,6},{6,7},{7,8},{8,9},{9,10},{10,1... | collective-permute-start | bytes 98312 | tf_op jit(solution)/shard_map/while/body/eval_jaxpr/ppermute | solution.py:23
  329.2 7.8 collective-permute-start.8
  339.3 8.8 %collective-permute-start.5 = (f32[16,2,8,256]{3,2,0,1:T(8,128)S(1)}, f32[16,2,8,256]{3,2,0,1:T(8,128)S(1)}, u32[]{:S(2)}, u32[]{:S(2)}) collective-permute-start(f32[16,2,8,256]{3,2,0,1:T(8,128)S(1)} %broadcast_select_fusion.5), channel_id=1, source_target_pairs={{32,0},{64,32},{96,64},{128,96},{160,128},{192,160},{224,192},{33,... | collective-permute-start | bytes 786440 | tf_op jit(solution)/shard_map/while/body/eval_jaxpr/ppermute | solution.py:32
  348.2 11.2 %collective-permute-start.6 = (f32[16,2,1,256]{3,2,0,1:T(1,128)S(1)}, f32[16,2,1,256]{3,2,0,1:T(1,128)S(1)}, u32[]{:S(2)}, u32[]{:S(2)}) collective-permute-start(f32[16,2,1,256]{3,2,0,1:T(1,128)S(1)} %get-tuple-element.699), channel_id=1, source_target_pairs={{1,0},{2,1},{3,2},{4,3},{5,4},{6,5},{7,6},{8,7},{9,8},{10,9},{11,1... | collective-permute-start | bytes 98312 | tf_op jit(solution)/shard_map/while/body/eval_jaxpr/ppermute | solution.py:24
  350.1 10.3 %collective-permute-start.7 = (f32[16,2,1,256]{3,2,0,1:T(1,128)S(1)}, f32[16,2,1,256]{3,2,0,1:T(1,128)S(1)}, u32[]{:S(2)}, u32[]{:S(2)}) collective-permute-start(f32[16,2,1,256]{3,2,0,1:T(1,128)S(1)} %get-tuple-element.700), channel_id=1, source_target_pairs={{0,1},{1,2},{2,3},{3,4},{4,5},{5,6},{6,7},{7,8},{8,9},{9,10},{10,1... | collective-permute-start | bytes 98312 | tf_op jit(solution)/shard_map/while/body/eval_jaxpr/ppermute | solution.py:23
  371.4 7.9 collective-permute-start.5
  379.4 11.2 %collective-permute-start.6 = (f32[16,2,1,256]{3,2,0,1:T(1,128)S(1)}, f32[16,2,1,256]{3,2,0,1:T(1,128)S(1)}, u32[]{:S(2)}, u32[]{:S(2)}) collective-permute-start(f32[16,2,1,256]{3,2,0,1:T(1,128)S(1)} %get-tuple-element.699), channel_id=1, source_target_pairs={{1,0},{2,1},{3,2},{4,3},{5,4},{6,5},{7,6},{8,7},{9,8},{10,9},{11,1... | collective-permute-start | bytes 98312 | tf_op jit(solution)/shard_map/while/body/eval_jaxpr/ppermute | solution.py:24
  381.3 10.2 %collective-permute-start.7 = (f32[16,2,1,256]{3,2,0,1:T(1,128)S(1)}, f32[16,2,1,256]{3,2,0,1:T(1,128)S(1)}, u32[]{:S(2)}, u32[]{:S(2)}) collective-permute-start(f32[16,2,1,256]{3,2,0,1:T(1,128)S(1)} %get-tuple-element.700), channel_id=1, source_target_pairs={{0,1},{1,2},{2,3},{3,4},{4,5},{5,6},{6,7},{7,8},{8,9},{9,10},{10,1... | collective-permute-start | bytes 98312 | tf_op jit(solution)/shard_map/while/body/eval_jaxpr/ppermute | solution.py:23
  392.6 7.8 collective-permute-start.8
  402.7 7.8 collective-permute-start.5
  410.6 11.1 %collective-permute-start.6 = (f32[16,2,1,256]{3,2,0,1:T(1,128)S(1)}, f32[16,2,1,256]{3,2,0,1:T(1,128)S(1)}, u32[]{:S(2)}, u32[]{:S(2)}) collective-permute-start(f32[16,2,1,256]{3,2,0,1:T(1,128)S(1)} %get-tuple-element.699), channel_id=1, source_target_pairs={{1,0},{2,1},{3,2},{4,3},{5,4},{6,5},{7,6},{8,7},{9,8},{10,9},{11,1... | collective-permute-start | bytes 98312 | tf_op jit(solution)/shard_map/while/body/eval_jaxpr/ppermute | solution.py:24
  412.5 10.2 %collective-permute-start.7 = (f32[16,2,1,256]{3,2,0,1:T(1,128)S(1)}, f32[16,2,1,256]{3,2,0,1:T(1,128)S(1)}, u32[]{:S(2)}, u32[]{:S(2)}) collective-permute-start(f32[16,2,1,256]{3,2,0,1:T(1,128)S(1)} %get-tuple-element.700), channel_id=1, source_target_pairs={{0,1},{1,2},{2,3},{3,4},{4,5},{5,6},{6,7},{7,8},{8,9},{9,10},{10,1... | collective-permute-start | bytes 98312 | tf_op jit(solution)/shard_map/while/body/eval_jaxpr/ppermute | solution.py:23
  423.7 7.8 collective-permute-start.8
  433.8 7.8 collective-permute-start.5
  441.6 11.0 %collective-permute-start.6 = (f32[16,2,1,256]{3,2,0,1:T(1,128)S(1)}, f32[16,2,1,256]{3,2,0,1:T(1,128)S(1)}, u32[]{:S(2)}, u32[]{:S(2)}) collective-permute-start(f32[16,2,1,256]{3,2,0,1:T(1,128)S(1)} %get-tuple-element.699), channel_id=1, source_target_pairs={{1,0},{2,1},{3,2},{4,3},{5,4},{6,5},{7,6},{8,7},{9,8},{10,9},{11,1... | collective-permute-start | bytes 98312 | tf_op jit(solution)/shard_map/while/body/eval_jaxpr/ppermute | solution.py:24
  443.6 10.2 %collective-permute-start.7 = (f32[16,2,1,256]{3,2,0,1:T(1,128)S(1)}, f32[16,2,1,256]{3,2,0,1:T(1,128)S(1)}, u32[]{:S(2)}, u32[]{:S(2)}) collective-permute-start(f32[16,2,1,256]{3,2,0,1:T(1,128)S(1)} %get-tuple-element.700), channel_id=1, source_target_pairs={{0,1},{1,2},{2,3},{3,4},{4,5},{5,6},{6,7},{7,8},{8,9},{9,10},{10,1... | collective-permute-start | bytes 98312 | tf_op jit(solution)/shard_map/while/body/eval_jaxpr/ppermute | solution.py:23
  454.8 7.8 collective-permute-start.8
  472.7 10.9 %collective-permute-start.6 = (f32[16,2,1,256]{3,2,0,1:T(1,128)S(1)}, f32[16,2,1,256]{3,2,0,1:T(1,128)S(1)}, u32[]{:S(2)}, u32[]{:S(2)}) collective-permute-start(f32[16,2,1,256]{3,2,0,1:T(1,128)S(1)} %get-tuple-element.699), channel_id=1, source_target_pairs={{1,0},{2,1},{3,2},{4,3},{5,4},{6,5},{7,6},{8,7},{9,8},{10,9},{11,1... | collective-permute-start | bytes 98312 | tf_op jit(solution)/shard_map/while/body/eval_jaxpr/ppermute | solution.py:24
  474.6 10.0 %collective-permute-start.7 = (f32[16,2,1,256]{3,2,0,1:T(1,128)S(1)}, f32[16,2,1,256]{3,2,0,1:T(1,128)S(1)}, u32[]{:S(2)}, u32[]{:S(2)}) collective-permute-start(f32[16,2,1,256]{3,2,0,1:T(1,128)S(1)} %get-tuple-element.700), channel_id=1, source_target_pairs={{0,1},{1,2},{2,3},{3,4},{4,5},{5,6},{6,7},{7,8},{8,9},{9,10},{10,1... | collective-permute-start | bytes 98312 | tf_op jit(solution)/shard_map/while/body/eval_jaxpr/ppermute | solution.py:23
  485.6 8.0 collective-permute-start.8
  495.9 8.0 collective-permute-start.5
  504.0 10.7 %collective-permute-start.6 = (f32[16,2,1,256]{3,2,0,1:T(1,128)S(1)}, f32[16,2,1,256]{3,2,0,1:T(1,128)S(1)}, u32[]{:S(2)}, u32[]{:S(2)}) collective-permute-start(f32[16,2,1,256]{3,2,0,1:T(1,128)S(1)} %get-tuple-element.699), channel_id=1, source_target_pairs={{1,0},{2,1},{3,2},{4,3},{5,4},{6,5},{7,6},{8,7},{9,8},{10,9},{11,1... | collective-permute-start | bytes 98312 | tf_op jit(solution)/shard_map/while/body/eval_jaxpr/ppermute | solution.py:24
  505.9 9.7 %collective-permute-start.7 = (f32[16,2,1,256]{3,2,0,1:T(1,128)S(1)}, f32[16,2,1,256]{3,2,0,1:T(1,128)S(1)}, u32[]{:S(2)}, u32[]{:S(2)}) collective-permute-start(f32[16,2,1,256]{3,2,0,1:T(1,128)S(1)} %get-tuple-element.700), channel_id=1, source_target_pairs={{0,1},{1,2},{2,3},{3,4},{4,5},{5,6},{6,7},{7,8},{8,9},{9,10},{10,1... | collective-permute-start | bytes 98312 | tf_op jit(solution)/shard_map/while/body/eval_jaxpr/ppermute | solution.py:23
  526.6 8.0 collective-permute-start.5
  534.7 9.4 %collective-permute-start.6 = (f32[16,2,1,256]{3,2,0,1:T(1,128)S(1)}, f32[16,2,1,256]{3,2,0,1:T(1,128)S(1)}, u32[]{:S(2)}, u32[]{:S(2)}) collective-permute-start(f32[16,2,1,256]{3,2,0,1:T(1,128)S(1)} %get-tuple-element.699), channel_id=1, source_target_pairs={{1,0},{2,1},{3,2},{4,3},{5,4},{6,5},{7,6},{8,7},{9,8},{10,9},{11,1... | collective-permute-start | bytes 98312 | tf_op jit(solution)/shard_map/while/body/eval_jaxpr/ppermute | solution.py:24
  536.6 8.4 collective-permute-start.7
  561.6 12.1 %collective-permute-start.17 = (f32[16,2,1,8,256]{4,3,2,0,1:T(8,128)S(1)}, f32[16,2,1,8,256]{4,3,2,0,1:T(8,128)S(1)}, u32[]{:S(2)}, u32[]{:S(2)}) collective-permute-start(f32[16,2,1,8,256]{4,3,2,0,1:T(8,128)S(1)} %get-tuple-element.550), channel_id=1, source_target_pairs={{32,0},{64,32},{96,64},{128,96},{160,128},{192,160},{224,192},{33,... | collective-permute-start | bytes 786440 | tf_op jit(solution)/shard_map/ppermute | solution.py:24
  573.9 10.8 %collective-permute-start.18 = (f32[16,2,4,1,256]{4,3,2,0,1:T(1,128)S(1)}, f32[16,2,4,1,256]{4,3,2,0,1:T(1,128)S(1)}, u32[]{:S(2)}, u32[]{:S(2)}) collective-permute-start(f32[16,2,4,1,256]{4,3,2,0,1:T(1,128)S(1)} %get-tuple-element.543), channel_id=1, source_target_pairs={{0,1},{1,2},{2,3},{3,4},{4,5},{5,6},{6,7},{7,8},{8,9},{9,10},{10,1... | collective-permute-start | bytes 393224 | tf_op jit(solution)/shard_map/ppermute | solution.py:23
  582.4 7.8 collective-permute-start.19
  (48 other events, 756.9 us)
where the time goes:
time: 868 us; the launch traced here: 865 us
  starting transfers between devices  390 us (45%)
  blocking collectives  186 us (21%)
  waiting for transfers between devices  132 us (15%)
  local copies, waits for them, and re-layouts  89.7 us (10%)
  other arithmetic  63.6 us (7%)
    ppermute x38, starting transfers between devices, extended(): before = lax.ppermute(last, axis, up)  271 us
    psum x1, blocking collectives, per_device(): lax.psum((local_real, local_imag, local_norm), ('depth', 'tile'))  113 us
    ppermute x16, waiting for transfers between devices, shifted(): lax.ppermute(value, axis, [(source, source + steps) for source in range(l...  81.1 us
    gather x2, local copies, waits for them, and re-layouts, per_device(): jnp.take_along_axis(flattened, jnp.broadcast_to(local_index[:, None, :],...  78.9 us
    psum x1, blocking collectives, per_device(): misfit = lax.psum(partial_misfit, ('depth', 'tile'))  73.3 us
    ppermute x38, starting transfers between devices, extended(): after = lax.ppermute(leading, axis, down)  71.8 us
    ppermute x16, starting transfers between devices, shifted(): lax.ppermute(value, axis, [(source, source + steps) for source in range(l...  46.6 us
    ppermute x38, waiting for transfers between devices, extended(): before = lax.ppermute(last, axis, up)  35.5 us
  transfers between devices with their start and end apart: 92, of which 51 were waited for; matrix products, arithmetic and copies ran while one was open for 7% of the time, Pallas kernels for 0%

commit v1 on v0

--- a/solution.py
+++ b/solution.py
@@ -227,14 +227,6 @@
         image_field[:, 0] * image_field[:, 0] + image_field[:, 1] * image_field[:, 1],
         axis=(1, 2, 3),
     )
-    dot_real, dot_imag, image_norm = lax.psum(
-        (local_real, local_imag, local_norm), ("depth", "tile")
-    )
-    step_re = (dot_real / image_norm)[:, None, None, None]
-    step_im = (dot_imag / image_norm)[:, None, None, None]
-    new_re = warm_field[:, 0] + step_re * search[:, 0] - step_im * search[:, 1]
-    new_im = warm_field[:, 1] + step_re * search[:, 1] + step_im * search[:, 0]
-    new_field = jnp.stack([new_re, new_im], axis=1)
     plane_cells = full_width * long_len
     rec_depth = receiver_cell // plane_cells
     rec_width = receiver_cell // long_len % full_width
@@ -247,19 +239,36 @@
         & (local_width >= 0)
         & (local_width < width_len)
     )
-    local_index = jnp.where(
-        is_owned, (local_depth * width_len + local_width) * long_len + rec_long, 0
-    )
-    flattened = new_field.reshape(shot_count, 2, layer_len * width_len * long_len)
-    sampled = jnp.take_along_axis(
-        flattened,
-        jnp.broadcast_to(local_index[:, None, :], (shot_count, 2, local_index.shape[1])),
-        axis=2,
-    )
-    data_miss = sampled - observed
-    squared = jnp.sum(data_miss * data_miss, axis=1)
-    partial_misfit = 0.5 * jnp.sum(jnp.where(is_owned, squared, 0.0), axis=1)
-    misfit = lax.psum(partial_misfit, ("depth", "tile"))
+    row_count = layer_len * width_len
+    local_row = jnp.where(is_owned, local_depth * width_len + local_width, -1)
+    row_hot = (local_row[:, :, None] == jnp.arange(row_count, dtype=jnp.int32)).astype(jnp.float32)
+    both_fields = jnp.concatenate([warm_field, search], axis=1).reshape(
+        shot_count, 4, row_count, long_len
+    )
+    picked_rows = jnp.einsum(
+        "srk,sqky->sqry", row_hot, both_fields, precision=lax.Precision.HIGHEST
+    )
+    col_hot = rec_long[:, None, :, None] == jnp.arange(long_len, dtype=jnp.int32)
+    picked = jnp.sum(jnp.where(col_hot, picked_rows, 0.0), axis=-1)
+    packed = jnp.concatenate(
+        [jnp.stack([local_real, local_imag, local_norm], axis=1), picked.reshape(shot_count, -1)],
+        axis=1,
+    )
+    packed = lax.psum(packed, ("depth", "tile"))
+    dot_real, dot_imag, image_norm = packed[:, 0], packed[:, 1], packed[:, 2]
+    picked = packed[:, 3:].reshape(shot_count, 4, -1)
+    step_re = (dot_real / image_norm)[:, None, None, None]
+    step_im = (dot_imag / image_norm)[:, None, None, None]
+    new_re = warm_field[:, 0] + step_re * search[:, 0] - step_im * search[:, 1]
+    new_im = warm_field[:, 1] + step_re * search[:, 1] + step_im * search[:, 0]
+    new_field = jnp.stack([new_re, new_im], axis=1)
+    rec_re = (dot_real / image_norm)[:, None]
+    rec_im = (dot_imag / image_norm)[:, None]
+    sampled_re = picked[:, 0] + rec_re * picked[:, 2] - rec_im * picked[:, 3]
+    sampled_im = picked[:, 1] + rec_re * picked[:, 3] + rec_im * picked[:, 2]
+    miss_re = sampled_re - observed[:, 0]
+    miss_im = sampled_im - observed[:, 1]
+    misfit = 0.5 * jnp.sum(miss_re * miss_re + miss_im * miss_im, axis=1)
     adjoint_wide = extended(adjoint_field, (("tile", 3),), 1)
     adjoint_re = adjoint_wide[:, 0]
     adjoint_im = adjoint_wide[:, 1]

time: 868 us -> 899 us (1.036)
  waiting for transfers between devices: 132 us -> 393 us
  blocking collectives: 186 us -> 0 us
  local copies, waits for them, and re-layouts: 89.7 us -> 11.3 us
  between operations: 1.36 us -> 14.7 us
  starting transfers between devices: 390 us -> 401 us
    psum x0 -> x1, waiting for transfers between devices: none -> 275 us  [per_device(): packed = lax.psum(packed, ('depth', 'tile'))]
    psum x2 -> x0, blocking collectives: 186 us -> none  [the longest x1 113 us: per_device(): lax.psum((local_real, local_imag, local_norm), ('depth', 'tile'))]
    gather x2 -> x0, local copies, waits for them, and re-layouts: 78.9 us -> none  [per_device(): jnp.take_along_axis(flattened, jnp.broadcast_to(local_index[:, None, :],...]
    ppermute x38, starting transfers between devices: 271 us -> 284 us  [extended(): before = lax.ppermute(last, axis, up)]
    ppermute x38, waiting for transfers between devices: 15.4 us -> 5.91 us  [extended(): after = lax.ppermute(leading, axis, down)]
  transfers between devices with their start and end apart: 92 -> 93, of which waited for: 51 -> 50; matrix products, arithmetic and copies ran while one was open for 7% -> 8% of each run, Pallas kernels for 0% -> 0%
where the time goes in v1:
time: 899 us; the launch traced here: 896 us
  starting transfers between devices  401 us (45%)
  waiting for transfers between devices  393 us (44%)
  other arithmetic  65.2 us (7%)
  between operations  14.7 us (2%)
  local copies, waits for them, and re-layouts  11.3 us (1%)
    ppermute x38, starting transfers between devices, extended(): before = lax.ppermute(last, axis, up)  284 us
    psum x1, waiting for transfers between devices, per_device(): packed = lax.psum(packed, ('depth', 'tile'))  275 us
    ppermute x16, waiting for transfers between devices, shifted(): lax.ppermute(value, axis, [(source, source + steps) for source in range(l...  80.2 us
    ppermute x38, starting transfers between devices, extended(): after = lax.ppermute(leading, axis, down)  71.8 us
    ppermute x16, starting transfers between devices, shifted(): lax.ppermute(value, axis, [(source, source + steps) for source in range(l...  44.6 us
    ppermute x38, waiting for transfers between devices, extended(): before = lax.ppermute(last, axis, up)  32.3 us
    concatenate x36, other arithmetic, extended(): shard = jnp.concatenate([before, shard, after], axis=dim)  20.3 us
  transfers between devices with their start and end apart: 93, of which 50 were waited for; matrix products, arithmetic and copies ran while one was open for 8% of the time, Pallas kernels for 0%

profile of v1, /device:TPU:1, one launch (start us, length us, event | category | flops | bytes accessed | tf_op | source)
XLA Modules:
  0.0 895.7 jit_solution(5374901224782929633)
XLA Ops:
  8.4 3.9 collective-permute-start.10
  14.4 5.2 collective-permute-start.14
  32.3 5.1 collective-permute-start.12
  40.9 5.1 collective-permute-start.20
  50.7 3.6 fusion.119
  54.6 255.1 %while.36 = (s32[]{:T(128)}, f32[16,2,2,8,256]{4,3,2,1,0:T(8,128)S(1)}, f32[16,2,8,256]{3,2,1,0:T(8,128)S(1)}, s32[]{:T(128)}, f32[2,8,256]{2,1,0:T(8,128)S(1)},...) while((s32[]{:T(128)}, ...), condition=%wide.region_1.2_spmd.clone, body=%wide.region_0.1_spmd.clone.sunk | while | flops 5369095 | bytes 13800788 | solution.py:214
  54.7 3.7 collective-permute-start
  58.4 3.8 collective-permute-done
  64.1 8.4 collective-permute-start.2
  77.1 5.8 collective-permute-start.4
  85.2 3.7 collective-permute-start
  88.9 3.3 collective-permute-done
  94.1 9.8 %collective-permute-start.2 = (f32[16,2,1,256]{3,2,1,0:T(1,128)S(1)}, f32[16,2,1,256]{3,2,1,0:T(1,128)S(1)}, u32[]{:S(2)}, u32[]{:S(2)}) collective-permute-start(f32[16,2,1,256]{3,2,1,0:T(1,128)S(1)} %get-tuple-element.707), channel_id=1, source_target_pairs={{0,1},{1,2},{2,3},{3,4},{4,5},{5,6},{6,7},{7,8},{8,9},{9,10},{10,1... | collective-permute-start | bytes 98312 | tf_op jit(solution)/shard_map/while/body/eval_jaxpr/ppermute | solution.py:23
  108.4 5.7 collective-permute-start.4
  116.4 4.8 collective-permute-start
  126.5 9.8 %collective-permute-start.2 = (f32[16,2,1,256]{3,2,1,0:T(1,128)S(1)}, f32[16,2,1,256]{3,2,1,0:T(1,128)S(1)}, u32[]{:S(2)}, u32[]{:S(2)}) collective-permute-start(f32[16,2,1,256]{3,2,1,0:T(1,128)S(1)} %get-tuple-element.707), channel_id=1, source_target_pairs={{0,1},{1,2},{2,3},{3,4},{4,5},{5,6},{6,7},{7,8},{8,9},{9,10},{10,1... | collective-permute-start | bytes 98312 | tf_op jit(solution)/shard_map/while/body/eval_jaxpr/ppermute | solution.py:23
  140.8 5.7 collective-permute-start.4
  149.0 4.4 collective-permute-start
  153.4 3.3 collective-permute-done
  158.6 9.8 %collective-permute-start.2 = (f32[16,2,1,256]{3,2,1,0:T(1,128)S(1)}, f32[16,2,1,256]{3,2,1,0:T(1,128)S(1)}, u32[]{:S(2)}, u32[]{:S(2)}) collective-permute-start(f32[16,2,1,256]{3,2,1,0:T(1,128)S(1)} %get-tuple-element.707), channel_id=1, source_target_pairs={{0,1},{1,2},{2,3},{3,4},{4,5},{5,6},{6,7},{7,8},{8,9},{9,10},{10,1... | collective-permute-start | bytes 98312 | tf_op jit(solution)/shard_map/while/body/eval_jaxpr/ppermute | solution.py:23
  173.0 5.7 collective-permute-start.4
  181.2 4.4 collective-permute-start
  185.6 3.3 collective-permute-done
  190.8 9.8 %collective-permute-start.2 = (f32[16,2,1,256]{3,2,1,0:T(1,128)S(1)}, f32[16,2,1,256]{3,2,1,0:T(1,128)S(1)}, u32[]{:S(2)}, u32[]{:S(2)}) collective-permute-start(f32[16,2,1,256]{3,2,1,0:T(1,128)S(1)} %get-tuple-element.707), channel_id=1, source_target_pairs={{0,1},{1,2},{2,3},{3,4},{4,5},{5,6},{6,7},{7,8},{8,9},{9,10},{10,1... | collective-permute-start | bytes 98312 | tf_op jit(solution)/shard_map/while/body/eval_jaxpr/ppermute | solution.py:23
  205.2 5.7 collective-permute-start.4
  213.4 4.4 collective-permute-start
  223.0 9.8 %collective-permute-start.2 = (f32[16,2,1,256]{3,2,1,0:T(1,128)S(1)}, f32[16,2,1,256]{3,2,1,0:T(1,128)S(1)}, u32[]{:S(2)}, u32[]{:S(2)}) collective-permute-start(f32[16,2,1,256]{3,2,1,0:T(1,128)S(1)} %get-tuple-element.707), channel_id=1, source_target_pairs={{0,1},{1,2},{2,3},{3,4},{4,5},{5,6},{6,7},{7,8},{8,9},{9,10},{10,1... | collective-permute-start | bytes 98312 | tf_op jit(solution)/shard_map/while/body/eval_jaxpr/ppermute | solution.py:23
  237.4 5.7 collective-permute-start.4
  245.6 4.4 collective-permute-start
  255.3 9.8 %collective-permute-start.2 = (f32[16,2,1,256]{3,2,1,0:T(1,128)S(1)}, f32[16,2,1,256]{3,2,1,0:T(1,128)S(1)}, u32[]{:S(2)}, u32[]{:S(2)}) collective-permute-start(f32[16,2,1,256]{3,2,1,0:T(1,128)S(1)} %get-tuple-element.707), channel_id=1, source_target_pairs={{0,1},{1,2},{2,3},{3,4},{4,5},{5,6},{6,7},{7,8},{8,9},{9,10},{10,1... | collective-permute-start | bytes 98312 | tf_op jit(solution)/shard_map/while/body/eval_jaxpr/ppermute | solution.py:23
  269.6 5.7 collective-permute-start.4
  277.8 4.4 collective-permute-start
  287.5 9.8 %collective-permute-start.2 = (f32[16,2,1,256]{3,2,1,0:T(1,128)S(1)}, f32[16,2,1,256]{3,2,1,0:T(1,128)S(1)}, u32[]{:S(2)}, u32[]{:S(2)}) collective-permute-start(f32[16,2,1,256]{3,2,1,0:T(1,128)S(1)} %get-tuple-element.707), channel_id=1, source_target_pairs={{0,1},{1,2},{2,3},{3,4},{4,5},{5,6},{6,7},{7,8},{8,9},{9,10},{10,1... | collective-permute-start | bytes 98312 | tf_op jit(solution)/shard_map/while/body/eval_jaxpr/ppermute | solution.py:23
  301.8 5.7 collective-permute-start.4
  309.8 256.7 %while.37 = (s32[]{:T(128)}, f32[16,2,2,8,256]{4,3,2,1,0:T(8,128)S(1)}, f32[16,2,8,256]{3,2,0,1:T(8,128)S(1)}, s32[]{:T(128)}, f32[16,2,2,8,256]{4,3,0,1,2:T(8,1...) while((s32[]{:T(128)}, ...), condition=%wide.region_3.4_spmd.clone, body=%wide.region_2.3_spmd.clone.sunk | while | flops 5318663 | bytes 15177044 | solution.py:214
  311.2 6.9 collective-permute-done.5
  320.0 10.3 %collective-permute-start.7 = (f32[16,2,1,256]{3,2,0,1:T(1,128)S(1)}, f32[16,2,1,256]{3,2,0,1:T(1,128)S(1)}, u32[]{:S(2)}, u32[]{:S(2)}) collective-permute-start(f32[16,2,1,256]{3,2,0,1:T(1,128)S(1)} %get-tuple-element.730), channel_id=1, source_target_pairs={{0,1},{1,2},{2,3},{3,4},{4,5},{5,6},{6,7},{7,8},{8,9},{9,10},{10,1... | collective-permute-start | bytes 98312 | tf_op jit(solution)/shard_map/while/body/eval_jaxpr/ppermute | solution.py:23
  334.3 5.7 collective-permute-start.9
  343.6 6.9 collective-permute-done.5
  352.5 10.1 %collective-permute-start.7 = (f32[16,2,1,256]{3,2,0,1:T(1,128)S(1)}, f32[16,2,1,256]{3,2,0,1:T(1,128)S(1)}, u32[]{:S(2)}, u32[]{:S(2)}) collective-permute-start(f32[16,2,1,256]{3,2,0,1:T(1,128)S(1)} %get-tuple-element.730), channel_id=1, source_target_pairs={{0,1},{1,2},{2,3},{3,4},{4,5},{5,6},{6,7},{7,8},{8,9},{9,10},{10,1... | collective-permute-start | bytes 98312 | tf_op jit(solution)/shard_map/while/body/eval_jaxpr/ppermute | solution.py:23
  366.5 5.7 collective-permute-start.9
  375.9 6.6 collective-permute-done.5
  384.5 10.1 %collective-permute-start.7 = (f32[16,2,1,256]{3,2,0,1:T(1,128)S(1)}, f32[16,2,1,256]{3,2,0,1:T(1,128)S(1)}, u32[]{:S(2)}, u32[]{:S(2)}) collective-permute-start(f32[16,2,1,256]{3,2,0,1:T(1,128)S(1)} %get-tuple-element.730), channel_id=1, source_target_pairs={{0,1},{1,2},{2,3},{3,4},{4,5},{5,6},{6,7},{7,8},{8,9},{9,10},{10,1... | collective-permute-start | bytes 98312 | tf_op jit(solution)/shard_map/while/body/eval_jaxpr/ppermute | solution.py:23
  398.5 5.7 collective-permute-start.9
  407.9 6.6 collective-permute-done.5
  416.5 10.1 %collective-permute-start.7 = (f32[16,2,1,256]{3,2,0,1:T(1,128)S(1)}, f32[16,2,1,256]{3,2,0,1:T(1,128)S(1)}, u32[]{:S(2)}, u32[]{:S(2)}) collective-permute-start(f32[16,2,1,256]{3,2,0,1:T(1,128)S(1)} %get-tuple-element.730), channel_id=1, source_target_pairs={{0,1},{1,2},{2,3},{3,4},{4,5},{5,6},{6,7},{7,8},{8,9},{9,10},{10,1... | collective-permute-start | bytes 98312 | tf_op jit(solution)/shard_map/while/body/eval_jaxpr/ppermute | solution.py:23
  430.5 5.7 collective-permute-start.9
  439.9 6.6 collective-permute-done.5
  448.5 10.1 %collective-permute-start.7 = (f32[16,2,1,256]{3,2,0,1:T(1,128)S(1)}, f32[16,2,1,256]{3,2,0,1:T(1,128)S(1)}, u32[]{:S(2)}, u32[]{:S(2)}) collective-permute-start(f32[16,2,1,256]{3,2,0,1:T(1,128)S(1)} %get-tuple-element.730), channel_id=1, source_target_pairs={{0,1},{1,2},{2,3},{3,4},{4,5},{5,6},{6,7},{7,8},{8,9},{9,10},{10,1... | collective-permute-start | bytes 98312 | tf_op jit(solution)/shard_map/while/body/eval_jaxpr/ppermute | solution.py:23
  462.5 5.7 collective-permute-start.9
  471.9 6.6 collective-permute-done.5
  480.5 10.1 %collective-permute-start.7 = (f32[16,2,1,256]{3,2,0,1:T(1,128)S(1)}, f32[16,2,1,256]{3,2,0,1:T(1,128)S(1)}, u32[]{:S(2)}, u32[]{:S(2)}) collective-permute-start(f32[16,2,1,256]{3,2,0,1:T(1,128)S(1)} %get-tuple-element.730), channel_id=1, source_target_pairs={{0,1},{1,2},{2,3},{3,4},{4,5},{5,6},{6,7},{7,8},{8,9},{9,10},{10,1... | collective-permute-start | bytes 98312 | tf_op jit(solution)/shard_map/while/body/eval_jaxpr/ppermute | solution.py:23
  494.5 5.7 collective-permute-start.9
  503.9 6.6 collective-permute-done.5
  512.5 10.1 %collective-permute-start.7 = (f32[16,2,1,256]{3,2,0,1:T(1,128)S(1)}, f32[16,2,1,256]{3,2,0,1:T(1,128)S(1)}, u32[]{:S(2)}, u32[]{:S(2)}) collective-permute-start(f32[16,2,1,256]{3,2,0,1:T(1,128)S(1)} %get-tuple-element.730), channel_id=1, source_target_pairs={{0,1},{1,2},{2,3},{3,4},{4,5},{5,6},{6,7},{7,8},{8,9},{9,10},{10,1... | collective-permute-start | bytes 98312 | tf_op jit(solution)/shard_map/while/body/eval_jaxpr/ppermute | solution.py:23
  526.6 5.7 collective-permute-start.9
  535.9 6.6 collective-permute-done.5
  544.5 10.1 %collective-permute-start.7 = (f32[16,2,1,256]{3,2,0,1:T(1,128)S(1)}, f32[16,2,1,256]{3,2,0,1:T(1,128)S(1)}, u32[]{:S(2)}, u32[]{:S(2)}) collective-permute-start(f32[16,2,1,256]{3,2,0,1:T(1,128)S(1)} %get-tuple-element.730), channel_id=1, source_target_pairs={{0,1},{1,2},{2,3},{3,4},{4,5},{5,6},{6,7},{7,8},{8,9},{9,10},{10,1... | collective-permute-start | bytes 98312 | tf_op jit(solution)/shard_map/while/body/eval_jaxpr/ppermute | solution.py:23
  558.6 5.7 collective-permute-start.9
  566.6 4.3 collective-permute-start.16
  574.7 5.8 collective-permute-done.17
  580.7 10.6 %collective-permute-start.18 = (f32[16,2,4,1,256]{4,3,2,0,1:T(1,128)S(1)}, f32[16,2,4,1,256]{4,3,2,0,1:T(1,128)S(1)}, u32[]{:S(2)}, u32[]{:S(2)}) collective-permute-start(f32[16,2,4,1,256]{4,3,2,0,1:T(1,128)S(1)} %get-tuple-element.567), channel_id=1, source_target_pairs={{0,1},{1,2},{2,3},{3,4},{4,5},{5,6},{6,7},{7,8},{8,9},{9,10},{10,1... | collective-permute-start | bytes 393224 | tf_op jit(solution)/shard_map/ppermute | solution.py:23
  593.4 8.1 fusion.50
  609.6 274.7 %all-reduce.13.cloned.1.call-done = f32[16,1027]{1,0:T(8,128)} async-done(((f32[16,1027]{1,0:T(8,128)}), f32[16,1027]{1,0:T(8,128)}) %all-reduce.13.cloned.1.call-update) | async-done | bytes 65744 | tf_op jit(solution)/shard_map/psum | solution.py:257
  (451 shorter events, 200.6 us)
Async XLA Ops:
  7.2 877.1 %all-reduce.13.cloned.1.call-start = ((), (), s32[]{:S(2)}) async-start(), calls=%async_computation | async-start | bytes 147456 | tf_op jit(solution)/shard_map/psum | solution.py:257
  8.4 23.0 %collective-permute-start.10 = (f32[16,2,1,8,256]{4,3,2,0,1:T(8,128)S(1)}, f32[16,2,1,8,256]{4,3,2,0,1:T(8,128)S(1)}, u32[]{:S(2)}, u32[]{:S(2)}) collective-permute-start(f32[16,2,1,8,256]{4,3,2,0,1:T(8,128)S(1)} %get-tuple-element.576), channel_id=1, source_target_pairs={{0,32},{32,64},{64,96},{96,128},{128,160},{160,192},{192,224},{1,3... | collective-permute-start | bytes 786440 | tf_op jit(solution)/shard_map/ppermute | solution.py:23
  12.3 19.1 %collective-permute-start.11 = (f32[16,2,1,8,256]{4,3,2,0,1:T(8,128)S(1)}, f32[16,2,1,8,256]{4,3,2,0,1:T(8,128)S(1)}, u32[]{:S(2)}, u32[]{:S(2)}) collective-permute-start(f32[16,2,1,8,256]{4,3,2,0,1:T(8,128)S(1)} %get-tuple-element.575), channel_id=1, source_target_pairs={{32,0},{64,32},{96,64},{128,96},{160,128},{192,160},{224,192},{33,... | collective-permute-start | bytes 786440 | tf_op jit(solution)/shard_map/ppermute | solution.py:24
  14.4 31.6 %collective-permute-start.14 = (f32[2,1,256]{2,1,0:T(1,128)S(1)}, f32[2,1,256]{2,1,0:T(1,128)S(1)}, u32[]{:S(2)}, u32[]{:S(2)}) collective-permute-start(f32[2,1,256]{2,1,0:T(1,128)S(1)} %get-tuple-element.587), channel_id=1, source_target_pairs={{0,1},{1,2},{2,3},{3,4},{4,5},{5,6},{6,7},{7,8},{8,9},{9,10},{10,1... | collective-permute-start | bytes 6152 | tf_op jit(solution)/shard_map/ppermute | solution.py:23
  19.6 28.4 %collective-permute-start.15 = (f32[2,1,256]{2,1,0:T(1,128)S(1)}, f32[2,1,256]{2,1,0:T(1,128)S(1)}, u32[]{:S(2)}, u32[]{:S(2)}) collective-permute-start(f32[2,1,256]{2,1,0:T(1,128)S(1)} %get-tuple-element.588), channel_id=1, source_target_pairs={{1,0},{2,1},{3,2},{4,3},{5,4},{6,5},{7,6},{8,7},{9,8},{10,9},{11,1... | collective-permute-start | bytes 6152 | tf_op jit(solution)/shard_map/ppermute | solution.py:24
  32.3 15.7 %collective-permute-start.12 = (f32[16,2,4,1,256]{4,3,2,0,1:T(1,128)}, f32[16,2,4,1,256]{4,3,2,0,1:T(1,128)}, u32[]{:S(2)}, u32[]{:S(2)}) collective-permute-start(f32[16,2,4,1,256]{4,3,2,0,1:T(1,128)} %get-tuple-element.569), channel_id=1, source_target_pairs={{0,1},{1,2},{2,3},{3,4},{4,5},{5,6},{6,7},{7,8},{8,9},{9,10},{10,1... | collective-permute-start | bytes 393224 | tf_op jit(solution)/shard_map/ppermute | solution.py:23
  37.5 10.6 %collective-permute-start.13 = (f32[16,2,4,1,256]{4,3,2,0,1:T(1,128)}, f32[16,2,4,1,256]{4,3,2,0,1:T(1,128)}, u32[]{:S(2)}, u32[]{:S(2)}) collective-permute-start(f32[16,2,4,1,256]{4,3,2,0,1:T(1,128)} %get-tuple-element.570), channel_id=1, source_target_pairs={{1,0},{2,1},{3,2},{4,3},{5,4},{6,5},{7,6},{8,7},{9,8},{10,9},{11,1... | collective-permute-start | bytes 393224 | tf_op jit(solution)/shard_map/ppermute | solution.py:24
  40.9 530.1 %collective-permute-start.20 = (f32[16,2,2,1,256]{4,3,2,0,1:T(1,128)}, f32[16,2,2,1,256]{4,3,2,0,1:T(1,128)}, u32[]{:S(2)}, u32[]{:S(2)}) collective-permute-start(f32[16,2,2,1,256]{4,3,2,0,1:T(1,128)} %get-tuple-element.571), channel_id=1, source_target_pairs={{0,1},{1,2},{2,3},{3,4},{4,5},{5,6},{6,7},{7,8},{8,9},{9,10},{10,1... | collective-permute-start | bytes 196616 | tf_op jit(solution)/shard_map/ppermute | solution.py:23
  46.1 525.0 %collective-permute-start.21 = (f32[16,2,2,1,256]{4,3,2,0,1:T(1,128)}, f32[16,2,2,1,256]{4,3,2,0,1:T(1,128)}, u32[]{:S(2)}, u32[]{:S(2)}) collective-permute-start(f32[16,2,2,1,256]{4,3,2,0,1:T(1,128)} %get-tuple-element.572), channel_id=1, source_target_pairs={{1,0},{2,1},{3,2},{4,3},{5,4},{6,5},{7,6},{8,7},{9,8},{10,9},{11,1... | collective-permute-start | bytes 196616 | tf_op jit(solution)/shard_map/ppermute | solution.py:24
  62.2 10.4 %collective-permute-start.1 = (f32[16,2,1,256]{3,2,1,0:T(1,128)S(1)}, f32[16,2,1,256]{3,2,1,0:T(1,128)S(1)}, u32[]{:S(2)}, u32[]{:S(2)}) collective-permute-start(f32[16,2,1,256]{3,2,1,0:T(1,128)S(1)} %get-tuple-element.706), channel_id=1, source_target_pairs={{1,0},{2,1},{3,2},{4,3},{5,4},{6,5},{7,6},{8,7},{9,8},{10,9},{11,1... | collective-permute-start | bytes 98312 | tf_op jit(solution)/shard_map/while/body/eval_jaxpr/ppermute | solution.py:24
  64.1 9.5 %collective-permute-start.2 = (f32[16,2,1,256]{3,2,1,0:T(1,128)S(1)}, f32[16,2,1,256]{3,2,1,0:T(1,128)S(1)}, u32[]{:S(2)}, u32[]{:S(2)}) collective-permute-start(f32[16,2,1,256]{3,2,1,0:T(1,128)S(1)} %get-tuple-element.707), channel_id=1, source_target_pairs={{0,1},{1,2},{2,3},{3,4},{4,5},{5,6},{6,7},{7,8},{8,9},{9,10},{10,1... | collective-permute-start | bytes 98312 | tf_op jit(solution)/shard_map/while/body/eval_jaxpr/ppermute | solution.py:23
  75.2 7.7 collective-permute-start.3
  92.2 11.7 %collective-permute-start.1 = (f32[16,2,1,256]{3,2,1,0:T(1,128)S(1)}, f32[16,2,1,256]{3,2,1,0:T(1,128)S(1)}, u32[]{:S(2)}, u32[]{:S(2)}) collective-permute-start(f32[16,2,1,256]{3,2,1,0:T(1,128)S(1)} %get-tuple-element.706), channel_id=1, source_target_pairs={{1,0},{2,1},{3,2},{4,3},{5,4},{6,5},{7,6},{8,7},{9,8},{10,9},{11,1... | collective-permute-start | bytes 98312 | tf_op jit(solution)/shard_map/while/body/eval_jaxpr/ppermute | solution.py:24
  94.1 10.8 %collective-permute-start.2 = (f32[16,2,1,256]{3,2,1,0:T(1,128)S(1)}, f32[16,2,1,256]{3,2,1,0:T(1,128)S(1)}, u32[]{:S(2)}, u32[]{:S(2)}) collective-permute-start(f32[16,2,1,256]{3,2,1,0:T(1,128)S(1)} %get-tuple-element.707), channel_id=1, source_target_pairs={{0,1},{1,2},{2,3},{3,4},{4,5},{5,6},{6,7},{7,8},{8,9},{9,10},{10,1... | collective-permute-start | bytes 98312 | tf_op jit(solution)/shard_map/while/body/eval_jaxpr/ppermute | solution.py:23
  116.4 8.1 collective-permute-start
  124.5 11.8 %collective-permute-start.1 = (f32[16,2,1,256]{3,2,1,0:T(1,128)S(1)}, f32[16,2,1,256]{3,2,1,0:T(1,128)S(1)}, u32[]{:S(2)}, u32[]{:S(2)}) collective-permute-start(f32[16,2,1,256]{3,2,1,0:T(1,128)S(1)} %get-tuple-element.706), channel_id=1, source_target_pairs={{1,0},{2,1},{3,2},{4,3},{5,4},{6,5},{7,6},{8,7},{9,8},{10,9},{11,1... | collective-permute-start | bytes 98312 | tf_op jit(solution)/shard_map/while/body/eval_jaxpr/ppermute | solution.py:24
  126.5 10.8 %collective-permute-start.2 = (f32[16,2,1,256]{3,2,1,0:T(1,128)S(1)}, f32[16,2,1,256]{3,2,1,0:T(1,128)S(1)}, u32[]{:S(2)}, u32[]{:S(2)}) collective-permute-start(f32[16,2,1,256]{3,2,1,0:T(1,128)S(1)} %get-tuple-element.707), channel_id=1, source_target_pairs={{0,1},{1,2},{2,3},{3,4},{4,5},{5,6},{6,7},{7,8},{8,9},{9,10},{10,1... | collective-permute-start | bytes 98312 | tf_op jit(solution)/shard_map/while/body/eval_jaxpr/ppermute | solution.py:23
  149.0 7.7 collective-permute-start
  156.7 11.8 %collective-permute-start.1 = (f32[16,2,1,256]{3,2,1,0:T(1,128)S(1)}, f32[16,2,1,256]{3,2,1,0:T(1,128)S(1)}, u32[]{:S(2)}, u32[]{:S(2)}) collective-permute-start(f32[16,2,1,256]{3,2,1,0:T(1,128)S(1)} %get-tuple-element.706), channel_id=1, source_target_pairs={{1,0},{2,1},{3,2},{4,3},{5,4},{6,5},{7,6},{8,7},{9,8},{10,9},{11,1... | collective-permute-start | bytes 98312 | tf_op jit(solution)/shard_map/while/body/eval_jaxpr/ppermute | solution.py:24
  158.6 10.8 %collective-permute-start.2 = (f32[16,2,1,256]{3,2,1,0:T(1,128)S(1)}, f32[16,2,1,256]{3,2,1,0:T(1,128)S(1)}, u32[]{:S(2)}, u32[]{:S(2)}) collective-permute-start(f32[16,2,1,256]{3,2,1,0:T(1,128)S(1)} %get-tuple-element.707), channel_id=1, source_target_pairs={{0,1},{1,2},{2,3},{3,4},{4,5},{5,6},{6,7},{7,8},{8,9},{9,10},{10,1... | collective-permute-start | bytes 98312 | tf_op jit(solution)/shard_map/while/body/eval_jaxpr/ppermute | solution.py:23
  181.2 7.7 collective-permute-start
  188.9 11.8 %collective-permute-start.1 = (f32[16,2,1,256]{3,2,1,0:T(1,128)S(1)}, f32[16,2,1,256]{3,2,1,0:T(1,128)S(1)}, u32[]{:S(2)}, u32[]{:S(2)}) collective-permute-start(f32[16,2,1,256]{3,2,1,0:T(1,128)S(1)} %get-tuple-element.706), channel_id=1, source_target_pairs={{1,0},{2,1},{3,2},{4,3},{5,4},{6,5},{7,6},{8,7},{9,8},{10,9},{11,1... | collective-permute-start | bytes 98312 | tf_op jit(solution)/shard_map/while/body/eval_jaxpr/ppermute | solution.py:24
  190.8 10.8 %collective-permute-start.2 = (f32[16,2,1,256]{3,2,1,0:T(1,128)S(1)}, f32[16,2,1,256]{3,2,1,0:T(1,128)S(1)}, u32[]{:S(2)}, u32[]{:S(2)}) collective-permute-start(f32[16,2,1,256]{3,2,1,0:T(1,128)S(1)} %get-tuple-element.707), channel_id=1, source_target_pairs={{0,1},{1,2},{2,3},{3,4},{4,5},{5,6},{6,7},{7,8},{8,9},{9,10},{10,1... | collective-permute-start | bytes 98312 | tf_op jit(solution)/shard_map/while/body/eval_jaxpr/ppermute | solution.py:23
  213.4 7.7 collective-permute-start
  221.1 11.8 %collective-permute-start.1 = (f32[16,2,1,256]{3,2,1,0:T(1,128)S(1)}, f32[16,2,1,256]{3,2,1,0:T(1,128)S(1)}, u32[]{:S(2)}, u32[]{:S(2)}) collective-permute-start(f32[16,2,1,256]{3,2,1,0:T(1,128)S(1)} %get-tuple-element.706), channel_id=1, source_target_pairs={{1,0},{2,1},{3,2},{4,3},{5,4},{6,5},{7,6},{8,7},{9,8},{10,9},{11,1... | collective-permute-start | bytes 98312 | tf_op jit(solution)/shard_map/while/body/eval_jaxpr/ppermute | solution.py:24
  223.0 10.8 %collective-permute-start.2 = (f32[16,2,1,256]{3,2,1,0:T(1,128)S(1)}, f32[16,2,1,256]{3,2,1,0:T(1,128)S(1)}, u32[]{:S(2)}, u32[]{:S(2)}) collective-permute-start(f32[16,2,1,256]{3,2,1,0:T(1,128)S(1)} %get-tuple-element.707), channel_id=1, source_target_pairs={{0,1},{1,2},{2,3},{3,4},{4,5},{5,6},{6,7},{7,8},{8,9},{9,10},{10,1... | collective-permute-start | bytes 98312 | tf_op jit(solution)/shard_map/while/body/eval_jaxpr/ppermute | solution.py:23
  245.6 7.7 collective-permute-start
  253.3 11.8 %collective-permute-start.1 = (f32[16,2,1,256]{3,2,1,0:T(1,128)S(1)}, f32[16,2,1,256]{3,2,1,0:T(1,128)S(1)}, u32[]{:S(2)}, u32[]{:S(2)}) collective-permute-start(f32[16,2,1,256]{3,2,1,0:T(1,128)S(1)} %get-tuple-element.706), channel_id=1, source_target_pairs={{1,0},{2,1},{3,2},{4,3},{5,4},{6,5},{7,6},{8,7},{9,8},{10,9},{11,1... | collective-permute-start | bytes 98312 | tf_op jit(solution)/shard_map/while/body/eval_jaxpr/ppermute | solution.py:24
  255.3 10.8 %collective-permute-start.2 = (f32[16,2,1,256]{3,2,1,0:T(1,128)S(1)}, f32[16,2,1,256]{3,2,1,0:T(1,128)S(1)}, u32[]{:S(2)}, u32[]{:S(2)}) collective-permute-start(f32[16,2,1,256]{3,2,1,0:T(1,128)S(1)} %get-tuple-element.707), channel_id=1, source_target_pairs={{0,1},{1,2},{2,3},{3,4},{4,5},{5,6},{6,7},{7,8},{8,9},{9,10},{10,1... | collective-permute-start | bytes 98312 | tf_op jit(solution)/shard_map/while/body/eval_jaxpr/ppermute | solution.py:23
  277.8 7.7 collective-permute-start
  285.5 11.8 %collective-permute-start.1 = (f32[16,2,1,256]{3,2,1,0:T(1,128)S(1)}, f32[16,2,1,256]{3,2,1,0:T(1,128)S(1)}, u32[]{:S(2)}, u32[]{:S(2)}) collective-permute-start(f32[16,2,1,256]{3,2,1,0:T(1,128)S(1)} %get-tuple-element.706), channel_id=1, source_target_pairs={{1,0},{2,1},{3,2},{4,3},{5,4},{6,5},{7,6},{8,7},{9,8},{10,9},{11,1... | collective-permute-start | bytes 98312 | tf_op jit(solution)/shard_map/while/body/eval_jaxpr/ppermute | solution.py:24
  287.5 10.8 %collective-permute-start.2 = (f32[16,2,1,256]{3,2,1,0:T(1,128)S(1)}, f32[16,2,1,256]{3,2,1,0:T(1,128)S(1)}, u32[]{:S(2)}, u32[]{:S(2)}) collective-permute-start(f32[16,2,1,256]{3,2,1,0:T(1,128)S(1)} %get-tuple-element.707), channel_id=1, source_target_pairs={{0,1},{1,2},{2,3},{3,4},{4,5},{5,6},{6,7},{7,8},{8,9},{9,10},{10,1... | collective-permute-start | bytes 98312 | tf_op jit(solution)/shard_map/while/body/eval_jaxpr/ppermute | solution.py:23
  309.9 8.2 collective-permute-start.5
  318.1 12.3 %collective-permute-start.6 = (f32[16,2,1,256]{3,2,0,1:T(1,128)S(1)}, f32[16,2,1,256]{3,2,0,1:T(1,128)S(1)}, u32[]{:S(2)}, u32[]{:S(2)}) collective-permute-start(f32[16,2,1,256]{3,2,0,1:T(1,128)S(1)} %get-tuple-element.729), channel_id=1, source_target_pairs={{1,0},{2,1},{3,2},{4,3},{5,4},{6,5},{7,6},{8,7},{9,8},{10,9},{11,1... | collective-permute-start | bytes 98312 | tf_op jit(solution)/shard_map/while/body/eval_jaxpr/ppermute | solution.py:24
  320.0 11.3 %collective-permute-start.7 = (f32[16,2,1,256]{3,2,0,1:T(1,128)S(1)}, f32[16,2,1,256]{3,2,0,1:T(1,128)S(1)}, u32[]{:S(2)}, u32[]{:S(2)}) collective-permute-start(f32[16,2,1,256]{3,2,0,1:T(1,128)S(1)} %get-tuple-element.730), channel_id=1, source_target_pairs={{0,1},{1,2},{2,3},{3,4},{4,5},{5,6},{6,7},{7,8},{8,9},{9,10},{10,1... | collective-permute-start | bytes 98312 | tf_op jit(solution)/shard_map/while/body/eval_jaxpr/ppermute | solution.py:23
  332.4 7.7 collective-permute-start.8
  342.3 8.2 collective-permute-start.5
  350.5 12.1 %collective-permute-start.6 = (f32[16,2,1,256]{3,2,0,1:T(1,128)S(1)}, f32[16,2,1,256]{3,2,0,1:T(1,128)S(1)}, u32[]{:S(2)}, u32[]{:S(2)}) collective-permute-start(f32[16,2,1,256]{3,2,0,1:T(1,128)S(1)} %get-tuple-element.729), channel_id=1, source_target_pairs={{1,0},{2,1},{3,2},{4,3},{5,4},{6,5},{7,6},{8,7},{9,8},{10,9},{11,1... | collective-permute-start | bytes 98312 | tf_op jit(solution)/shard_map/while/body/eval_jaxpr/ppermute | solution.py:24
  352.5 11.1 %collective-permute-start.7 = (f32[16,2,1,256]{3,2,0,1:T(1,128)S(1)}, f32[16,2,1,256]{3,2,0,1:T(1,128)S(1)}, u32[]{:S(2)}, u32[]{:S(2)}) collective-permute-start(f32[16,2,1,256]{3,2,0,1:T(1,128)S(1)} %get-tuple-element.730), channel_id=1, source_target_pairs={{0,1},{1,2},{2,3},{3,4},{4,5},{5,6},{6,7},{7,8},{8,9},{9,10},{10,1... | collective-permute-start | bytes 98312 | tf_op jit(solution)/shard_map/while/body/eval_jaxpr/ppermute | solution.py:23
  364.6 7.7 collective-permute-start.8
  374.6 7.9 collective-permute-start.5
  382.5 12.1 %collective-permute-start.6 = (f32[16,2,1,256]{3,2,0,1:T(1,128)S(1)}, f32[16,2,1,256]{3,2,0,1:T(1,128)S(1)}, u32[]{:S(2)}, u32[]{:S(2)}) collective-permute-start(f32[16,2,1,256]{3,2,0,1:T(1,128)S(1)} %get-tuple-element.729), channel_id=1, source_target_pairs={{1,0},{2,1},{3,2},{4,3},{5,4},{6,5},{7,6},{8,7},{9,8},{10,9},{11,1... | collective-permute-start | bytes 98312 | tf_op jit(solution)/shard_map/while/body/eval_jaxpr/ppermute | solution.py:24
  384.5 11.1 %collective-permute-start.7 = (f32[16,2,1,256]{3,2,0,1:T(1,128)S(1)}, f32[16,2,1,256]{3,2,0,1:T(1,128)S(1)}, u32[]{:S(2)}, u32[]{:S(2)}) collective-permute-start(f32[16,2,1,256]{3,2,0,1:T(1,128)S(1)} %get-tuple-element.730), channel_id=1, source_target_pairs={{0,1},{1,2},{2,3},{3,4},{4,5},{5,6},{6,7},{7,8},{8,9},{9,10},{10,1... | collective-permute-start | bytes 98312 | tf_op jit(solution)/shard_map/while/body/eval_jaxpr/ppermute | solution.py:23
  396.6 7.7 collective-permute-start.8
  406.6 7.9 collective-permute-start.5
  414.5 12.1 %collective-permute-start.6 = (f32[16,2,1,256]{3,2,0,1:T(1,128)S(1)}, f32[16,2,1,256]{3,2,0,1:T(1,128)S(1)}, u32[]{:S(2)}, u32[]{:S(2)}) collective-permute-start(f32[16,2,1,256]{3,2,0,1:T(1,128)S(1)} %get-tuple-element.729), channel_id=1, source_target_pairs={{1,0},{2,1},{3,2},{4,3},{5,4},{6,5},{7,6},{8,7},{9,8},{10,9},{11,1... | collective-permute-start | bytes 98312 | tf_op jit(solution)/shard_map/while/body/eval_jaxpr/ppermute | solution.py:24
  416.5 11.1 %collective-permute-start.7 = (f32[16,2,1,256]{3,2,0,1:T(1,128)S(1)}, f32[16,2,1,256]{3,2,0,1:T(1,128)S(1)}, u32[]{:S(2)}, u32[]{:S(2)}) collective-permute-start(f32[16,2,1,256]{3,2,0,1:T(1,128)S(1)} %get-tuple-element.730), channel_id=1, source_target_pairs={{0,1},{1,2},{2,3},{3,4},{4,5},{5,6},{6,7},{7,8},{8,9},{9,10},{10,1... | collective-permute-start | bytes 98312 | tf_op jit(solution)/shard_map/while/body/eval_jaxpr/ppermute | solution.py:23
  428.6 7.7 collective-permute-start.8
  438.6 7.9 collective-permute-start.5
  446.5 12.1 %collective-permute-start.6 = (f32[16,2,1,256]{3,2,0,1:T(1,128)S(1)}, f32[16,2,1,256]{3,2,0,1:T(1,128)S(1)}, u32[]{:S(2)}, u32[]{:S(2)}) collective-permute-start(f32[16,2,1,256]{3,2,0,1:T(1,128)S(1)} %get-tuple-element.729), channel_id=1, source_target_pairs={{1,0},{2,1},{3,2},{4,3},{5,4},{6,5},{7,6},{8,7},{9,8},{10,9},{11,1... | collective-permute-start | bytes 98312 | tf_op jit(solution)/shard_map/while/body/eval_jaxpr/ppermute | solution.py:24
  448.5 11.1 %collective-permute-start.7 = (f32[16,2,1,256]{3,2,0,1:T(1,128)S(1)}, f32[16,2,1,256]{3,2,0,1:T(1,128)S(1)}, u32[]{:S(2)}, u32[]{:S(2)}) collective-permute-start(f32[16,2,1,256]{3,2,0,1:T(1,128)S(1)} %get-tuple-element.730), channel_id=1, source_target_pairs={{0,1},{1,2},{2,3},{3,4},{4,5},{5,6},{6,7},{7,8},{8,9},{9,10},{10,1... | collective-permute-start | bytes 98312 | tf_op jit(solution)/shard_map/while/body/eval_jaxpr/ppermute | solution.py:23
  460.6 7.7 collective-permute-start.8
  470.6 7.9 collective-permute-start.5
  478.5 12.1 %collective-permute-start.6 = (f32[16,2,1,256]{3,2,0,1:T(1,128)S(1)}, f32[16,2,1,256]{3,2,0,1:T(1,128)S(1)}, u32[]{:S(2)}, u32[]{:S(2)}) collective-permute-start(f32[16,2,1,256]{3,2,0,1:T(1,128)S(1)} %get-tuple-element.729), channel_id=1, source_target_pairs={{1,0},{2,1},{3,2},{4,3},{5,4},{6,5},{7,6},{8,7},{9,8},{10,9},{11,1... | collective-permute-start | bytes 98312 | tf_op jit(solution)/shard_map/while/body/eval_jaxpr/ppermute | solution.py:24
  480.5 11.1 %collective-permute-start.7 = (f32[16,2,1,256]{3,2,0,1:T(1,128)S(1)}, f32[16,2,1,256]{3,2,0,1:T(1,128)S(1)}, u32[]{:S(2)}, u32[]{:S(2)}) collective-permute-start(f32[16,2,1,256]{3,2,0,1:T(1,128)S(1)} %get-tuple-element.730), channel_id=1, source_target_pairs={{0,1},{1,2},{2,3},{3,4},{4,5},{5,6},{6,7},{7,8},{8,9},{9,10},{10,1... | collective-permute-start | bytes 98312 | tf_op jit(solution)/shard_map/while/body/eval_jaxpr/ppermute | solution.py:23
  502.6 7.9 collective-permute-start.5
  510.6 12.0 %collective-permute-start.6 = (f32[16,2,1,256]{3,2,0,1:T(1,128)S(1)}, f32[16,2,1,256]{3,2,0,1:T(1,128)S(1)}, u32[]{:S(2)}, u32[]{:S(2)}) collective-permute-start(f32[16,2,1,256]{3,2,0,1:T(1,128)S(1)} %get-tuple-element.729), channel_id=1, source_target_pairs={{1,0},{2,1},{3,2},{4,3},{5,4},{6,5},{7,6},{8,7},{9,8},{10,9},{11,1... | collective-permute-start | bytes 98312 | tf_op jit(solution)/shard_map/while/body/eval_jaxpr/ppermute | solution.py:24
  512.5 11.1 %collective-permute-start.7 = (f32[16,2,1,256]{3,2,0,1:T(1,128)S(1)}, f32[16,2,1,256]{3,2,0,1:T(1,128)S(1)}, u32[]{:S(2)}, u32[]{:S(2)}) collective-permute-start(f32[16,2,1,256]{3,2,0,1:T(1,128)S(1)} %get-tuple-element.730), channel_id=1, source_target_pairs={{0,1},{1,2},{2,3},{3,4},{4,5},{5,6},{6,7},{7,8},{8,9},{9,10},{10,1... | collective-permute-start | bytes 98312 | tf_op jit(solution)/shard_map/while/body/eval_jaxpr/ppermute | solution.py:23
  534.6 7.9 collective-permute-start.5
  542.6 12.0 %collective-permute-start.6 = (f32[16,2,1,256]{3,2,0,1:T(1,128)S(1)}, f32[16,2,1,256]{3,2,0,1:T(1,128)S(1)}, u32[]{:S(2)}, u32[]{:S(2)}) collective-permute-start(f32[16,2,1,256]{3,2,0,1:T(1,128)S(1)} %get-tuple-element.729), channel_id=1, source_target_pairs={{1,0},{2,1},{3,2},{4,3},{5,4},{6,5},{7,6},{8,7},{9,8},{10,9},{11,1... | collective-permute-start | bytes 98312 | tf_op jit(solution)/shard_map/while/body/eval_jaxpr/ppermute | solution.py:24
  544.5 11.1 %collective-permute-start.7 = (f32[16,2,1,256]{3,2,0,1:T(1,128)S(1)}, f32[16,2,1,256]{3,2,0,1:T(1,128)S(1)}, u32[]{:S(2)}, u32[]{:S(2)}) collective-permute-start(f32[16,2,1,256]{3,2,0,1:T(1,128)S(1)} %get-tuple-element.730), channel_id=1, source_target_pairs={{0,1},{1,2},{2,3},{3,4},{4,5},{5,6},{6,7},{7,8},{8,9},{9,10},{10,1... | collective-permute-start | bytes 98312 | tf_op jit(solution)/shard_map/while/body/eval_jaxpr/ppermute | solution.py:23
  566.6 8.0 collective-permute-start.16
  580.7 20.9 %collective-permute-start.18 = (f32[16,2,4,1,256]{4,3,2,0,1:T(1,128)S(1)}, f32[16,2,4,1,256]{4,3,2,0,1:T(1,128)S(1)}, u32[]{:S(2)}, u32[]{:S(2)}) collective-permute-start(f32[16,2,4,1,256]{4,3,2,0,1:T(1,128)S(1)} %get-tuple-element.567), channel_id=1, source_target_pairs={{0,1},{1,2},{2,3},{3,4},{4,5},{5,6},{6,7},{7,8},{8,9},{9,10},{10,1... | collective-permute-start | bytes 393224 | tf_op jit(solution)/shard_map/ppermute | solution.py:23
  591.3 10.4 %collective-permute-start.19 = (f32[16,2,4,1,256]{4,3,2,0,1:T(1,128)S(1)}, f32[16,2,4,1,256]{4,3,2,0,1:T(1,128)S(1)}, u32[]{:S(2)}, u32[]{:S(2)}) collective-permute-start(f32[16,2,4,1,256]{4,3,2,0,1:T(1,128)S(1)} %get-tuple-element.568), channel_id=1, source_target_pairs={{1,0},{2,1},{3,2},{4,3},{5,4},{6,5},{7,6},{8,7},{9,8},{10,9},{11,1... | collective-permute-start | bytes 393224 | tf_op jit(solution)/shard_map/ppermute | solution.py:24
  (46 other events, 381.7 us)
Sparse Core Ops, SparseCore 0:
  608.3 275.9 all-reduce.12

commit v2 on v0

--- a/solution.py
+++ b/solution.py
@@ -154,68 +154,63 @@
     source_re = jnp.where(hits, SOURCE_AMPLITUDE, 0.0).astype(jnp.float32)
     forcing = jnp.stack([source_re, jnp.zeros_like(source_re)], axis=1)
     residual = forcing - apply_operator(warm_field)
-    inv_re, inv_im = inverse_diagonal(slowness_sq, damping)
+
+    shots_here = shot_count // depth_count
+    reach = -(-(full_depth - 1) // width_len)
+    halo = reach * width_len
+    window = width_len + 2 * halo
+
+    def with_neighbour_rows(block):
+        pieces = [shifted(block, "tile", step) for step in range(reach, 0, -1)]
+        pieces.append(block)
+        pieces += [shifted(block, "tile", -step) for step in range(1, reach + 1)]
+        return jnp.concatenate(pieces, axis=-2)
+
+    spread = jnp.broadcast_to(slowness_sq[None], (depth_count,) + slowness_sq.shape)
+    slowness_all = lax.all_to_all(spread, "depth", 0, 1, tiled=True)[0]
+    slowness_ext = with_neighbour_rows(slowness_all)
+    rows_ext = tile_index * width_len - halo + jnp.arange(window, dtype=jnp.int32)
+    damping_ext = damping_field(
+        pml_width,
+        jnp.arange(full_depth, dtype=jnp.float32),
+        rows_ext.astype(jnp.float32),
+        full_depth * 1.0,
+        full_width * 1.0,
+    )[:, :, None]
+    inv_re, inv_im = inverse_diagonal(slowness_ext, damping_ext)
+    row_valid = ((rows_ext >= 0) & (rows_ext < full_width))[:, None]
 
     def couple(plane_in):
-        with_rims = extended(plane_in, (("tile", 2),), 1)
-        return plane_coupling(pad_long(with_rims), width_len, long_len)
-
-    def down_section(source_part, incoming):
-        previous = incoming
-        layers_out = []
-        for layer_no in range(layer_len):
-            source_term = source_part[:, :, layer_no] + couple(previous)
-            previous = complex_scale(inv_re[layer_no], inv_im[layer_no], source_term)
-            layers_out.append(previous)
-        return jnp.stack(layers_out, axis=2)
-
-    def up_section(downward_part, incoming):
-        previous = incoming
-        layers_out = [None] * layer_len
-        for layer_no in range(layer_len - 1, -1, -1):
-            previous = downward_part[:, :, layer_no] + complex_scale(
-                inv_re[layer_no], inv_im[layer_no], couple(previous)
-            )
-            layers_out[layer_no] = previous
-        return jnp.stack(layers_out, axis=2)
-
-    groups = 1
-    per_group = shot_count // groups
-
-    def run_chain(inputs, downward):
-        position = depth_index if downward else depth_count - 1 - depth_index
-
-        def segment_body(segment_no, state_pair):
-            result, outgoing = state_pair
-            if downward:
-                incoming = shifted(outgoing, "depth", 1)
-            else:
-                incoming = shifted(outgoing, "depth", -1)
-            group_no = segment_no - position
-            is_valid = jnp.logical_and(group_no >= 0, group_no < groups)
-            group_start = jnp.clip(group_no, 0, groups - 1) * per_group
-            if downward:
-                updated = down_section(inputs, incoming)
-                edge_plane = updated[:, :, layer_len - 1]
-            else:
-                updated = up_section(inputs, incoming)
-                edge_plane = updated[:, :, 0]
-            current = result
-            result = lax.dynamic_update_slice_in_dim(
-                result, jnp.where(is_valid, updated, current), group_start, 0
-            )
-            outgoing = jnp.where(is_valid, edge_plane, outgoing)
-            return (result, outgoing)
-
-        initial = (
-            jnp.zeros_like(inputs),
-            jnp.zeros((per_group, 2, width_len, long_len), jnp.float32),
+        return plane_coupling(
+            jnp.pad(plane_in, [(0, 0)] * (plane_in.ndim - 2) + [(1, 1), (1, 1)]),
+            window,
+            long_len,
         )
-        final_pair = lax.fori_loop(0, depth_count + groups - 1, segment_body, initial)
-        return final_pair[0]
-
-    downward = run_chain(residual, True)
-    search = run_chain(downward, False)
+
+    residual_t = lax.all_to_all(residual, "depth", 0, 2, tiled=True)
+    residual_ext = with_neighbour_rows(residual_t)
+    previous = jnp.zeros((shots_here, 2, window, long_len), jnp.float32)
+    layers_out = []
+    for layer_no in range(full_depth):
+        source_term = residual_ext[:, :, layer_no] + couple(previous)
+        previous = jnp.where(
+            row_valid, complex_scale(inv_re[layer_no], inv_im[layer_no], source_term), 0.0
+        )
+        layers_out.append(previous[:, :, halo : halo + width_len])
+    downward_t = jnp.stack(layers_out, axis=2)
+    downward_ext = with_neighbour_rows(downward_t)
+    previous = jnp.zeros((shots_here, 2, window, long_len), jnp.float32)
+    layers_out = [None] * full_depth
+    for layer_no in range(full_depth - 1, -1, -1):
+        previous = jnp.where(
+            row_valid,
+            downward_ext[:, :, layer_no]
+            + complex_scale(inv_re[layer_no], inv_im[layer_no], couple(previous)),
+            0.0,
+        )
+        layers_out[layer_no] = previous[:, :, halo : halo + width_len]
+    search_t = jnp.stack(layers_out, axis=2)
+    search = lax.all_to_all(search_t, "depth", 2, 0, tiled=True)
     image_field = apply_operator(search)
     local_real = jnp.sum(
         image_field[:, 0] * residual[:, 0] + image_field[:, 1] * residual[:, 1], axis=(1, 2, 3)
@@ -247,15 +242,17 @@
         & (local_width >= 0)
         & (local_width < width_len)
     )
-    local_index = jnp.where(
-        is_owned, (local_depth * width_len + local_width) * long_len + rec_long, 0
-    )
-    flattened = new_field.reshape(shot_count, 2, layer_len * width_len * long_len)
-    sampled = jnp.take_along_axis(
-        flattened,
-        jnp.broadcast_to(local_index[:, None, :], (shot_count, 2, local_index.shape[1])),
-        axis=2,
-    )
+    row_count = layer_len * width_len
+    local_row = jnp.where(is_owned, local_depth * width_len + local_width, -1)
+    row_hot = (local_row[:, :, None] == jnp.arange(row_count, dtype=jnp.int32)).astype(jnp.float32)
+    picked_rows = jnp.einsum(
+        "srk,sqky->sqry",
+        row_hot,
+        new_field.reshape(shot_count, 2, row_count, long_len),
+        precision=lax.Precision.HIGHEST,
+    )
+    col_hot = rec_long[:, None, :, None] == jnp.arange(long_len, dtype=jnp.int32)
+    sampled = jnp.sum(jnp.where(col_hot, picked_rows, 0.0), axis=-1)
     data_miss = sampled - observed
     squared = jnp.sum(data_miss * data_miss, axis=1)
     partial_misfit = 0.5 * jnp.sum(jnp.where(is_owned, squared, 0.0), axis=1)

time: 868 us -> 415 us (0.48)
  starting transfers between devices: 390 us -> 99.7 us
  local copies, waits for them, and re-layouts: 89.7 us -> 18.7 us
  waiting for transfers between devices: 132 us -> 66.8 us
  blocking collectives: 186 us -> 159 us
    ppermute x38 -> x6, starting transfers between devices: 271 us -> 28.3 us  [extended(): before = lax.ppermute(last, axis, up)]
    gather x2 -> x0, local copies, waits for them, and re-layouts: 78.9 us -> none  [per_device(): jnp.take_along_axis(flattened, jnp.broadcast_to(local_index[:, None, :],...]
    ppermute x38 -> x6, starting transfers between devices: 71.8 us -> 10.8 us  [extended(): after = lax.ppermute(leading, axis, down)]
    ppermute x16 -> x12, waiting for transfers between devices: 81.1 us -> 39.5 us  [shifted(): lax.ppermute(value, axis, [(source, source + steps) for source in range(l...]
    ppermute x38 -> x6, waiting for transfers between devices: 35.5 us -> 1.78 us  [extended(): before = lax.ppermute(last, axis, up)]
    psum x1, blocking collectives: 113 us -> 86.3 us  [per_device(): lax.psum((local_real, local_imag, local_norm), ('depth', 'tile'))]
    concatenate x36 -> x4, other arithmetic: 20 us -> 1.01 us  [extended(): shard = jnp.concatenate([before, shard, after], axis=dim)]
    all_to_all x0 -> x3, starting transfers between devices: none -> 17.1 us  [the longest x1 6.52 us: per_device(): slowness_all = lax.all_to_all(spread, 'depth', 0, 1, tiled=True)[0]]
  transfers between devices with their start and end apart: 92 -> 27, of which waited for: 51 -> 9; matrix products, arithmetic and copies ran while one was open for 7% -> 12% of each run, Pallas kernels for 0% -> 0%
where the time goes in v2:
time: 415 us; the launch traced here: 413 us
  blocking collectives  159 us (38%)
  starting transfers between devices  99.7 us (24%)
  waiting for transfers between devices  66.8 us (16%)
  other arithmetic  61.9 us (15%)
  local copies, waits for them, and re-layouts  18.7 us (5%)
  matrix products  4.36 us (1%)
    psum x1, blocking collectives, per_device(): lax.psum((local_real, local_imag, local_norm), ('depth', 'tile'))  86.3 us
    psum x1, blocking collectives, per_device(): misfit = lax.psum(partial_misfit, ('depth', 'tile'))  73.2 us
    ppermute x12, starting transfers between devices, shifted(): lax.ppermute(value, axis, [(source, source + steps) for source in range(l...  43.5 us
    ppermute x12, waiting for transfers between devices, shifted(): lax.ppermute(value, axis, [(source, source + steps) for source in range(l...  39.5 us
    ppermute x6, starting transfers between devices, extended(): before = lax.ppermute(last, axis, up)  28.3 us
    add x16, other arithmetic, per_device(): source_term = residual_ext[:, :, layer_no] + couple(previous)  18.1 us
    select_n x15, other arithmetic, per_device(): jnp.where(row_valid, downward_ext[:, :, layer_no] + complex_scale(inv_re[...  15 us
    unnamed x76, local copies, waits for them, and re-layouts  13.1 us
  transfers between devices with their start and end apart: 27, of which 9 were waited for; matrix products, arithmetic and copies ran while one was open for 12% of the time, Pallas kernels for 0%

profile of v2, /device:TPU:1, one launch (start us, length us, event | category | flops | bytes accessed | tf_op | source)
XLA Modules:
  0.0 413.0 jit_solution(17609136724476679147)
XLA Ops:
  0.7 1.1 fusion.733
  1.8 3.9 collective-permute-start.4
  5.7 1.3 collective-permute-start.5
  7.8 5.2 %collective-permute-start.8 = (f32[2,1,256]{2,1,0:T(1,128)S(1)}, f32[2,1,256]{2,1,0:T(1,128)S(1)}, u32[]{:S(2)}, u32[]{:S(2)}) collective-permute-start(f32[2,1,256]{2,1,0:T(1,128)S(1)} %get-tuple-element.137), channel_id=1, source_target_pairs={{0,1},{1,2},{2,3},{3,4},{4,5},{5,6},{6,7},{7,8},{8,9},{9,10},{10,1... | collective-permute-start | bytes 6152 | tf_op jit(solution)/shard_map/ppermute | solution.py:23
  13.0 1.9 collective-permute-start.9
  15.0 1.4 broadcast_in_dim.191
  16.3 6.5 %all-to-all-start = ((f32[8,2,8,256]{3,2,1,0:T(8,128)}), f32[8,2,8,256]{3,2,1,0:T(8,128)S(1)}, u32[]{:S(2)}, u32[]{:S(2)}) async-start(f32[8,2,8,256]{3,2,1,0:T(8,128)} %broadcast_in_dim.191), calls=%async_computation | async-start | bytes 262144 | tf_op jit(solution)/shard_map/all_to_all | solution.py:170
  24.2 1.3 multiply_add_fusion.35
  25.6 1.3 multiply_add_fusion.37
  27.1 1.3 multiply_add_fusion.34
  28.4 1.3 multiply_add_fusion.36
  30.7 1.1 copy.58
  31.9 4.1 collective-permute-start
  36.3 6.0 %collective-permute-start.6 = (f32[16,2,4,1,256]{4,3,2,0,1:T(1,128)S(1)}, f32[16,2,4,1,256]{4,3,2,0,1:T(1,128)S(1)}, u32[]{:S(2)}, u32[]{:S(2)}) collective-permute-start(f32[16,2,4,1,256]{4,3,2,0,1:T(1,128)S(1)} %get-tuple-element.28), channel_id=1, source_target_pairs={{0,1},{1,2},{2,3},{3,4},{4,5},{5,6},{6,7},{7,8},{8,9},{9,10},{10,1... | collective-permute-start | bytes 393224 | tf_op jit(solution)/shard_map/ppermute | solution.py:23
  42.4 1.9 collective-permute-start.7
  44.3 5.1 %collective-permute-start.1 = (f32[16,8,256]{2,1,0:T(8,128)S(1)}, f32[16,8,256]{2,1,0:T(8,128)S(1)}, u32[]{:S(2)}, u32[]{:S(2)}) collective-permute-start(f32[16,8,256]{2,1,0:T(8,128)S(1)} %bitcast.540), channel_id=1, source_target_pairs={{0,1},{1,2},{2,3},{3,4},{4,5},{5,6},{6,7},{7,8},{8,9},{9,10},{10,1... | collective-permute-start | bytes 393224 | tf_op jit(solution)/shard_map/ppermute | solution.py:32
  49.5 1.9 collective-permute-start.2
  51.4 1.3 collective-permute-start.3
  54.2 2.7 fusion.68
  57.9 5.4 %all-to-all-start.1 = ((f32[16,2,2,8,256]{4,3,2,1,0:T(8,128)}), f32[16,2,2,8,256]{4,3,2,1,0:T(8,128)S(1)}, u32[]{:S(2)}, u32[]{:S(2)}) async-start(f32[16,2,2,8,256]{4,3,2,1,0:T(8,128)} %copy_subtract_fusion), calls=%async_computation.1 | async-start | bytes 1048576 | tf_op jit(solution)/shard_map/all_to_all | solution.py:190
  63.5 7.6 %all-to-all-done.1 = f32[16,2,2,8,256]{4,3,2,1,0:T(8,128)S(1)} async-done(((f32[16,2,2,8,256]{4,3,2,1,0:T(8,128)}), f32[16,2,2,8,256]{4,3,2,1,0:T(8,128)S(1)}, u32[]{:S(2)}, u32[]{:S(2)}) %all-to-all-start.1) | async-done | bytes 524320 | tf_op jit(solution)/shard_map/all_to_all | solution.py:190
  71.1 7.7 %collective-permute-start.10 = (f32[2,2,16,8,256]{4,3,2,1,0:T(8,128)S(1)}, f32[2,2,16,8,256]{4,3,2,1,0:T(8,128)S(1)}, u32[]{:S(2)}, u32[]{:S(2)}) collective-permute-start(f32[2,2,16,8,256]{4,3,2,1,0:T(8,128)S(1)} %bitcast.530), channel_id=1, source_target_pairs={{0,2},{1,3},{2,4},{3,5},{4,6},{5,7},{6,8},{7,9},{8,10},{9,11},{10,... | collective-permute-start | bytes 1572872 | tf_op jit(solution)/shard_map/ppermute | solution.py:32
  79.1 6.2 %collective-permute-start.11 = (f32[2,2,16,8,256]{4,3,2,1,0:T(8,128)S(1)}, f32[2,2,16,8,256]{4,3,2,1,0:T(8,128)S(1)}, u32[]{:S(2)}, u32[]{:S(2)}) collective-permute-start(f32[2,2,16,8,256]{4,3,2,1,0:T(8,128)S(1)} %bitcast.531), channel_id=1, source_target_pairs={{0,1},{1,2},{2,3},{3,4},{4,5},{5,6},{6,7},{7,8},{8,9},{9,10},{10,1... | collective-permute-start | bytes 1572872 | tf_op jit(solution)/shard_map/ppermute | solution.py:32
  85.4 1.9 collective-permute-start.12
  87.3 1.5 collective-permute-start.13
  88.9 24.0 %collective-permute-done.11 = f32[2,2,16,8,256]{4,3,2,1,0:T(8,128)S(1)} collective-permute-done((f32[2,2,16,8,256]{4,3,2,1,0:T(8,128)S(1)}, f32[2,2,16,8,256]{4,3,2,1,0:T(8,128)S(1)}, u32[]{:S(2)}, u32[]{:S(2)}) %collective-permute-start.11) | collective-permute-done | bytes 524320 | tf_op jit(solution)/shard_map/ppermute | solution.py:32
  114.6 1.2 fusion.197
  116.0 1.2 fusion.214
  117.3 1.2 fusion.231
  118.7 1.2 fusion.248
  120.1 1.2 fusion.265
  121.4 1.2 fusion.282
  122.8 1.2 fusion.299
  124.2 1.2 fusion.316
  125.5 1.2 fusion.333
  126.9 1.2 fusion.350
  128.3 1.2 fusion.367
  129.7 1.3 fusion.384
  131.1 1.2 fusion.401
  132.5 1.2 fusion.418
  134.0 1.3 collective-permute-start.14
  135.3 9.0 %collective-permute-start.15 = (f32[2,2,16,8,256]{4,3,1,0,2:T(8,128)S(1)}, f32[2,2,16,8,256]{4,3,1,0,2:T(8,128)S(1)}, u32[]{:S(2)}, u32[]{:S(2)}) collective-permute-start(f32[2,2,16,8,256]{4,3,1,0,2:T(8,128)S(1)} %get-tuple-element.14), channel_id=1, source_target_pairs={{0,1},{1,2},{2,3},{3,4},{4,5},{5,6},{6,7},{7,8},{8,9},{9,10},{10,1... | collective-permute-start | bytes 1572872 | tf_op jit(solution)/shard_map/ppermute | solution.py:32
  144.5 1.9 collective-permute-start.22
  146.4 2.4 collective-permute-start.23
  148.9 1.9 collective-permute-start.16
  150.8 1.5 collective-permute-start.17
  153.6 11.5 %collective-permute-done.16 = f32[2,2,16,8,256]{4,3,1,0,2:T(8,128)S(1)} collective-permute-done((f32[2,2,16,8,256]{4,3,1,0,2:T(8,128)S(1)}, f32[2,2,16,8,256]{4,3,1,0,2:T(8,128)S(1)}, u32[]{:S(2)}, u32[]{:S(2)}) %collective-permute-start.16) | collective-permute-done | bytes 524320 | tf_op jit(solution)/shard_map/ppermute | solution.py:32
  165.2 3.0 collective-permute-done.17
  168.2 1.4 copy-done.1
  184.6 1.0 fusion.704
  199.9 5.2 %all-to-all-start.2 = ((f32[2,2,16,8,256]{4,3,1,0,2:T(8,128)}), f32[2,2,16,8,256]{4,3,1,0,2:T(8,128)S(1)}, u32[]{:S(2)}, u32[]{:S(2)}) async-start(f32[2,2,16,8,256]{4,3,1,0,2:T(8,128)} %constant_dynamic-update-slice_fusion.49), calls=%async_computation.2 | async-start | bytes 1048576 | tf_op jit(solution)/shard_map/all_to_all | solution.py:213
  205.8 6.9 %all-to-all-done.2 = f32[2,2,16,8,256]{4,3,1,0,2:T(8,128)S(1)} async-done(((f32[2,2,16,8,256]{4,3,1,0,2:T(8,128)}), f32[2,2,16,8,256]{4,3,1,0,2:T(8,128)S(1)}, u32[]{:S(2)}, u32[]{:S(2)}) %all-to-all-start.2) | async-done | bytes 524320 | tf_op jit(solution)/shard_map/all_to_all | solution.py:213
  212.8 2.5 collective-permute-start.18
  215.5 1.3 collective-permute-start.19
  216.8 1.8 collective-permute-done.18
  218.6 5.4 %collective-permute-done.19 = f32[16,2,1,8,256]{4,3,2,0,1:T(8,128)S(1)} collective-permute-done((f32[16,2,1,8,256]{4,3,2,0,1:T(8,128)S(1)}, f32[16,2,1,8,256]{4,3,2,0,1:T(8,128)S(1)}, u32[]{:S(2)}, u32[]{:S(2)}) %collective-permute-start.19) | collective-permute-done | bytes 262176 | tf_op jit(solution)/shard_map/ppermute | solution.py:24
  224.2 8.7 %collective-permute-start.20 = (f32[16,2,4,1,256]{4,3,2,0,1:T(1,128)S(1)}, f32[16,2,4,1,256]{4,3,2,0,1:T(1,128)S(1)}, u32[]{:S(2)}, u32[]{:S(2)}) collective-permute-start(f32[16,2,4,1,256]{4,3,2,0,1:T(1,128)S(1)} %get-tuple-element.26), channel_id=1, source_target_pairs={{0,1},{1,2},{2,3},{3,4},{4,5},{5,6},{6,7},{7,8},{8,9},{9,10},{10,1... | collective-permute-start | bytes 393224 | tf_op jit(solution)/shard_map/ppermute | solution.py:23
  232.9 1.9 collective-permute-start.21
  235.1 5.6 %collective-permute-done.21 = f32[16,2,4,1,256]{4,3,2,0,1:T(1,128)S(1)} collective-permute-done((f32[16,2,4,1,256]{4,3,2,0,1:T(1,128)S(1)}, f32[16,2,4,1,256]{4,3,2,0,1:T(1,128)S(1)}, u32[]{:S(2)}, u32[]{:S(2)}) %collective-permute-start.21) | collective-permute-done | bytes 131104 | tf_op jit(solution)/shard_map/ppermute | solution.py:24
  242.1 2.7 fusion.111
  245.0 1.3 add_reduce_fusion.1
  246.3 86.3 %all-reduce.38 = (f32[16]{0:T(128)S(1)}, f32[16]{0:T(128)S(1)}, f32[16]{0:T(128)S(1)}) all-reduce(f32[16]{0:T(128)S(1)} %get-tuple-element.7, f32[16]{0:T(128)S(1)} %get-tuple-element.8, f32[16]{0:T(128)S(1)} %get-tuple-element.6), channel_id=1, replica_groups=mesh['depth'=8,'tile'=32] {'depth','tile'}, use_global_device_ids=true, to_apply=%region_5.6 | all-reduce | flops 48 | bytes 384 | tf_op jit(solution)/shard_map/psum | solution.py:225
  334.3 4.4 %fusion = f32[16,2,256]{2,1,0:T(2,128)S(1)} fusion(pred[16,256,256]{1,2,0:T(8,128)(4,1)S(1)} %iota_compare_fusion, f32[16,1,16,256]{3,2,1,0:T(8,128)S(1)} %bitcast.538, f32[16,1,16,256]{3,2,1,0:T(8,128)S(1)} %bitcast.537, s32[16,256]{1,0:T(8,128)S(1)} %get-tuple-element.12), kind=kOutput, calls=%fused_computation.37 | convolution fusion | flops 407035904 | bytes 1622016 | tf_op jit(solution)/shard_map/srk,sqky->sqry/dot_general | solution.py:248
  338.9 73.2 %psum.31 = f32[16]{0:T(128)} all-reduce(f32[16]{0:T(128)S(1)} %broadcast_multiply_fusion.1), channel_id=1, replica_groups=mesh['depth'=8,'tile'=32] {'depth','tile'}, use_global_device_ids=true, to_apply=%region_9.10 | all-reduce | flops 16 | bytes 128 | tf_op jit(solution)/shard_map/psum | solution.py:259
  (226 shorter events, 46.0 us)
Async XLA Ops:
  0.6 35.5 %copy-start = (f32[16,2,2,8,256]{4,3,2,1,0:T(8,128)S(1)}, f32[16,2,2,8,256]{4,3,2,1,0:T(8,128)}, u32[]{:S(2)}) copy-start(f32[16,2,2,8,256]{4,3,2,1,0:T(8,128)} %param.7) | copy-start | bytes 1572868
  0.6 43.7 %copy-start.4 = (f32[2,8,256]{2,1,0:T(8,128)S(1)}, f32[2,8,256]{2,1,0:T(8,128)}, u32[]{:S(2)}) copy-start(f32[2,8,256]{2,1,0:T(8,128)} %param.8) | copy-start | bytes 49156
  1.8 34.3 %collective-permute-start.4 = (f32[16,2,1,8,256]{4,3,2,0,1:T(8,128)S(1)}, f32[16,2,1,8,256]{4,3,2,0,1:T(8,128)S(1)}, u32[]{:S(2)}, u32[]{:S(2)}) collective-permute-start(f32[16,2,1,8,256]{4,3,2,0,1:T(8,128)S(1)} %get-tuple-element.69), channel_id=1, source_target_pairs={{0,32},{32,64},{64,96},{96,128},{128,160},{160,192},{192,224},{1,3... | collective-permute-start | bytes 786440 | tf_op jit(solution)/shard_map/ppermute | solution.py:23
  5.7 30.4 %collective-permute-start.5 = (f32[16,2,1,8,256]{4,3,2,0,1:T(8,128)S(1)}, f32[16,2,1,8,256]{4,3,2,0,1:T(8,128)S(1)}, u32[]{:S(2)}, u32[]{:S(2)}) collective-permute-start(f32[16,2,1,8,256]{4,3,2,0,1:T(8,128)S(1)} %get-tuple-element.68), channel_id=1, source_target_pairs={{32,0},{64,32},{96,64},{128,96},{160,128},{192,160},{224,192},{33,... | collective-permute-start | bytes 786440 | tf_op jit(solution)/shard_map/ppermute | solution.py:24
  7.8 36.4 %collective-permute-start.8 = (f32[2,1,256]{2,1,0:T(1,128)S(1)}, f32[2,1,256]{2,1,0:T(1,128)S(1)}, u32[]{:S(2)}, u32[]{:S(2)}) collective-permute-start(f32[2,1,256]{2,1,0:T(1,128)S(1)} %get-tuple-element.137), channel_id=1, source_target_pairs={{0,1},{1,2},{2,3},{3,4},{4,5},{5,6},{6,7},{7,8},{8,9},{9,10},{10,1... | collective-permute-start | bytes 6152 | tf_op jit(solution)/shard_map/ppermute | solution.py:23
  13.0 31.3 %collective-permute-start.9 = (f32[2,1,256]{2,1,0:T(1,128)S(1)}, f32[2,1,256]{2,1,0:T(1,128)S(1)}, u32[]{:S(2)}, u32[]{:S(2)}) collective-permute-start(f32[2,1,256]{2,1,0:T(1,128)S(1)} %get-tuple-element.138), channel_id=1, source_target_pairs={{1,0},{2,1},{3,2},{4,3},{5,4},{6,5},{7,6},{8,7},{9,8},{10,9},{11,1... | collective-permute-start | bytes 6152 | tf_op jit(solution)/shard_map/ppermute | solution.py:24
  16.3 15.6 %all-to-all-start = ((f32[8,2,8,256]{3,2,1,0:T(8,128)}), f32[8,2,8,256]{3,2,1,0:T(8,128)S(1)}, u32[]{:S(2)}, u32[]{:S(2)}) async-start(f32[8,2,8,256]{3,2,1,0:T(8,128)} %broadcast_in_dim.191), calls=%async_computation | async-start | bytes 262144 | tf_op jit(solution)/shard_map/all_to_all | solution.py:170
  31.9 19.5 %collective-permute-start = (f32[16,8,256]{2,1,0:T(8,128)S(1)}, f32[16,8,256]{2,1,0:T(8,128)S(1)}, u32[]{:S(2)}, u32[]{:S(2)}) collective-permute-start(f32[16,8,256]{2,1,0:T(8,128)S(1)} %bitcast.539), channel_id=1, source_target_pairs={{0,2},{1,3},{2,4},{3,5},{4,6},{5,7},{6,8},{7,9},{8,10},{9,11},{10,... | collective-permute-start | bytes 393224 | tf_op jit(solution)/shard_map/ppermute | solution.py:32
  36.3 16.4 %collective-permute-start.6 = (f32[16,2,4,1,256]{4,3,2,0,1:T(1,128)S(1)}, f32[16,2,4,1,256]{4,3,2,0,1:T(1,128)S(1)}, u32[]{:S(2)}, u32[]{:S(2)}) collective-permute-start(f32[16,2,4,1,256]{4,3,2,0,1:T(1,128)S(1)} %get-tuple-element.28), channel_id=1, source_target_pairs={{0,1},{1,2},{2,3},{3,4},{4,5},{5,6},{6,7},{7,8},{8,9},{9,10},{10,1... | collective-permute-start | bytes 393224 | tf_op jit(solution)/shard_map/ppermute | solution.py:23
  42.4 10.4 %collective-permute-start.7 = (f32[16,2,4,1,256]{4,3,2,0,1:T(1,128)S(1)}, f32[16,2,4,1,256]{4,3,2,0,1:T(1,128)S(1)}, u32[]{:S(2)}, u32[]{:S(2)}) collective-permute-start(f32[16,2,4,1,256]{4,3,2,0,1:T(1,128)S(1)} %get-tuple-element.29), channel_id=1, source_target_pairs={{1,0},{2,1},{3,2},{4,3},{5,4},{6,5},{7,6},{8,7},{9,8},{10,9},{11,1... | collective-permute-start | bytes 393224 | tf_op jit(solution)/shard_map/ppermute | solution.py:24
  44.3 19.0 %collective-permute-start.1 = (f32[16,8,256]{2,1,0:T(8,128)S(1)}, f32[16,8,256]{2,1,0:T(8,128)S(1)}, u32[]{:S(2)}, u32[]{:S(2)}) collective-permute-start(f32[16,8,256]{2,1,0:T(8,128)S(1)} %bitcast.540), channel_id=1, source_target_pairs={{0,1},{1,2},{2,3},{3,4},{4,5},{5,6},{6,7},{7,8},{8,9},{9,10},{10,1... | collective-permute-start | bytes 393224 | tf_op jit(solution)/shard_map/ppermute | solution.py:32
  49.5 13.9 %collective-permute-start.2 = (f32[16,8,256]{2,1,0:T(8,128)S(1)}, f32[16,8,256]{2,1,0:T(8,128)S(1)}, u32[]{:S(2)}, u32[]{:S(2)}) collective-permute-start(f32[16,8,256]{2,1,0:T(8,128)S(1)} %bitcast.541), channel_id=1, source_target_pairs={{1,0},{2,1},{3,2},{4,3},{5,4},{6,5},{7,6},{8,7},{9,8},{10,9},{11,1... | collective-permute-start | bytes 393224 | tf_op jit(solution)/shard_map/ppermute | solution.py:32
  51.4 12.0 %collective-permute-start.3 = (f32[16,8,256]{2,1,0:T(8,128)S(1)}, f32[16,8,256]{2,1,0:T(8,128)S(1)}, u32[]{:S(2)}, u32[]{:S(2)}) collective-permute-start(f32[16,8,256]{2,1,0:T(8,128)S(1)} %bitcast.542), channel_id=1, source_target_pairs={{2,0},{3,1},{4,2},{5,3},{6,4},{7,5},{8,6},{9,7},{10,8},{11,9},{12,... | collective-permute-start | bytes 393224 | tf_op jit(solution)/shard_map/ppermute | solution.py:32
  57.9 13.2 %all-to-all-start.1 = ((f32[16,2,2,8,256]{4,3,2,1,0:T(8,128)}), f32[16,2,2,8,256]{4,3,2,1,0:T(8,128)S(1)}, u32[]{:S(2)}, u32[]{:S(2)}) async-start(f32[16,2,2,8,256]{4,3,2,1,0:T(8,128)} %copy_subtract_fusion), calls=%async_computation.1 | async-start | bytes 1048576 | tf_op jit(solution)/shard_map/all_to_all | solution.py:190
  71.1 17.8 %collective-permute-start.10 = (f32[2,2,16,8,256]{4,3,2,1,0:T(8,128)S(1)}, f32[2,2,16,8,256]{4,3,2,1,0:T(8,128)S(1)}, u32[]{:S(2)}, u32[]{:S(2)}) collective-permute-start(f32[2,2,16,8,256]{4,3,2,1,0:T(8,128)S(1)} %bitcast.530), channel_id=1, source_target_pairs={{0,2},{1,3},{2,4},{3,5},{4,6},{5,7},{6,8},{7,9},{8,10},{9,11},{10,... | collective-permute-start | bytes 1572872 | tf_op jit(solution)/shard_map/ppermute | solution.py:32
  79.1 33.8 %collective-permute-start.11 = (f32[2,2,16,8,256]{4,3,2,1,0:T(8,128)S(1)}, f32[2,2,16,8,256]{4,3,2,1,0:T(8,128)S(1)}, u32[]{:S(2)}, u32[]{:S(2)}) collective-permute-start(f32[2,2,16,8,256]{4,3,2,1,0:T(8,128)S(1)} %bitcast.531), channel_id=1, source_target_pairs={{0,1},{1,2},{2,3},{3,4},{4,5},{5,6},{6,7},{7,8},{8,9},{9,10},{10,1... | collective-permute-start | bytes 1572872 | tf_op jit(solution)/shard_map/ppermute | solution.py:32
  85.4 27.6 %collective-permute-start.12 = (f32[2,2,16,8,256]{4,3,2,1,0:T(8,128)S(1)}, f32[2,2,16,8,256]{4,3,2,1,0:T(8,128)S(1)}, u32[]{:S(2)}, u32[]{:S(2)}) collective-permute-start(f32[2,2,16,8,256]{4,3,2,1,0:T(8,128)S(1)} %bitcast.532), channel_id=1, source_target_pairs={{1,0},{2,1},{3,2},{4,3},{5,4},{6,5},{7,6},{8,7},{9,8},{10,9},{11,1... | collective-permute-start | bytes 1572872 | tf_op jit(solution)/shard_map/ppermute | solution.py:32
  87.3 25.8 %collective-permute-start.13 = (f32[2,2,16,8,256]{4,3,2,1,0:T(8,128)S(1)}, f32[2,2,16,8,256]{4,3,2,1,0:T(8,128)S(1)}, u32[]{:S(2)}, u32[]{:S(2)}) collective-permute-start(f32[2,2,16,8,256]{4,3,2,1,0:T(8,128)S(1)} %bitcast.533), channel_id=1, source_target_pairs={{2,0},{3,1},{4,2},{5,3},{6,4},{7,5},{8,6},{9,7},{10,8},{11,9},{12,... | collective-permute-start | bytes 1572872 | tf_op jit(solution)/shard_map/ppermute | solution.py:32
  113.1 1.5 copy-start.2
  129.6 14.8 %copy-start.3 = (f32[16,2,2,8,256]{4,3,2,1,0:T(8,128)S(1)}, f32[16,2,2,8,256]{4,3,2,1,0:T(8,128)}, u32[]{:S(2)}) copy-start(f32[16,2,2,8,256]{4,3,2,1,0:T(8,128)} %param.9) | copy-start | bytes 1572868
  129.7 19.2 %copy-start.6 = (s32[16,256]{1,0:T(8,128)S(1)}, s32[16,256]{1,0:T(8,128)}, u32[]{:S(2)}) copy-start(s32[16,256]{1,0:T(8,128)} %param.12) | copy-start | bytes 49156
  134.0 16.8 %collective-permute-start.14 = (f32[2,2,16,8,256]{4,3,1,0,2:T(8,128)S(1)}, f32[2,2,16,8,256]{4,3,1,0,2:T(8,128)S(1)}, u32[]{:S(2)}, u32[]{:S(2)}) collective-permute-start(f32[2,2,16,8,256]{4,3,1,0,2:T(8,128)S(1)} %get-tuple-element.14), channel_id=1, source_target_pairs={{0,2},{1,3},{2,4},{3,5},{4,6},{5,7},{6,8},{7,9},{8,10},{9,11},{10,... | collective-permute-start | bytes 1572872 | tf_op jit(solution)/shard_map/ppermute | solution.py:32
  135.3 18.0 %collective-permute-start.15 = (f32[2,2,16,8,256]{4,3,1,0,2:T(8,128)S(1)}, f32[2,2,16,8,256]{4,3,1,0,2:T(8,128)S(1)}, u32[]{:S(2)}, u32[]{:S(2)}) collective-permute-start(f32[2,2,16,8,256]{4,3,1,0,2:T(8,128)S(1)} %get-tuple-element.14), channel_id=1, source_target_pairs={{0,1},{1,2},{2,3},{3,4},{4,5},{5,6},{6,7},{7,8},{8,9},{9,10},{10,1... | collective-permute-start | bytes 1572872 | tf_op jit(solution)/shard_map/ppermute | solution.py:32
  144.5 70.8 %collective-permute-start.22 = (f32[16,2,2,1,256]{4,3,2,0,1:T(1,128)S(1)}, f32[16,2,2,1,256]{4,3,2,0,1:T(1,128)S(1)}, u32[]{:S(2)}, u32[]{:S(2)}) collective-permute-start(f32[16,2,2,1,256]{4,3,2,0,1:T(1,128)S(1)} %get-tuple-element.64), channel_id=1, source_target_pairs={{0,1},{1,2},{2,3},{3,4},{4,5},{5,6},{6,7},{7,8},{8,9},{9,10},{10,1... | collective-permute-start | bytes 196616 | tf_op jit(solution)/shard_map/ppermute | solution.py:23
  146.4 68.9 %collective-permute-start.23 = (f32[16,2,2,1,256]{4,3,2,0,1:T(1,128)S(1)}, f32[16,2,2,1,256]{4,3,2,0,1:T(1,128)S(1)}, u32[]{:S(2)}, u32[]{:S(2)}) collective-permute-start(f32[16,2,2,1,256]{4,3,2,0,1:T(1,128)S(1)} %get-tuple-element.65), channel_id=1, source_target_pairs={{1,0},{2,1},{3,2},{4,3},{5,4},{6,5},{7,6},{8,7},{9,8},{10,9},{11,1... | collective-permute-start | bytes 196616 | tf_op jit(solution)/shard_map/ppermute | solution.py:24
  148.9 16.3 %collective-permute-start.16 = (f32[2,2,16,8,256]{4,3,1,0,2:T(8,128)S(1)}, f32[2,2,16,8,256]{4,3,1,0,2:T(8,128)S(1)}, u32[]{:S(2)}, u32[]{:S(2)}) collective-permute-start(f32[2,2,16,8,256]{4,3,1,0,2:T(8,128)S(1)} %get-tuple-element.14), channel_id=1, source_target_pairs={{1,0},{2,1},{3,2},{4,3},{5,4},{6,5},{7,6},{8,7},{9,8},{10,9},{11,1... | collective-permute-start | bytes 1572872 | tf_op jit(solution)/shard_map/ppermute | solution.py:32
  150.8 17.3 %collective-permute-start.17 = (f32[2,2,16,8,256]{4,3,1,0,2:T(8,128)S(1)}, f32[2,2,16,8,256]{4,3,1,0,2:T(8,128)S(1)}, u32[]{:S(2)}, u32[]{:S(2)}) collective-permute-start(f32[2,2,16,8,256]{4,3,1,0,2:T(8,128)S(1)} %get-tuple-element.14), channel_id=1, source_target_pairs={{2,0},{3,1},{4,2},{5,3},{6,4},{7,5},{8,6},{9,7},{10,8},{11,9},{12,... | collective-permute-start | bytes 1572872 | tf_op jit(solution)/shard_map/ppermute | solution.py:32
  168.2 1.5 copy-start.1
  199.9 12.7 %all-to-all-start.2 = ((f32[2,2,16,8,256]{4,3,1,0,2:T(8,128)}), f32[2,2,16,8,256]{4,3,1,0,2:T(8,128)S(1)}, u32[]{:S(2)}, u32[]{:S(2)}) async-start(f32[2,2,16,8,256]{4,3,1,0,2:T(8,128)} %constant_dynamic-update-slice_fusion.49), calls=%async_computation.2 | async-start | bytes 1048576 | tf_op jit(solution)/shard_map/all_to_all | solution.py:213
  212.8 5.8 %collective-permute-start.18 = (f32[16,2,1,8,256]{4,3,2,0,1:T(8,128)S(1)}, f32[16,2,1,8,256]{4,3,2,0,1:T(8,128)S(1)}, u32[]{:S(2)}, u32[]{:S(2)}) collective-permute-start(f32[16,2,1,8,256]{4,3,2,0,1:T(8,128)S(1)} %get-tuple-element.67), channel_id=1, source_target_pairs={{0,32},{32,64},{64,96},{96,128},{128,160},{160,192},{192,224},{1,3... | collective-permute-start | bytes 786440 | tf_op jit(solution)/shard_map/ppermute | solution.py:23
  215.5 8.5 %collective-permute-start.19 = (f32[16,2,1,8,256]{4,3,2,0,1:T(8,128)S(1)}, f32[16,2,1,8,256]{4,3,2,0,1:T(8,128)S(1)}, u32[]{:S(2)}, u32[]{:S(2)}) collective-permute-start(f32[16,2,1,8,256]{4,3,2,0,1:T(8,128)S(1)} %get-tuple-element.66), channel_id=1, source_target_pairs={{32,0},{64,32},{96,64},{128,96},{160,128},{192,160},{224,192},{33,... | collective-permute-start | bytes 786440 | tf_op jit(solution)/shard_map/ppermute | solution.py:24
  224.2 11.0 %collective-permute-start.20 = (f32[16,2,4,1,256]{4,3,2,0,1:T(1,128)S(1)}, f32[16,2,4,1,256]{4,3,2,0,1:T(1,128)S(1)}, u32[]{:S(2)}, u32[]{:S(2)}) collective-permute-start(f32[16,2,4,1,256]{4,3,2,0,1:T(1,128)S(1)} %get-tuple-element.26), channel_id=1, source_target_pairs={{0,1},{1,2},{2,3},{3,4},{4,5},{5,6},{6,7},{7,8},{8,9},{9,10},{10,1... | collective-permute-start | bytes 393224 | tf_op jit(solution)/shard_map/ppermute | solution.py:23
  232.9 7.8 %collective-permute-start.21 = (f32[16,2,4,1,256]{4,3,2,0,1:T(1,128)S(1)}, f32[16,2,4,1,256]{4,3,2,0,1:T(1,128)S(1)}, u32[]{:S(2)}, u32[]{:S(2)}) collective-permute-start(f32[16,2,4,1,256]{4,3,2,0,1:T(1,128)S(1)} %get-tuple-element.27), channel_id=1, source_target_pairs={{1,0},{2,1},{3,2},{4,3},{5,4},{6,5},{7,6},{8,7},{9,8},{10,9},{11,1... | collective-permute-start | bytes 393224 | tf_op jit(solution)/shard_map/ppermute | solution.py:24
  334.3 4.4 %copy-start.5 = (f32[16,2,256]{2,1,0:T(2,128)S(1)}, f32[16,2,256]{2,1,0:T(2,128)}, u32[]{:S(2)}) copy-start(f32[16,2,256]{2,1,0:T(2,128)} %param.10) | copy-start | bytes 98308

commit v3 on v2

--- a/solution.py
+++ b/solution.py
@@ -222,14 +222,6 @@
         image_field[:, 0] * image_field[:, 0] + image_field[:, 1] * image_field[:, 1],
         axis=(1, 2, 3),
     )
-    dot_real, dot_imag, image_norm = lax.psum(
-        (local_real, local_imag, local_norm), ("depth", "tile")
-    )
-    step_re = (dot_real / image_norm)[:, None, None, None]
-    step_im = (dot_imag / image_norm)[:, None, None, None]
-    new_re = warm_field[:, 0] + step_re * search[:, 0] - step_im * search[:, 1]
-    new_im = warm_field[:, 1] + step_re * search[:, 1] + step_im * search[:, 0]
-    new_field = jnp.stack([new_re, new_im], axis=1)
     plane_cells = full_width * long_len
     rec_depth = receiver_cell // plane_cells
     rec_width = receiver_cell // long_len % full_width
@@ -245,18 +237,44 @@
     row_count = layer_len * width_len
     local_row = jnp.where(is_owned, local_depth * width_len + local_width, -1)
     row_hot = (local_row[:, :, None] == jnp.arange(row_count, dtype=jnp.int32)).astype(jnp.float32)
+    both_fields = jnp.concatenate([warm_field, search], axis=1).reshape(
+        shot_count, 4, row_count, long_len
+    )
     picked_rows = jnp.einsum(
-        "srk,sqky->sqry",
-        row_hot,
-        new_field.reshape(shot_count, 2, row_count, long_len),
-        precision=lax.Precision.HIGHEST,
+        "srk,sqky->sqry", row_hot, both_fields, precision=lax.Precision.HIGHEST
     )
     col_hot = rec_long[:, None, :, None] == jnp.arange(long_len, dtype=jnp.int32)
-    sampled = jnp.sum(jnp.where(col_hot, picked_rows, 0.0), axis=-1)
-    data_miss = sampled - observed
-    squared = jnp.sum(data_miss * data_miss, axis=1)
-    partial_misfit = 0.5 * jnp.sum(jnp.where(is_owned, squared, 0.0), axis=1)
-    misfit = lax.psum(partial_misfit, ("depth", "tile"))
+    picked = jnp.sum(jnp.where(col_hot, picked_rows, 0.0), axis=-1)
+    gap_re = picked[:, 0] - observed[:, 0]
+    gap_im = picked[:, 1] - observed[:, 1]
+    dir_re = picked[:, 2]
+    dir_im = picked[:, 3]
+
+    def owned_sum(values):
+        return jnp.sum(jnp.where(is_owned, values, 0.0), axis=1)
+
+    gap_norm = owned_sum(gap_re * gap_re + gap_im * gap_im)
+    cross_re = owned_sum(gap_re * dir_re + gap_im * dir_im)
+    cross_im = owned_sum(gap_re * dir_im - gap_im * dir_re)
+    dir_norm = owned_sum(dir_re * dir_re + dir_im * dir_im)
+    packed = jnp.stack(
+        [local_real, local_imag, local_norm, gap_norm, cross_re, cross_im, dir_norm], axis=1
+    )
+    packed = lax.psum(packed, ("depth", "tile"))
+    dot_real, dot_imag, image_norm = packed[:, 0], packed[:, 1], packed[:, 2]
+    gap_norm, cross_re, cross_im, dir_norm = packed[:, 3], packed[:, 4], packed[:, 5], packed[:, 6]
+    step_re = (dot_real / image_norm)[:, None, None, None]
+    step_im = (dot_imag / image_norm)[:, None, None, None]
+    new_re = warm_field[:, 0] + step_re * search[:, 0] - step_im * search[:, 1]
+    new_im = warm_field[:, 1] + step_re * search[:, 1] + step_im * search[:, 0]
+    new_field = jnp.stack([new_re, new_im], axis=1)
+    scale_re = dot_real / image_norm
+    scale_im = dot_imag / image_norm
+    misfit = 0.5 * (
+        gap_norm
+        + 2.0 * (scale_re * cross_re - scale_im * cross_im)
+        + (scale_re * scale_re + scale_im * scale_im) * dir_norm
+    )
     adjoint_wide = extended(adjoint_field, (("tile", 3),), 1)
     adjoint_re = adjoint_wide[:, 0]
     adjoint_im = adjoint_wide[:, 1]

time: 415 us -> 348 us (0.84)
  blocking collectives: 159 us -> 78.6 us
  starting transfers between devices: 99.7 us -> 125 us
  waiting for transfers between devices: 66.8 us -> 48.1 us
  matrix products: 4.36 us -> 9.14 us
    psum x2 -> x1, blocking collectives: 159 us -> 78.6 us  [per_device(): packed = lax.psum(packed, ('depth', 'tile'))]
    ppermute x6, starting transfers between devices: 10.8 us -> 32.8 us  [extended(): after = lax.ppermute(leading, axis, down)]
    ppermute x12, waiting for transfers between devices: 39.5 us -> 19.4 us  [shifted(): lax.ppermute(value, axis, [(source, source + steps) for source in range(l...]
    ppermute x6, starting transfers between devices: 28.3 us -> 34.1 us  [extended(): before = lax.ppermute(last, axis, up)]
    dot_general x1, matrix products: 4.36 us -> 9.14 us  [per_device(): jnp.einsum('srk,sqky->sqry', row_hot, both_fields, precision=lax.Precisio...]
  transfers between devices with their start and end apart: 27 -> 27, of which waited for: 9 -> 7; matrix products, arithmetic and copies ran while one was open for 12% -> 23% of each run, Pallas kernels for 0% -> 0%
where the time goes in v3:
time: 348 us; the launch traced here: 346 us
  starting transfers between devices  125 us (36%)
  blocking collectives  78.6 us (23%)
  other arithmetic  62.9 us (18%)
  waiting for transfers between devices  48.1 us (14%)
  local copies, waits for them, and re-layouts  19.9 us (6%)
  matrix products  9.14 us (3%)
    psum x1, blocking collectives, per_device(): packed = lax.psum(packed, ('depth', 'tile'))  78.6 us
    ppermute x12, starting transfers between devices, shifted(): lax.ppermute(value, axis, [(source, source + steps) for source in range(l...  42.5 us
    ppermute x6, starting transfers between devices, extended(): before = lax.ppermute(last, axis, up)  34.1 us
    ppermute x6, starting transfers between devices, extended(): after = lax.ppermute(leading, axis, down)  32.8 us
    ppermute x12, waiting for transfers between devices, shifted(): lax.ppermute(value, axis, [(source, source + steps) for source in range(l...  19.4 us
    add x16, other arithmetic, per_device(): source_term = residual_ext[:, :, layer_no] + couple(previous)  18.1 us
    select_n x15, other arithmetic, per_device(): jnp.where(row_valid, downward_ext[:, :, layer_no] + complex_scale(inv_re[...  15 us
    ppermute x6, waiting for transfers between devices, extended(): after = lax.ppermute(leading, axis, down)  13.8 us
  transfers between devices with their start and end apart: 27, of which 7 were waited for; matrix products, arithmetic and copies ran while one was open for 23% of the time, Pallas kernels for 0%

profile of v3, /device:TPU:1, one launch (start us, length us, event | category | flops | bytes accessed | tf_op | source)
XLA Modules:
  0.0 345.8 jit_solution(15563696335859970555)
XLA Ops:
  0.6 1.1 fusion.746
  1.8 3.9 %collective-permute-start.4 = (f32[16,2,1,8,256]{4,3,2,0,1:T(8,128)S(1)}, f32[16,2,1,8,256]{4,3,2,0,1:T(8,128)S(1)}, u32[]{:S(2)}, u32[]{:S(2)}) collective-permute-start(f32[16,2,1,8,256]{4,3,2,0,1:T(8,128)S(1)} %get-tuple-element.76), channel_id=1, source_target_pairs={{0,32},{32,64},{64,96},{96,128},{128,160},{160,192},{192,224},{1,3... | collective-permute-start | bytes 786440 | tf_op jit(solution)/shard_map/ppermute | solution.py:23
  5.7 1.3 collective-permute-start.5
  7.8 5.2 %collective-permute-start.8 = (f32[2,1,256]{2,1,0:T(1,128)S(1)}, f32[2,1,256]{2,1,0:T(1,128)S(1)}, u32[]{:S(2)}, u32[]{:S(2)}) collective-permute-start(f32[2,1,256]{2,1,0:T(1,128)S(1)} %get-tuple-element.150), channel_id=1, source_target_pairs={{0,1},{1,2},{2,3},{3,4},{4,5},{5,6},{6,7},{7,8},{8,9},{9,10},{10,1... | collective-permute-start | bytes 6152 | tf_op jit(solution)/shard_map/ppermute | solution.py:23
  13.0 1.9 collective-permute-start.9
  15.0 1.4 broadcast_in_dim.194
  16.4 6.5 %all-to-all-start = ((f32[8,2,8,256]{3,2,1,0:T(8,128)}), f32[8,2,8,256]{3,2,1,0:T(8,128)S(1)}, u32[]{:S(2)}, u32[]{:S(2)}) async-start(f32[8,2,8,256]{3,2,1,0:T(8,128)} %broadcast_in_dim.194), calls=%async_computation | async-start | bytes 262144 | tf_op jit(solution)/shard_map/all_to_all | solution.py:170
  22.9 1.3 fusion.744
  24.2 5.4 %collective-permute-start.22 = (f32[16,2,2,1,256]{4,3,2,0,1:T(1,128)S(1)}, f32[16,2,2,1,256]{4,3,2,0,1:T(1,128)S(1)}, u32[]{:S(2)}, u32[]{:S(2)}) collective-permute-start(f32[16,2,2,1,256]{4,3,2,0,1:T(1,128)S(1)} %get-tuple-element.71), channel_id=1, source_target_pairs={{0,1},{1,2},{2,3},{3,4},{4,5},{5,6},{6,7},{7,8},{8,9},{9,10},{10,1... | collective-permute-start | bytes 196616 | tf_op jit(solution)/shard_map/ppermute | solution.py:23
  30.9 1.2 multiply_add_fusion.35
  32.1 1.2 multiply_add_fusion.37
  33.5 1.2 multiply_add_fusion.34
  34.7 1.2 multiply_add_fusion.36
  36.8 1.1 copy.108
  38.1 4.4 %collective-permute-start = (f32[16,8,256]{2,1,0:T(8,128)S(1)}, f32[16,8,256]{2,1,0:T(8,128)S(1)}, u32[]{:S(2)}, u32[]{:S(2)}) collective-permute-start(f32[16,8,256]{2,1,0:T(8,128)S(1)} %bitcast.592), channel_id=1, source_target_pairs={{0,2},{1,3},{2,4},{3,5},{4,6},{5,7},{6,8},{7,9},{8,10},{9,11},{10,... | collective-permute-start | bytes 393224 | tf_op jit(solution)/shard_map/ppermute | solution.py:32
  42.8 2.2 collective-permute-start.6
  45.0 2.1 collective-permute-start.7
  47.2 4.9 %collective-permute-start.1 = (f32[16,8,256]{2,1,0:T(8,128)S(1)}, f32[16,8,256]{2,1,0:T(8,128)S(1)}, u32[]{:S(2)}, u32[]{:S(2)}) collective-permute-start(f32[16,8,256]{2,1,0:T(8,128)S(1)} %bitcast.593), channel_id=1, source_target_pairs={{0,1},{1,2},{2,3},{3,4},{4,5},{5,6},{6,7},{7,8},{8,9},{9,10},{10,1... | collective-permute-start | bytes 393224 | tf_op jit(solution)/shard_map/ppermute | solution.py:32
  52.1 1.9 collective-permute-start.2
  54.1 1.3 collective-permute-start.3
  56.8 2.7 fusion.71
  60.6 5.4 %all-to-all-start.1 = ((f32[16,2,2,8,256]{4,3,2,1,0:T(8,128)}), f32[16,2,2,8,256]{4,3,2,1,0:T(8,128)S(1)}, u32[]{:S(2)}, u32[]{:S(2)}) async-start(f32[16,2,2,8,256]{4,3,2,1,0:T(8,128)} %copy_subtract_fusion), calls=%async_computation.1 | async-start | bytes 1048576 | tf_op jit(solution)/shard_map/all_to_all | solution.py:190
  66.1 7.8 %all-to-all-done.1 = f32[16,2,2,8,256]{4,3,2,1,0:T(8,128)S(1)} async-done(((f32[16,2,2,8,256]{4,3,2,1,0:T(8,128)}), f32[16,2,2,8,256]{4,3,2,1,0:T(8,128)S(1)}, u32[]{:S(2)}, u32[]{:S(2)}) %all-to-all-start.1) | async-done | bytes 524320 | tf_op jit(solution)/shard_map/all_to_all | solution.py:190
  74.0 7.4 %collective-permute-start.10 = (f32[2,2,16,8,256]{4,3,2,1,0:T(8,128)S(1)}, f32[2,2,16,8,256]{4,3,2,1,0:T(8,128)S(1)}, u32[]{:S(2)}, u32[]{:S(2)}) collective-permute-start(f32[2,2,16,8,256]{4,3,2,1,0:T(8,128)S(1)} %bitcast.585), channel_id=1, source_target_pairs={{0,2},{1,3},{2,4},{3,5},{4,6},{5,7},{6,8},{7,9},{8,10},{9,11},{10,... | collective-permute-start | bytes 1572872 | tf_op jit(solution)/shard_map/ppermute | solution.py:32
  81.8 6.2 %collective-permute-start.11 = (f32[2,2,16,8,256]{4,3,2,1,0:T(8,128)S(1)}, f32[2,2,16,8,256]{4,3,2,1,0:T(8,128)S(1)}, u32[]{:S(2)}, u32[]{:S(2)}) collective-permute-start(f32[2,2,16,8,256]{4,3,2,1,0:T(8,128)S(1)} %bitcast.586), channel_id=1, source_target_pairs={{0,1},{1,2},{2,3},{3,4},{4,5},{5,6},{6,7},{7,8},{8,9},{9,10},{10,1... | collective-permute-start | bytes 1572872 | tf_op jit(solution)/shard_map/ppermute | solution.py:32
  88.1 1.9 collective-permute-start.12
  90.0 1.3 collective-permute-start.13
  91.4 24.0 %collective-permute-start.23 = (f32[16,2,2,1,256]{4,3,2,0,1:T(1,128)S(1)}, f32[16,2,2,1,256]{4,3,2,0,1:T(1,128)S(1)}, u32[]{:S(2)}, u32[]{:S(2)}) collective-permute-start(f32[16,2,2,1,256]{4,3,2,0,1:T(1,128)S(1)} %get-tuple-element.72), channel_id=1, source_target_pairs={{1,0},{2,1},{3,2},{4,3},{5,4},{6,5},{7,6},{8,7},{9,8},{10,9},{11,1... | collective-permute-start | bytes 196616 | tf_op jit(solution)/shard_map/ppermute | solution.py:24
  118.0 1.2 fusion.197
  119.3 1.2 fusion.214
  120.7 1.2 fusion.231
  122.1 1.2 fusion.248
  123.4 1.2 fusion.265
  124.8 1.2 fusion.282
  126.2 1.2 fusion.299
  127.5 1.2 fusion.316
  128.9 1.2 fusion.333
  130.3 1.2 fusion.350
  131.6 1.2 fusion.367
  133.0 1.2 fusion.384
  134.4 1.2 fusion.401
  135.7 1.2 fusion.418
  137.3 4.8 %collective-permute-start.14 = (f32[2,2,16,8,256]{4,3,1,0,2:T(8,128)S(1)}, f32[2,2,16,8,256]{4,3,1,0,2:T(8,128)S(1)}, u32[]{:S(2)}, u32[]{:S(2)}) collective-permute-start(f32[2,2,16,8,256]{4,3,1,0,2:T(8,128)S(1)} %get-tuple-element.21), channel_id=1, source_target_pairs={{0,2},{1,3},{2,4},{3,5},{4,6},{5,7},{6,8},{7,9},{8,10},{9,11},{10,... | collective-permute-start | bytes 1572872 | tf_op jit(solution)/shard_map/ppermute | solution.py:32
  142.2 4.8 %collective-permute-start.15 = (f32[2,2,16,8,256]{4,3,1,0,2:T(8,128)S(1)}, f32[2,2,16,8,256]{4,3,1,0,2:T(8,128)S(1)}, u32[]{:S(2)}, u32[]{:S(2)}) collective-permute-start(f32[2,2,16,8,256]{4,3,1,0,2:T(8,128)S(1)} %get-tuple-element.21), channel_id=1, source_target_pairs={{0,1},{1,2},{2,3},{3,4},{4,5},{5,6},{6,7},{7,8},{8,9},{9,10},{10,1... | collective-permute-start | bytes 1572872 | tf_op jit(solution)/shard_map/ppermute | solution.py:32
  147.1 1.6 iota_compare_fusion
  148.7 1.9 collective-permute-start.16
  150.6 1.5 collective-permute-done.14
  152.1 1.5 collective-permute-start.17
  153.7 17.0 %collective-permute-done.15 = f32[2,2,16,8,256]{4,3,1,0,2:T(8,128)S(1)} collective-permute-done((f32[2,2,16,8,256]{4,3,1,0,2:T(8,128)S(1)}, f32[2,2,16,8,256]{4,3,1,0,2:T(8,128)S(1)}, u32[]{:S(2)}, u32[]{:S(2)}) %collective-permute-start.15) | collective-permute-done | bytes 524320 | tf_op jit(solution)/shard_map/ppermute | solution.py:32
  171.1 1.4 copy-done.1
  175.2 1.0 fusion.686
  190.1 1.1 fusion.708
  202.8 3.5 %all-to-all-start.2 = ((f32[2,2,16,8,256]{4,3,1,0,2:T(8,128)}), f32[2,2,16,8,256]{4,3,1,0,2:T(8,128)S(1)}, u32[]{:S(2)}, u32[]{:S(2)}) async-start(f32[2,2,16,8,256]{4,3,1,0,2:T(8,128)} %constant_dynamic-update-slice_fusion.49), calls=%async_computation.2 | async-start | bytes 1048576 | tf_op jit(solution)/shard_map/all_to_all | solution.py:213
  206.8 7.0 %all-to-all-done.2 = f32[2,2,16,8,256]{4,3,1,0,2:T(8,128)S(1)} async-done(((f32[2,2,16,8,256]{4,3,1,0,2:T(8,128)}), f32[2,2,16,8,256]{4,3,1,0,2:T(8,128)S(1)}, u32[]{:S(2)}, u32[]{:S(2)}) %all-to-all-start.2) | async-done | bytes 524320 | tf_op jit(solution)/shard_map/all_to_all | solution.py:213
  213.9 2.5 collective-permute-start.18
  216.4 9.1 %fusion = f32[16,4,256]{2,1,0:T(4,128)S(1)} fusion(pred[16,256,256]{1,2,0:T(8,128)(4,1)} %iota_compare_fusion, f32[16,2,16,256]{3,2,1,0:T(8,128)S(1)} %bitcast.579, f32[16,2,16,256]{3,2,1,0:T(8,128)S(1)} %bitcast.584, s32[16,256]{1,0:T(8,128)S(1)} %get-tuple-element.19), kind=kOutput, calls=%fused_computation.1 | convolution fusion | flops 814006272 | bytes 2179072 | tf_op jit(solution)/shard_map/srk,sqky->sqry/dot_general | solution.py:243
  225.6 1.3 collective-permute-start.19
  227.0 8.5 %collective-permute-done.19 = f32[16,2,1,8,256]{4,3,2,0,1:T(8,128)S(1)} collective-permute-done((f32[16,2,1,8,256]{4,3,2,0,1:T(8,128)S(1)}, f32[16,2,1,8,256]{4,3,2,0,1:T(8,128)S(1)}, u32[]{:S(2)}, u32[]{:S(2)}) %collective-permute-start.19) | collective-permute-done | bytes 262176 | tf_op jit(solution)/shard_map/ppermute | solution.py:24
  235.7 14.9 %collective-permute-start.20 = (f32[16,2,4,1,256]{4,3,2,0,1:T(1,128)S(1)}, f32[16,2,4,1,256]{4,3,2,0,1:T(1,128)S(1)}, u32[]{:S(2)}, u32[]{:S(2)}) collective-permute-start(f32[16,2,4,1,256]{4,3,2,0,1:T(1,128)S(1)} %get-tuple-element.33), channel_id=1, source_target_pairs={{0,1},{1,2},{2,3},{3,4},{4,5},{5,6},{6,7},{7,8},{8,9},{9,10},{10,1... | collective-permute-start | bytes 393224 | tf_op jit(solution)/shard_map/ppermute | solution.py:23
  250.6 2.2 collective-permute-start.21
  253.1 5.3 %collective-permute-done.21 = f32[16,2,4,1,256]{4,3,2,0,1:T(1,128)S(1)} collective-permute-done((f32[16,2,4,1,256]{4,3,2,0,1:T(1,128)S(1)}, f32[16,2,4,1,256]{4,3,2,0,1:T(1,128)S(1)}, u32[]{:S(2)}, u32[]{:S(2)}) %collective-permute-start.21) | collective-permute-done | bytes 131104 | tf_op jit(solution)/shard_map/ppermute | solution.py:24
  259.8 2.7 fusion.114
  262.7 1.3 subtract_reduce_fusion
  264.0 78.6 %psum.7 = f32[16,7]{0,1:T(8,128)S(1)} all-reduce(f32[16,7]{0,1:T(8,128)S(1)} %stack.375), channel_id=1, replica_groups=mesh['depth'=8,'tile'=32] {'depth','tile'}, use_global_device_ids=true, to_apply=%region_8.9 | all-reduce | flops 112 | bytes 896 | tf_op jit(solution)/shard_map/psum | solution.py:263
  (227 shorter events, 44.8 us)
Async XLA Ops:
  0.6 41.9 %copy-start = (f32[16,2,2,8,256]{4,3,2,1,0:T(8,128)S(1)}, f32[16,2,2,8,256]{4,3,2,1,0:T(8,128)}, u32[]{:S(2)}) copy-start(f32[16,2,2,8,256]{4,3,2,1,0:T(8,128)} %param.7) | copy-start | bytes 1572868
  1.8 45.4 %copy-start.4 = (f32[2,8,256]{2,1,0:T(8,128)S(1)}, f32[2,8,256]{2,1,0:T(8,128)}, u32[]{:S(2)}) copy-start(f32[2,8,256]{2,1,0:T(8,128)} %param.8) | copy-start | bytes 49156
  1.8 36.3 %collective-permute-start.4 = (f32[16,2,1,8,256]{4,3,2,0,1:T(8,128)S(1)}, f32[16,2,1,8,256]{4,3,2,0,1:T(8,128)S(1)}, u32[]{:S(2)}, u32[]{:S(2)}) collective-permute-start(f32[16,2,1,8,256]{4,3,2,0,1:T(8,128)S(1)} %get-tuple-element.76), channel_id=1, source_target_pairs={{0,32},{32,64},{64,96},{96,128},{128,160},{160,192},{192,224},{1,3... | collective-permute-start | bytes 786440 | tf_op jit(solution)/shard_map/ppermute | solution.py:23
  5.7 36.8 %collective-permute-start.5 = (f32[16,2,1,8,256]{4,3,2,0,1:T(8,128)S(1)}, f32[16,2,1,8,256]{4,3,2,0,1:T(8,128)S(1)}, u32[]{:S(2)}, u32[]{:S(2)}) collective-permute-start(f32[16,2,1,8,256]{4,3,2,0,1:T(8,128)S(1)} %get-tuple-element.75), channel_id=1, source_target_pairs={{32,0},{64,32},{96,64},{128,96},{160,128},{192,160},{224,192},{33,... | collective-permute-start | bytes 786440 | tf_op jit(solution)/shard_map/ppermute | solution.py:24
  7.8 37.2 %collective-permute-start.8 = (f32[2,1,256]{2,1,0:T(1,128)S(1)}, f32[2,1,256]{2,1,0:T(1,128)S(1)}, u32[]{:S(2)}, u32[]{:S(2)}) collective-permute-start(f32[2,1,256]{2,1,0:T(1,128)S(1)} %get-tuple-element.150), channel_id=1, source_target_pairs={{0,1},{1,2},{2,3},{3,4},{4,5},{5,6},{6,7},{7,8},{8,9},{9,10},{10,1... | collective-permute-start | bytes 6152 | tf_op jit(solution)/shard_map/ppermute | solution.py:23
  13.0 34.1 %collective-permute-start.9 = (f32[2,1,256]{2,1,0:T(1,128)S(1)}, f32[2,1,256]{2,1,0:T(1,128)S(1)}, u32[]{:S(2)}, u32[]{:S(2)}) collective-permute-start(f32[2,1,256]{2,1,0:T(1,128)S(1)} %get-tuple-element.151), channel_id=1, source_target_pairs={{1,0},{2,1},{3,2},{4,3},{5,4},{6,5},{7,6},{8,7},{9,8},{10,9},{11,1... | collective-permute-start | bytes 6152 | tf_op jit(solution)/shard_map/ppermute | solution.py:24
  16.4 21.7 %all-to-all-start = ((f32[8,2,8,256]{3,2,1,0:T(8,128)}), f32[8,2,8,256]{3,2,1,0:T(8,128)S(1)}, u32[]{:S(2)}, u32[]{:S(2)}) async-start(f32[8,2,8,256]{3,2,1,0:T(8,128)} %broadcast_in_dim.194), calls=%async_computation | async-start | bytes 262144 | tf_op jit(solution)/shard_map/all_to_all | solution.py:170
  24.2 182.1 %collective-permute-start.22 = (f32[16,2,2,1,256]{4,3,2,0,1:T(1,128)S(1)}, f32[16,2,2,1,256]{4,3,2,0,1:T(1,128)S(1)}, u32[]{:S(2)}, u32[]{:S(2)}) collective-permute-start(f32[16,2,2,1,256]{4,3,2,0,1:T(1,128)S(1)} %get-tuple-element.71), channel_id=1, source_target_pairs={{0,1},{1,2},{2,3},{3,4},{4,5},{5,6},{6,7},{7,8},{8,9},{9,10},{10,1... | collective-permute-start | bytes 196616 | tf_op jit(solution)/shard_map/ppermute | solution.py:23
  38.1 14.1 %collective-permute-start = (f32[16,8,256]{2,1,0:T(8,128)S(1)}, f32[16,8,256]{2,1,0:T(8,128)S(1)}, u32[]{:S(2)}, u32[]{:S(2)}) collective-permute-start(f32[16,8,256]{2,1,0:T(8,128)S(1)} %bitcast.592), channel_id=1, source_target_pairs={{0,2},{1,3},{2,4},{3,5},{4,6},{5,7},{6,8},{7,9},{8,10},{9,11},{10,... | collective-permute-start | bytes 393224 | tf_op jit(solution)/shard_map/ppermute | solution.py:32
  42.8 11.3 %collective-permute-start.6 = (f32[16,2,4,1,256]{4,3,2,0,1:T(1,128)S(1)}, f32[16,2,4,1,256]{4,3,2,0,1:T(1,128)S(1)}, u32[]{:S(2)}, u32[]{:S(2)}) collective-permute-start(f32[16,2,4,1,256]{4,3,2,0,1:T(1,128)S(1)} %get-tuple-element.35), channel_id=1, source_target_pairs={{0,1},{1,2},{2,3},{3,4},{4,5},{5,6},{6,7},{7,8},{8,9},{9,10},{10,1... | collective-permute-start | bytes 393224 | tf_op jit(solution)/shard_map/ppermute | solution.py:23
  45.0 10.4 %collective-permute-start.7 = (f32[16,2,4,1,256]{4,3,2,0,1:T(1,128)S(1)}, f32[16,2,4,1,256]{4,3,2,0,1:T(1,128)S(1)}, u32[]{:S(2)}, u32[]{:S(2)}) collective-permute-start(f32[16,2,4,1,256]{4,3,2,0,1:T(1,128)S(1)} %get-tuple-element.36), channel_id=1, source_target_pairs={{1,0},{2,1},{3,2},{4,3},{5,4},{6,5},{7,6},{8,7},{9,8},{10,9},{11,1... | collective-permute-start | bytes 393224 | tf_op jit(solution)/shard_map/ppermute | solution.py:24
  47.2 18.8 %collective-permute-start.1 = (f32[16,8,256]{2,1,0:T(8,128)S(1)}, f32[16,8,256]{2,1,0:T(8,128)S(1)}, u32[]{:S(2)}, u32[]{:S(2)}) collective-permute-start(f32[16,8,256]{2,1,0:T(8,128)S(1)} %bitcast.593), channel_id=1, source_target_pairs={{0,1},{1,2},{2,3},{3,4},{4,5},{5,6},{6,7},{7,8},{8,9},{9,10},{10,1... | collective-permute-start | bytes 393224 | tf_op jit(solution)/shard_map/ppermute | solution.py:32
  52.1 13.9 %collective-permute-start.2 = (f32[16,8,256]{2,1,0:T(8,128)S(1)}, f32[16,8,256]{2,1,0:T(8,128)S(1)}, u32[]{:S(2)}, u32[]{:S(2)}) collective-permute-start(f32[16,8,256]{2,1,0:T(8,128)S(1)} %bitcast.594), channel_id=1, source_target_pairs={{1,0},{2,1},{3,2},{4,3},{5,4},{6,5},{7,6},{8,7},{9,8},{10,9},{11,1... | collective-permute-start | bytes 393224 | tf_op jit(solution)/shard_map/ppermute | solution.py:32
  54.1 12.0 %collective-permute-start.3 = (f32[16,8,256]{2,1,0:T(8,128)S(1)}, f32[16,8,256]{2,1,0:T(8,128)S(1)}, u32[]{:S(2)}, u32[]{:S(2)}) collective-permute-start(f32[16,8,256]{2,1,0:T(8,128)S(1)} %bitcast.595), channel_id=1, source_target_pairs={{2,0},{3,1},{4,2},{5,3},{6,4},{7,5},{8,6},{9,7},{10,8},{11,9},{12,... | collective-permute-start | bytes 393224 | tf_op jit(solution)/shard_map/ppermute | solution.py:32
  60.6 13.4 %all-to-all-start.1 = ((f32[16,2,2,8,256]{4,3,2,1,0:T(8,128)}), f32[16,2,2,8,256]{4,3,2,1,0:T(8,128)S(1)}, u32[]{:S(2)}, u32[]{:S(2)}) async-start(f32[16,2,2,8,256]{4,3,2,1,0:T(8,128)} %copy_subtract_fusion), calls=%async_computation.1 | async-start | bytes 1048576 | tf_op jit(solution)/shard_map/all_to_all | solution.py:190
  74.0 17.4 %collective-permute-start.10 = (f32[2,2,16,8,256]{4,3,2,1,0:T(8,128)S(1)}, f32[2,2,16,8,256]{4,3,2,1,0:T(8,128)S(1)}, u32[]{:S(2)}, u32[]{:S(2)}) collective-permute-start(f32[2,2,16,8,256]{4,3,2,1,0:T(8,128)S(1)} %bitcast.585), channel_id=1, source_target_pairs={{0,2},{1,3},{2,4},{3,5},{4,6},{5,7},{6,8},{7,9},{8,10},{9,11},{10,... | collective-permute-start | bytes 1572872 | tf_op jit(solution)/shard_map/ppermute | solution.py:32
  81.8 34.5 %collective-permute-start.11 = (f32[2,2,16,8,256]{4,3,2,1,0:T(8,128)S(1)}, f32[2,2,16,8,256]{4,3,2,1,0:T(8,128)S(1)}, u32[]{:S(2)}, u32[]{:S(2)}) collective-permute-start(f32[2,2,16,8,256]{4,3,2,1,0:T(8,128)S(1)} %bitcast.586), channel_id=1, source_target_pairs={{0,1},{1,2},{2,3},{3,4},{4,5},{5,6},{6,7},{7,8},{8,9},{9,10},{10,1... | collective-permute-start | bytes 1572872 | tf_op jit(solution)/shard_map/ppermute | solution.py:32
  88.1 28.3 %collective-permute-start.12 = (f32[2,2,16,8,256]{4,3,2,1,0:T(8,128)S(1)}, f32[2,2,16,8,256]{4,3,2,1,0:T(8,128)S(1)}, u32[]{:S(2)}, u32[]{:S(2)}) collective-permute-start(f32[2,2,16,8,256]{4,3,2,1,0:T(8,128)S(1)} %bitcast.587), channel_id=1, source_target_pairs={{1,0},{2,1},{3,2},{4,3},{5,4},{6,5},{7,6},{8,7},{9,8},{10,9},{11,1... | collective-permute-start | bytes 1572872 | tf_op jit(solution)/shard_map/ppermute | solution.py:32
  90.0 26.5 %collective-permute-start.13 = (f32[2,2,16,8,256]{4,3,2,1,0:T(8,128)S(1)}, f32[2,2,16,8,256]{4,3,2,1,0:T(8,128)S(1)}, u32[]{:S(2)}, u32[]{:S(2)}) collective-permute-start(f32[2,2,16,8,256]{4,3,2,1,0:T(8,128)S(1)} %bitcast.588), channel_id=1, source_target_pairs={{2,0},{3,1},{4,2},{5,3},{6,4},{7,5},{8,6},{9,7},{10,8},{11,9},{12,... | collective-permute-start | bytes 1572872 | tf_op jit(solution)/shard_map/ppermute | solution.py:32
  91.4 115.0 %collective-permute-start.23 = (f32[16,2,2,1,256]{4,3,2,0,1:T(1,128)S(1)}, f32[16,2,2,1,256]{4,3,2,0,1:T(1,128)S(1)}, u32[]{:S(2)}, u32[]{:S(2)}) collective-permute-start(f32[16,2,2,1,256]{4,3,2,0,1:T(1,128)S(1)} %get-tuple-element.72), channel_id=1, source_target_pairs={{1,0},{2,1},{3,2},{4,3},{5,4},{6,5},{7,6},{8,7},{9,8},{10,9},{11,1... | collective-permute-start | bytes 196616 | tf_op jit(solution)/shard_map/ppermute | solution.py:24
  116.5 1.5 copy-start.2
  132.9 9.2 %copy-start.6 = (s32[16,256]{1,0:T(8,128)S(1)}, s32[16,256]{1,0:T(8,128)}, u32[]{:S(2)}) copy-start(s32[16,256]{1,0:T(8,128)} %param.12) | copy-start | bytes 49156
  137.3 14.8 %collective-permute-start.14 = (f32[2,2,16,8,256]{4,3,1,0,2:T(8,128)S(1)}, f32[2,2,16,8,256]{4,3,1,0,2:T(8,128)S(1)}, u32[]{:S(2)}, u32[]{:S(2)}) collective-permute-start(f32[2,2,16,8,256]{4,3,1,0,2:T(8,128)S(1)} %get-tuple-element.21), channel_id=1, source_target_pairs={{0,2},{1,3},{2,4},{3,5},{4,6},{5,7},{6,8},{7,9},{8,10},{9,11},{10,... | collective-permute-start | bytes 1572872 | tf_op jit(solution)/shard_map/ppermute | solution.py:32
  142.2 28.5 %collective-permute-start.15 = (f32[2,2,16,8,256]{4,3,1,0,2:T(8,128)S(1)}, f32[2,2,16,8,256]{4,3,1,0,2:T(8,128)S(1)}, u32[]{:S(2)}, u32[]{:S(2)}) collective-permute-start(f32[2,2,16,8,256]{4,3,1,0,2:T(8,128)S(1)} %get-tuple-element.21), channel_id=1, source_target_pairs={{0,1},{1,2},{2,3},{3,4},{4,5},{5,6},{6,7},{7,8},{8,9},{9,10},{10,1... | collective-permute-start | bytes 1572872 | tf_op jit(solution)/shard_map/ppermute | solution.py:32
  148.7 22.2 %collective-permute-start.16 = (f32[2,2,16,8,256]{4,3,1,0,2:T(8,128)S(1)}, f32[2,2,16,8,256]{4,3,1,0,2:T(8,128)S(1)}, u32[]{:S(2)}, u32[]{:S(2)}) collective-permute-start(f32[2,2,16,8,256]{4,3,1,0,2:T(8,128)S(1)} %get-tuple-element.21), channel_id=1, source_target_pairs={{1,0},{2,1},{3,2},{4,3},{5,4},{6,5},{7,6},{8,7},{9,8},{10,9},{11,1... | collective-permute-start | bytes 1572872 | tf_op jit(solution)/shard_map/ppermute | solution.py:32
  152.1 18.9 %collective-permute-start.17 = (f32[2,2,16,8,256]{4,3,1,0,2:T(8,128)S(1)}, f32[2,2,16,8,256]{4,3,1,0,2:T(8,128)S(1)}, u32[]{:S(2)}, u32[]{:S(2)}) collective-permute-start(f32[2,2,16,8,256]{4,3,1,0,2:T(8,128)S(1)} %get-tuple-element.21), channel_id=1, source_target_pairs={{2,0},{3,1},{4,2},{5,3},{6,4},{7,5},{8,6},{9,7},{10,8},{11,9},{12,... | collective-permute-start | bytes 1572872 | tf_op jit(solution)/shard_map/ppermute | solution.py:32
  171.0 1.5 copy-start.1
  190.1 16.2 %copy-start.3 = (f32[16,2,2,8,256]{4,3,2,1,0:T(8,128)S(1)}, f32[16,2,2,8,256]{4,3,2,1,0:T(8,128)}, u32[]{:S(2)}) copy-start(f32[16,2,2,8,256]{4,3,2,1,0:T(8,128)} %param.9) | copy-start | bytes 1572868
  202.8 11.0 %all-to-all-start.2 = ((f32[2,2,16,8,256]{4,3,1,0,2:T(8,128)}), f32[2,2,16,8,256]{4,3,1,0,2:T(8,128)S(1)}, u32[]{:S(2)}, u32[]{:S(2)}) async-start(f32[2,2,16,8,256]{4,3,1,0,2:T(8,128)} %constant_dynamic-update-slice_fusion.49), calls=%async_computation.2 | async-start | bytes 1048576 | tf_op jit(solution)/shard_map/all_to_all | solution.py:213
  213.9 13.0 %collective-permute-start.18 = (f32[16,2,1,8,256]{4,3,2,0,1:T(8,128)S(1)}, f32[16,2,1,8,256]{4,3,2,0,1:T(8,128)S(1)}, u32[]{:S(2)}, u32[]{:S(2)}) collective-permute-start(f32[16,2,1,8,256]{4,3,2,0,1:T(8,128)S(1)} %get-tuple-element.74), channel_id=1, source_target_pairs={{0,32},{32,64},{64,96},{96,128},{128,160},{160,192},{192,224},{1,3... | collective-permute-start | bytes 786440 | tf_op jit(solution)/shard_map/ppermute | solution.py:23
  225.5 27.3 %copy-start.5 = (f32[16,2,256]{2,1,0:T(2,128)S(1)}, f32[16,2,256]{2,1,0:T(2,128)}, u32[]{:S(2)}) copy-start(f32[16,2,256]{2,1,0:T(2,128)} %param.10) | copy-start | bytes 98308
  225.6 9.9 %collective-permute-start.19 = (f32[16,2,1,8,256]{4,3,2,0,1:T(8,128)S(1)}, f32[16,2,1,8,256]{4,3,2,0,1:T(8,128)S(1)}, u32[]{:S(2)}, u32[]{:S(2)}) collective-permute-start(f32[16,2,1,8,256]{4,3,2,0,1:T(8,128)S(1)} %get-tuple-element.73), channel_id=1, source_target_pairs={{32,0},{64,32},{96,64},{128,96},{160,128},{192,160},{224,192},{33,... | collective-permute-start | bytes 786440 | tf_op jit(solution)/shard_map/ppermute | solution.py:24
  235.7 17.4 %collective-permute-start.20 = (f32[16,2,4,1,256]{4,3,2,0,1:T(1,128)S(1)}, f32[16,2,4,1,256]{4,3,2,0,1:T(1,128)S(1)}, u32[]{:S(2)}, u32[]{:S(2)}) collective-permute-start(f32[16,2,4,1,256]{4,3,2,0,1:T(1,128)S(1)} %get-tuple-element.33), channel_id=1, source_target_pairs={{0,1},{1,2},{2,3},{3,4},{4,5},{5,6},{6,7},{7,8},{8,9},{9,10},{10,1... | collective-permute-start | bytes 393224 | tf_op jit(solution)/shard_map/ppermute | solution.py:23
  250.6 7.8 %collective-permute-start.21 = (f32[16,2,4,1,256]{4,3,2,0,1:T(1,128)S(1)}, f32[16,2,4,1,256]{4,3,2,0,1:T(1,128)S(1)}, u32[]{:S(2)}, u32[]{:S(2)}) collective-permute-start(f32[16,2,4,1,256]{4,3,2,0,1:T(1,128)S(1)} %get-tuple-element.34), channel_id=1, source_target_pairs={{1,0},{2,1},{3,2},{4,3},{5,4},{6,5},{7,6},{8,7},{9,8},{10,9},{11,1... | collective-permute-start | bytes 393224 | tf_op jit(solution)/shard_map/ppermute | solution.py:24

commit v4 on v3

--- a/solution.py
+++ b/solution.py
@@ -2,6 +2,9 @@
 import jax.numpy as jnp
 from jax import lax
 from jax.sharding import PartitionSpec as P
+from jax.experimental import pallas as pl
+from jax.experimental.pallas import tpu as pltpu
+import functools
 
 WAVE_SCALE = 1.9
 PML_DAMP = 2.0
@@ -30,6 +33,78 @@
     count = lax.axis_size(axis)
     leading, last = (max(0, -steps), min(count, count - steps))
     return lax.ppermute(value, axis, [(source, source + steps) for source in range(leading, last)])
+
+
+def all_sum_kernel(depth_count, tile_count, x_ref, out_ref, tile_slots, depth_slots, part,
+                   copy_sem, tile_send, tile_recv, depth_send, depth_recv):
+    me_d = lax.axis_index("depth")
+    me_t = lax.axis_index("tile")
+    mesh_ids = pl.DeviceIdType.MESH
+    barrier = pltpu.get_barrier_semaphore()
+    for k in range(1, tile_count):
+        pl.semaphore_signal(barrier, inc=1, device_id=(me_d, lax.rem(me_t + k, tile_count)),
+                            device_id_type=mesh_ids)
+    for k in range(1, depth_count):
+        pl.semaphore_signal(barrier, inc=1, device_id=(lax.rem(me_d + k, depth_count), me_t),
+                            device_id_type=mesh_ids)
+    pl.semaphore_wait(barrier, tile_count + depth_count - 2)
+
+    def exchange(src, slots, send_sems, recv_sems, me, count, peer_of):
+        own = pltpu.make_async_copy(src, slots.at[me], copy_sem)
+        own.start()
+        sends = []
+        for k in range(1, count):
+            copy = pltpu.make_async_remote_copy(
+                src_ref=src, dst_ref=slots.at[me], send_sem=send_sems.at[k],
+                recv_sem=recv_sems.at[me], device_id=peer_of(lax.rem(me + k, count)),
+                device_id_type=mesh_ids)
+            copy.start()
+            sends.append(copy)
+        own.wait()
+        for k in range(1, count):
+            sender = lax.rem(me + count - k, count)
+            pltpu.make_async_remote_copy(
+                src_ref=src, dst_ref=slots.at[sender], send_sem=send_sems.at[k],
+                recv_sem=recv_sems.at[sender], device_id=peer_of(sender),
+                device_id_type=mesh_ids).wait_recv()
+        for copy in sends:
+            copy.wait_send()
+        total = slots[0]
+        for j in range(1, count):
+            total = total + slots[j]
+        return total
+
+    part[...] = exchange(x_ref, tile_slots, tile_send, tile_recv, me_t, tile_count,
+                         lambda t: (me_d, t))
+    out_ref[...] = exchange(part, depth_slots, depth_send, depth_recv, me_d, depth_count,
+                            lambda d: (d, me_t))
+
+
+def all_sum(values):
+    depth_count = lax.axis_size("depth")
+    tile_count = lax.axis_size("tile")
+    size = values.size
+    block = 8 * 128
+    padded = -(-size // block) * block
+    flat = jnp.pad(values.reshape(-1), (0, padded - size)).reshape(padded // 128, 128)
+    summed = pl.pallas_call(
+        functools.partial(all_sum_kernel, depth_count, tile_count),
+        out_shape=jax.ShapeDtypeStruct(flat.shape, jnp.float32),
+        in_specs=[pl.BlockSpec(memory_space=pltpu.VMEM)],
+        out_specs=pl.BlockSpec(memory_space=pltpu.VMEM),
+        scratch_shapes=[
+            pltpu.VMEM((tile_count,) + flat.shape, jnp.float32),
+            pltpu.VMEM((depth_count,) + flat.shape, jnp.float32),
+            pltpu.VMEM(flat.shape, jnp.float32),
+            pltpu.SemaphoreType.DMA,
+            pltpu.SemaphoreType.DMA((tile_count,)),
+            pltpu.SemaphoreType.DMA((tile_count,)),
+            pltpu.SemaphoreType.DMA((depth_count,)),
+            pltpu.SemaphoreType.DMA((depth_count,)),
+        ],
+        compiler_params=pltpu.CompilerParams(collective_id=0, has_side_effects=True),
+    )(flat)
+    return summed.reshape(-1)[:size].reshape(values.shape)
 
 
 def damping_ramp(distance, extent):
@@ -260,7 +335,7 @@
     packed = jnp.stack(
         [local_real, local_imag, local_norm, gap_norm, cross_re, cross_im, dir_norm], axis=1
     )
-    packed = lax.psum(packed, ("depth", "tile"))
+    packed = all_sum(packed)
     dot_real, dot_imag, image_norm = packed[:, 0], packed[:, 1], packed[:, 2]
     gap_norm, cross_re, cross_im, dir_norm = packed[:, 3], packed[:, 4], packed[:, 5], packed[:, 6]
     step_re = (dot_real / image_norm)[:, None, None, None]

time: 348 us -> 292 us (0.84)
  blocking collectives: 78.6 us -> 0 us
  Pallas kernels: 0 us -> 20.5 us
    psum x1 -> x0, blocking collectives: 78.6 us -> none  [per_device(): packed = lax.psum(packed, ('depth', 'tile'))]
    pallas_call x0 -> x1, Pallas kernels: none -> 20.5 us  [all_sum(): pl.pallas_call(functools.partial(all_sum_kernel, depth_count, tile_count)...]
  transfers between devices with their start and end apart: 27 -> 27, of which waited for: 7 -> 7; matrix products, arithmetic and copies ran while one was open for 23% -> 28% of each run, Pallas kernels for 0% -> 0%
where the time goes in v4:
time: 292 us; the launch traced here: 290 us
  starting transfers between devices  125 us (43%)
  other arithmetic  63.5 us (22%)
  waiting for transfers between devices  48 us (16%)
  local copies, waits for them, and re-layouts  21.4 us (7%)
  Pallas kernels  20.5 us (7%)
  matrix products  9.15 us (3%)
    ppermute x12, starting transfers between devices, shifted(): lax.ppermute(value, axis, [(source, source + steps) for source in range(l...  42.5 us
    ppermute x6, starting transfers between devices, extended(): before = lax.ppermute(last, axis, up)  34.1 us
    ppermute x6, starting transfers between devices, extended(): after = lax.ppermute(leading, axis, down)  32.8 us
    pallas_call x1, Pallas kernels, all_sum(): pl.pallas_call(functools.partial(all_sum_kernel, depth_count, tile_count)...  20.5 us
    ppermute x12, waiting for transfers between devices, shifted(): lax.ppermute(value, axis, [(source, source + steps) for source in range(l...  19.3 us
    add x16, other arithmetic, per_device(): source_term = residual_ext[:, :, layer_no] + couple(previous)  18.1 us
    select_n x15, other arithmetic, per_device(): jnp.where(row_valid, downward_ext[:, :, layer_no] + complex_scale(inv_re[...  15 us
    ppermute x6, waiting for transfers between devices, extended(): after = lax.ppermute(leading, axis, down)  13.8 us
  transfers between devices with their start and end apart: 27, of which 7 were waited for; matrix products, arithmetic and copies ran while one was open for 28% of the time, Pallas kernels for 0%

profile of v4, /device:TPU:1, one launch (start us, length us, event | category | flops | bytes accessed | tf_op | source)
XLA Modules:
  0.0 289.6 jit_solution(11533956506454585871)
XLA Ops:
  0.6 1.1 fusion.739
  1.8 3.9 %collective-permute-start.4 = (f32[16,2,1,8,256]{4,3,2,0,1:T(8,128)S(1)}, f32[16,2,1,8,256]{4,3,2,0,1:T(8,128)S(1)}, u32[]{:S(2)}, u32[]{:S(2)}) collective-permute-start(f32[16,2,1,8,256]{4,3,2,0,1:T(8,128)S(1)} %get-tuple-element.79), channel_id=1, source_target_pairs={{0,32},{32,64},{64,96},{96,128},{128,160},{160,192},{192,224},{1,3... | collective-permute-start | bytes 786440 | tf_op jit(solution)/shard_map/ppermute | solution.py:26
  5.7 1.3 collective-permute-start.5
  7.8 5.2 %collective-permute-start.8 = (f32[2,1,256]{2,1,0:T(1,128)S(1)}, f32[2,1,256]{2,1,0:T(1,128)S(1)}, u32[]{:S(2)}, u32[]{:S(2)}) collective-permute-start(f32[2,1,256]{2,1,0:T(1,128)S(1)} %get-tuple-element.153), channel_id=1, source_target_pairs={{0,1},{1,2},{2,3},{3,4},{4,5},{5,6},{6,7},{7,8},{8,9},{9,10},{10,1... | collective-permute-start | bytes 6152 | tf_op jit(solution)/shard_map/ppermute | solution.py:26
  13.0 1.9 collective-permute-start.9
  15.0 1.4 broadcast_in_dim.194
  16.4 6.5 %all-to-all-start = ((f32[8,2,8,256]{3,2,1,0:T(8,128)}), f32[8,2,8,256]{3,2,1,0:T(8,128)S(1)}, u32[]{:S(2)}, u32[]{:S(2)}) async-start(f32[8,2,8,256]{3,2,1,0:T(8,128)} %broadcast_in_dim.194), calls=%async_computation | async-start | bytes 262144 | tf_op jit(solution)/shard_map/all_to_all | solution.py:245
  22.9 1.3 fusion.737
  24.2 5.4 %collective-permute-start.22 = (f32[16,2,2,1,256]{4,3,2,0,1:T(1,128)S(1)}, f32[16,2,2,1,256]{4,3,2,0,1:T(1,128)S(1)}, u32[]{:S(2)}, u32[]{:S(2)}) collective-permute-start(f32[16,2,2,1,256]{4,3,2,0,1:T(1,128)S(1)} %get-tuple-element.74), channel_id=1, source_target_pairs={{0,1},{1,2},{2,3},{3,4},{4,5},{5,6},{6,7},{7,8},{8,9},{9,10},{10,1... | collective-permute-start | bytes 196616 | tf_op jit(solution)/shard_map/ppermute | solution.py:26
  31.0 1.2 multiply_add_fusion.35
  32.2 1.2 multiply_add_fusion.37
  33.6 1.3 multiply_add_fusion.34
  34.9 1.3 multiply_add_fusion.36
  37.1 1.1 copy.111
  38.4 4.4 %collective-permute-start = (f32[16,8,256]{2,1,0:T(8,128)S(1)}, f32[16,8,256]{2,1,0:T(8,128)S(1)}, u32[]{:S(2)}, u32[]{:S(2)}) collective-permute-start(f32[16,8,256]{2,1,0:T(8,128)S(1)} %bitcast.567), channel_id=1, source_target_pairs={{0,2},{1,3},{2,4},{3,5},{4,6},{5,7},{6,8},{7,9},{8,10},{9,11},{10,... | collective-permute-start | bytes 393224 | tf_op jit(solution)/shard_map/ppermute | solution.py:35
  43.1 2.2 collective-permute-start.6
  45.3 2.1 collective-permute-start.7
  47.5 4.9 %collective-permute-start.1 = (f32[16,8,256]{2,1,0:T(8,128)S(1)}, f32[16,8,256]{2,1,0:T(8,128)S(1)}, u32[]{:S(2)}, u32[]{:S(2)}) collective-permute-start(f32[16,8,256]{2,1,0:T(8,128)S(1)} %bitcast.568), channel_id=1, source_target_pairs={{0,1},{1,2},{2,3},{3,4},{4,5},{5,6},{6,7},{7,8},{8,9},{9,10},{10,1... | collective-permute-start | bytes 393224 | tf_op jit(solution)/shard_map/ppermute | solution.py:35
  52.4 1.9 collective-permute-start.2
  54.4 1.3 collective-permute-start.3
  57.1 2.7 fusion.71
  60.9 5.4 %all-to-all-start.1 = ((f32[16,2,2,8,256]{4,3,2,1,0:T(8,128)}), f32[16,2,2,8,256]{4,3,2,1,0:T(8,128)S(1)}, u32[]{:S(2)}, u32[]{:S(2)}) async-start(f32[16,2,2,8,256]{4,3,2,1,0:T(8,128)} %copy_subtract_fusion), calls=%async_computation.1 | async-start | bytes 1048576 | tf_op jit(solution)/shard_map/all_to_all | solution.py:265
  66.4 7.8 %all-to-all-done.1 = f32[16,2,2,8,256]{4,3,2,1,0:T(8,128)S(1)} async-done(((f32[16,2,2,8,256]{4,3,2,1,0:T(8,128)}), f32[16,2,2,8,256]{4,3,2,1,0:T(8,128)S(1)}, u32[]{:S(2)}, u32[]{:S(2)}) %all-to-all-start.1) | async-done | bytes 524320 | tf_op jit(solution)/shard_map/all_to_all | solution.py:265
  74.3 7.4 %collective-permute-start.10 = (f32[2,2,16,8,256]{4,3,2,1,0:T(8,128)S(1)}, f32[2,2,16,8,256]{4,3,2,1,0:T(8,128)S(1)}, u32[]{:S(2)}, u32[]{:S(2)}) collective-permute-start(f32[2,2,16,8,256]{4,3,2,1,0:T(8,128)S(1)} %bitcast.560), channel_id=1, source_target_pairs={{0,2},{1,3},{2,4},{3,5},{4,6},{5,7},{6,8},{7,9},{8,10},{9,11},{10,... | collective-permute-start | bytes 1572872 | tf_op jit(solution)/shard_map/ppermute | solution.py:35
  82.0 6.2 %collective-permute-start.11 = (f32[2,2,16,8,256]{4,3,2,1,0:T(8,128)S(1)}, f32[2,2,16,8,256]{4,3,2,1,0:T(8,128)S(1)}, u32[]{:S(2)}, u32[]{:S(2)}) collective-permute-start(f32[2,2,16,8,256]{4,3,2,1,0:T(8,128)S(1)} %bitcast.561), channel_id=1, source_target_pairs={{0,1},{1,2},{2,3},{3,4},{4,5},{5,6},{6,7},{7,8},{8,9},{9,10},{10,1... | collective-permute-start | bytes 1572872 | tf_op jit(solution)/shard_map/ppermute | solution.py:35
  88.4 1.9 collective-permute-start.12
  90.3 1.3 collective-permute-start.13
  91.7 24.0 %collective-permute-start.23 = (f32[16,2,2,1,256]{4,3,2,0,1:T(1,128)S(1)}, f32[16,2,2,1,256]{4,3,2,0,1:T(1,128)S(1)}, u32[]{:S(2)}, u32[]{:S(2)}) collective-permute-start(f32[16,2,2,1,256]{4,3,2,0,1:T(1,128)S(1)} %get-tuple-element.75), channel_id=1, source_target_pairs={{1,0},{2,1},{3,2},{4,3},{5,4},{6,5},{7,6},{8,7},{9,8},{10,9},{11,1... | collective-permute-start | bytes 196616 | tf_op jit(solution)/shard_map/ppermute | solution.py:27
  118.3 1.2 fusion.197
  119.6 1.2 fusion.214
  121.0 1.2 fusion.231
  122.4 1.2 fusion.248
  123.7 1.2 fusion.265
  125.1 1.2 fusion.282
  126.5 1.2 fusion.299
  127.8 1.2 fusion.316
  129.2 1.2 fusion.333
  130.6 1.2 fusion.350
  131.9 1.2 fusion.367
  133.3 1.2 fusion.384
  134.7 1.2 fusion.401
  136.1 1.2 fusion.418
  137.6 4.8 %collective-permute-start.14 = (f32[2,2,16,8,256]{4,3,1,0,2:T(8,128)S(1)}, f32[2,2,16,8,256]{4,3,1,0,2:T(8,128)S(1)}, u32[]{:S(2)}, u32[]{:S(2)}) collective-permute-start(f32[2,2,16,8,256]{4,3,1,0,2:T(8,128)S(1)} %get-tuple-element.24), channel_id=1, source_target_pairs={{0,2},{1,3},{2,4},{3,5},{4,6},{5,7},{6,8},{7,9},{8,10},{9,11},{10,... | collective-permute-start | bytes 1572872 | tf_op jit(solution)/shard_map/ppermute | solution.py:35
  142.5 4.8 %collective-permute-start.15 = (f32[2,2,16,8,256]{4,3,1,0,2:T(8,128)S(1)}, f32[2,2,16,8,256]{4,3,1,0,2:T(8,128)S(1)}, u32[]{:S(2)}, u32[]{:S(2)}) collective-permute-start(f32[2,2,16,8,256]{4,3,1,0,2:T(8,128)S(1)} %get-tuple-element.24), channel_id=1, source_target_pairs={{0,1},{1,2},{2,3},{3,4},{4,5},{5,6},{6,7},{7,8},{8,9},{9,10},{10,1... | collective-permute-start | bytes 1572872 | tf_op jit(solution)/shard_map/ppermute | solution.py:35
  147.4 1.6 iota_compare_fusion
  149.0 1.9 collective-permute-start.16
  150.9 1.5 collective-permute-done.14
  152.4 1.5 collective-permute-start.17
  154.0 17.0 %collective-permute-done.15 = f32[2,2,16,8,256]{4,3,1,0,2:T(8,128)S(1)} collective-permute-done((f32[2,2,16,8,256]{4,3,1,0,2:T(8,128)S(1)}, f32[2,2,16,8,256]{4,3,1,0,2:T(8,128)S(1)}, u32[]{:S(2)}, u32[]{:S(2)}) %collective-permute-start.15) | collective-permute-done | bytes 524320 | tf_op jit(solution)/shard_map/ppermute | solution.py:35
  171.4 1.4 copy-done.1
  175.5 1.0 fusion.686
  190.5 1.1 fusion.708
  203.0 3.5 %all-to-all-start.2 = ((f32[2,2,16,8,256]{4,3,1,0,2:T(8,128)}), f32[2,2,16,8,256]{4,3,1,0,2:T(8,128)S(1)}, u32[]{:S(2)}, u32[]{:S(2)}) async-start(f32[2,2,16,8,256]{4,3,1,0,2:T(8,128)} %constant_dynamic-update-slice_fusion.49), calls=%async_computation.2 | async-start | bytes 1048576 | tf_op jit(solution)/shard_map/all_to_all | solution.py:288
  207.0 7.0 %all-to-all-done.2 = f32[2,2,16,8,256]{4,3,1,0,2:T(8,128)S(1)} async-done(((f32[2,2,16,8,256]{4,3,1,0,2:T(8,128)}), f32[2,2,16,8,256]{4,3,1,0,2:T(8,128)S(1)}, u32[]{:S(2)}, u32[]{:S(2)}) %all-to-all-start.2) | async-done | bytes 524320 | tf_op jit(solution)/shard_map/all_to_all | solution.py:288
  214.1 2.5 collective-permute-start.18
  216.6 9.2 %fusion = f32[16,4,256]{2,1,0:T(4,128)S(1)} fusion(pred[16,256,256]{1,2,0:T(8,128)(4,1)} %iota_compare_fusion, f32[16,2,16,256]{3,2,1,0:T(8,128)S(1)} %bitcast.554, f32[16,2,16,256]{3,2,1,0:T(8,128)S(1)} %bitcast.559, s32[16,256]{1,0:T(8,128)S(1)} %get-tuple-element.22), kind=kOutput, calls=%fused_computation.1 | convolution fusion | flops 814006272 | bytes 2179072 | tf_op jit(solution)/shard_map/srk,sqky->sqry/dot_general | solution.py:318
  225.8 1.3 collective-permute-start.19
  227.2 8.5 %collective-permute-done.19 = f32[16,2,1,8,256]{4,3,2,0,1:T(8,128)S(1)} collective-permute-done((f32[16,2,1,8,256]{4,3,2,0,1:T(8,128)S(1)}, f32[16,2,1,8,256]{4,3,2,0,1:T(8,128)S(1)}, u32[]{:S(2)}, u32[]{:S(2)}) %collective-permute-start.19) | collective-permute-done | bytes 262176 | tf_op jit(solution)/shard_map/ppermute | solution.py:27
  235.9 14.9 %collective-permute-start.20 = (f32[16,2,4,1,256]{4,3,2,0,1:T(1,128)S(1)}, f32[16,2,4,1,256]{4,3,2,0,1:T(1,128)S(1)}, u32[]{:S(2)}, u32[]{:S(2)}) collective-permute-start(f32[16,2,4,1,256]{4,3,2,0,1:T(1,128)S(1)} %get-tuple-element.36), channel_id=1, source_target_pairs={{0,1},{1,2},{2,3},{3,4},{4,5},{5,6},{6,7},{7,8},{8,9},{9,10},{10,1... | collective-permute-start | bytes 393224 | tf_op jit(solution)/shard_map/ppermute | solution.py:26
  250.8 2.2 collective-permute-start.21
  253.3 5.3 %collective-permute-done.21 = f32[16,2,4,1,256]{4,3,2,0,1:T(1,128)S(1)} collective-permute-done((f32[16,2,4,1,256]{4,3,2,0,1:T(1,128)S(1)}, f32[16,2,4,1,256]{4,3,2,0,1:T(1,128)S(1)}, u32[]{:S(2)}, u32[]{:S(2)}) %collective-permute-start.21) | collective-permute-done | bytes 131104 | tf_op jit(solution)/shard_map/ppermute | solution.py:27
  260.0 2.7 fusion.114
  262.9 1.3 subtract_reduce_fusion
  265.0 20.5 %shard_map.94 = f32[8,128]{1,0:T(8,128)} custom-call(f32[8,128]{1,0:T(8,128)} %pad_bitcast_fusion.x_ref), custom_call_target="tpu_custom_call" | custom-call | tf_op jit(solution)/shard_map/pallas_call | solution.py:90
  (233 shorter events, 46.5 us)
Async XLA Ops:
  0.6 42.2 %copy-start = (f32[16,2,2,8,256]{4,3,2,1,0:T(8,128)S(1)}, f32[16,2,2,8,256]{4,3,2,1,0:T(8,128)}, u32[]{:S(2)}) copy-start(f32[16,2,2,8,256]{4,3,2,1,0:T(8,128)} %param.7) | copy-start | bytes 1572868
  1.8 45.7 %copy-start.4 = (f32[2,8,256]{2,1,0:T(8,128)S(1)}, f32[2,8,256]{2,1,0:T(8,128)}, u32[]{:S(2)}) copy-start(f32[2,8,256]{2,1,0:T(8,128)} %param.8) | copy-start | bytes 49156
  1.8 36.6 %collective-permute-start.4 = (f32[16,2,1,8,256]{4,3,2,0,1:T(8,128)S(1)}, f32[16,2,1,8,256]{4,3,2,0,1:T(8,128)S(1)}, u32[]{:S(2)}, u32[]{:S(2)}) collective-permute-start(f32[16,2,1,8,256]{4,3,2,0,1:T(8,128)S(1)} %get-tuple-element.79), channel_id=1, source_target_pairs={{0,32},{32,64},{64,96},{96,128},{128,160},{160,192},{192,224},{1,3... | collective-permute-start | bytes 786440 | tf_op jit(solution)/shard_map/ppermute | solution.py:26
  5.7 37.1 %collective-permute-start.5 = (f32[16,2,1,8,256]{4,3,2,0,1:T(8,128)S(1)}, f32[16,2,1,8,256]{4,3,2,0,1:T(8,128)S(1)}, u32[]{:S(2)}, u32[]{:S(2)}) collective-permute-start(f32[16,2,1,8,256]{4,3,2,0,1:T(8,128)S(1)} %get-tuple-element.78), channel_id=1, source_target_pairs={{32,0},{64,32},{96,64},{128,96},{160,128},{192,160},{224,192},{33,... | collective-permute-start | bytes 786440 | tf_op jit(solution)/shard_map/ppermute | solution.py:27
  7.8 37.5 %collective-permute-start.8 = (f32[2,1,256]{2,1,0:T(1,128)S(1)}, f32[2,1,256]{2,1,0:T(1,128)S(1)}, u32[]{:S(2)}, u32[]{:S(2)}) collective-permute-start(f32[2,1,256]{2,1,0:T(1,128)S(1)} %get-tuple-element.153), channel_id=1, source_target_pairs={{0,1},{1,2},{2,3},{3,4},{4,5},{5,6},{6,7},{7,8},{8,9},{9,10},{10,1... | collective-permute-start | bytes 6152 | tf_op jit(solution)/shard_map/ppermute | solution.py:26
  13.0 34.4 %collective-permute-start.9 = (f32[2,1,256]{2,1,0:T(1,128)S(1)}, f32[2,1,256]{2,1,0:T(1,128)S(1)}, u32[]{:S(2)}, u32[]{:S(2)}) collective-permute-start(f32[2,1,256]{2,1,0:T(1,128)S(1)} %get-tuple-element.154), channel_id=1, source_target_pairs={{1,0},{2,1},{3,2},{4,3},{5,4},{6,5},{7,6},{8,7},{9,8},{10,9},{11,1... | collective-permute-start | bytes 6152 | tf_op jit(solution)/shard_map/ppermute | solution.py:27
  16.4 22.0 %all-to-all-start = ((f32[8,2,8,256]{3,2,1,0:T(8,128)}), f32[8,2,8,256]{3,2,1,0:T(8,128)S(1)}, u32[]{:S(2)}, u32[]{:S(2)}) async-start(f32[8,2,8,256]{3,2,1,0:T(8,128)} %broadcast_in_dim.194), calls=%async_computation | async-start | bytes 262144 | tf_op jit(solution)/shard_map/all_to_all | solution.py:245
  24.2 182.3 %collective-permute-start.22 = (f32[16,2,2,1,256]{4,3,2,0,1:T(1,128)S(1)}, f32[16,2,2,1,256]{4,3,2,0,1:T(1,128)S(1)}, u32[]{:S(2)}, u32[]{:S(2)}) collective-permute-start(f32[16,2,2,1,256]{4,3,2,0,1:T(1,128)S(1)} %get-tuple-element.74), channel_id=1, source_target_pairs={{0,1},{1,2},{2,3},{3,4},{4,5},{5,6},{6,7},{7,8},{8,9},{9,10},{10,1... | collective-permute-start | bytes 196616 | tf_op jit(solution)/shard_map/ppermute | solution.py:26
  38.4 14.1 %collective-permute-start = (f32[16,8,256]{2,1,0:T(8,128)S(1)}, f32[16,8,256]{2,1,0:T(8,128)S(1)}, u32[]{:S(2)}, u32[]{:S(2)}) collective-permute-start(f32[16,8,256]{2,1,0:T(8,128)S(1)} %bitcast.567), channel_id=1, source_target_pairs={{0,2},{1,3},{2,4},{3,5},{4,6},{5,7},{6,8},{7,9},{8,10},{9,11},{10,... | collective-permute-start | bytes 393224 | tf_op jit(solution)/shard_map/ppermute | solution.py:35
  43.1 11.3 %collective-permute-start.6 = (f32[16,2,4,1,256]{4,3,2,0,1:T(1,128)S(1)}, f32[16,2,4,1,256]{4,3,2,0,1:T(1,128)S(1)}, u32[]{:S(2)}, u32[]{:S(2)}) collective-permute-start(f32[16,2,4,1,256]{4,3,2,0,1:T(1,128)S(1)} %get-tuple-element.38), channel_id=1, source_target_pairs={{0,1},{1,2},{2,3},{3,4},{4,5},{5,6},{6,7},{7,8},{8,9},{9,10},{10,1... | collective-permute-start | bytes 393224 | tf_op jit(solution)/shard_map/ppermute | solution.py:26
  45.3 10.4 %collective-permute-start.7 = (f32[16,2,4,1,256]{4,3,2,0,1:T(1,128)S(1)}, f32[16,2,4,1,256]{4,3,2,0,1:T(1,128)S(1)}, u32[]{:S(2)}, u32[]{:S(2)}) collective-permute-start(f32[16,2,4,1,256]{4,3,2,0,1:T(1,128)S(1)} %get-tuple-element.39), channel_id=1, source_target_pairs={{1,0},{2,1},{3,2},{4,3},{5,4},{6,5},{7,6},{8,7},{9,8},{10,9},{11,1... | collective-permute-start | bytes 393224 | tf_op jit(solution)/shard_map/ppermute | solution.py:27
  47.5 18.8 %collective-permute-start.1 = (f32[16,8,256]{2,1,0:T(8,128)S(1)}, f32[16,8,256]{2,1,0:T(8,128)S(1)}, u32[]{:S(2)}, u32[]{:S(2)}) collective-permute-start(f32[16,8,256]{2,1,0:T(8,128)S(1)} %bitcast.568), channel_id=1, source_target_pairs={{0,1},{1,2},{2,3},{3,4},{4,5},{5,6},{6,7},{7,8},{8,9},{9,10},{10,1... | collective-permute-start | bytes 393224 | tf_op jit(solution)/shard_map/ppermute | solution.py:35
  52.4 13.9 %collective-permute-start.2 = (f32[16,8,256]{2,1,0:T(8,128)S(1)}, f32[16,8,256]{2,1,0:T(8,128)S(1)}, u32[]{:S(2)}, u32[]{:S(2)}) collective-permute-start(f32[16,8,256]{2,1,0:T(8,128)S(1)} %bitcast.569), channel_id=1, source_target_pairs={{1,0},{2,1},{3,2},{4,3},{5,4},{6,5},{7,6},{8,7},{9,8},{10,9},{11,1... | collective-permute-start | bytes 393224 | tf_op jit(solution)/shard_map/ppermute | solution.py:35
  54.4 12.0 %collective-permute-start.3 = (f32[16,8,256]{2,1,0:T(8,128)S(1)}, f32[16,8,256]{2,1,0:T(8,128)S(1)}, u32[]{:S(2)}, u32[]{:S(2)}) collective-permute-start(f32[16,8,256]{2,1,0:T(8,128)S(1)} %bitcast.570), channel_id=1, source_target_pairs={{2,0},{3,1},{4,2},{5,3},{6,4},{7,5},{8,6},{9,7},{10,8},{11,9},{12,... | collective-permute-start | bytes 393224 | tf_op jit(solution)/shard_map/ppermute | solution.py:35
  60.9 13.4 %all-to-all-start.1 = ((f32[16,2,2,8,256]{4,3,2,1,0:T(8,128)}), f32[16,2,2,8,256]{4,3,2,1,0:T(8,128)S(1)}, u32[]{:S(2)}, u32[]{:S(2)}) async-start(f32[16,2,2,8,256]{4,3,2,1,0:T(8,128)} %copy_subtract_fusion), calls=%async_computation.1 | async-start | bytes 1048576 | tf_op jit(solution)/shard_map/all_to_all | solution.py:265
  74.3 17.4 %collective-permute-start.10 = (f32[2,2,16,8,256]{4,3,2,1,0:T(8,128)S(1)}, f32[2,2,16,8,256]{4,3,2,1,0:T(8,128)S(1)}, u32[]{:S(2)}, u32[]{:S(2)}) collective-permute-start(f32[2,2,16,8,256]{4,3,2,1,0:T(8,128)S(1)} %bitcast.560), channel_id=1, source_target_pairs={{0,2},{1,3},{2,4},{3,5},{4,6},{5,7},{6,8},{7,9},{8,10},{9,11},{10,... | collective-permute-start | bytes 1572872 | tf_op jit(solution)/shard_map/ppermute | solution.py:35
  82.0 34.5 %collective-permute-start.11 = (f32[2,2,16,8,256]{4,3,2,1,0:T(8,128)S(1)}, f32[2,2,16,8,256]{4,3,2,1,0:T(8,128)S(1)}, u32[]{:S(2)}, u32[]{:S(2)}) collective-permute-start(f32[2,2,16,8,256]{4,3,2,1,0:T(8,128)S(1)} %bitcast.561), channel_id=1, source_target_pairs={{0,1},{1,2},{2,3},{3,4},{4,5},{5,6},{6,7},{7,8},{8,9},{9,10},{10,1... | collective-permute-start | bytes 1572872 | tf_op jit(solution)/shard_map/ppermute | solution.py:35
  88.4 28.3 %collective-permute-start.12 = (f32[2,2,16,8,256]{4,3,2,1,0:T(8,128)S(1)}, f32[2,2,16,8,256]{4,3,2,1,0:T(8,128)S(1)}, u32[]{:S(2)}, u32[]{:S(2)}) collective-permute-start(f32[2,2,16,8,256]{4,3,2,1,0:T(8,128)S(1)} %bitcast.562), channel_id=1, source_target_pairs={{1,0},{2,1},{3,2},{4,3},{5,4},{6,5},{7,6},{8,7},{9,8},{10,9},{11,1... | collective-permute-start | bytes 1572872 | tf_op jit(solution)/shard_map/ppermute | solution.py:35
  90.3 26.5 %collective-permute-start.13 = (f32[2,2,16,8,256]{4,3,2,1,0:T(8,128)S(1)}, f32[2,2,16,8,256]{4,3,2,1,0:T(8,128)S(1)}, u32[]{:S(2)}, u32[]{:S(2)}) collective-permute-start(f32[2,2,16,8,256]{4,3,2,1,0:T(8,128)S(1)} %bitcast.563), channel_id=1, source_target_pairs={{2,0},{3,1},{4,2},{5,3},{6,4},{7,5},{8,6},{9,7},{10,8},{11,9},{12,... | collective-permute-start | bytes 1572872 | tf_op jit(solution)/shard_map/ppermute | solution.py:35
  91.7 114.8 %collective-permute-start.23 = (f32[16,2,2,1,256]{4,3,2,0,1:T(1,128)S(1)}, f32[16,2,2,1,256]{4,3,2,0,1:T(1,128)S(1)}, u32[]{:S(2)}, u32[]{:S(2)}) collective-permute-start(f32[16,2,2,1,256]{4,3,2,0,1:T(1,128)S(1)} %get-tuple-element.75), channel_id=1, source_target_pairs={{1,0},{2,1},{3,2},{4,3},{5,4},{6,5},{7,6},{8,7},{9,8},{10,9},{11,1... | collective-permute-start | bytes 196616 | tf_op jit(solution)/shard_map/ppermute | solution.py:27
  116.8 1.5 copy-start.2
  133.2 9.2 %copy-start.6 = (s32[16,256]{1,0:T(8,128)S(1)}, s32[16,256]{1,0:T(8,128)}, u32[]{:S(2)}) copy-start(s32[16,256]{1,0:T(8,128)} %param.12) | copy-start | bytes 49156
  137.6 14.8 %collective-permute-start.14 = (f32[2,2,16,8,256]{4,3,1,0,2:T(8,128)S(1)}, f32[2,2,16,8,256]{4,3,1,0,2:T(8,128)S(1)}, u32[]{:S(2)}, u32[]{:S(2)}) collective-permute-start(f32[2,2,16,8,256]{4,3,1,0,2:T(8,128)S(1)} %get-tuple-element.24), channel_id=1, source_target_pairs={{0,2},{1,3},{2,4},{3,5},{4,6},{5,7},{6,8},{7,9},{8,10},{9,11},{10,... | collective-permute-start | bytes 1572872 | tf_op jit(solution)/shard_map/ppermute | solution.py:35
  142.5 28.5 %collective-permute-start.15 = (f32[2,2,16,8,256]{4,3,1,0,2:T(8,128)S(1)}, f32[2,2,16,8,256]{4,3,1,0,2:T(8,128)S(1)}, u32[]{:S(2)}, u32[]{:S(2)}) collective-permute-start(f32[2,2,16,8,256]{4,3,1,0,2:T(8,128)S(1)} %get-tuple-element.24), channel_id=1, source_target_pairs={{0,1},{1,2},{2,3},{3,4},{4,5},{5,6},{6,7},{7,8},{8,9},{9,10},{10,1... | collective-permute-start | bytes 1572872 | tf_op jit(solution)/shard_map/ppermute | solution.py:35
  149.0 22.2 %collective-permute-start.16 = (f32[2,2,16,8,256]{4,3,1,0,2:T(8,128)S(1)}, f32[2,2,16,8,256]{4,3,1,0,2:T(8,128)S(1)}, u32[]{:S(2)}, u32[]{:S(2)}) collective-permute-start(f32[2,2,16,8,256]{4,3,1,0,2:T(8,128)S(1)} %get-tuple-element.24), channel_id=1, source_target_pairs={{1,0},{2,1},{3,2},{4,3},{5,4},{6,5},{7,6},{8,7},{9,8},{10,9},{11,1... | collective-permute-start | bytes 1572872 | tf_op jit(solution)/shard_map/ppermute | solution.py:35
  152.4 18.9 %collective-permute-start.17 = (f32[2,2,16,8,256]{4,3,1,0,2:T(8,128)S(1)}, f32[2,2,16,8,256]{4,3,1,0,2:T(8,128)S(1)}, u32[]{:S(2)}, u32[]{:S(2)}) collective-permute-start(f32[2,2,16,8,256]{4,3,1,0,2:T(8,128)S(1)} %get-tuple-element.24), channel_id=1, source_target_pairs={{2,0},{3,1},{4,2},{5,3},{6,4},{7,5},{8,6},{9,7},{10,8},{11,9},{12,... | collective-permute-start | bytes 1572872 | tf_op jit(solution)/shard_map/ppermute | solution.py:35
  171.3 1.5 copy-start.1
  190.4 16.1 %copy-start.3 = (f32[16,2,2,8,256]{4,3,2,1,0:T(8,128)S(1)}, f32[16,2,2,8,256]{4,3,2,1,0:T(8,128)}, u32[]{:S(2)}) copy-start(f32[16,2,2,8,256]{4,3,2,1,0:T(8,128)} %param.9) | copy-start | bytes 1572868
  203.0 11.0 %all-to-all-start.2 = ((f32[2,2,16,8,256]{4,3,1,0,2:T(8,128)}), f32[2,2,16,8,256]{4,3,1,0,2:T(8,128)S(1)}, u32[]{:S(2)}, u32[]{:S(2)}) async-start(f32[2,2,16,8,256]{4,3,1,0,2:T(8,128)} %constant_dynamic-update-slice_fusion.49), calls=%async_computation.2 | async-start | bytes 1048576 | tf_op jit(solution)/shard_map/all_to_all | solution.py:288
  214.1 13.0 %collective-permute-start.18 = (f32[16,2,1,8,256]{4,3,2,0,1:T(8,128)S(1)}, f32[16,2,1,8,256]{4,3,2,0,1:T(8,128)S(1)}, u32[]{:S(2)}, u32[]{:S(2)}) collective-permute-start(f32[16,2,1,8,256]{4,3,2,0,1:T(8,128)S(1)} %get-tuple-element.77), channel_id=1, source_target_pairs={{0,32},{32,64},{64,96},{96,128},{128,160},{160,192},{192,224},{1,3... | collective-permute-start | bytes 786440 | tf_op jit(solution)/shard_map/ppermute | solution.py:26
  225.7 27.2 %copy-start.5 = (f32[16,2,256]{2,1,0:T(2,128)S(1)}, f32[16,2,256]{2,1,0:T(2,128)}, u32[]{:S(2)}) copy-start(f32[16,2,256]{2,1,0:T(2,128)} %param.10) | copy-start | bytes 98308
  225.8 9.9 %collective-permute-start.19 = (f32[16,2,1,8,256]{4,3,2,0,1:T(8,128)S(1)}, f32[16,2,1,8,256]{4,3,2,0,1:T(8,128)S(1)}, u32[]{:S(2)}, u32[]{:S(2)}) collective-permute-start(f32[16,2,1,8,256]{4,3,2,0,1:T(8,128)S(1)} %get-tuple-element.76), channel_id=1, source_target_pairs={{32,0},{64,32},{96,64},{128,96},{160,128},{192,160},{224,192},{33,... | collective-permute-start | bytes 786440 | tf_op jit(solution)/shard_map/ppermute | solution.py:27
  235.9 17.4 %collective-permute-start.20 = (f32[16,2,4,1,256]{4,3,2,0,1:T(1,128)S(1)}, f32[16,2,4,1,256]{4,3,2,0,1:T(1,128)S(1)}, u32[]{:S(2)}, u32[]{:S(2)}) collective-permute-start(f32[16,2,4,1,256]{4,3,2,0,1:T(1,128)S(1)} %get-tuple-element.36), channel_id=1, source_target_pairs={{0,1},{1,2},{2,3},{3,4},{4,5},{5,6},{6,7},{7,8},{8,9},{9,10},{10,1... | collective-permute-start | bytes 393224 | tf_op jit(solution)/shard_map/ppermute | solution.py:26
  250.8 7.8 %collective-permute-start.21 = (f32[16,2,4,1,256]{4,3,2,0,1:T(1,128)S(1)}, f32[16,2,4,1,256]{4,3,2,0,1:T(1,128)S(1)}, u32[]{:S(2)}, u32[]{:S(2)}) collective-permute-start(f32[16,2,4,1,256]{4,3,2,0,1:T(1,128)S(1)} %get-tuple-element.37), channel_id=1, source_target_pairs={{1,0},{2,1},{3,2},{4,3},{5,4},{6,5},{7,6},{8,7},{9,8},{10,9},{11,1... | collective-permute-start | bytes 393224 | tf_op jit(solution)/shard_map/ppermute | solution.py:27

commit v5 on v4

--- a/solution.py
+++ b/solution.py
@@ -206,31 +206,14 @@
     full_depth = layer_len * depth_count
     full_width = width_len * tile_count
     depth_cells = depth_index * layer_len + jnp.arange(layer_len, dtype=jnp.int32)
-    width_cells = tile_index * width_len + jnp.arange(width_len, dtype=jnp.int32)
     width_wide = (tile_index * width_len - 1 + jnp.arange(width_len + 2, dtype=jnp.int32)).astype(
         jnp.float32
     )
     damping_wide = damping_field(
         pml_width, depth_cells.astype(jnp.float32), width_wide, full_depth * 1.0, full_width * 1.0
     )[:, :, None]
-    damping = damping_wide[:, 1:-1]
-    slowness_wide = extended(slowness_sq, (("tile", 1),), 1)
-
-    def apply_operator(values):
-        padded = extended(values, (("depth", 2), ("tile", 3)), 1)
-        negative = laplacian_from_padded(pad_long(padded), layer_len, width_len, long_len)
-        mass = lateral_smooth(pad_long(padded[:, :, 1:-1] * slowness_wide), width_len, long_len)
-        return combine_operator(negative, mass, damping)
-
-    cell_index = (
-        depth_cells[:, None, None] * full_width + width_cells[None, :, None]
-    ) * long_len + jnp.arange(long_len, dtype=jnp.int32)[None, None, :]
-    hits = cell_index[None] == source_cell[:, None, None, None]
-    source_re = jnp.where(hits, SOURCE_AMPLITUDE, 0.0).astype(jnp.float32)
-    forcing = jnp.stack([source_re, jnp.zeros_like(source_re)], axis=1)
-    residual = forcing - apply_operator(warm_field)
-
     shots_here = shot_count // depth_count
+    shot_start = depth_index * shots_here
     reach = -(-(full_depth - 1) // width_len)
     halo = reach * width_len
     window = width_len + 2 * halo
@@ -255,6 +238,25 @@
     inv_re, inv_im = inverse_diagonal(slowness_ext, damping_ext)
     row_valid = ((rows_ext >= 0) & (rows_ext < full_width))[:, None]
 
+    def apply_window(values, slowness, damping, rows_out):
+        padded = jnp.pad(values, [(0, 0), (0, 0), (1, 1), (0, 0), (1, 1)])
+        negative = laplacian_from_padded(padded, full_depth, rows_out, long_len)
+        mass = lateral_smooth(pad_long(values * slowness), rows_out, long_len)
+        return combine_operator(negative, mass, damping)
+
+    warm_t = lax.all_to_all(warm_field, "depth", 0, 2, tiled=True)
+    warm_ext = with_neighbour_rows(warm_t)
+    warm_pad = jnp.pad(warm_ext, [(0, 0), (0, 0), (0, 0), (1, 1), (0, 0)])
+    slowness_pad = jnp.pad(slowness_ext, [(0, 0), (1, 1), (0, 0)])
+    cell_index = (
+        jnp.arange(full_depth, dtype=jnp.int32)[:, None, None] * full_width + rows_ext[None, :, None]
+    ) * long_len + jnp.arange(long_len, dtype=jnp.int32)[None, None, :]
+    my_sources = lax.dynamic_slice_in_dim(source_cell, shot_start, shots_here)
+    hits = (cell_index[None] == my_sources[:, None, None, None]) & row_valid[None, None]
+    source_re = jnp.where(hits, SOURCE_AMPLITUDE, 0.0).astype(jnp.float32)
+    forcing = jnp.stack([source_re, jnp.zeros_like(source_re)], axis=1)
+    residual_ext = forcing - apply_window(warm_pad, slowness_pad, damping_ext, window)
+
     def couple(plane_in):
         return plane_coupling(
             jnp.pad(plane_in, [(0, 0)] * (plane_in.ndim - 2) + [(1, 1), (1, 1)]),
@@ -262,8 +264,6 @@
             long_len,
         )
 
-    residual_t = lax.all_to_all(residual, "depth", 0, 2, tiled=True)
-    residual_ext = with_neighbour_rows(residual_t)
     previous = jnp.zeros((shots_here, 2, window, long_len), jnp.float32)
     layers_out = []
     for layer_no in range(full_depth):
@@ -283,10 +283,16 @@
             + complex_scale(inv_re[layer_no], inv_im[layer_no], couple(previous)),
             0.0,
         )
-        layers_out[layer_no] = previous[:, :, halo : halo + width_len]
-    search_t = jnp.stack(layers_out, axis=2)
-    search = lax.all_to_all(search_t, "depth", 2, 0, tiled=True)
-    image_field = apply_operator(search)
+        layers_out[layer_no] = previous[:, :, halo - 1 : halo + width_len + 1]
+    search_rim = jnp.stack(layers_out, axis=2)
+    search_t = search_rim[:, :, :, 1:-1]
+    image_field = apply_window(
+        extended(search_t, (("tile", 3),), 1),
+        slowness_ext[:, halo - 1 : halo + width_len + 1],
+        damping_ext[:, halo : halo + width_len],
+        width_len,
+    )
+    residual = residual_ext[:, :, :, halo : halo + width_len]
     local_real = jnp.sum(
         image_field[:, 0] * residual[:, 0] + image_field[:, 1] * residual[:, 1], axis=(1, 2, 3)
     )
@@ -297,31 +303,27 @@
         image_field[:, 0] * image_field[:, 0] + image_field[:, 1] * image_field[:, 1],
         axis=(1, 2, 3),
     )
+    my_receivers = lax.dynamic_slice_in_dim(receiver_cell, shot_start, shots_here)
+    my_observed = lax.dynamic_slice_in_dim(observed, shot_start, shots_here)
     plane_cells = full_width * long_len
-    rec_depth = receiver_cell // plane_cells
-    rec_width = receiver_cell // long_len % full_width
-    rec_long = receiver_cell % long_len
-    local_depth = rec_depth - depth_index * layer_len
+    rec_depth = my_receivers // plane_cells
+    rec_width = my_receivers // long_len % full_width
+    rec_long = my_receivers % long_len
     local_width = rec_width - tile_index * width_len
-    is_owned = (
-        (local_depth >= 0)
-        & (local_depth < layer_len)
-        & (local_width >= 0)
-        & (local_width < width_len)
-    )
-    row_count = layer_len * width_len
-    local_row = jnp.where(is_owned, local_depth * width_len + local_width, -1)
+    is_owned = (local_width >= 0) & (local_width < width_len)
+    row_count = full_depth * width_len
+    local_row = jnp.where(is_owned, rec_depth * width_len + local_width, -1)
     row_hot = (local_row[:, :, None] == jnp.arange(row_count, dtype=jnp.int32)).astype(jnp.float32)
-    both_fields = jnp.concatenate([warm_field, search], axis=1).reshape(
-        shot_count, 4, row_count, long_len
+    both_fields = jnp.concatenate([warm_t, search_t], axis=1).reshape(
+        shots_here, 4, row_count, long_len
     )
     picked_rows = jnp.einsum(
         "srk,sqky->sqry", row_hot, both_fields, precision=lax.Precision.HIGHEST
     )
     col_hot = rec_long[:, None, :, None] == jnp.arange(long_len, dtype=jnp.int32)
     picked = jnp.sum(jnp.where(col_hot, picked_rows, 0.0), axis=-1)
-    gap_re = picked[:, 0] - observed[:, 0]
-    gap_im = picked[:, 1] - observed[:, 1]
+    gap_re = picked[:, 0] - my_observed[:, 0]
+    gap_im = picked[:, 1] - my_observed[:, 1]
     dir_re = picked[:, 2]
     dir_im = picked[:, 3]
 
@@ -332,19 +334,26 @@
     cross_re = owned_sum(gap_re * dir_re + gap_im * dir_im)
     cross_im = owned_sum(gap_re * dir_im - gap_im * dir_re)
     dir_norm = owned_sum(dir_re * dir_re + dir_im * dir_im)
-    packed = jnp.stack(
+    mine = jnp.stack(
         [local_real, local_imag, local_norm, gap_norm, cross_re, cross_im, dir_norm], axis=1
+    )
+    packed = lax.dynamic_update_slice_in_dim(
+        jnp.zeros((shot_count, mine.shape[1]), jnp.float32), mine, shot_start, 0
     )
     packed = all_sum(packed)
     dot_real, dot_imag, image_norm = packed[:, 0], packed[:, 1], packed[:, 2]
     gap_norm, cross_re, cross_im, dir_norm = packed[:, 3], packed[:, 4], packed[:, 5], packed[:, 6]
-    step_re = (dot_real / image_norm)[:, None, None, None]
-    step_im = (dot_imag / image_norm)[:, None, None, None]
-    new_re = warm_field[:, 0] + step_re * search[:, 0] - step_im * search[:, 1]
-    new_im = warm_field[:, 1] + step_re * search[:, 1] + step_im * search[:, 0]
-    new_field = jnp.stack([new_re, new_im], axis=1)
     scale_re = dot_real / image_norm
     scale_im = dot_imag / image_norm
+    step_re = lax.dynamic_slice_in_dim(scale_re, shot_start, shots_here)[:, None, None, None]
+    step_im = lax.dynamic_slice_in_dim(scale_im, shot_start, shots_here)[:, None, None, None]
+    new_re_t = warm_t[:, 0] + step_re * search_t[:, 0] - step_im * search_t[:, 1]
+    new_im_t = warm_t[:, 1] + step_re * search_t[:, 1] + step_im * search_t[:, 0]
+    new_field = lax.all_to_all(
+        jnp.stack([new_re_t, new_im_t], axis=1), "depth", 2, 0, tiled=True
+    )
+    new_re = new_field[:, 0]
+    new_im = new_field[:, 1]
     misfit = 0.5 * (
         gap_norm
         + 2.0 * (scale_re * cross_re - scale_im * cross_im)

time: 292 us -> 307 us (1.051)
  other arithmetic: 63.5 us -> 112 us
  starting transfers between devices: 125 us -> 83.7 us
  local copies, waits for them, and re-layouts: 21.4 us -> 30.5 us
  matrix products: 9.15 us -> 2.48 us
  Pallas kernels: 20.5 us -> 24.8 us
    sub x2 -> x3, other arithmetic: 5.44 us -> 43.9 us  [laplacian_from_padded(): summed - LAP_WEIGHTS[order_no] * padded[..., 1 + off_depth:1 + off_depth...]
    ppermute x6 -> x2, starting transfers between devices: 32.8 us -> 4.1 us  [extended(): after = lax.ppermute(leading, axis, down)]
    ppermute x6 -> x2, starting transfers between devices: 34.1 us -> 15.5 us  [extended(): before = lax.ppermute(last, axis, up)]
    ppermute x12, waiting for transfers between devices: 19.3 us -> 37.8 us  [shifted(): lax.ppermute(value, axis, [(source, source + steps) for source in range(l...]
    ppermute x6 -> x2, waiting for transfers between devices: 13.8 us -> 3.69 us  [extended(): after = lax.ppermute(leading, axis, down)]
    ppermute x12, starting transfers between devices: 42.5 us -> 49.9 us  [shifted(): lax.ppermute(value, axis, [(source, source + steps) for source in range(l...]
    all_to_all x2, waiting for transfers between devices: 14.9 us -> 7.51 us  [the longest x1 7.51 us: per_device(): lax.all_to_all(jnp.stack([new_re_t, new_im_t], axis=1), 'depth', 2, 0, ti...]
    dot_general x1, matrix products: 9.15 us -> 2.48 us  [per_device(): jnp.einsum('srk,sqky->sqry', row_hot, both_fields, precision=lax.Precisio...]
  transfers between devices with their start and end apart: 27 -> 19, of which waited for: 7 -> 8; matrix products, arithmetic and copies ran while one was open for 28% -> 45% of each run, Pallas kernels for 0% -> 8%
where the time goes in v5:
time: 307 us; the launch traced here: 305 us
  other arithmetic  112 us (36%)
  starting transfers between devices  83.7 us (27%)
  waiting for transfers between devices  49 us (16%)
  local copies, waits for them, and re-layouts  30.5 us (10%)
  Pallas kernels  24.8 us (8%)
    ppermute x12, starting transfers between devices, shifted(): lax.ppermute(value, axis, [(source, source + steps) for source in range(l...  49.9 us
    sub x3, other arithmetic, laplacian_from_padded(): summed - LAP_WEIGHTS[order_no] * padded[..., 1 + off_depth:1 + off_depth...  43.9 us
    ppermute x12, waiting for transfers between devices, shifted(): lax.ppermute(value, axis, [(source, source + steps) for source in range(l...  37.8 us
    pallas_call x1, Pallas kernels, all_sum(): pl.pallas_call(functools.partial(all_sum_kernel, depth_count, tile_count)...  24.8 us
    add x16, other arithmetic, per_device(): source_term = residual_ext[:, :, layer_no] + couple(previous)  18.3 us
    unnamed x204, local copies, waits for them, and re-layouts  16.7 us
    ppermute x2, starting transfers between devices, extended(): before = lax.ppermute(last, axis, up)  15.5 us
    select_n x15, other arithmetic, per_device(): jnp.where(row_valid, downward_ext[:, :, layer_no] + complex_scale(inv_re[...  15 us
  transfers between devices with their start and end apart: 19, of which 8 were waited for; matrix products, arithmetic and copies ran while one was open for 45% of the time, Pallas kernels for 8%

profile of v5, /device:TPU:1, one launch (start us, length us, event | category | flops | bytes accessed | tf_op | source)
XLA Modules:
  0.0 305.1 jit_solution(3814410509354585511)
XLA Ops:
  0.6 1.4 broadcast_in_dim.195
  2.0 5.9 %all-to-all-start.1 = ((f32[8,2,8,256]{3,2,1,0:T(8,128)}), f32[8,2,8,256]{3,2,1,0:T(8,128)S(1)}, u32[]{:S(2)}, u32[]{:S(2)}) async-start(f32[8,2,8,256]{3,2,1,0:T(8,128)} %broadcast_in_dim.195), calls=%async_computation.1 | async-start | bytes 262144 | tf_op jit(solution)/shard_map/all_to_all | solution.py:228
  7.9 2.0 fusion.739
  9.9 5.2 %collective-permute-start.14 = (f32[16,2,2,1,256]{4,3,2,0,1:T(1,128)}, f32[16,2,2,1,256]{4,3,2,0,1:T(1,128)}, u32[]{:S(2)}, u32[]{:S(2)}) collective-permute-start(f32[16,2,2,1,256]{4,3,2,0,1:T(1,128)} %get-tuple-element.80), channel_id=1, source_target_pairs={{0,1},{1,2},{2,3},{3,4},{4,5},{5,6},{6,7},{7,8},{8,9},{9,10},{10,1... | collective-permute-start | bytes 196616 | tf_op jit(solution)/shard_map/ppermute | solution.py:26
  15.1 1.9 collective-permute-start.15
  18.3 1.3 multiply_add_fusion.36
  19.7 1.2 multiply_add_fusion.37
  22.0 1.3 and_select_fusion
  23.4 1.2 multiply_add_fusion.35
  24.6 1.3 multiply_add_fusion.34
  25.9 4.8 %all-to-all-start = ((f32[16,2,2,8,256]{4,3,2,1,0:T(8,128)}), f32[16,2,2,8,256]{4,3,2,1,0:T(8,128)S(1)}, u32[]{:S(2)}, u32[]{:S(2)}) async-start(f32[16,2,2,8,256]{4,3,2,1,0:T(8,128)} %param.7), calls=%async_computation | async-start | bytes 1048576 | tf_op jit(solution)/shard_map/all_to_all | solution.py:247
  30.7 6.0 %collective-permute-start.1 = (f32[16,8,256]{2,1,0:T(8,128)S(1)}, f32[16,8,256]{2,1,0:T(8,128)S(1)}, u32[]{:S(2)}, u32[]{:S(2)}) collective-permute-start(f32[16,8,256]{2,1,0:T(8,128)S(1)} %bitcast.528), channel_id=1, source_target_pairs={{0,1},{1,2},{2,3},{3,4},{4,5},{5,6},{6,7},{7,8},{8,9},{9,10},{10,1... | collective-permute-start | bytes 393224 | tf_op jit(solution)/shard_map/ppermute | solution.py:35
  36.7 4.7 %collective-permute-start = (f32[16,8,256]{2,1,0:T(8,128)S(1)}, f32[16,8,256]{2,1,0:T(8,128)S(1)}, u32[]{:S(2)}, u32[]{:S(2)}) collective-permute-start(f32[16,8,256]{2,1,0:T(8,128)S(1)} %bitcast.529), channel_id=1, source_target_pairs={{0,2},{1,3},{2,4},{3,5},{4,6},{5,7},{6,8},{7,9},{8,10},{9,11},{10,... | collective-permute-start | bytes 393224 | tf_op jit(solution)/shard_map/ppermute | solution.py:35
  42.1 1.9 collective-permute-start.2
  44.0 1.3 collective-permute-start.3
  45.4 4.5 %collective-permute-done.2 = f32[16,8,256]{2,1,0:T(8,128)S(1)} collective-permute-done((f32[16,8,256]{2,1,0:T(8,128)S(1)}, f32[16,8,256]{2,1,0:T(8,128)S(1)}, u32[]{:S(2)}, u32[]{:S(2)}) %collective-permute-start.2) | collective-permute-done | bytes 131104 | tf_op jit(solution)/shard_map/ppermute | solution.py:35
  49.9 2.5 collective-permute-done.3
  52.5 4.9 %collective-permute-start.4 = (f32[2,2,16,8,256]{4,3,2,0,1:T(8,128)S(1)}, f32[2,2,16,8,256]{4,3,2,0,1:T(8,128)S(1)}, u32[]{:S(2)}, u32[]{:S(2)}) collective-permute-start(f32[2,2,16,8,256]{4,3,2,0,1:T(8,128)S(1)} %copy.228), channel_id=1, source_target_pairs={{0,2},{1,3},{2,4},{3,5},{4,6},{5,7},{6,8},{7,9},{8,10},{9,11},{10,... | collective-permute-start | bytes 1572872 | tf_op jit(solution)/shard_map/ppermute | solution.py:35
  57.8 5.6 %collective-permute-start.5 = (f32[2,2,16,8,256]{4,3,2,0,1:T(8,128)S(1)}, f32[2,2,16,8,256]{4,3,2,0,1:T(8,128)S(1)}, u32[]{:S(2)}, u32[]{:S(2)}) collective-permute-start(f32[2,2,16,8,256]{4,3,2,0,1:T(8,128)S(1)} %copy.228), channel_id=1, source_target_pairs={{0,1},{1,2},{2,3},{3,4},{4,5},{5,6},{6,7},{7,8},{8,9},{9,10},{10,1... | collective-permute-start | bytes 1572872 | tf_op jit(solution)/shard_map/ppermute | solution.py:35
  64.2 1.9 collective-permute-start.6
  67.2 1.3 collective-permute-start.7
  68.5 17.5 %collective-permute-done.5 = f32[2,2,16,8,256]{4,3,2,0,1:T(8,128)S(1)} collective-permute-done((f32[2,2,16,8,256]{4,3,2,0,1:T(8,128)S(1)}, f32[2,2,16,8,256]{4,3,2,0,1:T(8,128)S(1)}, u32[]{:S(2)}, u32[]{:S(2)}) %collective-permute-start.5) | collective-permute-done | bytes 524320 | tf_op jit(solution)/shard_map/ppermute | solution.py:35
  86.2 1.5 copy-done.3
  87.7 2.5 broadcast_multiply_fusion
  90.2 40.8 %fusion.60 = f32[2,2,16,40,256]{4,3,2,0,1:T(8,128)} fusion(f32[2,2,16,42,256]{4,3,2,0,1:T(8,128)} %get-tuple-element.22, f32[2,2,16,40,256]{4,3,2,0,1:T(8,128)} %copy-done.3), kind=kLoop, calls=%fused_computation.114 | loop fusion | flops 34734080 | bytes 13631488 | tf_op jit(solution)/shard_map/sub | solution.py:138
  131.0 4.8 %fusion.8 = f32[2,2,16,40,256]{4,3,2,0,1:T(8,128)S(1)} fusion(f32[2,2,16,42,256]{4,3,2,0,1:T(8,128)S(1)} %get-tuple-element.21), kind=kLoop, calls=%fused_computation.62 | loop fusion | flops 11141120 | bytes 13631488 | tf_op jit(solution)/shard_map/add | solution.py:159
  139.1 1.3 fusion.198
  140.5 1.3 fusion.215
  142.0 1.3 fusion.232
  143.4 1.3 fusion.249
  144.8 1.3 fusion.266
  146.2 1.3 fusion.283
  147.7 1.3 fusion.300
  149.1 1.3 fusion.317
  150.5 1.3 fusion.334
  151.9 1.2 fusion.351
  153.3 1.3 fusion.368
  154.7 1.2 fusion.385
  156.1 1.3 fusion.402
  157.5 1.2 fusion.419
  168.7 2.1 collective-permute-start.8
  170.7 1.3 add_select_fusion
  172.0 15.8 %collective-permute-start.9 = (f32[2,2,16,8,256]{4,3,0,1,2:T(8,128)}, f32[2,2,16,8,256]{4,3,0,1,2:T(8,128)}, u32[]{:S(2)}, u32[]{:S(2)}) collective-permute-start(f32[2,2,16,8,256]{4,3,0,1,2:T(8,128)} %get-tuple-element.15), channel_id=1, source_target_pairs={{0,1},{1,2},{2,3},{3,4},{4,5},{5,6},{6,7},{7,8},{8,9},{9,10},{10,1... | collective-permute-start | bytes 1572872 | tf_op jit(solution)/shard_map/ppermute | solution.py:35
  187.9 1.4 constant_dynamic-slice_fusion.3
  192.1 2.9 collective-permute-start.10
  195.0 1.5 collective-permute-start.11
  196.5 1.1 constant_dynamic-update-slice_fusion.45
  197.7 1.1 constant_dynamic-update-slice_fusion.44
  199.8 7.8 %collective-permute-done.10 = f32[2,2,16,8,256]{4,3,0,1,2:T(8,128)S(1)} collective-permute-done((f32[2,2,16,8,256]{4,3,0,1,2:T(8,128)}, f32[2,2,16,8,256]{4,3,0,1,2:T(8,128)S(1)}, u32[]{:S(2)}, u32[]{:S(2)}) %collective-permute-start.10) | collective-permute-done | bytes 524320 | tf_op jit(solution)/shard_map/ppermute | solution.py:35
  207.5 5.3 %collective-permute-done.11 = f32[2,2,16,8,256]{4,3,0,1,2:T(8,128)S(1)} collective-permute-done((f32[2,2,16,8,256]{4,3,0,1,2:T(8,128)}, f32[2,2,16,8,256]{4,3,0,1,2:T(8,128)S(1)}, u32[]{:S(2)}, u32[]{:S(2)}) %collective-permute-start.11) | collective-permute-done | bytes 524320 | tf_op jit(solution)/shard_map/ppermute | solution.py:35
  213.0 1.5 copy-done.6
  217.2 1.0 fusion.687
  218.6 1.0 fusion.689
  220.0 1.0 fusion.691
  236.9 2.5 fusion.64
  239.4 10.3 %collective-permute-start.12 = (f32[2,2,16,1,256]{4,3,2,1,0:T(1,128)S(1)}, f32[2,2,16,1,256]{4,3,2,1,0:T(1,128)S(1)}, u32[]{:S(2)}, u32[]{:S(2)}) collective-permute-start(f32[2,2,16,1,256]{4,3,2,1,0:T(1,128)S(1)} %copy.328), channel_id=1, source_target_pairs={{0,1},{1,2},{2,3},{3,4},{4,5},{5,6},{6,7},{7,8},{8,9},{9,10},{10,1... | collective-permute-start | bytes 196616 | tf_op jit(solution)/shard_map/ppermute | solution.py:26
  249.8 2.2 collective-permute-start.13
  253.2 3.7 %collective-permute-done.13 = f32[2,2,16,1,256]{4,3,2,1,0:T(1,128)S(1)} collective-permute-done((f32[2,2,16,1,256]{4,3,2,1,0:T(1,128)S(1)}, f32[2,2,16,1,256]{4,3,2,1,0:T(1,128)S(1)}, u32[]{:S(2)}, u32[]{:S(2)}) %collective-permute-start.13) | collective-permute-done | bytes 65568 | tf_op jit(solution)/shard_map/ppermute | solution.py:27
  258.0 2.7 fusion.98
  261.3 1.3 subtract_reduce_fusion
  263.6 24.8 %shard_map.94 = f32[8,128]{1,0:T(8,128)} custom-call(f32[8,128]{1,0:T(8,128)} %pad_bitcast_fusion.x_ref), custom_call_target="tpu_custom_call" | custom-call | tf_op jit(solution)/shard_map/pallas_call | solution.py:90
  291.1 3.5 %all-to-all-start.2 = ((f32[2,2,16,8,256]{4,3,1,0,2:T(8,128)}), f32[2,2,16,8,256]{4,3,1,0,2:T(8,128)S(1)}, u32[]{:S(2)}, u32[]{:S(2)}) async-start(f32[2,2,16,8,256]{4,3,1,0,2:T(8,128)} %copy.301), calls=%async_computation.2 | async-start | bytes 1048576 | tf_op jit(solution)/shard_map/all_to_all | solution.py:352
  294.7 1.1 pad_maximum_fusion.1
  296.0 7.5 %all-to-all-done.2 = f32[2,2,16,8,256]{4,3,1,0,2:T(8,128)S(1)} async-done(((f32[2,2,16,8,256]{4,3,1,0,2:T(8,128)}), f32[2,2,16,8,256]{4,3,1,0,2:T(8,128)S(1)}, u32[]{:S(2)}, u32[]{:S(2)}) %all-to-all-start.2) | async-done | bytes 524320 | tf_op jit(solution)/shard_map/all_to_all | solution.py:352
  (356 shorter events, 51.2 us)
Async XLA Ops:
  2.0 23.8 %all-to-all-start.1 = ((f32[8,2,8,256]{3,2,1,0:T(8,128)}), f32[8,2,8,256]{3,2,1,0:T(8,128)S(1)}, u32[]{:S(2)}, u32[]{:S(2)}) async-start(f32[8,2,8,256]{3,2,1,0:T(8,128)} %broadcast_in_dim.195), calls=%async_computation.1 | async-start | bytes 262144 | tf_op jit(solution)/shard_map/all_to_all | solution.py:228
  9.9 284.7 %collective-permute-start.14 = (f32[16,2,2,1,256]{4,3,2,0,1:T(1,128)}, f32[16,2,2,1,256]{4,3,2,0,1:T(1,128)}, u32[]{:S(2)}, u32[]{:S(2)}) collective-permute-start(f32[16,2,2,1,256]{4,3,2,0,1:T(1,128)} %get-tuple-element.80), channel_id=1, source_target_pairs={{0,1},{1,2},{2,3},{3,4},{4,5},{5,6},{6,7},{7,8},{8,9},{9,10},{10,1... | collective-permute-start | bytes 196616 | tf_op jit(solution)/shard_map/ppermute | solution.py:26
  15.1 279.5 %collective-permute-start.15 = (f32[16,2,2,1,256]{4,3,2,0,1:T(1,128)}, f32[16,2,2,1,256]{4,3,2,0,1:T(1,128)}, u32[]{:S(2)}, u32[]{:S(2)}) collective-permute-start(f32[16,2,2,1,256]{4,3,2,0,1:T(1,128)} %get-tuple-element.81), channel_id=1, source_target_pairs={{1,0},{2,1},{3,2},{4,3},{5,4},{6,5},{7,6},{8,7},{9,8},{10,9},{11,1... | collective-permute-start | bytes 196616 | tf_op jit(solution)/shard_map/ppermute | solution.py:27
  25.9 26.6 %all-to-all-start = ((f32[16,2,2,8,256]{4,3,2,1,0:T(8,128)}), f32[16,2,2,8,256]{4,3,2,1,0:T(8,128)S(1)}, u32[]{:S(2)}, u32[]{:S(2)}) async-start(f32[16,2,2,8,256]{4,3,2,1,0:T(8,128)} %param.7), calls=%async_computation | async-start | bytes 1048576 | tf_op jit(solution)/shard_map/all_to_all | solution.py:247
  30.7 14.6 %collective-permute-start.1 = (f32[16,8,256]{2,1,0:T(8,128)S(1)}, f32[16,8,256]{2,1,0:T(8,128)S(1)}, u32[]{:S(2)}, u32[]{:S(2)}) collective-permute-start(f32[16,8,256]{2,1,0:T(8,128)S(1)} %bitcast.528), channel_id=1, source_target_pairs={{0,1},{1,2},{2,3},{3,4},{4,5},{5,6},{6,7},{7,8},{8,9},{9,10},{10,1... | collective-permute-start | bytes 393224 | tf_op jit(solution)/shard_map/ppermute | solution.py:35
  36.7 7.3 %collective-permute-start = (f32[16,8,256]{2,1,0:T(8,128)S(1)}, f32[16,8,256]{2,1,0:T(8,128)S(1)}, u32[]{:S(2)}, u32[]{:S(2)}) collective-permute-start(f32[16,8,256]{2,1,0:T(8,128)S(1)} %bitcast.529), channel_id=1, source_target_pairs={{0,2},{1,3},{2,4},{3,5},{4,6},{5,7},{6,8},{7,9},{8,10},{9,11},{10,... | collective-permute-start | bytes 393224 | tf_op jit(solution)/shard_map/ppermute | solution.py:35
  42.1 7.8 %collective-permute-start.2 = (f32[16,8,256]{2,1,0:T(8,128)S(1)}, f32[16,8,256]{2,1,0:T(8,128)S(1)}, u32[]{:S(2)}, u32[]{:S(2)}) collective-permute-start(f32[16,8,256]{2,1,0:T(8,128)S(1)} %bitcast.530), channel_id=1, source_target_pairs={{1,0},{2,1},{3,2},{4,3},{5,4},{6,5},{7,6},{8,7},{9,8},{10,9},{11,1... | collective-permute-start | bytes 393224 | tf_op jit(solution)/shard_map/ppermute | solution.py:35
  44.0 8.4 %collective-permute-start.3 = (f32[16,8,256]{2,1,0:T(8,128)S(1)}, f32[16,8,256]{2,1,0:T(8,128)S(1)}, u32[]{:S(2)}, u32[]{:S(2)}) collective-permute-start(f32[16,8,256]{2,1,0:T(8,128)S(1)} %bitcast.531), channel_id=1, source_target_pairs={{2,0},{3,1},{4,2},{5,3},{6,4},{7,5},{8,6},{9,7},{10,8},{11,9},{12,... | collective-permute-start | bytes 393224 | tf_op jit(solution)/shard_map/ppermute | solution.py:35
  45.3 18.8 %copy-start.10 = (f32[16,8,256]{2,1,0:T(8,128)}, f32[16,8,256]{2,1,0:T(8,128)S(1)}, u32[]{:S(2)}) copy-start(f32[16,8,256]{2,1,0:T(8,128)S(1)} %collective-permute-done.1) | copy-start | bytes 393220
  49.9 36.3 %copy-start.12 = (f32[16,8,256]{2,1,0:T(8,128)}, f32[16,8,256]{2,1,0:T(8,128)S(1)}, u32[]{:S(2)}) copy-start(f32[16,8,256]{2,1,0:T(8,128)S(1)} %collective-permute-done.2) | copy-start | bytes 393220
  52.5 33.6 %copy-start = (f32[2,2,8,2,8,256]{5,4,3,2,1,0:T(8,128)}, f32[2,2,8,2,8,256]{5,4,3,2,1,0:T(8,128)S(1)}, u32[]{:S(2)}) copy-start(f32[2,2,8,2,8,256]{5,4,3,2,1,0:T(8,128)S(1)} %copy.227) | copy-start | bytes 1572868
  52.5 14.6 %collective-permute-start.4 = (f32[2,2,16,8,256]{4,3,2,0,1:T(8,128)S(1)}, f32[2,2,16,8,256]{4,3,2,0,1:T(8,128)S(1)}, u32[]{:S(2)}, u32[]{:S(2)}) collective-permute-start(f32[2,2,16,8,256]{4,3,2,0,1:T(8,128)S(1)} %copy.228), channel_id=1, source_target_pairs={{0,2},{1,3},{2,4},{3,5},{4,6},{5,7},{6,8},{7,9},{8,10},{9,11},{10,... | collective-permute-start | bytes 1572872 | tf_op jit(solution)/shard_map/ppermute | solution.py:35
  57.8 28.2 %collective-permute-start.5 = (f32[2,2,16,8,256]{4,3,2,0,1:T(8,128)S(1)}, f32[2,2,16,8,256]{4,3,2,0,1:T(8,128)S(1)}, u32[]{:S(2)}, u32[]{:S(2)}) collective-permute-start(f32[2,2,16,8,256]{4,3,2,0,1:T(8,128)S(1)} %copy.228), channel_id=1, source_target_pairs={{0,1},{1,2},{2,3},{3,4},{4,5},{5,6},{6,7},{7,8},{8,9},{9,10},{10,1... | collective-permute-start | bytes 1572872 | tf_op jit(solution)/shard_map/ppermute | solution.py:35
  64.2 21.9 %collective-permute-start.6 = (f32[2,2,16,8,256]{4,3,2,0,1:T(8,128)S(1)}, f32[2,2,16,8,256]{4,3,2,0,1:T(8,128)S(1)}, u32[]{:S(2)}, u32[]{:S(2)}) collective-permute-start(f32[2,2,16,8,256]{4,3,2,0,1:T(8,128)S(1)} %copy.228), channel_id=1, source_target_pairs={{1,0},{2,1},{3,2},{4,3},{5,4},{6,5},{7,6},{8,7},{9,8},{10,9},{11,1... | collective-permute-start | bytes 1572872 | tf_op jit(solution)/shard_map/ppermute | solution.py:35
  67.0 70.9 %copy-start.15 = (f32[40,256]{1,0:T(8,128)}, f32[40,256]{1,0:T(8,128)S(1)}, u32[]{:S(2)}) copy-start(f32[40,256]{1,0:T(8,128)S(1)} %get-tuple-element.79) | copy-start | bytes 122884
  67.2 19.0 %collective-permute-start.7 = (f32[2,2,16,8,256]{4,3,2,0,1:T(8,128)S(1)}, f32[2,2,16,8,256]{4,3,2,0,1:T(8,128)S(1)}, u32[]{:S(2)}, u32[]{:S(2)}) collective-permute-start(f32[2,2,16,8,256]{4,3,2,0,1:T(8,128)S(1)} %copy.228), channel_id=1, source_target_pairs={{2,0},{3,1},{4,2},{5,3},{6,4},{7,5},{8,6},{9,7},{10,8},{11,9},{12,... | collective-permute-start | bytes 1572872 | tf_op jit(solution)/shard_map/ppermute | solution.py:35
  138.3 6.4 %copy-start.25 = (f32[40,256]{1,0:T(8,128)S(1)}, f32[40,256]{1,0:T(8,128)}, u32[]{:S(2)}) copy-start(f32[40,256]{1,0:T(8,128)} %get-tuple-element.58) | copy-start | bytes 122884
  138.3 6.4 %copy-start.34 = (f32[40,256]{1,0:T(8,128)S(1)}, f32[40,256]{1,0:T(8,128)}, u32[]{:S(2)}) copy-start(f32[40,256]{1,0:T(8,128)} %get-tuple-element.74) | copy-start | bytes 122884
  139.0 19.7 %copy-start.8 = (f32[2,2,40,256]{3,2,0,1:T(8,128)}, f32[2,2,40,256]{3,2,0,1:T(8,128)S(1)}, u32[]{:S(2)}) copy-start(f32[2,2,40,256]{3,2,0,1:T(8,128)S(1)} %maximum_select_fusion.1) | copy-start | bytes 491524
  139.0 7.0 %copy-start.29 = (f32[40,256]{1,0:T(8,128)S(1)}, f32[40,256]{1,0:T(8,128)}, u32[]{:S(2)}) copy-start(f32[40,256]{1,0:T(8,128)} %get-tuple-element.57) | copy-start | bytes 122884
  139.1 7.0 %copy-start.38 = (f32[40,256]{1,0:T(8,128)S(1)}, f32[40,256]{1,0:T(8,128)}, u32[]{:S(2)}) copy-start(f32[40,256]{1,0:T(8,128)} %get-tuple-element.73) | copy-start | bytes 122884
  140.5 7.0 %copy-start.33 = (f32[40,256]{1,0:T(8,128)S(1)}, f32[40,256]{1,0:T(8,128)}, u32[]{:S(2)}) copy-start(f32[40,256]{1,0:T(8,128)} %get-tuple-element.56) | copy-start | bytes 122884
  140.5 7.0 %copy-start.41 = (f32[40,256]{1,0:T(8,128)S(1)}, f32[40,256]{1,0:T(8,128)}, u32[]{:S(2)}) copy-start(f32[40,256]{1,0:T(8,128)} %get-tuple-element.72) | copy-start | bytes 122884
  141.9 7.0 %copy-start.36 = (f32[40,256]{1,0:T(8,128)S(1)}, f32[40,256]{1,0:T(8,128)}, u32[]{:S(2)}) copy-start(f32[40,256]{1,0:T(8,128)} %get-tuple-element.55) | copy-start | bytes 122884
  142.0 7.0 %copy-start.45 = (f32[40,256]{1,0:T(8,128)S(1)}, f32[40,256]{1,0:T(8,128)}, u32[]{:S(2)}) copy-start(f32[40,256]{1,0:T(8,128)} %get-tuple-element.71) | copy-start | bytes 122884
  143.4 7.0 %copy-start.40 = (f32[40,256]{1,0:T(8,128)S(1)}, f32[40,256]{1,0:T(8,128)}, u32[]{:S(2)}) copy-start(f32[40,256]{1,0:T(8,128)} %get-tuple-element.54) | copy-start | bytes 122884
  143.4 7.0 %copy-start.49 = (f32[40,256]{1,0:T(8,128)S(1)}, f32[40,256]{1,0:T(8,128)}, u32[]{:S(2)}) copy-start(f32[40,256]{1,0:T(8,128)} %get-tuple-element.70) | copy-start | bytes 122884
  144.8 7.0 %copy-start.43 = (f32[40,256]{1,0:T(8,128)S(1)}, f32[40,256]{1,0:T(8,128)}, u32[]{:S(2)}) copy-start(f32[40,256]{1,0:T(8,128)} %get-tuple-element.53) | copy-start | bytes 122884
  144.8 7.0 %copy-start.53 = (f32[40,256]{1,0:T(8,128)S(1)}, f32[40,256]{1,0:T(8,128)}, u32[]{:S(2)}) copy-start(f32[40,256]{1,0:T(8,128)} %get-tuple-element.69) | copy-start | bytes 122884
  146.2 6.9 %copy-start.47 = (f32[40,256]{1,0:T(8,128)S(1)}, f32[40,256]{1,0:T(8,128)}, u32[]{:S(2)}) copy-start(f32[40,256]{1,0:T(8,128)} %get-tuple-element.52) | copy-start | bytes 122884
  146.2 6.9 %copy-start.57 = (f32[40,256]{1,0:T(8,128)S(1)}, f32[40,256]{1,0:T(8,128)}, u32[]{:S(2)}) copy-start(f32[40,256]{1,0:T(8,128)} %get-tuple-element.68) | copy-start | bytes 122884
  147.6 6.9 %copy-start.51 = (f32[40,256]{1,0:T(8,128)S(1)}, f32[40,256]{1,0:T(8,128)}, u32[]{:S(2)}) copy-start(f32[40,256]{1,0:T(8,128)} %get-tuple-element.51) | copy-start | bytes 122884
  147.6 6.9 %copy-start.61 = (f32[40,256]{1,0:T(8,128)S(1)}, f32[40,256]{1,0:T(8,128)}, u32[]{:S(2)}) copy-start(f32[40,256]{1,0:T(8,128)} %get-tuple-element.67) | copy-start | bytes 122884
  149.1 6.9 %copy-start.55 = (f32[40,256]{1,0:T(8,128)S(1)}, f32[40,256]{1,0:T(8,128)}, u32[]{:S(2)}) copy-start(f32[40,256]{1,0:T(8,128)} %get-tuple-element.50) | copy-start | bytes 122884
  149.1 6.9 %copy-start.63 = (f32[40,256]{1,0:T(8,128)S(1)}, f32[40,256]{1,0:T(8,128)}, u32[]{:S(2)}) copy-start(f32[40,256]{1,0:T(8,128)} %get-tuple-element.66) | copy-start | bytes 122884
  150.5 6.9 %copy-start.59 = (f32[40,256]{1,0:T(8,128)S(1)}, f32[40,256]{1,0:T(8,128)}, u32[]{:S(2)}) copy-start(f32[40,256]{1,0:T(8,128)} %get-tuple-element.49) | copy-start | bytes 122884
  150.5 6.9 %copy-start.65 = (f32[40,256]{1,0:T(8,128)S(1)}, f32[40,256]{1,0:T(8,128)}, u32[]{:S(2)}) copy-start(f32[40,256]{1,0:T(8,128)} %get-tuple-element.65) | copy-start | bytes 122884
  153.3 14.0 %copy-start.69 = (f32[40,256]{1,0:T(8,128)S(1)}, f32[40,256]{1,0:T(8,128)}, u32[]{:S(2)}) copy-start(f32[40,256]{1,0:T(8,128)} %get-tuple-element.48) | copy-start | bytes 122884
  153.3 14.0 %copy-start.70 = (f32[40,256]{1,0:T(8,128)S(1)}, f32[40,256]{1,0:T(8,128)}, u32[]{:S(2)}) copy-start(f32[40,256]{1,0:T(8,128)} %get-tuple-element.64) | copy-start | bytes 122884
  154.6 35.5 %copy-start.11 = (f32[16,8,256]{2,1,0:T(8,128)S(1)}, f32[16,8,256]{2,1,0:T(8,128)}, u32[]{:S(2)}) copy-start(f32[16,8,256]{2,1,0:T(8,128)} %copy-done.10) | copy-start | bytes 393220
  156.0 35.1 %copy-start.1 = (f32[2,2,8,2,8,256]{5,4,3,2,1,0:T(8,128)S(1)}, f32[2,2,8,2,8,256]{5,4,3,2,1,0:T(8,128)}, u32[]{:S(2)}) copy-start(f32[2,2,8,2,8,256]{5,4,3,2,1,0:T(8,128)} %copy-done) | copy-start | bytes 1572868
  168.7 26.4 %collective-permute-start.8 = (f32[2,2,16,8,256]{4,3,0,1,2:T(8,128)}, f32[2,2,16,8,256]{4,3,0,1,2:T(8,128)}, u32[]{:S(2)}, u32[]{:S(2)}) collective-permute-start(f32[2,2,16,8,256]{4,3,0,1,2:T(8,128)} %get-tuple-element.15), channel_id=1, source_target_pairs={{0,2},{1,3},{2,4},{3,5},{4,6},{5,7},{6,8},{7,9},{8,10},{9,11},{10,... | collective-permute-start | bytes 1572872 | tf_op jit(solution)/shard_map/ppermute | solution.py:35
  172.0 25.6 %collective-permute-start.9 = (f32[2,2,16,8,256]{4,3,0,1,2:T(8,128)}, f32[2,2,16,8,256]{4,3,0,1,2:T(8,128)}, u32[]{:S(2)}, u32[]{:S(2)}) collective-permute-start(f32[2,2,16,8,256]{4,3,0,1,2:T(8,128)} %get-tuple-element.15), channel_id=1, source_target_pairs={{0,1},{1,2},{2,3},{3,4},{4,5},{5,6},{6,7},{7,8},{8,9},{9,10},{10,1... | collective-permute-start | bytes 1572872 | tf_op jit(solution)/shard_map/ppermute | solution.py:35
  191.1 8.6 %copy-start.71 = (f32[2,2,1,8,256]{4,3,0,1,2:T(8,128)S(1)}, f32[2,2,1,8,256]{4,3,0,1,2:T(8,128)}, u32[]{:S(2)}) copy-start(f32[2,2,1,8,256]{4,3,0,1,2:T(8,128)} %get-tuple-element.16) | copy-start | bytes 98308
  192.1 22.4 %copy-start.67 = (f32[2,1,40,256]{3,2,0,1:T(8,128)S(1)}, f32[2,1,40,256]{3,2,0,1:T(8,128)}, u32[]{:S(2)}) copy-start(f32[2,1,40,256]{3,2,0,1:T(8,128)} %get-tuple-element.114) | copy-start | bytes 245764
  192.1 22.4 %copy-start.68 = (f32[2,1,40,256]{3,2,0,1:T(8,128)S(1)}, f32[2,1,40,256]{3,2,0,1:T(8,128)}, u32[]{:S(2)}) copy-start(f32[2,1,40,256]{3,2,0,1:T(8,128)} %get-tuple-element.115) | copy-start | bytes 245764
  192.1 15.4 %collective-permute-start.10 = (f32[2,2,16,8,256]{4,3,0,1,2:T(8,128)}, f32[2,2,16,8,256]{4,3,0,1,2:T(8,128)S(1)}, u32[]{:S(2)}, u32[]{:S(2)}) collective-permute-start(f32[2,2,16,8,256]{4,3,0,1,2:T(8,128)} %get-tuple-element.15), channel_id=1, source_target_pairs={{1,0},{2,1},{3,2},{4,3},{5,4},{6,5},{7,6},{8,7},{9,8},{10,9},{11,1... | collective-permute-start | bytes 1572872 | tf_op jit(solution)/shard_map/ppermute | solution.py:35
  195.0 17.9 %collective-permute-start.11 = (f32[2,2,16,8,256]{4,3,0,1,2:T(8,128)}, f32[2,2,16,8,256]{4,3,0,1,2:T(8,128)S(1)}, u32[]{:S(2)}, u32[]{:S(2)}) collective-permute-start(f32[2,2,16,8,256]{4,3,0,1,2:T(8,128)} %get-tuple-element.15), channel_id=1, source_target_pairs={{2,0},{3,1},{4,2},{5,3},{6,4},{7,5},{8,6},{9,7},{10,8},{11,9},{12,... | collective-permute-start | bytes 1572872 | tf_op jit(solution)/shard_map/ppermute | solution.py:35
  197.6 18.2 %copy-start.60 = (f32[40,256]{1,0:T(8,128)S(1)}, f32[40,256]{1,0:T(8,128)}, u32[]{:S(2)}) copy-start(f32[40,256]{1,0:T(8,128)} %get-tuple-element.49) | copy-start | bytes 122884
  197.6 18.2 %copy-start.66 = (f32[40,256]{1,0:T(8,128)S(1)}, f32[40,256]{1,0:T(8,128)}, u32[]{:S(2)}) copy-start(f32[40,256]{1,0:T(8,128)} %get-tuple-element.65) | copy-start | bytes 122884
  199.5 17.6 %copy-start.56 = (f32[40,256]{1,0:T(8,128)S(1)}, f32[40,256]{1,0:T(8,128)}, u32[]{:S(2)}) copy-start(f32[40,256]{1,0:T(8,128)} %get-tuple-element.50) | copy-start | bytes 122884
  199.6 17.6 %copy-start.64 = (f32[40,256]{1,0:T(8,128)S(1)}, f32[40,256]{1,0:T(8,128)}, u32[]{:S(2)}) copy-start(f32[40,256]{1,0:T(8,128)} %get-tuple-element.66) | copy-start | bytes 122884
  199.7 18.9 %copy-start.52 = (f32[40,256]{1,0:T(8,128)S(1)}, f32[40,256]{1,0:T(8,128)}, u32[]{:S(2)}) copy-start(f32[40,256]{1,0:T(8,128)} %get-tuple-element.51) | copy-start | bytes 122884
  199.7 18.9 %copy-start.62 = (f32[40,256]{1,0:T(8,128)S(1)}, f32[40,256]{1,0:T(8,128)}, u32[]{:S(2)}) copy-start(f32[40,256]{1,0:T(8,128)} %get-tuple-element.67) | copy-start | bytes 122884
  212.9 7.0 %copy-start.48 = (f32[40,256]{1,0:T(8,128)S(1)}, f32[40,256]{1,0:T(8,128)}, u32[]{:S(2)}) copy-start(f32[40,256]{1,0:T(8,128)} %get-tuple-element.52) | copy-start | bytes 122884
  212.9 7.0 %copy-start.58 = (f32[40,256]{1,0:T(8,128)S(1)}, f32[40,256]{1,0:T(8,128)}, u32[]{:S(2)}) copy-start(f32[40,256]{1,0:T(8,128)} %get-tuple-element.68) | copy-start | bytes 122884
  216.9 5.9 %copy-start.50 = (f32[40,256]{1,0:T(8,128)S(1)}, f32[40,256]{1,0:T(8,128)}, u32[]{:S(2)}) copy-start(f32[40,256]{1,0:T(8,128)} %get-tuple-element.70) | copy-start | bytes 122884
  218.2 5.9 %copy-start.37 = (f32[40,256]{1,0:T(8,128)S(1)}, f32[40,256]{1,0:T(8,128)}, u32[]{:S(2)}) copy-start(f32[40,256]{1,0:T(8,128)} %get-tuple-element.55) | copy-start | bytes 122884
  218.3 5.9 %copy-start.46 = (f32[40,256]{1,0:T(8,128)S(1)}, f32[40,256]{1,0:T(8,128)}, u32[]{:S(2)}) copy-start(f32[40,256]{1,0:T(8,128)} %get-tuple-element.71) | copy-start | bytes 122884
  221.0 5.9 %copy-start.30 = (f32[40,256]{1,0:T(8,128)S(1)}, f32[40,256]{1,0:T(8,128)}, u32[]{:S(2)}) copy-start(f32[40,256]{1,0:T(8,128)} %get-tuple-element.57) | copy-start | bytes 122884
  239.4 13.7 %collective-permute-start.12 = (f32[2,2,16,1,256]{4,3,2,1,0:T(1,128)S(1)}, f32[2,2,16,1,256]{4,3,2,1,0:T(1,128)S(1)}, u32[]{:S(2)}, u32[]{:S(2)}) collective-permute-start(f32[2,2,16,1,256]{4,3,2,1,0:T(1,128)S(1)} %copy.328), channel_id=1, source_target_pairs={{0,1},{1,2},{2,3},{3,4},{4,5},{5,6},{6,7},{7,8},{8,9},{9,10},{10,1... | collective-permute-start | bytes 196616 | tf_op jit(solution)/shard_map/ppermute | solution.py:26
  249.8 7.1 %collective-permute-start.13 = (f32[2,2,16,1,256]{4,3,2,1,0:T(1,128)S(1)}, f32[2,2,16,1,256]{4,3,2,1,0:T(1,128)S(1)}, u32[]{:S(2)}, u32[]{:S(2)}) collective-permute-start(f32[2,2,16,1,256]{4,3,2,1,0:T(1,128)S(1)} %copy.329), channel_id=1, source_target_pairs={{1,0},{2,1},{3,2},{4,3},{5,4},{6,5},{7,6},{8,7},{9,8},{10,9},{11,1... | collective-permute-start | bytes 196616 | tf_op jit(solution)/shard_map/ppermute | solution.py:27
  262.5 32.1 %copy-start.9 = (f32[16,2,2,8,256]{4,3,2,1,0:T(8,128)S(1)}, f32[16,2,2,8,256]{4,3,2,1,0:T(8,128)}, u32[]{:S(2)}) copy-start(f32[16,2,2,8,256]{4,3,2,1,0:T(8,128)} %param.9) | copy-start | bytes 1572868
  291.1 12.3 %all-to-all-start.2 = ((f32[2,2,16,8,256]{4,3,1,0,2:T(8,128)}), f32[2,2,16,8,256]{4,3,1,0,2:T(8,128)S(1)}, u32[]{:S(2)}, u32[]{:S(2)}) async-start(f32[2,2,16,8,256]{4,3,1,0,2:T(8,128)} %copy.301), calls=%async_computation.2 | async-start | bytes 1048576 | tf_op jit(solution)/shard_map/all_to_all | solution.py:352
  (28 other events, 127.6 us)

commit v6 on v4

--- a/solution.py
+++ b/solution.py
@@ -84,7 +84,7 @@
     depth_count = lax.axis_size("depth")
     tile_count = lax.axis_size("tile")
     size = values.size
-    block = 8 * 128
+    block = 128
     padded = -(-size // block) * block
     flat = jnp.pad(values.reshape(-1), (0, padded - size)).reshape(padded // 128, 128)
     summed = pl.pallas_call(

time: 292 us -> 290 us (level)
  no operation moved by 1% of the time
where the time goes in v6:
time: 290 us; the launch traced here: 287 us
  starting transfers between devices  125 us (43%)
  other arithmetic  63.4 us (22%)
  waiting for transfers between devices  48 us (17%)
  local copies, waits for them, and re-layouts  21.4 us (7%)
  Pallas kernels  18.3 us (6%)
  matrix products  9.14 us (3%)
    ppermute x12, starting transfers between devices, shifted(): lax.ppermute(value, axis, [(source, source + steps) for source in range(l...  42.5 us
    ppermute x6, starting transfers between devices, extended(): before = lax.ppermute(last, axis, up)  34.1 us
    ppermute x6, starting transfers between devices, extended(): after = lax.ppermute(leading, axis, down)  32.8 us
    ppermute x12, waiting for transfers between devices, shifted(): lax.ppermute(value, axis, [(source, source + steps) for source in range(l...  19.4 us
    pallas_call x1, Pallas kernels, all_sum(): pl.pallas_call(functools.partial(all_sum_kernel, depth_count, tile_count)...  18.3 us
    add x16, other arithmetic, per_device(): source_term = residual_ext[:, :, layer_no] + couple(previous)  18.1 us
    select_n x15, other arithmetic, per_device(): jnp.where(row_valid, downward_ext[:, :, layer_no] + complex_scale(inv_re[...  15 us
    ppermute x6, waiting for transfers between devices, extended(): after = lax.ppermute(leading, axis, down)  13.8 us
  transfers between devices with their start and end apart: 27, of which 7 were waited for; matrix products, arithmetic and copies ran while one was open for 28% of the time, Pallas kernels for 0%

profile of v6, /device:TPU:1, one launch (start us, length us, event | category | flops | bytes accessed | tf_op | source)
XLA Modules:
  0.0 287.4 jit_solution(17911136906720729927)
XLA Ops:
  0.6 1.1 fusion.739
  1.8 3.9 %collective-permute-start.4 = (f32[16,2,1,8,256]{4,3,2,0,1:T(8,128)S(1)}, f32[16,2,1,8,256]{4,3,2,0,1:T(8,128)S(1)}, u32[]{:S(2)}, u32[]{:S(2)}) collective-permute-start(f32[16,2,1,8,256]{4,3,2,0,1:T(8,128)S(1)} %get-tuple-element.79), channel_id=1, source_target_pairs={{0,32},{32,64},{64,96},{96,128},{128,160},{160,192},{192,224},{1,3... | collective-permute-start | bytes 786440 | tf_op jit(solution)/shard_map/ppermute | solution.py:26
  5.7 1.3 collective-permute-start.5
  7.8 5.2 %collective-permute-start.8 = (f32[2,1,256]{2,1,0:T(1,128)S(1)}, f32[2,1,256]{2,1,0:T(1,128)S(1)}, u32[]{:S(2)}, u32[]{:S(2)}) collective-permute-start(f32[2,1,256]{2,1,0:T(1,128)S(1)} %get-tuple-element.153), channel_id=1, source_target_pairs={{0,1},{1,2},{2,3},{3,4},{4,5},{5,6},{6,7},{7,8},{8,9},{9,10},{10,1... | collective-permute-start | bytes 6152 | tf_op jit(solution)/shard_map/ppermute | solution.py:26
  13.0 1.9 collective-permute-start.9
  15.0 1.4 broadcast_in_dim.194
  16.4 6.5 %all-to-all-start = ((f32[8,2,8,256]{3,2,1,0:T(8,128)}), f32[8,2,8,256]{3,2,1,0:T(8,128)S(1)}, u32[]{:S(2)}, u32[]{:S(2)}) async-start(f32[8,2,8,256]{3,2,1,0:T(8,128)} %broadcast_in_dim.194), calls=%async_computation | async-start | bytes 262144 | tf_op jit(solution)/shard_map/all_to_all | solution.py:245
  22.9 1.3 fusion.737
  24.2 5.4 %collective-permute-start.22 = (f32[16,2,2,1,256]{4,3,2,0,1:T(1,128)S(1)}, f32[16,2,2,1,256]{4,3,2,0,1:T(1,128)S(1)}, u32[]{:S(2)}, u32[]{:S(2)}) collective-permute-start(f32[16,2,2,1,256]{4,3,2,0,1:T(1,128)S(1)} %get-tuple-element.74), channel_id=1, source_target_pairs={{0,1},{1,2},{2,3},{3,4},{4,5},{5,6},{6,7},{7,8},{8,9},{9,10},{10,1... | collective-permute-start | bytes 196616 | tf_op jit(solution)/shard_map/ppermute | solution.py:26
  30.9 1.3 multiply_add_fusion.35
  32.2 1.3 multiply_add_fusion.37
  33.7 1.2 multiply_add_fusion.34
  34.9 1.2 multiply_add_fusion.36
  37.1 1.1 copy.111
  38.3 4.4 %collective-permute-start = (f32[16,8,256]{2,1,0:T(8,128)S(1)}, f32[16,8,256]{2,1,0:T(8,128)S(1)}, u32[]{:S(2)}, u32[]{:S(2)}) collective-permute-start(f32[16,8,256]{2,1,0:T(8,128)S(1)} %bitcast.566), channel_id=1, source_target_pairs={{0,2},{1,3},{2,4},{3,5},{4,6},{5,7},{6,8},{7,9},{8,10},{9,11},{10,... | collective-permute-start | bytes 393224 | tf_op jit(solution)/shard_map/ppermute | solution.py:35
  43.0 2.2 collective-permute-start.6
  45.2 2.1 collective-permute-start.7
  47.4 4.9 %collective-permute-start.1 = (f32[16,8,256]{2,1,0:T(8,128)S(1)}, f32[16,8,256]{2,1,0:T(8,128)S(1)}, u32[]{:S(2)}, u32[]{:S(2)}) collective-permute-start(f32[16,8,256]{2,1,0:T(8,128)S(1)} %bitcast.567), channel_id=1, source_target_pairs={{0,1},{1,2},{2,3},{3,4},{4,5},{5,6},{6,7},{7,8},{8,9},{9,10},{10,1... | collective-permute-start | bytes 393224 | tf_op jit(solution)/shard_map/ppermute | solution.py:35
  52.4 1.9 collective-permute-start.2
  54.3 1.3 collective-permute-start.3
  57.1 2.7 fusion.71
  60.8 5.4 %all-to-all-start.1 = ((f32[16,2,2,8,256]{4,3,2,1,0:T(8,128)}), f32[16,2,2,8,256]{4,3,2,1,0:T(8,128)S(1)}, u32[]{:S(2)}, u32[]{:S(2)}) async-start(f32[16,2,2,8,256]{4,3,2,1,0:T(8,128)} %copy_subtract_fusion), calls=%async_computation.1 | async-start | bytes 1048576 | tf_op jit(solution)/shard_map/all_to_all | solution.py:265
  66.3 7.8 %all-to-all-done.1 = f32[16,2,2,8,256]{4,3,2,1,0:T(8,128)S(1)} async-done(((f32[16,2,2,8,256]{4,3,2,1,0:T(8,128)}), f32[16,2,2,8,256]{4,3,2,1,0:T(8,128)S(1)}, u32[]{:S(2)}, u32[]{:S(2)}) %all-to-all-start.1) | async-done | bytes 524320 | tf_op jit(solution)/shard_map/all_to_all | solution.py:265
  74.2 7.4 %collective-permute-start.10 = (f32[2,2,16,8,256]{4,3,2,1,0:T(8,128)S(1)}, f32[2,2,16,8,256]{4,3,2,1,0:T(8,128)S(1)}, u32[]{:S(2)}, u32[]{:S(2)}) collective-permute-start(f32[2,2,16,8,256]{4,3,2,1,0:T(8,128)S(1)} %bitcast.559), channel_id=1, source_target_pairs={{0,2},{1,3},{2,4},{3,5},{4,6},{5,7},{6,8},{7,9},{8,10},{9,11},{10,... | collective-permute-start | bytes 1572872 | tf_op jit(solution)/shard_map/ppermute | solution.py:35
  82.0 6.2 %collective-permute-start.11 = (f32[2,2,16,8,256]{4,3,2,1,0:T(8,128)S(1)}, f32[2,2,16,8,256]{4,3,2,1,0:T(8,128)S(1)}, u32[]{:S(2)}, u32[]{:S(2)}) collective-permute-start(f32[2,2,16,8,256]{4,3,2,1,0:T(8,128)S(1)} %bitcast.560), channel_id=1, source_target_pairs={{0,1},{1,2},{2,3},{3,4},{4,5},{5,6},{6,7},{7,8},{8,9},{9,10},{10,1... | collective-permute-start | bytes 1572872 | tf_op jit(solution)/shard_map/ppermute | solution.py:35
  88.3 1.9 collective-permute-start.12
  90.2 1.3 collective-permute-start.13
  91.6 24.0 %collective-permute-start.23 = (f32[16,2,2,1,256]{4,3,2,0,1:T(1,128)S(1)}, f32[16,2,2,1,256]{4,3,2,0,1:T(1,128)S(1)}, u32[]{:S(2)}, u32[]{:S(2)}) collective-permute-start(f32[16,2,2,1,256]{4,3,2,0,1:T(1,128)S(1)} %get-tuple-element.75), channel_id=1, source_target_pairs={{1,0},{2,1},{3,2},{4,3},{5,4},{6,5},{7,6},{8,7},{9,8},{10,9},{11,1... | collective-permute-start | bytes 196616 | tf_op jit(solution)/shard_map/ppermute | solution.py:27
  118.2 1.2 fusion.197
  119.6 1.2 fusion.214
  120.9 1.2 fusion.231
  122.3 1.2 fusion.248
  123.7 1.2 fusion.265
  125.0 1.2 fusion.282
  126.4 1.2 fusion.299
  127.8 1.2 fusion.316
  129.1 1.2 fusion.333
  130.5 1.2 fusion.350
  131.9 1.2 fusion.367
  133.3 1.2 fusion.384
  134.6 1.2 fusion.401
  136.0 1.2 fusion.418
  137.5 4.8 %collective-permute-start.14 = (f32[2,2,16,8,256]{4,3,1,0,2:T(8,128)S(1)}, f32[2,2,16,8,256]{4,3,1,0,2:T(8,128)S(1)}, u32[]{:S(2)}, u32[]{:S(2)}) collective-permute-start(f32[2,2,16,8,256]{4,3,1,0,2:T(8,128)S(1)} %get-tuple-element.24), channel_id=1, source_target_pairs={{0,2},{1,3},{2,4},{3,5},{4,6},{5,7},{6,8},{7,9},{8,10},{9,11},{10,... | collective-permute-start | bytes 1572872 | tf_op jit(solution)/shard_map/ppermute | solution.py:35
  142.4 4.8 %collective-permute-start.15 = (f32[2,2,16,8,256]{4,3,1,0,2:T(8,128)S(1)}, f32[2,2,16,8,256]{4,3,1,0,2:T(8,128)S(1)}, u32[]{:S(2)}, u32[]{:S(2)}) collective-permute-start(f32[2,2,16,8,256]{4,3,1,0,2:T(8,128)S(1)} %get-tuple-element.24), channel_id=1, source_target_pairs={{0,1},{1,2},{2,3},{3,4},{4,5},{5,6},{6,7},{7,8},{8,9},{9,10},{10,1... | collective-permute-start | bytes 1572872 | tf_op jit(solution)/shard_map/ppermute | solution.py:35
  147.3 1.6 iota_compare_fusion
  149.0 1.9 collective-permute-start.16
  150.9 1.5 collective-permute-done.14
  152.3 1.5 collective-permute-start.17
  153.9 17.0 %collective-permute-done.15 = f32[2,2,16,8,256]{4,3,1,0,2:T(8,128)S(1)} collective-permute-done((f32[2,2,16,8,256]{4,3,1,0,2:T(8,128)S(1)}, f32[2,2,16,8,256]{4,3,1,0,2:T(8,128)S(1)}, u32[]{:S(2)}, u32[]{:S(2)}) %collective-permute-start.15) | collective-permute-done | bytes 524320 | tf_op jit(solution)/shard_map/ppermute | solution.py:35
  171.3 1.4 copy-done.1
  175.4 1.0 fusion.686
  190.4 1.1 fusion.708
  203.0 3.5 %all-to-all-start.2 = ((f32[2,2,16,8,256]{4,3,1,0,2:T(8,128)}), f32[2,2,16,8,256]{4,3,1,0,2:T(8,128)S(1)}, u32[]{:S(2)}, u32[]{:S(2)}) async-start(f32[2,2,16,8,256]{4,3,1,0,2:T(8,128)} %constant_dynamic-update-slice_fusion.49), calls=%async_computation.2 | async-start | bytes 1048576 | tf_op jit(solution)/shard_map/all_to_all | solution.py:288
  207.0 7.0 %all-to-all-done.2 = f32[2,2,16,8,256]{4,3,1,0,2:T(8,128)S(1)} async-done(((f32[2,2,16,8,256]{4,3,1,0,2:T(8,128)}), f32[2,2,16,8,256]{4,3,1,0,2:T(8,128)S(1)}, u32[]{:S(2)}, u32[]{:S(2)}) %all-to-all-start.2) | async-done | bytes 524320 | tf_op jit(solution)/shard_map/all_to_all | solution.py:288
  214.1 2.5 collective-permute-start.18
  216.6 9.1 %fusion = f32[16,4,256]{2,1,0:T(4,128)S(1)} fusion(pred[16,256,256]{1,2,0:T(8,128)(4,1)} %iota_compare_fusion, f32[16,2,16,256]{3,2,1,0:T(8,128)S(1)} %bitcast.553, f32[16,2,16,256]{3,2,1,0:T(8,128)S(1)} %bitcast.558, s32[16,256]{1,0:T(8,128)S(1)} %get-tuple-element.22), kind=kOutput, calls=%fused_computation.1 | convolution fusion | flops 814006272 | bytes 2179072 | tf_op jit(solution)/shard_map/srk,sqky->sqry/dot_general | solution.py:318
  225.8 1.3 collective-permute-start.19
  227.2 8.5 %collective-permute-done.19 = f32[16,2,1,8,256]{4,3,2,0,1:T(8,128)S(1)} collective-permute-done((f32[16,2,1,8,256]{4,3,2,0,1:T(8,128)S(1)}, f32[16,2,1,8,256]{4,3,2,0,1:T(8,128)S(1)}, u32[]{:S(2)}, u32[]{:S(2)}) %collective-permute-start.19) | collective-permute-done | bytes 262176 | tf_op jit(solution)/shard_map/ppermute | solution.py:27
  235.9 14.9 %collective-permute-start.20 = (f32[16,2,4,1,256]{4,3,2,0,1:T(1,128)S(1)}, f32[16,2,4,1,256]{4,3,2,0,1:T(1,128)S(1)}, u32[]{:S(2)}, u32[]{:S(2)}) collective-permute-start(f32[16,2,4,1,256]{4,3,2,0,1:T(1,128)S(1)} %get-tuple-element.36), channel_id=1, source_target_pairs={{0,1},{1,2},{2,3},{3,4},{4,5},{5,6},{6,7},{7,8},{8,9},{9,10},{10,1... | collective-permute-start | bytes 393224 | tf_op jit(solution)/shard_map/ppermute | solution.py:26
  250.8 2.2 collective-permute-start.21
  253.3 5.3 %collective-permute-done.21 = f32[16,2,4,1,256]{4,3,2,0,1:T(1,128)S(1)} collective-permute-done((f32[16,2,4,1,256]{4,3,2,0,1:T(1,128)S(1)}, f32[16,2,4,1,256]{4,3,2,0,1:T(1,128)S(1)}, u32[]{:S(2)}, u32[]{:S(2)}) %collective-permute-start.21) | collective-permute-done | bytes 131104 | tf_op jit(solution)/shard_map/ppermute | solution.py:27
  260.0 2.7 fusion.114
  262.9 1.3 subtract_reduce_fusion
  265.0 18.3 %shard_map.94 = f32[1,128]{1,0:T(1,128)} custom-call(f32[1,128]{1,0:T(1,128)} %pad_bitcast_fusion.x_ref), custom_call_target="tpu_custom_call" | custom-call | tf_op jit(solution)/shard_map/pallas_call | solution.py:90
  (233 shorter events, 46.5 us)
Async XLA Ops:
  0.6 42.1 %copy-start = (f32[16,2,2,8,256]{4,3,2,1,0:T(8,128)S(1)}, f32[16,2,2,8,256]{4,3,2,1,0:T(8,128)}, u32[]{:S(2)}) copy-start(f32[16,2,2,8,256]{4,3,2,1,0:T(8,128)} %param.7) | copy-start | bytes 1572868
  1.8 45.6 %copy-start.4 = (f32[2,8,256]{2,1,0:T(8,128)S(1)}, f32[2,8,256]{2,1,0:T(8,128)}, u32[]{:S(2)}) copy-start(f32[2,8,256]{2,1,0:T(8,128)} %param.8) | copy-start | bytes 49156
  1.8 36.5 %collective-permute-start.4 = (f32[16,2,1,8,256]{4,3,2,0,1:T(8,128)S(1)}, f32[16,2,1,8,256]{4,3,2,0,1:T(8,128)S(1)}, u32[]{:S(2)}, u32[]{:S(2)}) collective-permute-start(f32[16,2,1,8,256]{4,3,2,0,1:T(8,128)S(1)} %get-tuple-element.79), channel_id=1, source_target_pairs={{0,32},{32,64},{64,96},{96,128},{128,160},{160,192},{192,224},{1,3... | collective-permute-start | bytes 786440 | tf_op jit(solution)/shard_map/ppermute | solution.py:26
  5.7 37.1 %collective-permute-start.5 = (f32[16,2,1,8,256]{4,3,2,0,1:T(8,128)S(1)}, f32[16,2,1,8,256]{4,3,2,0,1:T(8,128)S(1)}, u32[]{:S(2)}, u32[]{:S(2)}) collective-permute-start(f32[16,2,1,8,256]{4,3,2,0,1:T(8,128)S(1)} %get-tuple-element.78), channel_id=1, source_target_pairs={{32,0},{64,32},{96,64},{128,96},{160,128},{192,160},{224,192},{33,... | collective-permute-start | bytes 786440 | tf_op jit(solution)/shard_map/ppermute | solution.py:27
  7.8 37.4 %collective-permute-start.8 = (f32[2,1,256]{2,1,0:T(1,128)S(1)}, f32[2,1,256]{2,1,0:T(1,128)S(1)}, u32[]{:S(2)}, u32[]{:S(2)}) collective-permute-start(f32[2,1,256]{2,1,0:T(1,128)S(1)} %get-tuple-element.153), channel_id=1, source_target_pairs={{0,1},{1,2},{2,3},{3,4},{4,5},{5,6},{6,7},{7,8},{8,9},{9,10},{10,1... | collective-permute-start | bytes 6152 | tf_op jit(solution)/shard_map/ppermute | solution.py:26
  13.0 34.3 %collective-permute-start.9 = (f32[2,1,256]{2,1,0:T(1,128)S(1)}, f32[2,1,256]{2,1,0:T(1,128)S(1)}, u32[]{:S(2)}, u32[]{:S(2)}) collective-permute-start(f32[2,1,256]{2,1,0:T(1,128)S(1)} %get-tuple-element.154), channel_id=1, source_target_pairs={{1,0},{2,1},{3,2},{4,3},{5,4},{6,5},{7,6},{8,7},{9,8},{10,9},{11,1... | collective-permute-start | bytes 6152 | tf_op jit(solution)/shard_map/ppermute | solution.py:27
  16.4 22.0 %all-to-all-start = ((f32[8,2,8,256]{3,2,1,0:T(8,128)}), f32[8,2,8,256]{3,2,1,0:T(8,128)S(1)}, u32[]{:S(2)}, u32[]{:S(2)}) async-start(f32[8,2,8,256]{3,2,1,0:T(8,128)} %broadcast_in_dim.194), calls=%async_computation | async-start | bytes 262144 | tf_op jit(solution)/shard_map/all_to_all | solution.py:245
  24.2 182.3 %collective-permute-start.22 = (f32[16,2,2,1,256]{4,3,2,0,1:T(1,128)S(1)}, f32[16,2,2,1,256]{4,3,2,0,1:T(1,128)S(1)}, u32[]{:S(2)}, u32[]{:S(2)}) collective-permute-start(f32[16,2,2,1,256]{4,3,2,0,1:T(1,128)S(1)} %get-tuple-element.74), channel_id=1, source_target_pairs={{0,1},{1,2},{2,3},{3,4},{4,5},{5,6},{6,7},{7,8},{8,9},{9,10},{10,1... | collective-permute-start | bytes 196616 | tf_op jit(solution)/shard_map/ppermute | solution.py:26
  38.3 14.1 %collective-permute-start = (f32[16,8,256]{2,1,0:T(8,128)S(1)}, f32[16,8,256]{2,1,0:T(8,128)S(1)}, u32[]{:S(2)}, u32[]{:S(2)}) collective-permute-start(f32[16,8,256]{2,1,0:T(8,128)S(1)} %bitcast.566), channel_id=1, source_target_pairs={{0,2},{1,3},{2,4},{3,5},{4,6},{5,7},{6,8},{7,9},{8,10},{9,11},{10,... | collective-permute-start | bytes 393224 | tf_op jit(solution)/shard_map/ppermute | solution.py:35
  43.0 11.3 %collective-permute-start.6 = (f32[16,2,4,1,256]{4,3,2,0,1:T(1,128)S(1)}, f32[16,2,4,1,256]{4,3,2,0,1:T(1,128)S(1)}, u32[]{:S(2)}, u32[]{:S(2)}) collective-permute-start(f32[16,2,4,1,256]{4,3,2,0,1:T(1,128)S(1)} %get-tuple-element.38), channel_id=1, source_target_pairs={{0,1},{1,2},{2,3},{3,4},{4,5},{5,6},{6,7},{7,8},{8,9},{9,10},{10,1... | collective-permute-start | bytes 393224 | tf_op jit(solution)/shard_map/ppermute | solution.py:26
  45.2 10.4 %collective-permute-start.7 = (f32[16,2,4,1,256]{4,3,2,0,1:T(1,128)S(1)}, f32[16,2,4,1,256]{4,3,2,0,1:T(1,128)S(1)}, u32[]{:S(2)}, u32[]{:S(2)}) collective-permute-start(f32[16,2,4,1,256]{4,3,2,0,1:T(1,128)S(1)} %get-tuple-element.39), channel_id=1, source_target_pairs={{1,0},{2,1},{3,2},{4,3},{5,4},{6,5},{7,6},{8,7},{9,8},{10,9},{11,1... | collective-permute-start | bytes 393224 | tf_op jit(solution)/shard_map/ppermute | solution.py:27
  47.4 18.8 %collective-permute-start.1 = (f32[16,8,256]{2,1,0:T(8,128)S(1)}, f32[16,8,256]{2,1,0:T(8,128)S(1)}, u32[]{:S(2)}, u32[]{:S(2)}) collective-permute-start(f32[16,8,256]{2,1,0:T(8,128)S(1)} %bitcast.567), channel_id=1, source_target_pairs={{0,1},{1,2},{2,3},{3,4},{4,5},{5,6},{6,7},{7,8},{8,9},{9,10},{10,1... | collective-permute-start | bytes 393224 | tf_op jit(solution)/shard_map/ppermute | solution.py:35
  52.4 13.9 %collective-permute-start.2 = (f32[16,8,256]{2,1,0:T(8,128)S(1)}, f32[16,8,256]{2,1,0:T(8,128)S(1)}, u32[]{:S(2)}, u32[]{:S(2)}) collective-permute-start(f32[16,8,256]{2,1,0:T(8,128)S(1)} %bitcast.568), channel_id=1, source_target_pairs={{1,0},{2,1},{3,2},{4,3},{5,4},{6,5},{7,6},{8,7},{9,8},{10,9},{11,1... | collective-permute-start | bytes 393224 | tf_op jit(solution)/shard_map/ppermute | solution.py:35
  54.3 12.0 %collective-permute-start.3 = (f32[16,8,256]{2,1,0:T(8,128)S(1)}, f32[16,8,256]{2,1,0:T(8,128)S(1)}, u32[]{:S(2)}, u32[]{:S(2)}) collective-permute-start(f32[16,8,256]{2,1,0:T(8,128)S(1)} %bitcast.569), channel_id=1, source_target_pairs={{2,0},{3,1},{4,2},{5,3},{6,4},{7,5},{8,6},{9,7},{10,8},{11,9},{12,... | collective-permute-start | bytes 393224 | tf_op jit(solution)/shard_map/ppermute | solution.py:35
  60.8 13.4 %all-to-all-start.1 = ((f32[16,2,2,8,256]{4,3,2,1,0:T(8,128)}), f32[16,2,2,8,256]{4,3,2,1,0:T(8,128)S(1)}, u32[]{:S(2)}, u32[]{:S(2)}) async-start(f32[16,2,2,8,256]{4,3,2,1,0:T(8,128)} %copy_subtract_fusion), calls=%async_computation.1 | async-start | bytes 1048576 | tf_op jit(solution)/shard_map/all_to_all | solution.py:265
  74.2 17.4 %collective-permute-start.10 = (f32[2,2,16,8,256]{4,3,2,1,0:T(8,128)S(1)}, f32[2,2,16,8,256]{4,3,2,1,0:T(8,128)S(1)}, u32[]{:S(2)}, u32[]{:S(2)}) collective-permute-start(f32[2,2,16,8,256]{4,3,2,1,0:T(8,128)S(1)} %bitcast.559), channel_id=1, source_target_pairs={{0,2},{1,3},{2,4},{3,5},{4,6},{5,7},{6,8},{7,9},{8,10},{9,11},{10,... | collective-permute-start | bytes 1572872 | tf_op jit(solution)/shard_map/ppermute | solution.py:35
  82.0 34.5 %collective-permute-start.11 = (f32[2,2,16,8,256]{4,3,2,1,0:T(8,128)S(1)}, f32[2,2,16,8,256]{4,3,2,1,0:T(8,128)S(1)}, u32[]{:S(2)}, u32[]{:S(2)}) collective-permute-start(f32[2,2,16,8,256]{4,3,2,1,0:T(8,128)S(1)} %bitcast.560), channel_id=1, source_target_pairs={{0,1},{1,2},{2,3},{3,4},{4,5},{5,6},{6,7},{7,8},{8,9},{9,10},{10,1... | collective-permute-start | bytes 1572872 | tf_op jit(solution)/shard_map/ppermute | solution.py:35
  88.3 28.3 %collective-permute-start.12 = (f32[2,2,16,8,256]{4,3,2,1,0:T(8,128)S(1)}, f32[2,2,16,8,256]{4,3,2,1,0:T(8,128)S(1)}, u32[]{:S(2)}, u32[]{:S(2)}) collective-permute-start(f32[2,2,16,8,256]{4,3,2,1,0:T(8,128)S(1)} %bitcast.561), channel_id=1, source_target_pairs={{1,0},{2,1},{3,2},{4,3},{5,4},{6,5},{7,6},{8,7},{9,8},{10,9},{11,1... | collective-permute-start | bytes 1572872 | tf_op jit(solution)/shard_map/ppermute | solution.py:35
  90.2 26.5 %collective-permute-start.13 = (f32[2,2,16,8,256]{4,3,2,1,0:T(8,128)S(1)}, f32[2,2,16,8,256]{4,3,2,1,0:T(8,128)S(1)}, u32[]{:S(2)}, u32[]{:S(2)}) collective-permute-start(f32[2,2,16,8,256]{4,3,2,1,0:T(8,128)S(1)} %bitcast.562), channel_id=1, source_target_pairs={{2,0},{3,1},{4,2},{5,3},{6,4},{7,5},{8,6},{9,7},{10,8},{11,9},{12,... | collective-permute-start | bytes 1572872 | tf_op jit(solution)/shard_map/ppermute | solution.py:35
  91.6 115.0 %collective-permute-start.23 = (f32[16,2,2,1,256]{4,3,2,0,1:T(1,128)S(1)}, f32[16,2,2,1,256]{4,3,2,0,1:T(1,128)S(1)}, u32[]{:S(2)}, u32[]{:S(2)}) collective-permute-start(f32[16,2,2,1,256]{4,3,2,0,1:T(1,128)S(1)} %get-tuple-element.75), channel_id=1, source_target_pairs={{1,0},{2,1},{3,2},{4,3},{5,4},{6,5},{7,6},{8,7},{9,8},{10,9},{11,1... | collective-permute-start | bytes 196616 | tf_op jit(solution)/shard_map/ppermute | solution.py:27
  116.7 1.5 copy-start.2
  133.2 9.2 %copy-start.6 = (s32[16,256]{1,0:T(8,128)S(1)}, s32[16,256]{1,0:T(8,128)}, u32[]{:S(2)}) copy-start(s32[16,256]{1,0:T(8,128)} %param.12) | copy-start | bytes 49156
  137.5 14.8 %collective-permute-start.14 = (f32[2,2,16,8,256]{4,3,1,0,2:T(8,128)S(1)}, f32[2,2,16,8,256]{4,3,1,0,2:T(8,128)S(1)}, u32[]{:S(2)}, u32[]{:S(2)}) collective-permute-start(f32[2,2,16,8,256]{4,3,1,0,2:T(8,128)S(1)} %get-tuple-element.24), channel_id=1, source_target_pairs={{0,2},{1,3},{2,4},{3,5},{4,6},{5,7},{6,8},{7,9},{8,10},{9,11},{10,... | collective-permute-start | bytes 1572872 | tf_op jit(solution)/shard_map/ppermute | solution.py:35
  142.4 28.5 %collective-permute-start.15 = (f32[2,2,16,8,256]{4,3,1,0,2:T(8,128)S(1)}, f32[2,2,16,8,256]{4,3,1,0,2:T(8,128)S(1)}, u32[]{:S(2)}, u32[]{:S(2)}) collective-permute-start(f32[2,2,16,8,256]{4,3,1,0,2:T(8,128)S(1)} %get-tuple-element.24), channel_id=1, source_target_pairs={{0,1},{1,2},{2,3},{3,4},{4,5},{5,6},{6,7},{7,8},{8,9},{9,10},{10,1... | collective-permute-start | bytes 1572872 | tf_op jit(solution)/shard_map/ppermute | solution.py:35
  149.0 22.2 %collective-permute-start.16 = (f32[2,2,16,8,256]{4,3,1,0,2:T(8,128)S(1)}, f32[2,2,16,8,256]{4,3,1,0,2:T(8,128)S(1)}, u32[]{:S(2)}, u32[]{:S(2)}) collective-permute-start(f32[2,2,16,8,256]{4,3,1,0,2:T(8,128)S(1)} %get-tuple-element.24), channel_id=1, source_target_pairs={{1,0},{2,1},{3,2},{4,3},{5,4},{6,5},{7,6},{8,7},{9,8},{10,9},{11,1... | collective-permute-start | bytes 1572872 | tf_op jit(solution)/shard_map/ppermute | solution.py:35
  152.3 18.9 %collective-permute-start.17 = (f32[2,2,16,8,256]{4,3,1,0,2:T(8,128)S(1)}, f32[2,2,16,8,256]{4,3,1,0,2:T(8,128)S(1)}, u32[]{:S(2)}, u32[]{:S(2)}) collective-permute-start(f32[2,2,16,8,256]{4,3,1,0,2:T(8,128)S(1)} %get-tuple-element.24), channel_id=1, source_target_pairs={{2,0},{3,1},{4,2},{5,3},{6,4},{7,5},{8,6},{9,7},{10,8},{11,9},{12,... | collective-permute-start | bytes 1572872 | tf_op jit(solution)/shard_map/ppermute | solution.py:35
  171.3 1.5 copy-start.1
  190.4 16.2 %copy-start.3 = (f32[16,2,2,8,256]{4,3,2,1,0:T(8,128)S(1)}, f32[16,2,2,8,256]{4,3,2,1,0:T(8,128)}, u32[]{:S(2)}) copy-start(f32[16,2,2,8,256]{4,3,2,1,0:T(8,128)} %param.9) | copy-start | bytes 1572868
  203.0 11.0 %all-to-all-start.2 = ((f32[2,2,16,8,256]{4,3,1,0,2:T(8,128)}), f32[2,2,16,8,256]{4,3,1,0,2:T(8,128)S(1)}, u32[]{:S(2)}, u32[]{:S(2)}) async-start(f32[2,2,16,8,256]{4,3,1,0,2:T(8,128)} %constant_dynamic-update-slice_fusion.49), calls=%async_computation.2 | async-start | bytes 1048576 | tf_op jit(solution)/shard_map/all_to_all | solution.py:288
  214.1 13.0 %collective-permute-start.18 = (f32[16,2,1,8,256]{4,3,2,0,1:T(8,128)S(1)}, f32[16,2,1,8,256]{4,3,2,0,1:T(8,128)S(1)}, u32[]{:S(2)}, u32[]{:S(2)}) collective-permute-start(f32[16,2,1,8,256]{4,3,2,0,1:T(8,128)S(1)} %get-tuple-element.77), channel_id=1, source_target_pairs={{0,32},{32,64},{64,96},{96,128},{128,160},{160,192},{192,224},{1,3... | collective-permute-start | bytes 786440 | tf_op jit(solution)/shard_map/ppermute | solution.py:26
  225.8 27.3 %copy-start.5 = (f32[16,2,256]{2,1,0:T(2,128)S(1)}, f32[16,2,256]{2,1,0:T(2,128)}, u32[]{:S(2)}) copy-start(f32[16,2,256]{2,1,0:T(2,128)} %param.10) | copy-start | bytes 98308
  225.8 9.9 %collective-permute-start.19 = (f32[16,2,1,8,256]{4,3,2,0,1:T(8,128)S(1)}, f32[16,2,1,8,256]{4,3,2,0,1:T(8,128)S(1)}, u32[]{:S(2)}, u32[]{:S(2)}) collective-permute-start(f32[16,2,1,8,256]{4,3,2,0,1:T(8,128)S(1)} %get-tuple-element.76), channel_id=1, source_target_pairs={{32,0},{64,32},{96,64},{128,96},{160,128},{192,160},{224,192},{33,... | collective-permute-start | bytes 786440 | tf_op jit(solution)/shard_map/ppermute | solution.py:27
  235.9 17.4 %collective-permute-start.20 = (f32[16,2,4,1,256]{4,3,2,0,1:T(1,128)S(1)}, f32[16,2,4,1,256]{4,3,2,0,1:T(1,128)S(1)}, u32[]{:S(2)}, u32[]{:S(2)}) collective-permute-start(f32[16,2,4,1,256]{4,3,2,0,1:T(1,128)S(1)} %get-tuple-element.36), channel_id=1, source_target_pairs={{0,1},{1,2},{2,3},{3,4},{4,5},{5,6},{6,7},{7,8},{8,9},{9,10},{10,1... | collective-permute-start | bytes 393224 | tf_op jit(solution)/shard_map/ppermute | solution.py:26
  250.8 7.8 %collective-permute-start.21 = (f32[16,2,4,1,256]{4,3,2,0,1:T(1,128)S(1)}, f32[16,2,4,1,256]{4,3,2,0,1:T(1,128)S(1)}, u32[]{:S(2)}, u32[]{:S(2)}) collective-permute-start(f32[16,2,4,1,256]{4,3,2,0,1:T(1,128)S(1)} %get-tuple-element.37), channel_id=1, source_target_pairs={{1,0},{2,1},{3,2},{4,3},{5,4},{6,5},{7,6},{8,7},{9,8},{10,9},{11,1... | collective-permute-start | bytes 393224 | tf_op jit(solution)/shard_map/ppermute | solution.py:27

commit v7 on v6

--- a/solution.py
+++ b/solution.py
@@ -271,9 +271,12 @@
         previous = jnp.where(
             row_valid, complex_scale(inv_re[layer_no], inv_im[layer_no], source_term), 0.0
         )
-        layers_out.append(previous[:, :, halo : halo + width_len])
-    downward_t = jnp.stack(layers_out, axis=2)
-    downward_ext = with_neighbour_rows(downward_t)
+        layers_out.append(previous)
+    cut = min(halo // 2 + 1, full_depth)
+    downward_ext = jnp.stack(layers_out, axis=2)
+    if cut < full_depth:
+        late = with_neighbour_rows(downward_ext[:, :, cut:, halo : halo + width_len])
+        downward_ext = jnp.concatenate([downward_ext[:, :, :cut], late], axis=2)
     previous = jnp.zeros((shots_here, 2, window, long_len), jnp.float32)
     layers_out = [None] * full_depth
     for layer_no in range(full_depth - 1, -1, -1):

time: 290 us -> 250 us (0.86)
  other arithmetic: 63.4 us -> 43.5 us
  waiting for transfers between devices: 48 us -> 35.3 us
  starting transfers between devices: 125 us -> 117 us
  Pallas kernels: 18.3 us -> 22.2 us
    add x16, other arithmetic: 18.1 us -> 5.17 us  [per_device(): source_term = residual_ext[:, :, layer_no] + couple(previous)]
    ppermute x12, waiting for transfers between devices: 19.4 us -> 10.3 us  [shifted(): lax.ppermute(value, axis, [(source, source + steps) for source in range(l...]
    ppermute x6, starting transfers between devices: 34.1 us -> 26.4 us  [extended(): before = lax.ppermute(last, axis, up)]
    select_n x15, other arithmetic: 15 us -> 7.77 us  [per_device(): jnp.where(row_valid, downward_ext[:, :, layer_no] + complex_scale(inv_re[...]
    pallas_call x1, Pallas kernels: 18.3 us -> 22.2 us  [all_sum(): pl.pallas_call(functools.partial(all_sum_kernel, depth_count, tile_count)...]
    unnamed x76 -> x50, local copies, waits for them, and re-layouts: 13.1 us -> 11.8 us
  transfers between devices with their start and end apart: 27 -> 27, of which waited for: 7 -> 7; matrix products, arithmetic and copies ran while one was open for 28% -> 24% of each run, Pallas kernels for 0% -> 0%
where the time goes in v7:
time: 250 us; the launch traced here: 248 us
  starting transfers between devices  117 us (47%)
  other arithmetic  43.5 us (17%)
  waiting for transfers between devices  35.3 us (14%)
  Pallas kernels  22.2 us (9%)
  local copies, waits for them, and re-layouts  20.6 us (8%)
  matrix products  8.1 us (3%)
    ppermute x12, starting transfers between devices, shifted(): lax.ppermute(value, axis, [(source, source + steps) for source in range(l...  41.9 us
    ppermute x6, starting transfers between devices, extended(): after = lax.ppermute(leading, axis, down)  32.8 us
    ppermute x6, starting transfers between devices, extended(): before = lax.ppermute(last, axis, up)  26.4 us
    pallas_call x1, Pallas kernels, all_sum(): pl.pallas_call(functools.partial(all_sum_kernel, depth_count, tile_count)...  22.2 us
    unnamed x50, local copies, waits for them, and re-layouts  11.8 us
    ppermute x6, waiting for transfers between devices, extended(): after = lax.ppermute(leading, axis, down)  11 us
    ppermute x12, waiting for transfers between devices, shifted(): lax.ppermute(value, axis, [(source, source + steps) for source in range(l...  10.3 us
    dot_general x1, matrix products, per_device(): jnp.einsum('srk,sqky->sqry', row_hot, both_fields, precision=lax.Precisio...  8.1 us
  transfers between devices with their start and end apart: 27, of which 7 were waited for; matrix products, arithmetic and copies ran while one was open for 24% of the time, Pallas kernels for 0%

profile of v7, /device:TPU:1, one launch (start us, length us, event | category | flops | bytes accessed | tf_op | source)
XLA Modules:
  0.0 248.3 jit_solution(14003204122990267511)
XLA Ops:
  0.7 1.1 fusion.739
  1.8 3.9 %collective-permute-start.4 = (f32[16,2,1,8,256]{4,3,2,0,1:T(8,128)S(1)}, f32[16,2,1,8,256]{4,3,2,0,1:T(8,128)S(1)}, u32[]{:S(2)}, u32[]{:S(2)}) collective-permute-start(f32[16,2,1,8,256]{4,3,2,0,1:T(8,128)S(1)} %get-tuple-element.92), channel_id=1, source_target_pairs={{0,32},{32,64},{64,96},{96,128},{128,160},{160,192},{192,224},{1,3... | collective-permute-start | bytes 786440 | tf_op jit(solution)/shard_map/ppermute | solution.py:26
  5.8 1.3 collective-permute-start.5
  7.1 0.8 fusion.741
  7.9 5.2 %collective-permute-start.8 = (f32[2,1,256]{2,1,0:T(1,128)S(1)}, f32[2,1,256]{2,1,0:T(1,128)S(1)}, u32[]{:S(2)}, u32[]{:S(2)}) collective-permute-start(f32[2,1,256]{2,1,0:T(1,128)S(1)} %get-tuple-element.163), channel_id=1, source_target_pairs={{0,1},{1,2},{2,3},{3,4},{4,5},{5,6},{6,7},{7,8},{8,9},{9,10},{10,1... | collective-permute-start | bytes 6152 | tf_op jit(solution)/shard_map/ppermute | solution.py:26
  13.1 1.9 collective-permute-start.9
  15.0 1.4 broadcast_in_dim.196
  16.4 6.5 %all-to-all-start = ((f32[8,2,8,256]{3,2,1,0:T(8,128)}), f32[8,2,8,256]{3,2,1,0:T(8,128)S(1)}, u32[]{:S(2)}, u32[]{:S(2)}) async-start(f32[8,2,8,256]{3,2,1,0:T(8,128)} %broadcast_in_dim.196), calls=%async_computation | async-start | bytes 262144 | tf_op jit(solution)/shard_map/all_to_all | solution.py:245
  22.9 0.7 fusion.737
  23.6 5.4 %collective-permute-start.22 = (f32[16,2,2,1,256]{4,3,2,0,1:T(1,128)}, f32[16,2,2,1,256]{4,3,2,0,1:T(1,128)}, u32[]{:S(2)}, u32[]{:S(2)}) collective-permute-start(f32[16,2,2,1,256]{4,3,2,0,1:T(1,128)} %get-tuple-element.87), channel_id=1, source_target_pairs={{0,1},{1,2},{2,3},{3,4},{4,5},{5,6},{6,7},{7,8},{8,9},{9,10},{10,1... | collective-permute-start | bytes 196616 | tf_op jit(solution)/shard_map/ppermute | solution.py:26
  29.7 1.3 multiply_add_fusion.34
  31.1 1.3 multiply_add_fusion.36
  32.6 1.3 multiply_add_fusion.33
  33.8 1.3 multiply_add_fusion.35
  35.6 4.4 %collective-permute-start = (f32[16,8,256]{2,1,0:T(8,128)S(1)}, f32[16,8,256]{2,1,0:T(8,128)S(1)}, u32[]{:S(2)}, u32[]{:S(2)}) collective-permute-start(f32[16,8,256]{2,1,0:T(8,128)S(1)} %bitcast.453), channel_id=1, source_target_pairs={{0,2},{1,3},{2,4},{3,5},{4,6},{5,7},{6,8},{7,9},{8,10},{9,11},{10,... | collective-permute-start | bytes 393224 | tf_op jit(solution)/shard_map/ppermute | solution.py:35
  40.3 2.2 collective-permute-start.6
  42.5 2.1 collective-permute-start.7
  44.7 4.9 %collective-permute-start.1 = (f32[16,8,256]{2,1,0:T(8,128)S(1)}, f32[16,8,256]{2,1,0:T(8,128)}, u32[]{:S(2)}, u32[]{:S(2)}) collective-permute-start(f32[16,8,256]{2,1,0:T(8,128)S(1)} %bitcast.454), channel_id=1, source_target_pairs={{0,1},{1,2},{2,3},{3,4},{4,5},{5,6},{6,7},{7,8},{8,9},{9,10},{10,1... | collective-permute-start | bytes 393224 | tf_op jit(solution)/shard_map/ppermute | solution.py:35
  49.7 1.9 collective-permute-start.2
  51.6 1.3 collective-permute-start.3
  53.5 0.9 fusion.13
  54.3 2.7 %fusion.71 = f32[16,2,2,8,256]{4,3,2,0,1:T(8,128)S(1)} fusion(f32[16,2,4,10,256]{4,3,2,0,1:T(8,128)S(1)} %pad_maximum_fusion, f32[16,2,4,1,256]{4,3,2,0,1:T(1,128)S(1)} %collective-permute-done.7, f32[16,2,4,8,256]{4,3,2,0,1:T(8,128)S(1)} %constant_dynamic-update-slice_fusion.5, f32[16,2,1,8,256]{4,3,2,0,1:T(8,128)S(1)} %collective-permute-done.5, ...), kind=kLoop, calls=%fused_computation.390 | loop fusion | flops 7995392 | bytes 4194304 | tf_op jit(solution)/shard_map/sub | solution.py:138
  57.2 0.9 copy_subtract_fusion
  58.1 5.4 %all-to-all-start.1 = ((f32[16,2,2,8,256]{4,3,2,1,0:T(8,128)}), f32[16,2,2,8,256]{4,3,2,1,0:T(8,128)S(1)}, u32[]{:S(2)}, u32[]{:S(2)}) async-start(f32[16,2,2,8,256]{4,3,2,1,0:T(8,128)} %copy_subtract_fusion), calls=%async_computation.1 | async-start | bytes 1048576 | tf_op jit(solution)/shard_map/all_to_all | solution.py:265
  63.5 0.9 constant_dynamic-update-slice_fusion.3
  64.5 0.9 constant_dynamic-update-slice_fusion
  65.4 6.7 %all-to-all-done.1 = f32[16,2,2,8,256]{4,3,2,1,0:T(8,128)S(1)} async-done(((f32[16,2,2,8,256]{4,3,2,1,0:T(8,128)}), f32[16,2,2,8,256]{4,3,2,1,0:T(8,128)S(1)}, u32[]{:S(2)}, u32[]{:S(2)}) %all-to-all-start.1) | async-done | bytes 524320 | tf_op jit(solution)/shard_map/all_to_all | solution.py:265
  72.1 6.8 %collective-permute-start.10 = (f32[2,2,16,8,256]{4,3,2,1,0:T(8,128)S(1)}, f32[2,2,16,8,256]{4,3,2,1,0:T(8,128)S(1)}, u32[]{:S(2)}, u32[]{:S(2)}) collective-permute-start(f32[2,2,16,8,256]{4,3,2,1,0:T(8,128)S(1)} %bitcast.434), channel_id=1, source_target_pairs={{0,2},{1,3},{2,4},{3,5},{4,6},{5,7},{6,8},{7,9},{8,10},{9,11},{10,... | collective-permute-start | bytes 1572872 | tf_op jit(solution)/shard_map/ppermute | solution.py:35
  79.3 6.2 %collective-permute-start.11 = (f32[2,2,16,8,256]{4,3,2,1,0:T(8,128)S(1)}, f32[2,2,16,8,256]{4,3,2,1,0:T(8,128)S(1)}, u32[]{:S(2)}, u32[]{:S(2)}) collective-permute-start(f32[2,2,16,8,256]{4,3,2,1,0:T(8,128)S(1)} %bitcast.435), channel_id=1, source_target_pairs={{0,1},{1,2},{2,3},{3,4},{4,5},{5,6},{6,7},{7,8},{8,9},{9,10},{10,1... | collective-permute-start | bytes 1572872 | tf_op jit(solution)/shard_map/ppermute | solution.py:35
  85.6 1.9 collective-permute-start.12
  87.5 1.3 collective-permute-start.13
  88.9 24.0 %collective-permute-start.23 = (f32[16,2,2,1,256]{4,3,2,0,1:T(1,128)S(1)}, f32[16,2,2,1,256]{4,3,2,0,1:T(1,128)S(1)}, u32[]{:S(2)}, u32[]{:S(2)}) collective-permute-start(f32[16,2,2,1,256]{4,3,2,0,1:T(1,128)S(1)} %get-tuple-element.88), channel_id=1, source_target_pairs={{1,0},{2,1},{3,2},{4,3},{5,4},{6,5},{7,6},{8,7},{9,8},{10,9},{11,1... | collective-permute-start | bytes 196616 | tf_op jit(solution)/shard_map/ppermute | solution.py:27
  113.0 0.9 collective-permute-done.11
  122.0 4.8 %collective-permute-start.14 = (f32[2,2,7,8,256]{4,3,0,2,1:T(8,128)S(1)}, f32[2,2,7,8,256]{4,3,0,2,1:T(8,128)S(1)}, u32[]{:S(2)}, u32[]{:S(2)}) collective-permute-start(f32[2,2,7,8,256]{4,3,0,2,1:T(8,128)S(1)} %slice.2335), channel_id=1, source_target_pairs={{0,2},{1,3},{2,4},{3,5},{4,6},{5,7},{6,8},{7,9},{8,10},{9,11},{10,... | collective-permute-start | bytes 688136 | tf_op jit(solution)/shard_map/ppermute | solution.py:35
  126.8 1.6 iota_compare_fusion
  128.4 4.9 %collective-permute-start.15 = (f32[2,2,7,8,256]{4,3,0,2,1:T(8,128)S(1)}, f32[2,2,7,8,256]{4,3,0,2,1:T(8,128)S(1)}, u32[]{:S(2)}, u32[]{:S(2)}) collective-permute-start(f32[2,2,7,8,256]{4,3,0,2,1:T(8,128)S(1)} %slice.2335), channel_id=1, source_target_pairs={{0,1},{1,2},{2,3},{3,4},{4,5},{5,6},{6,7},{7,8},{8,9},{9,10},{10,1... | collective-permute-start | bytes 688136 | tf_op jit(solution)/shard_map/ppermute | solution.py:35
  133.4 1.9 collective-permute-start.16
  135.3 1.5 collective-permute-start.17
  136.9 6.4 %collective-permute-done.16 = f32[2,2,7,8,256]{4,3,0,2,1:T(8,128)S(1)} collective-permute-done((f32[2,2,7,8,256]{4,3,0,2,1:T(8,128)S(1)}, f32[2,2,7,8,256]{4,3,0,2,1:T(8,128)S(1)}, u32[]{:S(2)}, u32[]{:S(2)}) %collective-permute-start.16) | collective-permute-done | bytes 229408 | tf_op jit(solution)/shard_map/ppermute | solution.py:35
  143.3 3.0 %collective-permute-done.17 = f32[2,2,7,8,256]{4,3,0,2,1:T(8,128)S(1)} collective-permute-done((f32[2,2,7,8,256]{4,3,0,2,1:T(8,128)S(1)}, f32[2,2,7,8,256]{4,3,0,2,1:T(8,128)S(1)}, u32[]{:S(2)}, u32[]{:S(2)}) %collective-permute-start.17) | collective-permute-done | bytes 229408 | tf_op jit(solution)/shard_map/ppermute | solution.py:35
  146.4 1.0 copy-done.1
  147.4 1.0 fusion.681
  148.7 1.0 fusion.683
  150.1 1.0 fusion.685
  151.5 1.0 fusion.687
  152.8 1.0 fusion.689
  154.2 1.0 fusion.691
  155.6 1.0 fusion.693
  170.4 3.5 %all-to-all-start.2 = ((f32[2,2,16,8,256]{4,3,0,1,2:T(8,128)}), f32[2,2,16,8,256]{4,3,0,1,2:T(8,128)S(1)}, u32[]{:S(2)}, u32[]{:S(2)}) async-start(f32[2,2,16,8,256]{4,3,0,1,2:T(8,128)} %constant_dynamic-update-slice_fusion.18), calls=%async_computation.2 | async-start | bytes 1048576 | tf_op jit(solution)/shard_map/all_to_all | solution.py:291
  174.0 1.0 pad_maximum_fusion.2
  175.2 7.3 %all-to-all-done.2 = f32[2,2,16,8,256]{4,3,0,1,2:T(8,128)S(1)} async-done(((f32[2,2,16,8,256]{4,3,0,1,2:T(8,128)}), f32[2,2,16,8,256]{4,3,0,1,2:T(8,128)S(1)}, u32[]{:S(2)}, u32[]{:S(2)}) %all-to-all-start.2) | async-done | bytes 524320 | tf_op jit(solution)/shard_map/all_to_all | solution.py:291
  182.7 2.4 collective-permute-start.18
  185.1 8.1 %fusion = f32[16,4,256]{2,1,0:T(4,128)S(1)} fusion(pred[16,256,256]{1,2,0:T(8,128)(4,1)S(1)} %copy-done.2, f32[16,2,16,256]{3,2,1,0:T(8,128)S(1)} %bitcast.428, f32[16,2,16,256]{3,2,1,0:T(8,128)S(1)} %bitcast.433, s32[16,256]{1,0:T(8,128)S(1)} %get-tuple-element.22), kind=kOutput, calls=%fused_computation.1 | convolution fusion | flops 814006272 | bytes 2179072 | tf_op jit(solution)/shard_map/srk,sqky->sqry/dot_general | solution.py:321
  193.3 1.3 collective-permute-start.19
  194.7 5.7 %collective-permute-done.19 = f32[16,2,1,8,256]{4,3,2,0,1:T(8,128)S(1)} collective-permute-done((f32[16,2,1,8,256]{4,3,2,0,1:T(8,128)S(1)}, f32[16,2,1,8,256]{4,3,2,0,1:T(8,128)S(1)}, u32[]{:S(2)}, u32[]{:S(2)}) %collective-permute-start.19) | collective-permute-done | bytes 262176 | tf_op jit(solution)/shard_map/ppermute | solution.py:27
  200.6 7.2 %collective-permute-start.20 = (f32[16,2,4,1,256]{4,3,2,0,1:T(1,128)S(1)}, f32[16,2,4,1,256]{4,3,2,0,1:T(1,128)S(1)}, u32[]{:S(2)}, u32[]{:S(2)}) collective-permute-start(f32[16,2,4,1,256]{4,3,2,0,1:T(1,128)S(1)} %get-tuple-element.49), channel_id=1, source_target_pairs={{0,1},{1,2},{2,3},{3,4},{4,5},{5,6},{6,7},{7,8},{8,9},{9,10},{10,1... | collective-permute-start | bytes 393224 | tf_op jit(solution)/shard_map/ppermute | solution.py:26
  207.8 2.2 collective-permute-start.21
  210.3 5.3 %collective-permute-done.21 = f32[16,2,4,1,256]{4,3,2,0,1:T(1,128)S(1)} collective-permute-done((f32[16,2,4,1,256]{4,3,2,0,1:T(1,128)S(1)}, f32[16,2,4,1,256]{4,3,2,0,1:T(1,128)S(1)}, u32[]{:S(2)}, u32[]{:S(2)}) %collective-permute-start.21) | collective-permute-done | bytes 131104 | tf_op jit(solution)/shard_map/ppermute | solution.py:27
  216.2 0.9 fusion.27
  217.0 2.7 %fusion.114 = f32[16,2,2,8,256]{4,3,2,0,1:T(8,128)S(1)} fusion(f32[16,2,4,10,256]{4,3,2,0,1:T(8,128)S(1)} %pad_maximum_fusion.1, f32[16,2,4,1,256]{4,3,2,0,1:T(1,128)S(1)} %collective-permute-done.21, f32[16,2,4,8,256]{4,3,2,0,1:T(8,128)S(1)} %constant_dynamic-update-slice_fusion.34, f32[16,2,1,8,256]{4,3,2,0,1:T(8,128)S(1)} %collective-permute-done.19, ...), kind=kLoop, calls=%fused_computation.433 | loop fusion | flops 7995392 | bytes 4194304 | tf_op jit(solution)/shard_map/sub | solution.py:138
  219.9 1.3 subtract_reduce_fusion
  222.0 22.2 %shard_map.94 = f32[1,128]{1,0:T(1,128)} custom-call(f32[1,128]{1,0:T(1,128)} %pad_bitcast_fusion.x_ref), custom_call_target="tpu_custom_call" | custom-call | tf_op jit(solution)/shard_map/pallas_call | solution.py:90
  245.4 0.9 fusion.170
  246.9 0.8 copy.497
  (215 shorter events, 31.3 us)
Async XLA Ops:
  0.6 34.9 %copy-start = (f32[16,2,2,8,256]{4,3,2,1,0:T(8,128)S(1)}, f32[16,2,2,8,256]{4,3,2,1,0:T(8,128)}, u32[]{:S(2)}) copy-start(f32[16,2,2,8,256]{4,3,2,1,0:T(8,128)} %param.7) | copy-start | bytes 1572868
  0.6 22.3 %copy-start.3 = (f32[16,2,2,8,256]{4,3,2,1,0:T(8,128)S(1)}, f32[16,2,2,8,256]{4,3,2,1,0:T(8,128)}, u32[]{:S(2)}) copy-start(f32[16,2,2,8,256]{4,3,2,1,0:T(8,128)} %param.9) | copy-start | bytes 1572868
  0.7 28.4 %copy-start.8 = (s32[4]{0:T(128)S(1)}, s32[4]{0:T(128)}, u32[]{:S(2)}) copy-start(s32[4]{0:T(128)} %param.13) | copy-start | bytes 52
  0.7 34.5 %copy-start.6 = (s32[16,256]{1,0:T(8,128)S(1)}, s32[16,256]{1,0:T(8,128)}, u32[]{:S(2)}) copy-start(s32[16,256]{1,0:T(8,128)} %param.12) | copy-start | bytes 49156
  0.7 34.6 %copy-start.7 = (s32[16]{0:T(128)S(1)}, s32[16]{0:T(128)}, u32[]{:S(2)}) copy-start(s32[16]{0:T(128)} %param.11) | copy-start | bytes 196
  1.8 33.7 %collective-permute-start.4 = (f32[16,2,1,8,256]{4,3,2,0,1:T(8,128)S(1)}, f32[16,2,1,8,256]{4,3,2,0,1:T(8,128)S(1)}, u32[]{:S(2)}, u32[]{:S(2)}) collective-permute-start(f32[16,2,1,8,256]{4,3,2,0,1:T(8,128)S(1)} %get-tuple-element.92), channel_id=1, source_target_pairs={{0,32},{32,64},{64,96},{96,128},{128,160},{160,192},{192,224},{1,3... | collective-permute-start | bytes 786440 | tf_op jit(solution)/shard_map/ppermute | solution.py:26
  5.8 34.3 %collective-permute-start.5 = (f32[16,2,1,8,256]{4,3,2,0,1:T(8,128)S(1)}, f32[16,2,1,8,256]{4,3,2,0,1:T(8,128)S(1)}, u32[]{:S(2)}, u32[]{:S(2)}) collective-permute-start(f32[16,2,1,8,256]{4,3,2,0,1:T(8,128)S(1)} %get-tuple-element.91), channel_id=1, source_target_pairs={{32,0},{64,32},{96,64},{128,96},{160,128},{192,160},{224,192},{33,... | collective-permute-start | bytes 786440 | tf_op jit(solution)/shard_map/ppermute | solution.py:27
  7.9 34.6 %collective-permute-start.8 = (f32[2,1,256]{2,1,0:T(1,128)S(1)}, f32[2,1,256]{2,1,0:T(1,128)S(1)}, u32[]{:S(2)}, u32[]{:S(2)}) collective-permute-start(f32[2,1,256]{2,1,0:T(1,128)S(1)} %get-tuple-element.163), channel_id=1, source_target_pairs={{0,1},{1,2},{2,3},{3,4},{4,5},{5,6},{6,7},{7,8},{8,9},{9,10},{10,1... | collective-permute-start | bytes 6152 | tf_op jit(solution)/shard_map/ppermute | solution.py:26
  13.1 31.6 %collective-permute-start.9 = (f32[2,1,256]{2,1,0:T(1,128)S(1)}, f32[2,1,256]{2,1,0:T(1,128)S(1)}, u32[]{:S(2)}, u32[]{:S(2)}) collective-permute-start(f32[2,1,256]{2,1,0:T(1,128)S(1)} %get-tuple-element.164), channel_id=1, source_target_pairs={{1,0},{2,1},{3,2},{4,3},{5,4},{6,5},{7,6},{8,7},{9,8},{10,9},{11,1... | collective-permute-start | bytes 6152 | tf_op jit(solution)/shard_map/ppermute | solution.py:27
  16.4 19.2 %all-to-all-start = ((f32[8,2,8,256]{3,2,1,0:T(8,128)}), f32[8,2,8,256]{3,2,1,0:T(8,128)S(1)}, u32[]{:S(2)}, u32[]{:S(2)}) async-start(f32[8,2,8,256]{3,2,1,0:T(8,128)} %broadcast_in_dim.196), calls=%async_computation | async-start | bytes 262144 | tf_op jit(solution)/shard_map/all_to_all | solution.py:245
  23.6 150.3 %collective-permute-start.22 = (f32[16,2,2,1,256]{4,3,2,0,1:T(1,128)}, f32[16,2,2,1,256]{4,3,2,0,1:T(1,128)}, u32[]{:S(2)}, u32[]{:S(2)}) collective-permute-start(f32[16,2,2,1,256]{4,3,2,0,1:T(1,128)} %get-tuple-element.87), channel_id=1, source_target_pairs={{0,1},{1,2},{2,3},{3,4},{4,5},{5,6},{6,7},{7,8},{8,9},{9,10},{10,1... | collective-permute-start | bytes 196616 | tf_op jit(solution)/shard_map/ppermute | solution.py:26
  35.6 14.1 %collective-permute-start = (f32[16,8,256]{2,1,0:T(8,128)S(1)}, f32[16,8,256]{2,1,0:T(8,128)S(1)}, u32[]{:S(2)}, u32[]{:S(2)}) collective-permute-start(f32[16,8,256]{2,1,0:T(8,128)S(1)} %bitcast.453), channel_id=1, source_target_pairs={{0,2},{1,3},{2,4},{3,5},{4,6},{5,7},{6,8},{7,9},{8,10},{9,11},{10,... | collective-permute-start | bytes 393224 | tf_op jit(solution)/shard_map/ppermute | solution.py:35
  40.0 4.6 %copy-start.4 = (f32[2,8,256]{2,1,0:T(8,128)S(1)}, f32[2,8,256]{2,1,0:T(8,128)}, u32[]{:S(2)}) copy-start(f32[2,8,256]{2,1,0:T(8,128)} %param.8) | copy-start | bytes 49156
  40.3 11.3 %collective-permute-start.6 = (f32[16,2,4,1,256]{4,3,2,0,1:T(1,128)S(1)}, f32[16,2,4,1,256]{4,3,2,0,1:T(1,128)S(1)}, u32[]{:S(2)}, u32[]{:S(2)}) collective-permute-start(f32[16,2,4,1,256]{4,3,2,0,1:T(1,128)S(1)} %get-tuple-element.51), channel_id=1, source_target_pairs={{0,1},{1,2},{2,3},{3,4},{4,5},{5,6},{6,7},{7,8},{8,9},{9,10},{10,1... | collective-permute-start | bytes 393224 | tf_op jit(solution)/shard_map/ppermute | solution.py:26
  42.5 10.4 %collective-permute-start.7 = (f32[16,2,4,1,256]{4,3,2,0,1:T(1,128)S(1)}, f32[16,2,4,1,256]{4,3,2,0,1:T(1,128)S(1)}, u32[]{:S(2)}, u32[]{:S(2)}) collective-permute-start(f32[16,2,4,1,256]{4,3,2,0,1:T(1,128)S(1)} %get-tuple-element.52), channel_id=1, source_target_pairs={{1,0},{2,1},{3,2},{4,3},{5,4},{6,5},{7,6},{8,7},{9,8},{10,9},{11,1... | collective-permute-start | bytes 393224 | tf_op jit(solution)/shard_map/ppermute | solution.py:27
  44.7 18.8 %collective-permute-start.1 = (f32[16,8,256]{2,1,0:T(8,128)S(1)}, f32[16,8,256]{2,1,0:T(8,128)}, u32[]{:S(2)}, u32[]{:S(2)}) collective-permute-start(f32[16,8,256]{2,1,0:T(8,128)S(1)} %bitcast.454), channel_id=1, source_target_pairs={{0,1},{1,2},{2,3},{3,4},{4,5},{5,6},{6,7},{7,8},{8,9},{9,10},{10,1... | collective-permute-start | bytes 393224 | tf_op jit(solution)/shard_map/ppermute | solution.py:35
  49.7 14.8 %collective-permute-start.2 = (f32[16,8,256]{2,1,0:T(8,128)S(1)}, f32[16,8,256]{2,1,0:T(8,128)S(1)}, u32[]{:S(2)}, u32[]{:S(2)}) collective-permute-start(f32[16,8,256]{2,1,0:T(8,128)S(1)} %bitcast.455), channel_id=1, source_target_pairs={{1,0},{2,1},{3,2},{4,3},{5,4},{6,5},{7,6},{8,7},{9,8},{10,9},{11,1... | collective-permute-start | bytes 393224 | tf_op jit(solution)/shard_map/ppermute | solution.py:35
  51.6 12.9 %collective-permute-start.3 = (f32[16,8,256]{2,1,0:T(8,128)S(1)}, f32[16,8,256]{2,1,0:T(8,128)}, u32[]{:S(2)}, u32[]{:S(2)}) collective-permute-start(f32[16,8,256]{2,1,0:T(8,128)S(1)} %bitcast.456), channel_id=1, source_target_pairs={{2,0},{3,1},{4,2},{5,3},{6,4},{7,5},{8,6},{9,7},{10,8},{11,9},{12,... | collective-permute-start | bytes 393224 | tf_op jit(solution)/shard_map/ppermute | solution.py:35
  58.1 14.0 %all-to-all-start.1 = ((f32[16,2,2,8,256]{4,3,2,1,0:T(8,128)}), f32[16,2,2,8,256]{4,3,2,1,0:T(8,128)S(1)}, u32[]{:S(2)}, u32[]{:S(2)}) async-start(f32[16,2,2,8,256]{4,3,2,1,0:T(8,128)} %copy_subtract_fusion), calls=%async_computation.1 | async-start | bytes 1048576 | tf_op jit(solution)/shard_map/all_to_all | solution.py:265
  72.1 16.8 %collective-permute-start.10 = (f32[2,2,16,8,256]{4,3,2,1,0:T(8,128)S(1)}, f32[2,2,16,8,256]{4,3,2,1,0:T(8,128)S(1)}, u32[]{:S(2)}, u32[]{:S(2)}) collective-permute-start(f32[2,2,16,8,256]{4,3,2,1,0:T(8,128)S(1)} %bitcast.434), channel_id=1, source_target_pairs={{0,2},{1,3},{2,4},{3,5},{4,6},{5,7},{6,8},{7,9},{8,10},{9,11},{10,... | collective-permute-start | bytes 1572872 | tf_op jit(solution)/shard_map/ppermute | solution.py:35
  79.3 34.6 %collective-permute-start.11 = (f32[2,2,16,8,256]{4,3,2,1,0:T(8,128)S(1)}, f32[2,2,16,8,256]{4,3,2,1,0:T(8,128)S(1)}, u32[]{:S(2)}, u32[]{:S(2)}) collective-permute-start(f32[2,2,16,8,256]{4,3,2,1,0:T(8,128)S(1)} %bitcast.435), channel_id=1, source_target_pairs={{0,1},{1,2},{2,3},{3,4},{4,5},{5,6},{6,7},{7,8},{8,9},{9,10},{10,1... | collective-permute-start | bytes 1572872 | tf_op jit(solution)/shard_map/ppermute | solution.py:35
  85.6 28.3 %collective-permute-start.12 = (f32[2,2,16,8,256]{4,3,2,1,0:T(8,128)S(1)}, f32[2,2,16,8,256]{4,3,2,1,0:T(8,128)S(1)}, u32[]{:S(2)}, u32[]{:S(2)}) collective-permute-start(f32[2,2,16,8,256]{4,3,2,1,0:T(8,128)S(1)} %bitcast.436), channel_id=1, source_target_pairs={{1,0},{2,1},{3,2},{4,3},{5,4},{6,5},{7,6},{8,7},{9,8},{10,9},{11,1... | collective-permute-start | bytes 1572872 | tf_op jit(solution)/shard_map/ppermute | solution.py:35
  87.5 26.4 %collective-permute-start.13 = (f32[2,2,16,8,256]{4,3,2,1,0:T(8,128)S(1)}, f32[2,2,16,8,256]{4,3,2,1,0:T(8,128)S(1)}, u32[]{:S(2)}, u32[]{:S(2)}) collective-permute-start(f32[2,2,16,8,256]{4,3,2,1,0:T(8,128)S(1)} %bitcast.437), channel_id=1, source_target_pairs={{2,0},{3,1},{4,2},{5,3},{6,4},{7,5},{8,6},{9,7},{10,8},{11,9},{12,... | collective-permute-start | bytes 1572872 | tf_op jit(solution)/shard_map/ppermute | solution.py:35
  88.9 85.1 %collective-permute-start.23 = (f32[16,2,2,1,256]{4,3,2,0,1:T(1,128)S(1)}, f32[16,2,2,1,256]{4,3,2,0,1:T(1,128)S(1)}, u32[]{:S(2)}, u32[]{:S(2)}) collective-permute-start(f32[16,2,2,1,256]{4,3,2,0,1:T(1,128)S(1)} %get-tuple-element.88), channel_id=1, source_target_pairs={{1,0},{2,1},{3,2},{4,3},{5,4},{6,5},{7,6},{8,7},{9,8},{10,9},{11,1... | collective-permute-start | bytes 196616 | tf_op jit(solution)/shard_map/ppermute | solution.py:27
  122.0 13.3 %collective-permute-start.14 = (f32[2,2,7,8,256]{4,3,0,2,1:T(8,128)S(1)}, f32[2,2,7,8,256]{4,3,0,2,1:T(8,128)S(1)}, u32[]{:S(2)}, u32[]{:S(2)}) collective-permute-start(f32[2,2,7,8,256]{4,3,0,2,1:T(8,128)S(1)} %slice.2335), channel_id=1, source_target_pairs={{0,2},{1,3},{2,4},{3,5},{4,6},{5,7},{6,8},{7,9},{8,10},{9,11},{10,... | collective-permute-start | bytes 688136 | tf_op jit(solution)/shard_map/ppermute | solution.py:35
  128.4 8.5 %collective-permute-start.15 = (f32[2,2,7,8,256]{4,3,0,2,1:T(8,128)S(1)}, f32[2,2,7,8,256]{4,3,0,2,1:T(8,128)S(1)}, u32[]{:S(2)}, u32[]{:S(2)}) collective-permute-start(f32[2,2,7,8,256]{4,3,0,2,1:T(8,128)S(1)} %slice.2335), channel_id=1, source_target_pairs={{0,1},{1,2},{2,3},{3,4},{4,5},{5,6},{6,7},{7,8},{8,9},{9,10},{10,1... | collective-permute-start | bytes 688136 | tf_op jit(solution)/shard_map/ppermute | solution.py:35
  133.4 9.9 %collective-permute-start.16 = (f32[2,2,7,8,256]{4,3,0,2,1:T(8,128)S(1)}, f32[2,2,7,8,256]{4,3,0,2,1:T(8,128)S(1)}, u32[]{:S(2)}, u32[]{:S(2)}) collective-permute-start(f32[2,2,7,8,256]{4,3,0,2,1:T(8,128)S(1)} %slice.2335), channel_id=1, source_target_pairs={{1,0},{2,1},{3,2},{4,3},{5,4},{6,5},{7,6},{8,7},{9,8},{10,9},{11,1... | collective-permute-start | bytes 688136 | tf_op jit(solution)/shard_map/ppermute | solution.py:35
  135.3 11.0 %collective-permute-start.17 = (f32[2,2,7,8,256]{4,3,0,2,1:T(8,128)S(1)}, f32[2,2,7,8,256]{4,3,0,2,1:T(8,128)S(1)}, u32[]{:S(2)}, u32[]{:S(2)}) collective-permute-start(f32[2,2,7,8,256]{4,3,0,2,1:T(8,128)S(1)} %slice.2335), channel_id=1, source_target_pairs={{2,0},{3,1},{4,2},{5,3},{6,4},{7,5},{8,6},{9,7},{10,8},{11,9},{12,... | collective-permute-start | bytes 688136 | tf_op jit(solution)/shard_map/ppermute | solution.py:35
  146.4 1.0 copy-start.1
  170.4 12.1 %all-to-all-start.2 = ((f32[2,2,16,8,256]{4,3,0,1,2:T(8,128)}), f32[2,2,16,8,256]{4,3,0,1,2:T(8,128)S(1)}, u32[]{:S(2)}, u32[]{:S(2)}) async-start(f32[2,2,16,8,256]{4,3,0,1,2:T(8,128)} %constant_dynamic-update-slice_fusion.18), calls=%async_computation.2 | async-start | bytes 1048576 | tf_op jit(solution)/shard_map/all_to_all | solution.py:291
  182.6 2.6 %copy-start.2 = (pred[16,256,256]{1,2,0:T(8,128)(4,1)S(1)}, pred[16,256,256]{1,2,0:T(8,128)(4,1)}, u32[]{:S(2)}) copy-start(pred[16,256,256]{1,2,0:T(8,128)(4,1)} %iota_compare_fusion) | copy-start | bytes 3145732
  182.7 11.9 %collective-permute-start.18 = (f32[16,2,1,8,256]{4,3,2,0,1:T(8,128)S(1)}, f32[16,2,1,8,256]{4,3,2,0,1:T(8,128)S(1)}, u32[]{:S(2)}, u32[]{:S(2)}) collective-permute-start(f32[16,2,1,8,256]{4,3,2,0,1:T(8,128)S(1)} %get-tuple-element.90), channel_id=1, source_target_pairs={{0,32},{32,64},{64,96},{96,128},{128,160},{160,192},{192,224},{1,3... | collective-permute-start | bytes 786440 | tf_op jit(solution)/shard_map/ppermute | solution.py:26
  193.3 7.1 %collective-permute-start.19 = (f32[16,2,1,8,256]{4,3,2,0,1:T(8,128)S(1)}, f32[16,2,1,8,256]{4,3,2,0,1:T(8,128)S(1)}, u32[]{:S(2)}, u32[]{:S(2)}) collective-permute-start(f32[16,2,1,8,256]{4,3,2,0,1:T(8,128)S(1)} %get-tuple-element.89), channel_id=1, source_target_pairs={{32,0},{64,32},{96,64},{128,96},{160,128},{192,160},{224,192},{33,... | collective-permute-start | bytes 786440 | tf_op jit(solution)/shard_map/ppermute | solution.py:27
  194.6 15.4 %copy-start.5 = (f32[16,2,256]{2,1,0:T(2,128)S(1)}, f32[16,2,256]{2,1,0:T(2,128)}, u32[]{:S(2)}) copy-start(f32[16,2,256]{2,1,0:T(2,128)} %param.10) | copy-start | bytes 98308
  200.6 9.7 %collective-permute-start.20 = (f32[16,2,4,1,256]{4,3,2,0,1:T(1,128)S(1)}, f32[16,2,4,1,256]{4,3,2,0,1:T(1,128)S(1)}, u32[]{:S(2)}, u32[]{:S(2)}) collective-permute-start(f32[16,2,4,1,256]{4,3,2,0,1:T(1,128)S(1)} %get-tuple-element.49), channel_id=1, source_target_pairs={{0,1},{1,2},{2,3},{3,4},{4,5},{5,6},{6,7},{7,8},{8,9},{9,10},{10,1... | collective-permute-start | bytes 393224 | tf_op jit(solution)/shard_map/ppermute | solution.py:26
  207.8 7.8 %collective-permute-start.21 = (f32[16,2,4,1,256]{4,3,2,0,1:T(1,128)S(1)}, f32[16,2,4,1,256]{4,3,2,0,1:T(1,128)S(1)}, u32[]{:S(2)}, u32[]{:S(2)}) collective-permute-start(f32[16,2,4,1,256]{4,3,2,0,1:T(1,128)S(1)} %get-tuple-element.50), channel_id=1, source_target_pairs={{1,0},{2,1},{3,2},{4,3},{5,4},{6,5},{7,6},{8,7},{9,8},{10,9},{11,1... | collective-permute-start | bytes 393224 | tf_op jit(solution)/shard_map/ppermute | solution.py:27

commit v8 on v7

--- a/solution.py
+++ b/solution.py
@@ -263,7 +263,16 @@
         )
 
     residual_t = lax.all_to_all(residual, "depth", 0, 2, tiled=True)
-    residual_ext = with_neighbour_rows(residual_t)
+    if reach == 2:
+        near = residual_t[:, :, full_depth // 2 :]
+        early = with_neighbour_rows(residual_t[:, :, : full_depth // 2])
+        zero_rows = jnp.zeros(near.shape, near.dtype)
+        late = jnp.concatenate(
+            [zero_rows, shifted(near, "tile", 1), near, shifted(near, "tile", -1), zero_rows], axis=-2
+        )
+        residual_ext = jnp.concatenate([early, late], axis=2)
+    else:
+        residual_ext = with_neighbour_rows(residual_t)
     previous = jnp.zeros((shots_here, 2, window, long_len), jnp.float32)
     layers_out = []
     for layer_no in range(full_depth):

time: 250 us -> 268 us (1.072)
  waiting for transfers between devices: 35.3 us -> 52.9 us
  starting transfers between devices: 117 us -> 106 us
  other arithmetic: 43.5 us -> 51.7 us
    ppermute x6, starting transfers between devices: 32.8 us -> 10.5 us  [extended(): after = lax.ppermute(leading, axis, down)]
    ppermute x12 -> x14, waiting for transfers between devices: 10.3 us -> 21.9 us  [shifted(): lax.ppermute(value, axis, [(source, source + steps) for source in range(l...]
    ppermute x12 -> x14, starting transfers between devices: 41.9 us -> 49.8 us  [shifted(): lax.ppermute(value, axis, [(source, source + steps) for source in range(l...]
    add x16, other arithmetic: 5.17 us -> 11.6 us  [per_device(): source_term = residual_ext[:, :, layer_no] + couple(previous)]
    ppermute x6, waiting for transfers between devices: 11 us -> 16.4 us  [extended(): after = lax.ppermute(leading, axis, down)]
    ppermute x6, starting transfers between devices: 26.4 us -> 30.7 us  [extended(): before = lax.ppermute(last, axis, up)]
    unnamed x50 -> x79, local copies, waits for them, and re-layouts: 11.8 us -> 12.6 us
  transfers between devices with their start and end apart: 27 -> 29, of which waited for: 7 -> 10; matrix products, arithmetic and copies ran while one was open for 24% -> 25% of each run, Pallas kernels for 0% -> 0%
where the time goes in v8:
time: 268 us; the launch traced here: 266 us
  starting transfers between devices  106 us (40%)
  waiting for transfers between devices  52.9 us (20%)
  other arithmetic  51.7 us (19%)
  Pallas kernels  24.3 us (9%)
  local copies, waits for them, and re-layouts  20.5 us (8%)
  matrix products  8.1 us (3%)
    ppermute x14, starting transfers between devices, shifted(): lax.ppermute(value, axis, [(source, source + steps) for source in range(l...  49.8 us
    ppermute x6, starting transfers between devices, extended(): before = lax.ppermute(last, axis, up)  30.7 us
    pallas_call x1, Pallas kernels, all_sum(): pl.pallas_call(functools.partial(all_sum_kernel, depth_count, tile_count)...  24.3 us
    ppermute x14, waiting for transfers between devices, shifted(): lax.ppermute(value, axis, [(source, source + steps) for source in range(l...  21.9 us
    ppermute x6, waiting for transfers between devices, extended(): after = lax.ppermute(leading, axis, down)  16.4 us
    unnamed x79, local copies, waits for them, and re-layouts  12.6 us
    add x16, other arithmetic, per_device(): source_term = residual_ext[:, :, layer_no] + couple(previous)  11.6 us
    ppermute x6, starting transfers between devices, extended(): after = lax.ppermute(leading, axis, down)  10.5 us
  transfers between devices with their start and end apart: 29, of which 10 were waited for; matrix products, arithmetic and copies ran while one was open for 25% of the time, Pallas kernels for 0%

profile of v8, /device:TPU:1, one launch (start us, length us, event | category | flops | bytes accessed | tf_op | source)
XLA Modules:
  0.0 266.0 jit_solution(15318532619763121443)
XLA Ops:
  0.7 1.1 fusion.739
  1.8 3.9 %collective-permute-start.4 = (f32[16,2,1,8,256]{4,3,2,0,1:T(8,128)S(1)}, f32[16,2,1,8,256]{4,3,2,0,1:T(8,128)S(1)}, u32[]{:S(2)}, u32[]{:S(2)}) collective-permute-start(f32[16,2,1,8,256]{4,3,2,0,1:T(8,128)S(1)} %get-tuple-element.86), channel_id=1, source_target_pairs={{0,32},{32,64},{64,96},{96,128},{128,160},{160,192},{192,224},{1,3... | collective-permute-start | bytes 786440 | tf_op jit(solution)/shard_map/ppermute | solution.py:26
  5.8 1.3 collective-permute-start.5
  7.9 5.2 %collective-permute-start.8 = (f32[2,1,256]{2,1,0:T(1,128)S(1)}, f32[2,1,256]{2,1,0:T(1,128)S(1)}, u32[]{:S(2)}, u32[]{:S(2)}) collective-permute-start(f32[2,1,256]{2,1,0:T(1,128)S(1)} %get-tuple-element.157), channel_id=1, source_target_pairs={{0,1},{1,2},{2,3},{3,4},{4,5},{5,6},{6,7},{7,8},{8,9},{9,10},{10,1... | collective-permute-start | bytes 6152 | tf_op jit(solution)/shard_map/ppermute | solution.py:26
  13.1 1.9 collective-permute-start.9
  15.0 1.4 broadcast_in_dim.199
  16.4 6.5 %all-to-all-start = ((f32[8,2,8,256]{3,2,1,0:T(8,128)}), f32[8,2,8,256]{3,2,1,0:T(8,128)S(1)}, u32[]{:S(2)}, u32[]{:S(2)}) async-start(f32[8,2,8,256]{3,2,1,0:T(8,128)} %broadcast_in_dim.199), calls=%async_computation | async-start | bytes 262144 | tf_op jit(solution)/shard_map/all_to_all | solution.py:245
  23.6 1.2 multiply_add_fusion.34
  24.8 1.2 multiply_add_fusion.36
  26.1 1.3 multiply_add_fusion.33
  28.1 1.3 multiply_add_fusion.35
  32.3 4.1 %collective-permute-start = (f32[16,8,256]{2,1,0:T(8,128)S(1)}, f32[16,8,256]{2,1,0:T(8,128)S(1)}, u32[]{:S(2)}, u32[]{:S(2)}) collective-permute-start(f32[16,8,256]{2,1,0:T(8,128)S(1)} %bitcast.450), channel_id=1, source_target_pairs={{0,2},{1,3},{2,4},{3,5},{4,6},{5,7},{6,8},{7,9},{8,10},{9,11},{10,... | collective-permute-start | bytes 393224 | tf_op jit(solution)/shard_map/ppermute | solution.py:35
  36.5 6.0 %collective-permute-start.24 = (f32[16,2,2,1,256]{4,3,2,0,1:T(1,128)}, f32[16,2,2,1,256]{4,3,2,0,1:T(1,128)}, u32[]{:S(2)}, u32[]{:S(2)}) collective-permute-start(f32[16,2,2,1,256]{4,3,2,0,1:T(1,128)} %get-tuple-element.79), channel_id=1, source_target_pairs={{0,1},{1,2},{2,3},{3,4},{4,5},{5,6},{6,7},{7,8},{8,9},{9,10},{10,1... | collective-permute-start | bytes 196616 | tf_op jit(solution)/shard_map/ppermute | solution.py:26
  42.5 1.9 collective-permute-start.25
  44.5 5.1 %collective-permute-start.1 = (f32[16,8,256]{2,1,0:T(8,128)S(1)}, f32[16,8,256]{2,1,0:T(8,128)S(1)}, u32[]{:S(2)}, u32[]{:S(2)}) collective-permute-start(f32[16,8,256]{2,1,0:T(8,128)S(1)} %bitcast.451), channel_id=1, source_target_pairs={{0,1},{1,2},{2,3},{3,4},{4,5},{5,6},{6,7},{7,8},{8,9},{9,10},{10,1... | collective-permute-start | bytes 393224 | tf_op jit(solution)/shard_map/ppermute | solution.py:35
  49.7 1.9 collective-permute-start.2
  51.9 5.1 %collective-permute-start.6 = (f32[16,2,4,1,256]{4,3,2,0,1:T(1,128)S(1)}, f32[16,2,4,1,256]{4,3,2,0,1:T(1,128)S(1)}, u32[]{:S(2)}, u32[]{:S(2)}) collective-permute-start(f32[16,2,4,1,256]{4,3,2,0,1:T(1,128)S(1)} %get-tuple-element.43), channel_id=1, source_target_pairs={{0,1},{1,2},{2,3},{3,4},{4,5},{5,6},{6,7},{7,8},{8,9},{9,10},{10,1... | collective-permute-start | bytes 393224 | tf_op jit(solution)/shard_map/ppermute | solution.py:26
  57.1 1.9 collective-permute-start.7
  59.1 1.3 collective-permute-start.3
  60.4 4.5 %collective-permute-done.7 = f32[16,2,4,1,256]{4,3,2,0,1:T(1,128)S(1)} collective-permute-done((f32[16,2,4,1,256]{4,3,2,0,1:T(1,128)S(1)}, f32[16,2,4,1,256]{4,3,2,0,1:T(1,128)S(1)}, u32[]{:S(2)}, u32[]{:S(2)}) %collective-permute-start.7) | collective-permute-done | bytes 131104 | tf_op jit(solution)/shard_map/ppermute | solution.py:27
  66.3 2.7 %fusion.71 = f32[16,2,2,8,256]{4,3,2,0,1:T(8,128)S(1)} fusion(f32[16,2,4,10,256]{4,3,2,0,1:T(8,128)S(1)} %pad_maximum_fusion, f32[16,2,4,1,256]{4,3,2,0,1:T(1,128)S(1)} %collective-permute-done.7, f32[16,2,4,8,256]{4,3,2,0,1:T(8,128)S(1)} %constant_dynamic-update-slice_fusion.5, f32[16,2,1,8,256]{4,3,2,0,1:T(8,128)S(1)} %collective-permute-done.5, ...), kind=kLoop, calls=%fused_computation.390 | loop fusion | flops 7995392 | bytes 4194304 | tf_op jit(solution)/shard_map/sub | solution.py:138
  70.1 5.4 %all-to-all-start.1 = ((f32[16,2,2,8,256]{4,3,2,1,0:T(8,128)}), f32[16,2,2,8,256]{4,3,2,1,0:T(8,128)S(1)}, u32[]{:S(2)}, u32[]{:S(2)}) async-start(f32[16,2,2,8,256]{4,3,2,1,0:T(8,128)} %copy_subtract_fusion), calls=%async_computation.1 | async-start | bytes 1048576 | tf_op jit(solution)/shard_map/all_to_all | solution.py:265
  75.5 1.0 fusion.4
  76.6 6.5 %all-to-all-done.1 = f32[16,2,2,8,256]{4,3,2,1,0:T(8,128)S(1)} async-done(((f32[16,2,2,8,256]{4,3,2,1,0:T(8,128)}), f32[16,2,2,8,256]{4,3,2,1,0:T(8,128)S(1)}, u32[]{:S(2)}, u32[]{:S(2)}) %all-to-all-start.1) | async-done | bytes 524320 | tf_op jit(solution)/shard_map/all_to_all | solution.py:265
  83.1 4.0 %collective-permute-start.14 = (f32[2,2,8,8,256]{4,3,2,1,0:T(8,128)S(1)}, f32[2,2,8,8,256]{4,3,2,1,0:T(8,128)S(1)}, u32[]{:S(2)}, u32[]{:S(2)}) collective-permute-start(f32[2,2,8,8,256]{4,3,2,1,0:T(8,128)S(1)} %slice.2305), channel_id=1, source_target_pairs={{0,1},{1,2},{2,3},{3,4},{4,5},{5,6},{6,7},{7,8},{8,9},{9,10},{10,1... | collective-permute-start | bytes 786440 | tf_op jit(solution)/shard_map/ppermute | solution.py:35
  87.3 2.1 collective-permute-start.15
  89.3 1.1 collective-permute-done.14
  90.5 7.6 %collective-permute-start.10 = (f32[2,2,8,8,256]{4,3,0,1,2:T(8,128)S(1)}, f32[2,2,8,8,256]{4,3,0,1,2:T(8,128)S(1)}, u32[]{:S(2)}, u32[]{:S(2)}) collective-permute-start(f32[2,2,8,8,256]{4,3,0,1,2:T(8,128)S(1)} %copy.481), channel_id=1, source_target_pairs={{0,2},{1,3},{2,4},{3,5},{4,6},{5,7},{6,8},{7,9},{8,10},{9,11},{10,... | collective-permute-start | bytes 786440 | tf_op jit(solution)/shard_map/ppermute | solution.py:35
  98.1 7.1 %collective-permute-start.11 = (f32[2,2,8,8,256]{4,3,0,1,2:T(8,128)S(1)}, f32[2,2,8,8,256]{4,3,0,1,2:T(8,128)S(1)}, u32[]{:S(2)}, u32[]{:S(2)}) collective-permute-start(f32[2,2,8,8,256]{4,3,0,1,2:T(8,128)S(1)} %copy.481), channel_id=1, source_target_pairs={{0,1},{1,2},{2,3},{3,4},{4,5},{5,6},{6,7},{7,8},{8,9},{9,10},{10,1... | collective-permute-start | bytes 786440 | tf_op jit(solution)/shard_map/ppermute | solution.py:35
  105.2 1.9 collective-permute-start.12
  107.3 1.5 collective-permute-start.13
  108.9 6.6 %collective-permute-done.12 = f32[2,2,8,8,256]{4,3,0,1,2:T(8,128)S(1)} collective-permute-done((f32[2,2,8,8,256]{4,3,0,1,2:T(8,128)S(1)}, f32[2,2,8,8,256]{4,3,0,1,2:T(8,128)S(1)}, u32[]{:S(2)}, u32[]{:S(2)}) %collective-permute-start.12) | collective-permute-done | bytes 262176 | tf_op jit(solution)/shard_map/ppermute | solution.py:35
  115.4 3.8 %collective-permute-done.13 = f32[2,2,8,8,256]{4,3,0,1,2:T(8,128)S(1)} collective-permute-done((f32[2,2,8,8,256]{4,3,0,1,2:T(8,128)S(1)}, f32[2,2,8,8,256]{4,3,0,1,2:T(8,128)S(1)}, u32[]{:S(2)}, u32[]{:S(2)}) %collective-permute-start.13) | collective-permute-done | bytes 262176 | tf_op jit(solution)/shard_map/ppermute | solution.py:35
  120.3 1.2 fusion.180
  121.7 1.2 fusion.197
  123.0 1.2 fusion.214
  124.4 1.2 fusion.231
  125.8 1.2 fusion.248
  127.1 1.2 fusion.265
  128.5 1.2 fusion.282
  134.0 5.8 %collective-permute-start.16 = (f32[2,2,7,8,256]{4,3,0,2,1:T(8,128)S(1)}, f32[2,2,7,8,256]{4,3,0,2,1:T(8,128)S(1)}, u32[]{:S(2)}, u32[]{:S(2)}) collective-permute-start(f32[2,2,7,8,256]{4,3,0,2,1:T(8,128)S(1)} %slice.2345), channel_id=1, source_target_pairs={{0,2},{1,3},{2,4},{3,5},{4,6},{5,7},{6,8},{7,9},{8,10},{9,11},{10,... | collective-permute-start | bytes 688136 | tf_op jit(solution)/shard_map/ppermute | solution.py:35
  139.8 1.6 iota_compare_fusion
  141.4 4.0 %collective-permute-start.17 = (f32[2,2,7,8,256]{4,3,0,2,1:T(8,128)S(1)}, f32[2,2,7,8,256]{4,3,0,2,1:T(8,128)S(1)}, u32[]{:S(2)}, u32[]{:S(2)}) collective-permute-start(f32[2,2,7,8,256]{4,3,0,2,1:T(8,128)S(1)} %slice.2345), channel_id=1, source_target_pairs={{0,1},{1,2},{2,3},{3,4},{4,5},{5,6},{6,7},{7,8},{8,9},{9,10},{10,1... | collective-permute-start | bytes 688136 | tf_op jit(solution)/shard_map/ppermute | solution.py:35
  145.6 1.9 collective-permute-start.18
  147.5 1.5 collective-permute-start.19
  149.2 5.3 %collective-permute-done.18 = f32[2,2,7,8,256]{4,3,0,2,1:T(8,128)S(1)} collective-permute-done((f32[2,2,7,8,256]{4,3,0,2,1:T(8,128)S(1)}, f32[2,2,7,8,256]{4,3,0,2,1:T(8,128)S(1)}, u32[]{:S(2)}, u32[]{:S(2)}) %collective-permute-start.18) | collective-permute-done | bytes 229408 | tf_op jit(solution)/shard_map/ppermute | solution.py:35
  154.5 5.1 %collective-permute-done.19 = f32[2,2,7,8,256]{4,3,0,2,1:T(8,128)S(1)} collective-permute-done((f32[2,2,7,8,256]{4,3,0,2,1:T(8,128)S(1)}, f32[2,2,7,8,256]{4,3,0,2,1:T(8,128)S(1)}, u32[]{:S(2)}, u32[]{:S(2)}) %collective-permute-start.19) | collective-permute-done | bytes 229408 | tf_op jit(solution)/shard_map/ppermute | solution.py:35
  159.7 1.0 copy-done.3
  162.1 1.0 fusion.683
  163.4 1.0 fusion.685
  164.8 1.0 fusion.687
  183.6 3.5 %all-to-all-start.2 = ((f32[2,2,16,8,256]{4,3,0,1,2:T(8,128)}), f32[2,2,16,8,256]{4,3,0,1,2:T(8,128)S(1)}, u32[]{:S(2)}, u32[]{:S(2)}) async-start(f32[2,2,16,8,256]{4,3,0,1,2:T(8,128)} %constant_dynamic-update-slice_fusion.21), calls=%async_computation.2 | async-start | bytes 1048576 | tf_op jit(solution)/shard_map/all_to_all | solution.py:300
  187.1 1.1 pad_maximum_fusion.2
  188.4 8.1 %all-to-all-done.2 = f32[2,2,16,8,256]{4,3,0,1,2:T(8,128)S(1)} async-done(((f32[2,2,16,8,256]{4,3,0,1,2:T(8,128)}), f32[2,2,16,8,256]{4,3,0,1,2:T(8,128)S(1)}, u32[]{:S(2)}, u32[]{:S(2)}) %all-to-all-start.2) | async-done | bytes 524320 | tf_op jit(solution)/shard_map/all_to_all | solution.py:300
  196.6 2.7 %collective-permute-start.20 = (f32[16,2,1,8,256]{4,3,2,0,1:T(8,128)S(1)}, f32[16,2,1,8,256]{4,3,2,0,1:T(8,128)S(1)}, u32[]{:S(2)}, u32[]{:S(2)}) collective-permute-start(f32[16,2,1,8,256]{4,3,2,0,1:T(8,128)S(1)} %get-tuple-element.82), channel_id=1, source_target_pairs={{0,32},{32,64},{64,96},{96,128},{128,160},{160,192},{192,224},{1,3... | collective-permute-start | bytes 786440 | tf_op jit(solution)/shard_map/ppermute | solution.py:26
  199.4 8.1 %fusion = f32[16,4,256]{2,1,0:T(4,128)S(1)} fusion(pred[16,256,256]{1,2,0:T(8,128)(4,1)S(1)} %copy-done.4, f32[16,2,16,256]{3,2,1,0:T(8,128)S(1)} %bitcast.428, f32[16,2,16,256]{3,2,1,0:T(8,128)S(1)} %bitcast.433, s32[16,256]{1,0:T(8,128)S(1)} %copy-done.12), kind=kOutput, calls=%fused_computation.1 | convolution fusion | flops 814006272 | bytes 2179072 | tf_op jit(solution)/shard_map/srk,sqky->sqry/dot_general | solution.py:330
  207.5 1.3 collective-permute-start.21
  208.9 6.6 %collective-permute-done.21 = f32[16,2,1,8,256]{4,3,2,0,1:T(8,128)S(1)} collective-permute-done((f32[16,2,1,8,256]{4,3,2,0,1:T(8,128)S(1)}, f32[16,2,1,8,256]{4,3,2,0,1:T(8,128)S(1)}, u32[]{:S(2)}, u32[]{:S(2)}) %collective-permute-start.21) | collective-permute-done | bytes 262176 | tf_op jit(solution)/shard_map/ppermute | solution.py:27
  215.7 7.7 %collective-permute-start.22 = (f32[16,2,4,1,256]{4,3,2,0,1:T(1,128)S(1)}, f32[16,2,4,1,256]{4,3,2,0,1:T(1,128)S(1)}, u32[]{:S(2)}, u32[]{:S(2)}) collective-permute-start(f32[16,2,4,1,256]{4,3,2,0,1:T(1,128)S(1)} %get-tuple-element.41), channel_id=1, source_target_pairs={{0,1},{1,2},{2,3},{3,4},{4,5},{5,6},{6,7},{7,8},{8,9},{9,10},{10,1... | collective-permute-start | bytes 393224 | tf_op jit(solution)/shard_map/ppermute | solution.py:26
  223.4 2.2 collective-permute-start.23
  225.9 5.3 %collective-permute-done.23 = f32[16,2,4,1,256]{4,3,2,0,1:T(1,128)S(1)} collective-permute-done((f32[16,2,4,1,256]{4,3,2,0,1:T(1,128)S(1)}, f32[16,2,4,1,256]{4,3,2,0,1:T(1,128)S(1)}, u32[]{:S(2)}, u32[]{:S(2)}) %collective-permute-start.23) | collective-permute-done | bytes 131104 | tf_op jit(solution)/shard_map/ppermute | solution.py:27
  232.6 2.7 %fusion.114 = f32[16,2,2,8,256]{4,3,2,0,1:T(8,128)S(1)} fusion(f32[16,2,4,10,256]{4,3,2,0,1:T(8,128)S(1)} %pad_maximum_fusion.1, f32[16,2,4,1,256]{4,3,2,0,1:T(1,128)S(1)} %collective-permute-done.23, f32[16,2,4,8,256]{4,3,2,0,1:T(8,128)S(1)} %constant_dynamic-update-slice_fusion.37, f32[16,2,1,8,256]{4,3,2,0,1:T(8,128)S(1)} %collective-permute-done.21, ...), kind=kLoop, calls=%fused_computation.433 | loop fusion | flops 7995392 | bytes 4194304 | tf_op jit(solution)/shard_map/sub | solution.py:138
  235.5 1.3 subtract_reduce_fusion
  237.5 24.3 %shard_map.94 = f32[1,128]{1,0:T(1,128)} custom-call(f32[1,128]{1,0:T(1,128)} %pad_bitcast_fusion.x_ref), custom_call_target="tpu_custom_call" | custom-call | tf_op jit(solution)/shard_map/pallas_call | solution.py:90
  (250 shorter events, 41.5 us)
Async XLA Ops:
  0.6 35.8 %copy-start = (f32[16,2,2,8,256]{4,3,2,1,0:T(8,128)S(1)}, f32[16,2,2,8,256]{4,3,2,1,0:T(8,128)}, u32[]{:S(2)}) copy-start(f32[16,2,2,8,256]{4,3,2,1,0:T(8,128)} %param.7) | copy-start | bytes 1572868
  0.6 22.3 %copy-start.20 = (s32[4]{0:T(128)S(1)}, s32[4]{0:T(128)}, u32[]{:S(2)}) copy-start(s32[4]{0:T(128)} %param.13) | copy-start | bytes 52
  0.7 28.8 %copy-start.11 = (s32[16,256]{1,0:T(8,128)S(1)}, s32[16,256]{1,0:T(8,128)}, u32[]{:S(2)}) copy-start(s32[16,256]{1,0:T(8,128)} %param.12) | copy-start | bytes 49156
  0.7 29.4 %copy-start.5 = (f32[16,2,2,8,256]{4,3,2,1,0:T(8,128)S(1)}, f32[16,2,2,8,256]{4,3,2,1,0:T(8,128)}, u32[]{:S(2)}) copy-start(f32[16,2,2,8,256]{4,3,2,1,0:T(8,128)} %param.9) | copy-start | bytes 1572868
  0.7 30.1 %copy-start.19 = (s32[16]{0:T(128)S(1)}, s32[16]{0:T(128)}, u32[]{:S(2)}) copy-start(s32[16]{0:T(128)} %param.11) | copy-start | bytes 196
  1.8 42.6 %copy-start.8 = (f32[2,8,256]{2,1,0:T(8,128)S(1)}, f32[2,8,256]{2,1,0:T(8,128)}, u32[]{:S(2)}) copy-start(f32[2,8,256]{2,1,0:T(8,128)} %param.8) | copy-start | bytes 49156
  1.8 47.8 %collective-permute-start.4 = (f32[16,2,1,8,256]{4,3,2,0,1:T(8,128)S(1)}, f32[16,2,1,8,256]{4,3,2,0,1:T(8,128)S(1)}, u32[]{:S(2)}, u32[]{:S(2)}) collective-permute-start(f32[16,2,1,8,256]{4,3,2,0,1:T(8,128)S(1)} %get-tuple-element.86), channel_id=1, source_target_pairs={{0,32},{32,64},{64,96},{96,128},{128,160},{160,192},{192,224},{1,3... | collective-permute-start | bytes 786440 | tf_op jit(solution)/shard_map/ppermute | solution.py:26
  5.8 45.9 %collective-permute-start.5 = (f32[16,2,1,8,256]{4,3,2,0,1:T(8,128)S(1)}, f32[16,2,1,8,256]{4,3,2,0,1:T(8,128)S(1)}, u32[]{:S(2)}, u32[]{:S(2)}) collective-permute-start(f32[16,2,1,8,256]{4,3,2,0,1:T(8,128)S(1)} %get-tuple-element.85), channel_id=1, source_target_pairs={{32,0},{64,32},{96,64},{128,96},{160,128},{192,160},{224,192},{33,... | collective-permute-start | bytes 786440 | tf_op jit(solution)/shard_map/ppermute | solution.py:27
  7.9 28.6 %collective-permute-start.8 = (f32[2,1,256]{2,1,0:T(1,128)S(1)}, f32[2,1,256]{2,1,0:T(1,128)S(1)}, u32[]{:S(2)}, u32[]{:S(2)}) collective-permute-start(f32[2,1,256]{2,1,0:T(1,128)S(1)} %get-tuple-element.157), channel_id=1, source_target_pairs={{0,1},{1,2},{2,3},{3,4},{4,5},{5,6},{6,7},{7,8},{8,9},{9,10},{10,1... | collective-permute-start | bytes 6152 | tf_op jit(solution)/shard_map/ppermute | solution.py:26
  13.1 29.4 %collective-permute-start.9 = (f32[2,1,256]{2,1,0:T(1,128)S(1)}, f32[2,1,256]{2,1,0:T(1,128)S(1)}, u32[]{:S(2)}, u32[]{:S(2)}) collective-permute-start(f32[2,1,256]{2,1,0:T(1,128)S(1)} %get-tuple-element.158), channel_id=1, source_target_pairs={{1,0},{2,1},{3,2},{4,3},{5,4},{6,5},{7,6},{8,7},{9,8},{10,9},{11,1... | collective-permute-start | bytes 6152 | tf_op jit(solution)/shard_map/ppermute | solution.py:27
  16.4 15.9 %all-to-all-start = ((f32[8,2,8,256]{3,2,1,0:T(8,128)}), f32[8,2,8,256]{3,2,1,0:T(8,128)S(1)}, u32[]{:S(2)}, u32[]{:S(2)}) async-start(f32[8,2,8,256]{3,2,1,0:T(8,128)} %broadcast_in_dim.199), calls=%async_computation | async-start | bytes 262144 | tf_op jit(solution)/shard_map/all_to_all | solution.py:245
  24.8 2.7 %copy-start.15 = (f32[2]{0:T(128)}, f32[2]{0:T(128)S(1)}, u32[]{:S(2)}) copy-start(f32[2]{0:T(128)S(1)} %multiply_add_fusion.34) | copy-start | bytes 28
  27.4 0.5 copy-start.17
  27.9 41.1 %copy-start.13 = (f32[2,8]{1,0:T(2,128)}, f32[2,8]{1,0:T(2,128)S(1)}, u32[]{:S(2)}) copy-start(f32[2,8]{1,0:T(2,128)S(1)} %slice_bitcast_fusion.72) | copy-start | bytes 196
  32.3 12.2 %collective-permute-start = (f32[16,8,256]{2,1,0:T(8,128)S(1)}, f32[16,8,256]{2,1,0:T(8,128)S(1)}, u32[]{:S(2)}, u32[]{:S(2)}) collective-permute-start(f32[16,8,256]{2,1,0:T(8,128)S(1)} %bitcast.450), channel_id=1, source_target_pairs={{0,2},{1,3},{2,4},{3,5},{4,6},{5,7},{6,8},{7,9},{8,10},{9,11},{10,... | collective-permute-start | bytes 393224 | tf_op jit(solution)/shard_map/ppermute | solution.py:35
  36.5 150.6 %collective-permute-start.24 = (f32[16,2,2,1,256]{4,3,2,0,1:T(1,128)}, f32[16,2,2,1,256]{4,3,2,0,1:T(1,128)}, u32[]{:S(2)}, u32[]{:S(2)}) collective-permute-start(f32[16,2,2,1,256]{4,3,2,0,1:T(1,128)} %get-tuple-element.79), channel_id=1, source_target_pairs={{0,1},{1,2},{2,3},{3,4},{4,5},{5,6},{6,7},{7,8},{8,9},{9,10},{10,1... | collective-permute-start | bytes 196616 | tf_op jit(solution)/shard_map/ppermute | solution.py:26
  42.5 144.6 %collective-permute-start.25 = (f32[16,2,2,1,256]{4,3,2,0,1:T(1,128)}, f32[16,2,2,1,256]{4,3,2,0,1:T(1,128)}, u32[]{:S(2)}, u32[]{:S(2)}) collective-permute-start(f32[16,2,2,1,256]{4,3,2,0,1:T(1,128)} %get-tuple-element.80), channel_id=1, source_target_pairs={{1,0},{2,1},{3,2},{4,3},{5,4},{6,5},{7,6},{8,7},{9,8},{10,9},{11,1... | collective-permute-start | bytes 196616 | tf_op jit(solution)/shard_map/ppermute | solution.py:27
  44.5 20.8 %copy-start.6 = (f32[2,10,256]{2,1,0:T(8,128)}, f32[2,10,256]{2,1,0:T(8,128)S(1)}, u32[]{:S(2)}) copy-start(f32[2,10,256]{2,1,0:T(8,128)S(1)} %pad_maximum_fusion.14) | copy-start | bytes 61444
  44.5 12.6 %collective-permute-start.1 = (f32[16,8,256]{2,1,0:T(8,128)S(1)}, f32[16,8,256]{2,1,0:T(8,128)S(1)}, u32[]{:S(2)}, u32[]{:S(2)}) collective-permute-start(f32[16,8,256]{2,1,0:T(8,128)S(1)} %bitcast.451), channel_id=1, source_target_pairs={{0,1},{1,2},{2,3},{3,4},{4,5},{5,6},{6,7},{7,8},{8,9},{9,10},{10,1... | collective-permute-start | bytes 393224 | tf_op jit(solution)/shard_map/ppermute | solution.py:35
  49.7 25.8 %collective-permute-start.2 = (f32[16,8,256]{2,1,0:T(8,128)S(1)}, f32[16,8,256]{2,1,0:T(8,128)S(1)}, u32[]{:S(2)}, u32[]{:S(2)}) collective-permute-start(f32[16,8,256]{2,1,0:T(8,128)S(1)} %bitcast.452), channel_id=1, source_target_pairs={{1,0},{2,1},{3,2},{4,3},{5,4},{6,5},{7,6},{8,7},{9,8},{10,9},{11,1... | collective-permute-start | bytes 393224 | tf_op jit(solution)/shard_map/ppermute | solution.py:35
  51.9 7.2 %collective-permute-start.6 = (f32[16,2,4,1,256]{4,3,2,0,1:T(1,128)S(1)}, f32[16,2,4,1,256]{4,3,2,0,1:T(1,128)S(1)}, u32[]{:S(2)}, u32[]{:S(2)}) collective-permute-start(f32[16,2,4,1,256]{4,3,2,0,1:T(1,128)S(1)} %get-tuple-element.43), channel_id=1, source_target_pairs={{0,1},{1,2},{2,3},{3,4},{4,5},{5,6},{6,7},{7,8},{8,9},{9,10},{10,1... | collective-permute-start | bytes 393224 | tf_op jit(solution)/shard_map/ppermute | solution.py:26
  57.1 7.8 %collective-permute-start.7 = (f32[16,2,4,1,256]{4,3,2,0,1:T(1,128)S(1)}, f32[16,2,4,1,256]{4,3,2,0,1:T(1,128)S(1)}, u32[]{:S(2)}, u32[]{:S(2)}) collective-permute-start(f32[16,2,4,1,256]{4,3,2,0,1:T(1,128)S(1)} %get-tuple-element.44), channel_id=1, source_target_pairs={{1,0},{2,1},{3,2},{4,3},{5,4},{6,5},{7,6},{8,7},{9,8},{10,9},{11,1... | collective-permute-start | bytes 393224 | tf_op jit(solution)/shard_map/ppermute | solution.py:27
  59.1 16.4 %collective-permute-start.3 = (f32[16,8,256]{2,1,0:T(8,128)S(1)}, f32[16,8,256]{2,1,0:T(8,128)S(1)}, u32[]{:S(2)}, u32[]{:S(2)}) collective-permute-start(f32[16,8,256]{2,1,0:T(8,128)S(1)} %bitcast.454), channel_id=1, source_target_pairs={{2,0},{3,1},{4,2},{5,3},{6,4},{7,5},{8,6},{9,7},{10,8},{11,9},{12,... | collective-permute-start | bytes 393224 | tf_op jit(solution)/shard_map/ppermute | solution.py:35
  70.1 13.0 %all-to-all-start.1 = ((f32[16,2,2,8,256]{4,3,2,1,0:T(8,128)}), f32[16,2,2,8,256]{4,3,2,1,0:T(8,128)S(1)}, u32[]{:S(2)}, u32[]{:S(2)}) async-start(f32[16,2,2,8,256]{4,3,2,1,0:T(8,128)} %copy_subtract_fusion), calls=%async_computation.1 | async-start | bytes 1048576 | tf_op jit(solution)/shard_map/all_to_all | solution.py:265
  83.1 7.3 %collective-permute-start.14 = (f32[2,2,8,8,256]{4,3,2,1,0:T(8,128)S(1)}, f32[2,2,8,8,256]{4,3,2,1,0:T(8,128)S(1)}, u32[]{:S(2)}, u32[]{:S(2)}) collective-permute-start(f32[2,2,8,8,256]{4,3,2,1,0:T(8,128)S(1)} %slice.2305), channel_id=1, source_target_pairs={{0,1},{1,2},{2,3},{3,4},{4,5},{5,6},{6,7},{7,8},{8,9},{9,10},{10,1... | collective-permute-start | bytes 786440 | tf_op jit(solution)/shard_map/ppermute | solution.py:35
  87.1 3.3 %copy-start.1 = (f32[2,2,8,40,256]{4,3,2,1,0:T(8,128)S(1)}, f32[2,2,8,40,256]{4,3,2,1,0:T(8,128)}, u32[]{:S(2)}) copy-start(f32[2,2,8,40,256]{4,3,2,1,0:T(8,128)} %broadcast_dynamic-update-slice_fusion) | copy-start | bytes 3932164
  87.3 17.9 %collective-permute-start.15 = (f32[2,2,8,8,256]{4,3,2,1,0:T(8,128)S(1)}, f32[2,2,8,8,256]{4,3,2,1,0:T(8,128)S(1)}, u32[]{:S(2)}, u32[]{:S(2)}) collective-permute-start(f32[2,2,8,8,256]{4,3,2,1,0:T(8,128)S(1)} %slice.2305), channel_id=1, source_target_pairs={{1,0},{2,1},{3,2},{4,3},{5,4},{6,5},{7,6},{8,7},{9,8},{10,9},{11,1... | collective-permute-start | bytes 786440 | tf_op jit(solution)/shard_map/ppermute | solution.py:35
  90.5 16.8 %collective-permute-start.10 = (f32[2,2,8,8,256]{4,3,0,1,2:T(8,128)S(1)}, f32[2,2,8,8,256]{4,3,0,1,2:T(8,128)S(1)}, u32[]{:S(2)}, u32[]{:S(2)}) collective-permute-start(f32[2,2,8,8,256]{4,3,0,1,2:T(8,128)S(1)} %copy.481), channel_id=1, source_target_pairs={{0,2},{1,3},{2,4},{3,5},{4,6},{5,7},{6,8},{7,9},{8,10},{9,11},{10,... | collective-permute-start | bytes 786440 | tf_op jit(solution)/shard_map/ppermute | solution.py:35
  98.1 10.7 %collective-permute-start.11 = (f32[2,2,8,8,256]{4,3,0,1,2:T(8,128)S(1)}, f32[2,2,8,8,256]{4,3,0,1,2:T(8,128)S(1)}, u32[]{:S(2)}, u32[]{:S(2)}) collective-permute-start(f32[2,2,8,8,256]{4,3,0,1,2:T(8,128)S(1)} %copy.481), channel_id=1, source_target_pairs={{0,1},{1,2},{2,3},{3,4},{4,5},{5,6},{6,7},{7,8},{8,9},{9,10},{10,1... | collective-permute-start | bytes 786440 | tf_op jit(solution)/shard_map/ppermute | solution.py:35
  105.2 10.3 %collective-permute-start.12 = (f32[2,2,8,8,256]{4,3,0,1,2:T(8,128)S(1)}, f32[2,2,8,8,256]{4,3,0,1,2:T(8,128)S(1)}, u32[]{:S(2)}, u32[]{:S(2)}) collective-permute-start(f32[2,2,8,8,256]{4,3,0,1,2:T(8,128)S(1)} %copy.481), channel_id=1, source_target_pairs={{1,0},{2,1},{3,2},{4,3},{5,4},{6,5},{7,6},{8,7},{9,8},{10,9},{11,1... | collective-permute-start | bytes 786440 | tf_op jit(solution)/shard_map/ppermute | solution.py:35
  107.3 11.9 %collective-permute-start.13 = (f32[2,2,8,8,256]{4,3,0,1,2:T(8,128)S(1)}, f32[2,2,8,8,256]{4,3,0,1,2:T(8,128)S(1)}, u32[]{:S(2)}, u32[]{:S(2)}) collective-permute-start(f32[2,2,8,8,256]{4,3,0,1,2:T(8,128)S(1)} %copy.481), channel_id=1, source_target_pairs={{2,0},{3,1},{4,2},{5,3},{6,4},{7,5},{8,6},{9,7},{10,8},{11,9},{12,... | collective-permute-start | bytes 786440 | tf_op jit(solution)/shard_map/ppermute | solution.py:35
  119.2 1.1 copy-start.2
  133.4 6.5 %copy-start.9 = (s32[16,256]{1,0:T(8,128)S(1)}, s32[16,256]{1,0:T(8,128)}, u32[]{:S(2)}) copy-start(s32[16,256]{1,0:T(8,128)} %get-tuple-element.156) | copy-start | bytes 49156
  133.7 11.7 %copy-start.16 = (f32[2]{0:T(128)S(1)}, f32[2]{0:T(128)}, u32[]{:S(2)}) copy-start(f32[2]{0:T(128)} %copy-done.15) | copy-start | bytes 28
  133.7 11.7 %copy-start.18 = (f32[10]{0:T(128)S(1)}, f32[10]{0:T(128)}, u32[]{:S(2)}) copy-start(f32[10]{0:T(128)} %copy-done.17) | copy-start | bytes 124
  134.0 13.5 %collective-permute-start.16 = (f32[2,2,7,8,256]{4,3,0,2,1:T(8,128)S(1)}, f32[2,2,7,8,256]{4,3,0,2,1:T(8,128)S(1)}, u32[]{:S(2)}, u32[]{:S(2)}) collective-permute-start(f32[2,2,7,8,256]{4,3,0,2,1:T(8,128)S(1)} %slice.2345), channel_id=1, source_target_pairs={{0,2},{1,3},{2,4},{3,5},{4,6},{5,7},{6,8},{7,9},{8,10},{9,11},{10,... | collective-permute-start | bytes 688136 | tf_op jit(solution)/shard_map/ppermute | solution.py:35
  141.4 7.7 %collective-permute-start.17 = (f32[2,2,7,8,256]{4,3,0,2,1:T(8,128)S(1)}, f32[2,2,7,8,256]{4,3,0,2,1:T(8,128)S(1)}, u32[]{:S(2)}, u32[]{:S(2)}) collective-permute-start(f32[2,2,7,8,256]{4,3,0,2,1:T(8,128)S(1)} %slice.2345), channel_id=1, source_target_pairs={{0,1},{1,2},{2,3},{3,4},{4,5},{5,6},{6,7},{7,8},{8,9},{9,10},{10,1... | collective-permute-start | bytes 688136 | tf_op jit(solution)/shard_map/ppermute | solution.py:35
  145.6 8.9 %collective-permute-start.18 = (f32[2,2,7,8,256]{4,3,0,2,1:T(8,128)S(1)}, f32[2,2,7,8,256]{4,3,0,2,1:T(8,128)S(1)}, u32[]{:S(2)}, u32[]{:S(2)}) collective-permute-start(f32[2,2,7,8,256]{4,3,0,2,1:T(8,128)S(1)} %slice.2345), channel_id=1, source_target_pairs={{1,0},{2,1},{3,2},{4,3},{5,4},{6,5},{7,6},{8,7},{9,8},{10,9},{11,1... | collective-permute-start | bytes 688136 | tf_op jit(solution)/shard_map/ppermute | solution.py:35
  147.5 12.1 %collective-permute-start.19 = (f32[2,2,7,8,256]{4,3,0,2,1:T(8,128)S(1)}, f32[2,2,7,8,256]{4,3,0,2,1:T(8,128)S(1)}, u32[]{:S(2)}, u32[]{:S(2)}) collective-permute-start(f32[2,2,7,8,256]{4,3,0,2,1:T(8,128)S(1)} %slice.2345), channel_id=1, source_target_pairs={{2,0},{3,1},{4,2},{5,3},{6,4},{7,5},{8,6},{9,7},{10,8},{11,9},{12,... | collective-permute-start | bytes 688136 | tf_op jit(solution)/shard_map/ppermute | solution.py:35
  159.6 1.1 copy-start.3
  183.6 12.9 %all-to-all-start.2 = ((f32[2,2,16,8,256]{4,3,0,1,2:T(8,128)}), f32[2,2,16,8,256]{4,3,0,1,2:T(8,128)S(1)}, u32[]{:S(2)}, u32[]{:S(2)}) async-start(f32[2,2,16,8,256]{4,3,0,1,2:T(8,128)} %constant_dynamic-update-slice_fusion.21), calls=%async_computation.2 | async-start | bytes 1048576 | tf_op jit(solution)/shard_map/all_to_all | solution.py:300
  188.4 10.9 %copy-start.12 = (s32[16,256]{1,0:T(8,128)S(1)}, s32[16,256]{1,0:T(8,128)}, u32[]{:S(2)}) copy-start(s32[16,256]{1,0:T(8,128)} %get-tuple-element.22) | copy-start | bytes 49156
  196.5 2.9 %copy-start.4 = (pred[16,256,256]{1,2,0:T(8,128)(4,1)S(1)}, pred[16,256,256]{1,2,0:T(8,128)(4,1)}, u32[]{:S(2)}) copy-start(pred[16,256,256]{1,2,0:T(8,128)(4,1)} %iota_compare_fusion) | copy-start | bytes 3145732
  196.6 12.2 %collective-permute-start.20 = (f32[16,2,1,8,256]{4,3,2,0,1:T(8,128)S(1)}, f32[16,2,1,8,256]{4,3,2,0,1:T(8,128)S(1)}, u32[]{:S(2)}, u32[]{:S(2)}) collective-permute-start(f32[16,2,1,8,256]{4,3,2,0,1:T(8,128)S(1)} %get-tuple-element.82), channel_id=1, source_target_pairs={{0,32},{32,64},{64,96},{96,128},{128,160},{160,192},{192,224},{1,3... | collective-permute-start | bytes 786440 | tf_op jit(solution)/shard_map/ppermute | solution.py:26
  207.5 8.0 %collective-permute-start.21 = (f32[16,2,1,8,256]{4,3,2,0,1:T(8,128)S(1)}, f32[16,2,1,8,256]{4,3,2,0,1:T(8,128)S(1)}, u32[]{:S(2)}, u32[]{:S(2)}) collective-permute-start(f32[16,2,1,8,256]{4,3,2,0,1:T(8,128)S(1)} %get-tuple-element.81), channel_id=1, source_target_pairs={{32,0},{64,32},{96,64},{128,96},{160,128},{192,160},{224,192},{33,... | collective-permute-start | bytes 786440 | tf_op jit(solution)/shard_map/ppermute | solution.py:27
  208.8 16.8 %copy-start.10 = (f32[16,2,256]{2,1,0:T(2,128)S(1)}, f32[16,2,256]{2,1,0:T(2,128)}, u32[]{:S(2)}) copy-start(f32[16,2,256]{2,1,0:T(2,128)} %param.10) | copy-start | bytes 98308
  215.7 10.2 %collective-permute-start.22 = (f32[16,2,4,1,256]{4,3,2,0,1:T(1,128)S(1)}, f32[16,2,4,1,256]{4,3,2,0,1:T(1,128)S(1)}, u32[]{:S(2)}, u32[]{:S(2)}) collective-permute-start(f32[16,2,4,1,256]{4,3,2,0,1:T(1,128)S(1)} %get-tuple-element.41), channel_id=1, source_target_pairs={{0,1},{1,2},{2,3},{3,4},{4,5},{5,6},{6,7},{7,8},{8,9},{9,10},{10,1... | collective-permute-start | bytes 393224 | tf_op jit(solution)/shard_map/ppermute | solution.py:26
  223.4 7.8 %collective-permute-start.23 = (f32[16,2,4,1,256]{4,3,2,0,1:T(1,128)S(1)}, f32[16,2,4,1,256]{4,3,2,0,1:T(1,128)S(1)}, u32[]{:S(2)}, u32[]{:S(2)}) collective-permute-start(f32[16,2,4,1,256]{4,3,2,0,1:T(1,128)S(1)} %get-tuple-element.42), channel_id=1, source_target_pairs={{1,0},{2,1},{3,2},{4,3},{5,4},{6,5},{7,6},{8,7},{9,8},{10,9},{11,1... | collective-permute-start | bytes 393224 | tf_op jit(solution)/shard_map/ppermute | solution.py:27
  225.9 5.7 %copy-start.7 = (f32[2,10,256]{2,1,0:T(8,128)S(1)}, f32[2,10,256]{2,1,0:T(8,128)}, u32[]{:S(2)}) copy-start(f32[2,10,256]{2,1,0:T(8,128)} %copy-done.6) | copy-start | bytes 61444
  232.6 2.7 %copy-start.14 = (f32[2,8]{1,0:T(2,128)S(1)}, f32[2,8]{1,0:T(2,128)}, u32[]{:S(2)}) copy-start(f32[2,8]{1,0:T(2,128)} %copy-done.13) | copy-start | bytes 196
